TPU v7x, 32 devices: a whole 2x2x4 slice. The times are simulated.
32 devices in a mesh: tok: 8 (over z, y), grp: 4 (over x, core).
Axes of the slice: x: 2, y: 2, z: 4, core: 2. Of those that a mesh axis runs over, the one named last changes fastest.
Arguments:
- tokens: bfloat16 [4, 8192, 768], P('grp', 'tok'), may hold values from -6 to 6
- cotangent: bfloat16 [4, 8192, 768], P('grp', 'tok'), may hold values from -6 to 6
- lengths: int32 [4, 3], P('grp'), may hold values from 2048 to 4096, as said below
- clusters: int32 [4, 24, 8192], P('grp', None, 'tok'), may hold values from 0 to 31, as said below
- owners: int32 [12], replicated, may hold values from 0 to 3, as said below
- master: float32 [768, 12, 768], P('tok', 'grp')
- bases: float32 [2, 12, 768, 768], P(None, 'grp')
- moment_one: float32 [768, 12, 768], P('tok', 'grp')
- moment_two: float32 [768, 12, 768], P('tok', 'grp')
- vectors: float32 [12, 768], replicated
- vector_one: float32 [12, 768], replicated
- vector_two: float32 [12, 768], replicated
Outputs:
- output: bfloat16 [4, 8192, 768], P('grp', 'tok')
- grad_tokens: float32 [4, 8192, 768], P('grp', 'tok')
- new_moment_one: float32 [768, 12, 768], P('tok', 'grp')
- new_moment_two: float32 [768, 12, 768], P('tok', 'grp')
- new_master: float32 [768, 12, 768], P('tok', 'grp')
- new_vector_one: float32 [12, 768], replicated
- new_vector_two: float32 [12, 768], replicated
- new_vectors: float32 [12, 768], replicated
Inputs may be any that keep to these rules, and one draw needn't show every extreme that they name: `lengths`: in each group the items lie end to end and fill its 8192 tokens; 1 items have 4096 tokens and begin at multiples of 4096, all others have 2048. `clusters`: for every group, pair and item, each number below the item's length / 128 is given to exactly 128 of the item's tokens, and to the same number of tokens, 128 / (item length / 1024), from each run of 1024 consecutive tokens of the item. `owners`: every grp index owns exactly 12 / the size of grp blocks.
All inputs are finite; a program needn't handle non-finite values.
Results may differ from a plain program's by a relative error of at most 0.012.
The roundings to bfloat16 on the way count: a program that leaves them out, or rounds other values in their place, can miss the bound.
Values may be sent and summed in bfloat16 or wider, within the bound.
No kernel may reach another device: no remote copies, remote signals or barrier semaphores. Data moves between devices by JAX's collectives and lax.ppermute only.
A program may use at most 192 MiB of HBM per device.

v0:
```python
import jax
import jax.numpy as jnp
from jax import lax
from jax.sharding import PartitionSpec as P

D = 768
H = 12
FF = 3072
HEAD = 64
ROUNDS = 2
PAIRS = 24
CLUSTER = 128


EPS_NORM = 1e-05
ADAM_EPS = 1e-08
BETA_ONE = 0.5
BETA_TWO = 0.5
RATE_MATRIX = 0.025
RATE_VECTOR = 0.15
SQRT_HALF = 0.7071067811865476
INV_ROOT_TWO_PI = 0.3989422804014327


def inner_rows(left, right):
    return lax.dot_general(
        left, right, (((0,), (0,)), ((), ())), preferred_element_type=jnp.float32
    )


def outer_cols(left, right):
    return lax.dot_general(
        left, right, (((1,), (1,)), ((), ())), preferred_element_type=jnp.float32
    )


def normalize(values_in):
    centre = jnp.mean(values_in, axis=-1, keepdims=True)
    offset = values_in - centre
    spread = jnp.mean(offset * offset, axis=-1, keepdims=True)
    rstd = lax.rsqrt(spread + EPS_NORM)
    return (offset * rstd, rstd)


def norm_back(grad_normed, normed, rstd):
    first_mean = jnp.mean(grad_normed, axis=-1, keepdims=True)
    second_mean = jnp.mean(grad_normed * normed, axis=-1, keepdims=True)
    return rstd * (grad_normed - first_mean - normed * second_mean)


def gelu_slope(values_in):
    return (
        0.5 * (1.0 + lax.erf(values_in * SQRT_HALF))
        + values_in * jnp.exp(-0.5 * values_in * values_in) * INV_ROOT_TWO_PI
    )


def on_device(
    tokens,
    cotangent,
    lengths,
    clusters,
    owners,
    master,
    bases,
    moment_one,
    moment_two,
    vectors,
    vector_one,
    vector_two,
):
    n_tok = lax.axis_size("tok")
    tok_count = tokens.shape[1]
    rows_dev = master.shape[0]
    slot_block = jnp.argsort(owners, stable=True)
    block_slot = jnp.argsort(slot_block, stable=True)
    slot_part = lax.all_gather(master.astype(jnp.bfloat16), "grp", axis=1, tiled=True)
    weights = lax.all_gather(slot_part, "tok", axis=0, tiled=True)
    blocks = jnp.take(weights, block_slot, axis=1)
    w_qkv = blocks[:, 0:3, :].reshape(D, 3 * D)
    w_out = blocks[:, 3, :]
    w_up = blocks[:, 4 : 4 + FF // D, :].reshape(D, FF)
    w_down = jnp.transpose(blocks[:, 4 + FF // D :, :], (1, 0, 2)).reshape(FF, D)
    inputs = tokens[0]
    gain_one = vectors[0]
    shift_one = vectors[1]
    gain_two = vectors[2]
    shift_two = vectors[3]
    bias_qkv = jnp.concatenate([vectors[4], jnp.zeros((D,), jnp.float32), vectors[5]])
    qkv = (jnp.dot(inputs, w_qkv, preferred_element_type=jnp.float32) + bias_qkv).astype(
        jnp.bfloat16
    )
    heads = jnp.transpose(qkv.reshape(tok_count, 3, H, HEAD), (2, 0, 1, 3)).reshape(
        H, tok_count, 3 * HEAD
    )
    pair_rows = jnp.broadcast_to(heads[None], (ROUNDS, H, tok_count, 3 * HEAD)).reshape(
        PAIRS * tok_count, 3 * HEAD
    )
    position = lax.axis_index("tok") * tok_count + jnp.arange(tok_count, dtype=jnp.int32)
    item_lengths = lengths[0]
    item_ends = jnp.cumsum(item_lengths)
    item_starts = item_ends - item_lengths
    item_start = jnp.max(
        jnp.where(item_starts[None, :] <= position[:, None], item_starts[None, :], 0), axis=1
    )
    per_dev = tok_count // CLUSTER
    group_clusters = n_tok * per_dev
    pair_ids = jnp.arange(PAIRS, dtype=jnp.int32)[:, None]
    global_cluster = item_start[None, :] // CLUSTER + clusters[0]
    unit_ids = (pair_ids * group_clusters + global_cluster).reshape(-1)
    owner_ids = ((global_cluster + pair_ids * per_dev) % n_tok).reshape(-1)
    send_order = jnp.argsort(owner_ids * (PAIRS * group_clusters) + unit_ids, stable=True)
    restore = jnp.argsort(send_order, stable=True)
    slot_rows = PAIRS * tok_count // n_tok
    units_here = PAIRS * tok_count // CLUSTER
    sent_rows = pair_rows[send_order].reshape(n_tok, slot_rows // 2, 6 * HEAD)
    sent_units = unit_ids[send_order].reshape(n_tok, slot_rows)
    got_rows, got_units = (
        lax.all_to_all(sent_rows, "tok", split_axis=0, concat_axis=0, tiled=True),
        lax.all_to_all(sent_units, "tok", split_axis=0, concat_axis=0, tiled=True),
    )
    arrange = jnp.argsort(got_units.reshape(-1), stable=True)
    undo = jnp.argsort(arrange, stable=True)
    grouped = got_rows.reshape(PAIRS * tok_count, 3 * HEAD)[arrange].reshape(
        units_here, CLUSTER, 3 * HEAD
    )
    query_rows = grouped[..., :HEAD]
    key_rows = grouped[..., HEAD : 2 * HEAD]
    value_rows = grouped[..., 2 * HEAD :]
    score_scale = HEAD ** (-0.5)
    scores = (
        jnp.einsum("ucd,ued->uce", query_rows, key_rows, preferred_element_type=jnp.float32)
        * score_scale
    )
    row_max = jnp.max(scores, axis=-1, keepdims=True)
    row_total = jnp.sum(jnp.exp(scores - row_max), axis=-1, keepdims=True)
    log_total = row_max + jnp.log(row_total)
    probs = jnp.exp(scores - log_total)
    cluster_out = jnp.einsum(
        "uce,ued->ucd", probs.astype(jnp.bfloat16), value_rows, preferred_element_type=jnp.float32
    ).astype(jnp.bfloat16)
    back_rows = cluster_out.reshape(PAIRS * tok_count, HEAD)[undo].reshape(
        n_tok, slot_rows // 2, 2 * HEAD
    )
    home_rows = lax.all_to_all(back_rows, "tok", split_axis=0, concat_axis=0, tiled=True)
    home_rows = (
        home_rows.reshape(PAIRS * tok_count, HEAD)[restore]
        .reshape(ROUNDS, H, tok_count, HEAD)
        .astype(jnp.float32)
    )
    mixed_heads = 0.5 * (home_rows[0] + home_rows[1])
    mixed_low = jnp.transpose(mixed_heads, (1, 0, 2)).reshape(tok_count, D).astype(jnp.bfloat16)
    attention = jnp.dot(mixed_low, w_out, preferred_element_type=jnp.float32) + vectors[6]
    first_sum = inputs.astype(jnp.float32) + attention
    normed_one, rstd_one = normalize(first_sum)
    hidden = normed_one * gain_one + shift_one
    hidden_low = hidden.astype(jnp.bfloat16)
    up_proj = jnp.dot(hidden_low, w_up, preferred_element_type=jnp.float32) + vectors[8:].reshape(
        FF
    )
    act_low = jax.nn.gelu(up_proj, approximate=False).astype(jnp.bfloat16)
    down_proj = jnp.dot(act_low, w_down, preferred_element_type=jnp.float32) + vectors[7]
    second_sum = hidden + down_proj
    normed_two, rstd_two = normalize(second_sum)
    result = (normed_two * gain_two + shift_two).astype(jnp.bfloat16)
    grad_result = cotangent[0].astype(jnp.float32)
    grad_gain_two = jnp.sum(grad_result * normed_two, axis=0)
    grad_shift_two = jnp.sum(grad_result, axis=0)
    grad_second = norm_back(grad_result * gain_two, normed_two, rstd_two)
    grad_down_low = grad_second.astype(jnp.bfloat16)
    grad_w_down = inner_rows(act_low, grad_down_low)
    grad_bias_down = jnp.sum(grad_down_low.astype(jnp.float32), axis=0)
    grad_act = outer_cols(grad_down_low, w_down)
    grad_up_low = (grad_act * gelu_slope(up_proj)).astype(jnp.bfloat16)
    grad_w_up = inner_rows(hidden_low, grad_up_low)
    grad_bias_up = jnp.sum(grad_up_low.astype(jnp.float32), axis=0)
    grad_hidden = grad_second + outer_cols(grad_up_low, w_up)
    grad_gain_one = jnp.sum(grad_hidden * normed_one, axis=0)
    grad_shift_one = jnp.sum(grad_hidden, axis=0)
    grad_first = norm_back(grad_hidden * gain_one, normed_one, rstd_one)
    grad_attn_low = grad_first.astype(jnp.bfloat16)
    grad_w_out = inner_rows(mixed_low, grad_attn_low)
    grad_bias_out = jnp.sum(grad_attn_low.astype(jnp.float32), axis=0)
    grad_mixed = outer_cols(grad_attn_low, w_out)
    grad_heads = jnp.transpose((0.5 * grad_mixed).reshape(tok_count, H, HEAD), (1, 0, 2)).astype(
        jnp.bfloat16
    )
    grad_pairs = jnp.broadcast_to(grad_heads[None], (ROUNDS, H, tok_count, HEAD)).reshape(
        PAIRS * tok_count, HEAD
    )
    sent_grad = grad_pairs[send_order].reshape(n_tok, slot_rows // 2, 2 * HEAD)
    got_grad = lax.all_to_all(sent_grad, "tok", split_axis=0, concat_axis=0, tiled=True)
    grad_cluster = got_grad.reshape(PAIRS * tok_count, HEAD)[arrange].reshape(
        units_here, CLUSTER, HEAD
    )
    scores_again = (
        jnp.einsum("ucd,ued->uce", query_rows, key_rows, preferred_element_type=jnp.float32)
        * score_scale
    )
    probs_again = jnp.exp(scores_again - log_total)
    probs_low = probs_again.astype(jnp.bfloat16)
    grad_values = jnp.einsum(
        "uce,ucd->ued", probs_low, grad_cluster, preferred_element_type=jnp.float32
    )
    grad_probs = jnp.einsum(
        "ucd,ued->uce", grad_cluster, value_rows, preferred_element_type=jnp.float32
    )
    centre = jnp.sum(probs_again * grad_probs, axis=-1, keepdims=True)
    grad_scores = (probs_again * (grad_probs - centre)).astype(jnp.bfloat16)
    grad_query = (
        jnp.einsum("uce,ued->ucd", grad_scores, key_rows, preferred_element_type=jnp.float32)
        * score_scale
    )
    grad_keys = (
        jnp.einsum("uce,ucd->ued", grad_scores, query_rows, preferred_element_type=jnp.float32)
        * score_scale
    )
    grad_grouped = jnp.concatenate(
        [
            grad_query.astype(jnp.bfloat16),
            grad_keys.astype(jnp.bfloat16),
            grad_values.astype(jnp.bfloat16),
        ],
        axis=-1,
    )
    back_grad = grad_grouped.reshape(PAIRS * tok_count, 3 * HEAD)[undo].reshape(
        n_tok, slot_rows // 2, 6 * HEAD
    )
    home_grad = lax.all_to_all(back_grad, "tok", split_axis=0, concat_axis=0, tiled=True)
    home_grad = (
        home_grad.reshape(PAIRS * tok_count, 3 * HEAD)[restore]
        .reshape(ROUNDS, H, tok_count, 3, HEAD)
        .astype(jnp.float32)
    )
    grad_qkv = (home_grad[0] + home_grad[1]).astype(jnp.bfloat16)
    grad_qkv = jnp.transpose(grad_qkv, (1, 2, 0, 3)).reshape(tok_count, 3 * D)
    grad_w_qkv = inner_rows(inputs, grad_qkv)
    grad_bias_qkv = jnp.sum(grad_qkv.astype(jnp.float32), axis=0)
    grad_inputs = grad_first + outer_cols(grad_qkv, w_qkv)
    grad_blocks = jnp.concatenate(
        [
            grad_w_qkv.reshape(D, 3, D),
            grad_w_out[:, None, :],
            grad_w_up.reshape(D, FF // D, D),
            jnp.transpose(grad_w_down.reshape(FF // D, D, D), (1, 0, 2)),
        ],
        axis=1,
    )
    slot_grads = jnp.take(grad_blocks, slot_block, axis=1)
    vector_grads = jnp.concatenate(
        [
            jnp.stack(
                [
                    grad_gain_one,
                    grad_shift_one,
                    grad_gain_two,
                    grad_shift_two,
                    grad_bias_qkv[:D],
                    grad_bias_qkv[2 * D :],
                    grad_bias_out,
                    grad_bias_down,
                ]
            ),
            grad_bias_up.reshape(FF // D, D),
        ],
        axis=0,
    )
    vector_total = lax.psum(vector_grads, ("tok", "grp"))
    row_total = lax.psum_scatter(slot_grads, "tok", scatter_dimension=0, tiled=True)
    reduced = lax.psum_scatter(
        row_total.astype(jnp.bfloat16), "grp", scatter_dimension=1, tiled=True
    ).astype(jnp.float32)
    left_basis = bases[0]
    right_basis = bases[1]
    first_row = lax.axis_index("tok") * rows_dev
    turned_in = jnp.einsum("rse,sef->rsf", reduced, right_basis, precision=lax.Precision.HIGHEST)
    left_rows = lax.dynamic_slice_in_dim(left_basis, first_row, rows_dev, 1)
    picked = left_rows
    rotated = lax.psum_scatter(
        jnp.einsum("sri,rsf->isf", picked, turned_in, precision=lax.Precision.HIGHEST),
        "tok",
        scatter_dimension=0,
        tiled=True,
    )
    new_one = BETA_ONE * moment_one + (1.0 - BETA_ONE) * rotated
    new_two = BETA_TWO * moment_two + (1.0 - BETA_TWO) * rotated * rotated
    direction = new_one / (jnp.sqrt(new_two) + ADAM_EPS)
    turned_out = jnp.einsum("rse,sfe->rsf", direction, right_basis, precision=lax.Precision.HIGHEST)
    left_cols = lax.dynamic_slice_in_dim(left_basis, first_row, rows_dev, 2)
    picked = left_cols
    change = lax.psum_scatter(
        jnp.einsum("sir,rsf->isf", picked, turned_out, precision=lax.Precision.HIGHEST),
        "tok",
        scatter_dimension=0,
        tiled=True,
    )
    new_master = master - RATE_MATRIX * change
    new_vec_one = BETA_ONE * vector_one + (1.0 - BETA_ONE) * vector_total
    new_vec_two = BETA_TWO * vector_two + (1.0 - BETA_TWO) * vector_total * vector_total
    new_vectors = vectors - RATE_VECTOR * new_vec_one / (jnp.sqrt(new_vec_two) + ADAM_EPS)
    return (
        result[None],
        grad_inputs[None],
        new_one,
        new_two,
        new_master,
        new_vec_one,
        new_vec_two,
        new_vectors,
    )


def solution(mesh):
    return jax.shard_map(
        on_device,
        mesh=mesh,
        in_specs=(
            P("grp", "tok", None),
            P("grp", "tok", None),
            P("grp", None),
            P("grp", None, "tok"),
            P(),
            P("tok", "grp", None),
            P(None, "grp", None, None),
            P("tok", "grp", None),
            P("tok", "grp", None),
            P(),
            P(),
            P(),
        ),
        out_specs=(
            P("grp", "tok", None),
            P("grp", "tok", None),
            P("tok", "grp", None),
            P("tok", "grp", None),
            P("tok", "grp", None),
            P(),
            P(),
            P(),
        ),
        check_vma=False,
    )
```

profile of v0, /device:TPU:0, one launch (start us, length us, event | category | flops | bytes accessed | tf_op | source)
XLA Modules:
  0.0 2889.7 jit_solution(7646733344304736696)
XLA Ops:
  9.3 24.4 all-gather.3.cloned.1.call-done
  36.5 11.3 sort.92
  47.9 240.6 %gather_fusion.2 = s32[24576]{0:T(1024)} fusion(s32[24576]{0:T(1024)S(1)} %get-tuple-element.87, s32[24576]{0:T(1024)S(1)} %fusion.81), kind=kCustom, calls=%fused_computation.2 | custom fusion | bytes 294912 | tf_op jit(solution)/shard_map/gather | solution.py:117
  297.8 11.7 gather_fusion
  351.3 97.0 %gather_fusion.1 = bf16[24576,192]{1,0:T(8,128)(2,1)} fusion(bf16[24576,192]{1,0:T(8,128)(2,1)} %bitcast.157, s32[24576]{0:T(1024)S(1)} %copy-done.18), kind=kCustom, calls=%fused_computation.1 | custom fusion | bytes 18972672 | tf_op jit(solution)/shard_map/gather | solution.py:116
  448.3 19.1 reshape.261
  473.5 12.0 sort.93
  485.6 11.5 sort.94
  497.1 181.7 %all-to-all-done = bf16[8,1536,384]{2,1,0:T(8,128)(2,1)} async-done(((bf16[8,1536,384]{2,1,0:T(8,128)(2,1)}), bf16[8,1536,384]{2,1,0:T(8,128)(2,1)}, u32[]{:S(2)}, u32[]{:S(2)}) %all-to-all-start) | async-done | bytes 9437216 | tf_op jit(solution)/shard_map/all_to_all | solution.py:119
  678.8 18.8 reshape.262
  697.6 97.4 %gather_fusion.3 = bf16[24576,192]{1,0:T(8,128)(2,1)} fusion(bf16[24576,192]{1,0:T(8,128)(2,1)} %reshape.262, s32[24576]{0:T(1024)S(1)} %fusion.82), kind=kCustom, calls=%fused_computation.3 | custom fusion | bytes 18972672 | tf_op jit(solution)/shard_map/gather | solution.py:124
  795.0 13.8 multiply_reduce_fusion.1
  817.0 9.3 fusion.47
  830.8 85.7 %gather_fusion.4 = bf16[24576,64]{1,0:T(8,128)(2,1)} fusion(bf16[24576,64]{1,0:T(8,128)(2,1)} %bitcast.159, s32[24576]{0:T(1024)S(1)} %fusion.83), kind=kCustom, calls=%fused_computation.4 | custom fusion | bytes 6389760 | tf_op jit(solution)/shard_map/gather | solution.py:142
  916.5 9.0 reshape.266
  932.1 11.3 sort.95
  960.7 39.6 %all-to-all-done.2 = bf16[8,1536,128]{2,1,0:T(8,128)(2,1)S(1)} async-done(((bf16[8,1536,128]{2,1,0:T(8,128)(2,1)}), bf16[8,1536,128]{2,1,0:T(8,128)(2,1)S(1)}, u32[]{:S(2)}, u32[]{:S(2)}) %all-to-all-start.2) | async-done | bytes 3145760 | tf_op jit(solution)/shard_map/all_to_all | solution.py:145
  1006.1 85.8 %gather_fusion.5 = bf16[24576,64]{1,0:T(8,128)(2,1)} fusion(bf16[24576,64]{1,0:T(8,128)(2,1)} %reshape.267, s32[24576]{0:T(1024)S(1)} %fusion.84), kind=kCustom, calls=%fused_computation.5 | custom fusion | bytes 6389760 | tf_op jit(solution)/shard_map/gather | solution.py:147
  1103.3 36.1 %fusion.2 = (bf16[1024,3072]{1,0:T(8,128)(2,1)S(1)}, f32[1024,3072]{1,0:T(8,128)}) fusion(f32[3072]{0:T(1024)S(1)} %add.264, bf16[768,3072]{0,1:T(8,128)(2,1)} %bitcast.177, f32[1024,768]{0,1:T(8,128)S(1)} %get-tuple-element.94, f32[768]{0:T(1024)S(1)} %copy-done.41, f32[768]{0:T(1024)S(1)} %copy-done.35, f32[1024]{0:T(1024)S(1)} %add_rsqrt_fusion.1, ...), kind=kOutput, calls=%fused_computation.18 | convolution fusion | flops 5043388416 | bytes 26765312 | tf_op jit(solution)/shard_map/dot_general | solution.py:158
  1150.9 14.6 convert_reduce_fusion
  1165.5 9.9 multiply_reduce_fusion.2
  1192.9 85.8 %gather_fusion.6 = bf16[24576,64]{1,0:T(8,128)(2,1)} fusion(bf16[24576,64]{1,0:T(8,128)(2,1)} %bitcast.158, s32[24576]{0:T(1024)S(1)} %copy-done.19), kind=kCustom, calls=%fused_computation.6 | custom fusion | bytes 6389760 | tf_op jit(solution)/shard_map/gather | solution.py:191
  1278.7 9.0 reshape.271
  1287.7 74.9 %all_to_all.29 = bf16[8,1536,128]{2,1,0:T(8,128)(2,1)} all-to-all(bf16[8,1536,128]{2,1,0:T(8,128)(2,1)} %reshape.271), channel_id=1, replica_groups=mesh['tok'=8,'grp'=4] {'tok'}, dimensions={0} | all-to-all | bytes 6291456 | tf_op jit(solution)/shard_map/all_to_all | solution.py:192
  1371.3 85.7 %gather_fusion.7 = bf16[24576,64]{1,0:T(8,128)(2,1)} fusion(bf16[24576,64]{1,0:T(8,128)(2,1)} %reshape.272, s32[24576]{0:T(1024)S(1)} %copy-done.27), kind=kCustom, calls=%fused_computation.7 | custom fusion | bytes 6389760 | tf_op jit(solution)/shard_map/gather | solution.py:193
  1457.0 13.8 multiply_reduce_fusion
  1470.9 10.2 multiply_convert_fusion
  1483.8 9.5 multiply_convert_fusion.2
  1493.2 10.6 multiply_convert_fusion.1
  1517.7 14.8 copy.216
  1532.5 97.0 %gather_fusion.8 = bf16[24576,192]{1,0:T(8,128)(2,1)} fusion(bf16[24576,192]{1,0:T(8,128)(2,1)} %bitcast.156, s32[24576]{0:T(1024)S(1)} %copy-done.23), kind=kCustom, calls=%fused_computation.8 | custom fusion | bytes 18972672 | tf_op jit(solution)/shard_map/gather | solution.py:226
  1629.5 19.1 reshape.275
  1667.4 10.3 fusion.105
  1677.7 180.7 %all-to-all-done.4 = bf16[8,1536,384]{2,1,0:T(8,128)(2,1)} async-done(((bf16[8,1536,384]{2,1,0:T(8,128)(2,1)}), bf16[8,1536,384]{2,1,0:T(8,128)(2,1)}, u32[]{:S(2)}, u32[]{:S(2)}) %all-to-all-start.4) | async-done | bytes 9437216 | tf_op jit(solution)/shard_map/all_to_all | solution.py:229
  1858.4 18.8 reshape.276
  1877.2 97.0 %gather_fusion.9 = bf16[24576,192]{1,0:T(8,128)(2,1)} fusion(bf16[24576,192]{1,0:T(8,128)(2,1)} %reshape.276, s32[24576]{0:T(1024)S(1)} %copy-done.25), kind=kCustom, calls=%fused_computation.9 | custom fusion | bytes 18972672 | tf_op jit(solution)/shard_map/gather | solution.py:231
  2020.8 19.9 pad_maximum_fusion
  2040.7 20.8 gather_fusion.10
  2061.5 21.1 select_bitcast_fusion
  2082.6 447.6 %reduce-scatter.9.cloned.1.call-done = f32[96,12,768]{2,0,1:T(8,128)} async-done(((f32[768,12,768]{2,0,1:T(8,128)}), f32[96,12,768]{2,0,1:T(8,128)}) %reduce-scatter.9.cloned.1.call-update) | async-done | bytes 3538960 | tf_op jit(solution)/shard_map/reduce_scatter | solution.py:269
  2540.2 22.2 reduce-scatter.11.cloned.1.call-done
  2568.1 9.4 fusion.71
  2588.5 126.2 %reduce-scatter.13.cloned.1.call-done = f32[96,2304]{1,0:T(8,128)} async-done(((f32[768,2304]{1,0:T(8,128)}), f32[96,2304]{1,0:T(8,128)}) %reduce-scatter.13.cloned.1.call-update) | async-done | bytes 884752
  2719.1 10.4 fusion.61
  2729.5 10.8 fusion.65
  2758.8 10.0 add_bitcast_fusion
  2772.5 42.8 %psum.7 = f32[12,768]{1,0:T(8,128)S(1)} all-reduce(f32[12,768]{1,0:T(8,128)S(1)} %concatenate.15), channel_id=1, replica_groups=mesh['tok'=8,'grp'=4] {'tok','grp'}, use_global_device_ids=true, to_apply=%region_31.32 | all-reduce | flops 9216 | bytes 73728 | tf_op jit(solution)/shard_map/psum | solution.py:268
  2818.6 59.9 %reduce-scatter.15.cloned.1.call-done = f32[96,2304]{1,0:T(8,128)} async-done(((f32[768,2304]{1,0:T(8,128)}), f32[96,2304]{1,0:T(8,128)}) %reduce-scatter.15.cloned.1.call-update) | async-done | bytes 884752
  (251 shorter events, 296.0 us)
Async XLA Ops:
  7.2 26.5 all-gather.3.cloned.1.call-start
  9.2 288.6 %all-gather.5.cloned.1.call-start = ((), (), s32[]{:S(2)}) async-start(), calls=%async_computation.10 | async-start | bytes 15925248 | tf_op jit(solution)/shard_map/all_gather | solution.py:78
  47.8 240.7 %copy-start.28 = (s32[24576]{0:T(1024)}, s32[24576]{0:T(1024)S(1)}, u32[]{:S(2)}) copy-start(s32[24576]{0:T(1024)S(1)} %get-tuple-element.16) | copy-start | bytes 294916
  47.8 240.7 %copy-start.17 = (s32[24576]{0:T(1024)}, s32[24576]{0:T(1024)S(1)}, u32[]{:S(2)}) copy-start(s32[24576]{0:T(1024)S(1)} %fusion.81) | copy-start | bytes 294916
  47.8 246.7 %copy-start.47 = (s32[12]{0:T(128)S(1)}, s32[12]{0:T(128)}, u32[]{:S(2)}) copy-start(s32[12]{0:T(128)} %param.16) | copy-start | bytes 148
  47.9 249.2 %copy-start.30 = (f32[12,768]{1,0:T(8,128)S(1)}, f32[12,768]{1,0:T(8,128)}, u32[]{:S(2)}) copy-start(f32[12,768]{1,0:T(8,128)} %param.21) | copy-start | bytes 110596
  288.5 178.8 %all-to-all-start.1 = ((s32[8,1,3072]{2,1,0:T(1,128)}), s32[8,1,3072]{2,1,0:T(1,128)}, u32[]{:S(2)}, u32[]{:S(2)}) async-start(s32[8,1,3072]{2,1,0:T(1,128)} %bitcast.9), calls=%async_computation.1 | async-start | bytes 196608 | tf_op jit(solution)/shard_map/all_to_all | solution.py:120
  317.2 5.1 copy-start.1
  343.1 8.2 copy-start.18
  467.4 211.5 %all-to-all-start = ((bf16[8,1536,384]{2,1,0:T(8,128)(2,1)}), bf16[8,1536,384]{2,1,0:T(8,128)(2,1)}, u32[]{:S(2)}, u32[]{:S(2)}) async-start(bf16[8,1536,384]{2,1,0:T(8,128)(2,1)} %reshape.261), calls=%async_computation | async-start | bytes 18874368 | tf_op jit(solution)/shard_map/all_to_all | solution.py:119
  497.1 200.5 %copy-start.26 = (s32[24576]{0:T(1024)}, s32[24576]{0:T(1024)S(1)}, u32[]{:S(2)}) copy-start(s32[24576]{0:T(1024)S(1)} %fusion.82) | copy-start | bytes 294916
  497.1 333.7 %copy-start.22 = (s32[24576]{0:T(1024)}, s32[24576]{0:T(1024)S(1)}, u32[]{:S(2)}) copy-start(s32[24576]{0:T(1024)S(1)} %fusion.83) | copy-start | bytes 294916
  817.0 9.3 copy-start.11
  925.4 6.6 copy-start.29
  925.4 17.9 slice-start.4
  925.4 74.8 %all-to-all-start.2 = ((bf16[8,1536,128]{2,1,0:T(8,128)(2,1)}), bf16[8,1536,128]{2,1,0:T(8,128)(2,1)S(1)}, u32[]{:S(2)}, u32[]{:S(2)}) async-start(bf16[8,1536,128]{2,1,0:T(8,128)(2,1)} %reshape.266), calls=%async_computation.2 | async-start | bytes 6291456 | tf_op jit(solution)/shard_map/all_to_all | solution.py:145
  946.0 60.1 %copy-start.24 = (s32[24576]{0:T(1024)}, s32[24576]{0:T(1024)S(1)}, u32[]{:S(2)}) copy-start(s32[24576]{0:T(1024)S(1)} %fusion.84) | copy-start | bytes 294916
  1098.9 40.5 %slice-start.2 = ((s8[4718592]{0:T(1024)(128)(4,1)}), s8[4194304]{0:T(1024)(128)(4,1)S(1)}, s32[]{:S(2)}) async-start(s8[4718592]{0:T(1024)(128)(4,1)} %bitcast.185), calls=%async_computation.17 | async-start | bytes 8388608
  1103.3 36.1 %slice-start.3 = ((s8[4718592]{0:T(1024)(128)(4,1)}), s8[524288]{0:T(1024)(128)(4,1)S(1)}, s32[]{:S(2)}) async-start(s8[4718592]{0:T(1024)(128)(4,1)} %bitcast.185), calls=%async_computation.18 | async-start | bytes 1048576
  1103.3 36.1 %copy-start.43 = (f32[768]{0:T(1024)S(1)}, f32[768]{0:T(1024)}, u32[]{:S(2)}) copy-start(f32[768]{0:T(1024)} %get-tuple-element.68) | copy-start | bytes 9220
  1139.4 6.0 copy-start.50
  1139.4 6.4 copy-start.2
  1139.4 6.4 copy-start.34
  1147.7 17.8 slice-start
  1150.9 14.6 copy-start.15
  1150.9 14.6 slice-start.1
  1182.6 10.3 copy-start.19
  1287.7 83.7 %copy-start.27 = (s32[24576]{0:T(1024)S(1)}, s32[24576]{0:T(1024)}, u32[]{:S(2)}) copy-start(s32[24576]{0:T(1024)} %copy-done.26) | copy-start | bytes 294916
  1371.3 85.7 %copy-start.12 = (f32[192,128]{1,0:T(8,128)S(1)}, f32[192,128]{1,0:T(8,128)}, u32[]{:S(2)}) copy-start(f32[192,128]{1,0:T(8,128)} %copy-done.11) | copy-start | bytes 294916
  1503.8 8.8 copy-start.4
  1503.8 8.8 copy-start.5
  1517.7 14.8 copy-start.23
  1648.6 5.3 copy-start.49
  1648.6 5.4 copy-start.42
  1648.6 209.8 %all-to-all-start.4 = ((bf16[8,1536,384]{2,1,0:T(8,128)(2,1)}), bf16[8,1536,384]{2,1,0:T(8,128)(2,1)}, u32[]{:S(2)}, u32[]{:S(2)}) async-start(bf16[8,1536,384]{2,1,0:T(8,128)(2,1)} %reshape.275), calls=%async_computation.4 | async-start | bytes 18874368 | tf_op jit(solution)/shard_map/all_to_all | solution.py:229
  1653.9 876.3 %reduce-scatter.9.cloned.1.call-start = ((), (), s32[]{:S(2)}) async-start(), calls=%async_computation.11 | async-start | bytes 31850496 | tf_op jit(solution)/shard_map/reduce_scatter | solution.py:269
  1661.3 4.6 copy-start.10
  1677.7 199.5 %copy-start.25 = (s32[24576]{0:T(1024)S(1)}, s32[24576]{0:T(1024)}, u32[]{:S(2)}) copy-start(s32[24576]{0:T(1024)} %copy-done.24) | copy-start | bytes 294916
  2001.3 5.5 copy-start.13
  2006.9 5.9 copy-start.8
  2082.5 479.8 %reduce-scatter.11.cloned.1.call-start = ((), (), s32[]{:S(2)}) async-start(), calls=%async_computation.12 | async-start | bytes 2211840 | tf_op jit(solution)/shard_map/reduce_scatter | solution.py:270
  2533.7 180.9 %reduce-scatter.13.cloned.1.call-start = ((), (), s32[]{:S(2)}) async-start(), calls=%async_computation.13 | async-start | bytes 7962624
  2585.6 292.9 %reduce-scatter.15.cloned.1.call-start = ((), (), s32[]{:S(2)}) async-start(), calls=%async_computation.14 | async-start | bytes 7962624
  2719.1 21.2 copy-start.6
  2768.7 46.6 %copy-start.31 = (f32[12,768]{1,0:T(8,128)S(1)}, f32[12,768]{1,0:T(8,128)}, u32[]{:S(2)}) copy-start(f32[12,768]{1,0:T(8,128)} %param.21) | copy-start | bytes 110596
  2768.7 46.6 %copy-start.32 = (f32[12,768]{1,0:T(8,128)S(1)}, f32[12,768]{1,0:T(8,128)}, u32[]{:S(2)}) copy-start(f32[12,768]{1,0:T(8,128)} %param.23) | copy-start | bytes 110596
  2768.7 46.6 %copy-start.33 = (f32[12,768]{1,0:T(8,128)S(1)}, f32[12,768]{1,0:T(8,128)}, u32[]{:S(2)}) copy-start(f32[12,768]{1,0:T(8,128)} %param.22) | copy-start | bytes 110596
  2768.7 47.3 %copy-start.7 = (f32[96,3,768]{0,2,1:T(8,128)S(1)}, f32[96,3,768]{0,2,1:T(8,128)}, u32[]{:S(2)}) copy-start(f32[96,3,768]{0,2,1:T(8,128)} %copy-done.6) | copy-start | bytes 2654212
  (18 other events, 49.7 us)
Sparse Core Ops, SparseCore 0:
  10.1 23.4 all-gather.2
  35.8 195.6 all-gather.4
  2082.7 447.5 reduce-scatter.8
  2533.9 28.4 reduce-scatter.10
  2585.7 128.9 reduce-scatter.12
  2748.6 129.8 reduce-scatter.14
where the time goes:
time: 2900 us; the launch traced here: 2890 us
  local copies, waits for them, and re-layouts  1280 us (44%)
  waiting for transfers between devices  1080 us (37%)
  matrix products  217 us (7%)
  other arithmetic  159 us (5%)
  blocking collectives  118 us (4%)
    reduce_scatter x1, waiting for transfers between devices, on_device(): lax.psum_scatter(slot_grads, 'tok', scatter_dimension=0, tiled=True)  448 us
    gather x1, local copies, waits for them, and re-layouts, on_device(): sent_units = unit_ids[send_order].reshape(n_tok, slot_rows)  241 us
    unnamed x8, waiting for transfers between devices  186 us
    all_to_all x1, waiting for transfers between devices, on_device(): lax.all_to_all(sent_rows, 'tok', split_axis=0, concat_axis=0, tiled=True)  182 us
    all_to_all x1, waiting for transfers between devices, on_device(): lax.all_to_all(back_grad, 'tok', split_axis=0, concat_axis=0, tiled=True)  181 us
    gather x1, local copies, waits for them, and re-layouts, on_device(): got_rows.reshape(PAIRS * tok_count, 3 * HEAD)[arrange]  97.4 us
    gather x1, local copies, waits for them, and re-layouts, on_device(): grad_grouped.reshape(PAIRS * tok_count, 3 * HEAD)[undo]  97 us
    gather x1, local copies, waits for them, and re-layouts, on_device(): home_grad.reshape(PAIRS * tok_count, 3 * HEAD)[restore]  97 us
  transfers between devices with their start and end apart: 10, of which 8 were waited for; matrix products, arithmetic and copies ran while one was open for 19% of the time, Pallas kernels for 0%

commit v1 on v0

--- a/solution.py
+++ b/solution.py
@@ -1,6 +1,10 @@
+import functools
+
 import jax
 import jax.numpy as jnp
 from jax import lax
+from jax.experimental import pallas as pl
+from jax.experimental.pallas import tpu as pltpu
 from jax.sharding import PartitionSpec as P
 
 D = 768
@@ -10,7 +14,7 @@
 ROUNDS = 2
 PAIRS = 24
 CLUSTER = 128
-
+FFB = FF // D
 
 EPS_NORM = 1e-05
 ADAM_EPS = 1e-08
@@ -21,17 +25,22 @@
 SQRT_HALF = 0.7071067811865476
 INV_ROOT_TWO_PI = 0.3989422804014327
 
+BF16 = jnp.bfloat16
+F32 = jnp.float32
+
+UNIT = 4
+HEADS_OWN = H // UNIT
+LOCAL_PAIRS = ROUNDS * HEADS_OWN
+TILE = 128
+WIDE = 2 * TILE
+
 
 def inner_rows(left, right):
-    return lax.dot_general(
-        left, right, (((0,), (0,)), ((), ())), preferred_element_type=jnp.float32
-    )
+    return lax.dot_general(left, right, (((0,), (0,)), ((), ())), preferred_element_type=F32)
 
 
 def outer_cols(left, right):
-    return lax.dot_general(
-        left, right, (((1,), (1,)), ((), ())), preferred_element_type=jnp.float32
-    )
+    return lax.dot_general(left, right, (((1,), (1,)), ((), ())), preferred_element_type=F32)
 
 
 def normalize(values_in):
@@ -55,7 +64,556 @@
     )
 
 
-def on_device(
+def sort_body(order_ref, rows_ref, out_ref, column_ref):
+    count = rows_ref.shape[0]
+
+    @pl.when(pl.program_id(0) == 0)
+    def _():
+        column_ref[...] = jnp.transpose(order_ref[...])
+
+    head = pl.program_id(0)
+    chunk = 256
+    lane = lax.broadcasted_iota(jnp.int32, (chunk, count), 1)
+    for step in range(HEADS_OWN):
+
+        @pl.when(head == step)
+        def _():
+            for turn in range(ROUNDS):
+                pair = step * ROUNDS + turn
+                for part in range(count // chunk):
+                    where = pl.ds(part * chunk, chunk)
+                    picked = (column_ref[where, pair : pair + 1] == lane).astype(F32).astype(BF16)
+                    out_ref[turn, where, :] = jnp.dot(
+                        picked, rows_ref[...], preferred_element_type=F32
+                    ).astype(BF16)
+
+
+def sort_rows(order, rows, width):
+    count = rows.shape[0]
+    return pl.pallas_call(
+        sort_body,
+        grid=(HEADS_OWN,),
+        in_specs=[
+            pl.BlockSpec((8, count), lambda h: (0, 0)),
+            pl.BlockSpec((count, width), lambda h: (0, h)),
+        ],
+        out_specs=pl.BlockSpec((ROUNDS, count, width), lambda h: (h, 0, 0)),
+        out_shape=jax.ShapeDtypeStruct((LOCAL_PAIRS, count, width), BF16),
+        scratch_shapes=[pltpu.VMEM((count, 8), jnp.int32)],
+        compiler_params=pltpu.CompilerParams(vmem_limit_bytes=48 << 20),
+        name="sort_rows",
+    )(order, rows)
+
+
+def sort_grads_body(order_ref, rows_ref, out_ref, column_ref):
+    count = rows_ref.shape[0]
+
+    @pl.when(pl.program_id(0) == 0)
+    def _():
+        column_ref[...] = jnp.transpose(order_ref[...])
+
+    head = pl.program_id(0)
+    chunk = 256
+    lane = lax.broadcasted_iota(jnp.int32, (chunk, count), 1)
+    low = lax.broadcasted_iota(jnp.int32, (count, TILE), 1) < HEAD
+    for step in range(HEADS_OWN):
+
+        @pl.when(head == step)
+        def _():
+            tile = rows_ref[:, (step // 2) * TILE : (step // 2 + 1) * TILE]
+            mask = low if step % 2 == 0 else jnp.logical_not(low)
+            tile = jnp.where(mask, tile.astype(F32), 0.0).astype(BF16)
+            for turn in range(ROUNDS):
+                pair = step * ROUNDS + turn
+                for part in range(count // chunk):
+                    where = pl.ds(part * chunk, chunk)
+                    picked = (column_ref[where, pair : pair + 1] == lane).astype(F32).astype(BF16)
+                    out_ref[turn, where, :] = jnp.dot(
+                        picked, tile, preferred_element_type=F32
+                    ).astype(BF16)
+
+
+def sort_grads(order, rows):
+    count = rows.shape[0]
+    return pl.pallas_call(
+        sort_grads_body,
+        grid=(HEADS_OWN,),
+        in_specs=[
+            pl.BlockSpec((8, count), lambda h: (0, 0)),
+            pl.BlockSpec((count, WIDE), lambda h: (0, 0)),
+        ],
+        out_specs=pl.BlockSpec((ROUNDS, count, TILE), lambda h: (h, 0, 0)),
+        out_shape=jax.ShapeDtypeStruct((LOCAL_PAIRS, count, TILE), BF16),
+        scratch_shapes=[pltpu.VMEM((count, 8), jnp.int32)],
+        compiler_params=pltpu.CompilerParams(vmem_limit_bytes=48 << 20),
+        name="sort_grads",
+    )(order, rows)
+
+
+def clusters_of(count):
+    share_long = CLUSTER // UNIT
+    share_short = 2 * share_long
+    return (
+        [(tuple(range(UNIT)), share_long, count // share_long)],
+        [
+            (tuple(range(half * UNIT // 2, (half + 1) * UNIT // 2)), share_short, count // share_short)
+            for half in range(2)
+        ],
+    )
+
+
+def for_each_cluster(is_long, count, unroll, work):
+    long_plan, short_plan = clusters_of(count)
+    for wanted, plan in ((1, long_plan), (0, short_plan)):
+
+        @pl.when(is_long == wanted)
+        def _(plan=plan):
+            for runs, share, clusters in plan:
+
+                def step(group, carry, runs=runs, share=share):
+                    for inner in range(unroll):
+                        first = pl.multiple_of((group * unroll + inner) * share, share)
+                        work(runs, pl.ds(first, share), share)
+                    return carry
+
+                lax.fori_loop(0, clusters // unroll, step, 0)
+
+
+def softmax(rows):
+    first, second = rows[:, :TILE], rows[:, TILE:]
+    scores = outer_cols(first, second) * (HEAD**-0.5)
+    peak = jnp.max(scores, axis=-1, keepdims=True)
+    expo = jnp.exp(scores - peak)
+    return first, second, expo / jnp.sum(expo, axis=-1, keepdims=True)
+
+
+def attend_body(long_ref, *refs):
+    grouped, results = refs[:UNIT], refs[UNIT:]
+    count = grouped[0].shape[1]
+
+    def work(runs, where, share):
+        rows = jnp.concatenate([grouped[r][0, where, :] for r in runs], axis=0)
+        first, _, probs = softmax(rows)
+        mixed = jnp.dot(probs.astype(BF16), first, preferred_element_type=F32).astype(BF16)
+        for i, r in enumerate(runs):
+            results[r][0, where, :] = mixed[i * share : (i + 1) * share]
+
+    for_each_cluster(long_ref[0], count, 4, work)
+
+
+def attend(is_long, grouped):
+    count = grouped[0].shape[1]
+    return pl.pallas_call(
+        attend_body,
+        grid_spec=pltpu.PrefetchScalarGridSpec(
+            num_scalar_prefetch=1,
+            grid=(LOCAL_PAIRS,),
+            in_specs=[pl.BlockSpec((1, count, WIDE), lambda p, _: (p, 0, 0))] * UNIT,
+            out_specs=[pl.BlockSpec((1, count, TILE), lambda p, _: (p, 0, 0))] * UNIT,
+        ),
+        out_shape=[jax.ShapeDtypeStruct((LOCAL_PAIRS, count, TILE), BF16)] * UNIT,
+        compiler_params=pltpu.CompilerParams(vmem_limit_bytes=48 << 20),
+        name="attend",
+    )(is_long, *grouped)
+
+
+def attend_back_body(long_ref, *refs):
+    grouped, grads, results = refs[:UNIT], refs[UNIT : 2 * UNIT], refs[2 * UNIT :]
+    count = grouped[0].shape[1]
+    odd = (pl.program_id(0) // ROUNDS) % 2
+    lane = lax.broadcasted_iota(jnp.int32, (CLUSTER, TILE), 1)
+    value_lane = (lane < HEAD) == (odd == 0)
+    scale = HEAD**-0.5
+
+    def work(runs, where, share):
+        rows = jnp.concatenate([grouped[r][0, where, :] for r in runs], axis=0)
+        grad = jnp.concatenate([grads[r][0, where, :] for r in runs], axis=0)
+        first, second, probs = softmax(rows)
+        probs_low = probs.astype(BF16)
+        grad_probs = outer_cols(grad, first)
+        centre = jnp.sum(probs * grad_probs, axis=-1, keepdims=True)
+        grad_scores = (probs * (grad_probs - centre)).astype(BF16)
+        grad_values = inner_rows(probs_low, grad)
+        grad_query = jnp.dot(grad_scores, second, preferred_element_type=F32) * scale
+        grad_keys = inner_rows(grad_scores, first) * scale
+        tile_one = jnp.where(value_lane, grad_values, grad_query).astype(BF16)
+        tile_two = jnp.where(value_lane, 0.0, grad_keys).astype(BF16)
+        for i, r in enumerate(runs):
+            part = slice(i * share, (i + 1) * share)
+            results[r][0, where, 0:TILE] = tile_one[part]
+            results[r][0, where, TILE:WIDE] = tile_two[part]
+
+    for_each_cluster(long_ref[0], count, 4, work)
+
+
+def attend_back(is_long, grouped, grads):
+    count = grouped[0].shape[1]
+    return pl.pallas_call(
+        attend_back_body,
+        grid_spec=pltpu.PrefetchScalarGridSpec(
+            num_scalar_prefetch=1,
+            grid=(LOCAL_PAIRS,),
+            in_specs=[pl.BlockSpec((1, count, WIDE), lambda p, _: (p, 0, 0))] * UNIT
+            + [pl.BlockSpec((1, count, TILE), lambda p, _: (p, 0, 0))] * UNIT,
+            out_specs=[pl.BlockSpec((1, count, WIDE), lambda p, _: (p, 0, 0))] * UNIT,
+        ),
+        out_shape=[jax.ShapeDtypeStruct((LOCAL_PAIRS, count, WIDE), BF16)] * UNIT,
+        compiler_params=pltpu.CompilerParams(vmem_limit_bytes=48 << 20),
+        name="attend_back",
+    )(is_long, *grouped, *grads)
+
+
+def unsorted(order_ref, step, rows_ref, part, chunk):
+    count = rows_ref.shape[1]
+    row = lax.broadcasted_iota(jnp.int32, (chunk, count), 0) + part * chunk
+    total = None
+    for turn in range(ROUNDS):
+        pair = step * ROUNDS + turn
+        picked = (order_ref[pair : pair + 1, :] == row).astype(F32).astype(BF16)
+        more = jnp.dot(picked, rows_ref[turn], preferred_element_type=F32)
+        total = more if total is None else total + more
+    return total
+
+
+def mix_body(order_ref, rows_ref, out_ref):
+    count = rows_ref.shape[1]
+    chunk = 256
+    low = lax.broadcasted_iota(jnp.int32, (chunk, TILE), 1) < HEAD
+    head = pl.program_id(0)
+    for step in range(HEADS_OWN):
+
+        @pl.when(head == step)
+        def _():
+            for part in range(count // chunk):
+                where = pl.ds(part * chunk, chunk)
+                mean = (0.5 * unsorted(order_ref, step, rows_ref, part, chunk)).astype(BF16)
+                if step == 0:
+                    out_ref[where, 0:TILE] = mean
+                elif step == 1:
+                    out_ref[where, 0:TILE] = jnp.where(
+                        low, out_ref[where, 0:TILE].astype(F32), mean.astype(F32)
+                    ).astype(BF16)
+                else:
+                    out_ref[where, TILE:WIDE] = jnp.where(low, mean.astype(F32), 0.0).astype(BF16)
+
+
+def mix(order, rows):
+    count = rows.shape[1]
+    return pl.pallas_call(
+        mix_body,
+        grid=(HEADS_OWN,),
+        in_specs=[
+            pl.BlockSpec((8, count), lambda h: (0, 0)),
+            pl.BlockSpec((ROUNDS, count, TILE), lambda h: (h, 0, 0)),
+        ],
+        out_specs=pl.BlockSpec((count, WIDE), lambda h: (0, 0)),
+        out_shape=jax.ShapeDtypeStruct((count, WIDE), BF16),
+        compiler_params=pltpu.CompilerParams(vmem_limit_bytes=48 << 20),
+        name="mix",
+    )(order, rows)
+
+
+def gather_grads_body(order_ref, rows_ref, out_ref):
+    count = rows_ref.shape[1]
+    chunk = 256
+    head = pl.program_id(0)
+    for step in range(HEADS_OWN):
+
+        @pl.when(head == step)
+        def _():
+            for part in range(count // chunk):
+                where = pl.ds(part * chunk, chunk)
+                out_ref[where, :] = unsorted(order_ref, step, rows_ref, part, chunk).astype(BF16)
+
+
+def gather_grads(order, rows):
+    count = rows.shape[1]
+    return pl.pallas_call(
+        gather_grads_body,
+        grid=(HEADS_OWN,),
+        in_specs=[
+            pl.BlockSpec((8, count), lambda h: (0, 0)),
+            pl.BlockSpec((ROUNDS, count, WIDE), lambda h: (h, 0, 0)),
+        ],
+        out_specs=pl.BlockSpec((count, WIDE), lambda h: (0, h)),
+        out_shape=jax.ShapeDtypeStruct((count, HEADS_OWN * WIDE), BF16),
+        compiler_params=pltpu.CompilerParams(vmem_limit_bytes=48 << 20),
+        name="gather_grads",
+    )(order, rows)
+
+
+def swap(value, axis, bit):
+    size = lax.axis_size(axis)
+    return lax.ppermute(value, axis, [(i, i ^ bit) for i in range(size)])
+
+
+def gather_unit(rows):
+    near = swap(rows, "tok", 1)
+    far = swap(rows, "tok", 2)
+    half = rows.shape[0] // 2
+    across = jnp.concatenate([swap(near[:half], "tok", 2), swap(far[half:], "tok", 1)], axis=0)
+    return [rows, near, far, across]
+
+
+def exchange_unit(parts):
+    return [parts[0]] + [swap(parts[k], "tok", k) for k in range(1, UNIT)]
+
+
+def starts_of(lengths):
+    index = jnp.arange(lengths.shape[0])
+    return jnp.sum(jnp.where(index[None, :] < index[:, None], lengths[None, :], 0), axis=1)
+
+
+def pick(values, index):
+    return lax.dynamic_index_in_dim(values, index, 0, keepdims=False)
+
+
+def turn_rows(value, place):
+    n_tok = lax.axis_size("tok")
+    slots, rows, width = value.shape
+    parts = jnp.transpose(value.reshape(slots, n_tok, rows // n_tok, width), (1, 0, 2, 3))
+    got = lax.all_to_all(parts, "tok", split_axis=0, concat_axis=0, tiled=True)
+    got = jnp.stack([got[place.index(c)] for c in range(n_tok)], axis=2)
+    return got.reshape(slots, rows // n_tok, n_tok * width)
+
+
+def turn_columns(value, place):
+    n_tok = lax.axis_size("tok")
+    slots, rows, width = value.shape
+    parts = value.reshape(slots, rows, n_tok, width // n_tok)
+    parts = jnp.stack([parts[:, :, place[t]] for t in range(n_tok)], axis=0)
+    got = lax.all_to_all(parts, "tok", split_axis=0, concat_axis=0, tiled=True)
+    return jnp.transpose(got, (1, 0, 2, 3)).reshape(slots, n_tok * rows, width // n_tok)
+
+
+def split_heads(columns):
+    query, keys, values = (c.reshape(*c.shape[:-1], HEADS_OWN, HEAD) for c in columns)
+    zero = jnp.zeros_like(query[..., 0, :])
+    tiles = []
+    for h in range(HEADS_OWN):
+        q, k, v = query[..., h, :], keys[..., h, :], values[..., h, :]
+        tiles += [v, q, zero, k] if h % 2 == 0 else [q, v, k, zero]
+    return jnp.concatenate(tiles, axis=-1)
+
+
+def join_heads(tiles):
+    parts = tiles.reshape(*tiles.shape[:-1], HEADS_OWN, 4, HEAD)
+    query = [parts[..., h, 1 if h % 2 == 0 else 0, :] for h in range(HEADS_OWN)]
+    keys = [parts[..., h, 3 if h % 2 == 0 else 2, :] for h in range(HEADS_OWN)]
+    values = [parts[..., h, 0 if h % 2 == 0 else 1, :] for h in range(HEADS_OWN)]
+    return tuple(jnp.concatenate(p, axis=-1) for p in (query, keys, values))
+
+
+def fast(
+    tokens,
+    cotangent,
+    lengths,
+    clusters,
+    owners,
+    master,
+    bases,
+    moment_one,
+    moment_two,
+    vectors,
+    vector_one,
+    vector_two,
+):
+    n_tok = lax.axis_size("tok")
+    n_grp = lax.axis_size("grp")
+    tok = lax.axis_index("tok")
+    grp = lax.axis_index("grp")
+    tok_count = tokens.shape[1]
+    rows_dev = master.shape[0]
+    slots = master.shape[1]
+    blocks_all = slots * n_grp
+    member = tok % UNIT
+    unit = tok // UNIT
+    place = [2 * (t % UNIT) + t // UNIT for t in range(n_tok)]
+    own_width = HEADS_OWN * HEAD
+
+    slot_block = jnp.argsort(owners, stable=True).astype(jnp.int32)
+    block_slot = jnp.argsort(slot_block, stable=True).astype(jnp.int32)
+
+    by_member = jnp.transpose(
+        clusters[0].reshape(ROUNDS, UNIT, HEADS_OWN, tok_count), (1, 2, 0, 3)
+    ).reshape(UNIT, LOCAL_PAIRS, tok_count)
+    own_clusters = exchange_unit([pick(by_member, member ^ k) for k in range(UNIT)])
+    order = jnp.argsort(jnp.stack(own_clusters), axis=-1, stable=True).astype(jnp.int32)
+    order = jnp.pad(order, ((0, 0), (0, 8 - LOCAL_PAIRS), (0, 0)))
+    orders = [order[k] for k in range(UNIT)]
+    item_starts = starts_of(lengths[0])
+    unit_start = unit * UNIT * tok_count
+    middle = unit_start + UNIT // 2 * tok_count
+    start_of_middle = jnp.max(jnp.where(item_starts <= middle, item_starts, 0))
+    is_long = (start_of_middle <= unit_start).astype(jnp.int32).reshape(1)
+
+    inputs = tokens[0]
+    unit_inputs = gather_unit(inputs)
+
+    local = jnp.transpose(master.astype(BF16), (1, 0, 2))
+    weights = lax.all_gather(local, ("tok", "grp"), axis=0, tiled=False)
+    weights = weights.reshape(n_tok, n_grp * slots, rows_dev, D)
+    weights = jnp.transpose(weights, (1, 0, 2, 3)).reshape(blocks_all, D, D)
+    block = [pick(weights, block_slot[b]) for b in range(blocks_all)]
+    w_out = block[3]
+    w_up = block[4 : 4 + FFB]
+    w_down = block[4 + FFB :]
+
+    def columns_of(value, m):
+        return lax.dynamic_slice_in_dim(value, m * own_width, own_width, value.ndim - 1)
+
+    own_weights = split_heads([columns_of(block[i], member) for i in range(3)])
+    own_bias = split_heads(
+        [columns_of(vectors[4], member), jnp.zeros((own_width,), F32), columns_of(vectors[5], member)]
+    )
+    grouped = []
+    for k in range(UNIT):
+        qkv = (jnp.dot(unit_inputs[k], own_weights, preferred_element_type=F32) + own_bias).astype(BF16)
+        grouped.append(sort_rows(orders[k], qkv, WIDE))
+    sorted_out = attend(is_long, grouped)
+    mixed_parts = exchange_unit([mix(orders[k], sorted_out[k]) for k in range(UNIT)])
+    mixed_low = jnp.concatenate([m[:, :own_width] for m in mixed_parts], axis=1)
+
+    def rows_relative(value):
+        return jnp.concatenate(
+            [
+                lax.dynamic_slice_in_dim(value, (member ^ k) * own_width, own_width, 0)
+                for k in range(UNIT)
+            ],
+            axis=0,
+        )
+
+    w_out_relative = rows_relative(w_out)
+    gain_one, shift_one, gain_two, shift_two = (vectors[i] for i in range(4))
+    attention = jnp.dot(mixed_low, w_out_relative, preferred_element_type=F32) + vectors[6]
+    first_sum = inputs.astype(F32) + attention
+    normed_one, rstd_one = normalize(first_sum)
+    hidden = normed_one * gain_one + shift_one
+    hidden_low = hidden.astype(BF16)
+    up_proj = [
+        jnp.dot(hidden_low, w_up[j], preferred_element_type=F32) + vectors[8 + j] for j in range(FFB)
+    ]
+    act_low = [jax.nn.gelu(u, approximate=False).astype(BF16) for u in up_proj]
+    down_proj = vectors[7] + sum(
+        jnp.dot(act_low[j], w_down[j], preferred_element_type=F32) for j in range(FFB)
+    )
+    second_sum = hidden + down_proj
+    normed_two, rstd_two = normalize(second_sum)
+    result = (normed_two * gain_two + shift_two).astype(BF16)
+    grad_result = cotangent[0].astype(F32)
+    grad_gain_two = jnp.sum(grad_result * normed_two, axis=0)
+    grad_shift_two = jnp.sum(grad_result, axis=0)
+    grad_second = norm_back(grad_result * gain_two, normed_two, rstd_two)
+    grad_down_low = grad_second.astype(BF16)
+    grad_bias_down = jnp.sum(grad_down_low.astype(F32), axis=0)
+    turned_down = [inner_rows(grad_down_low, act_low[j]) for j in range(FFB)]
+    grad_up_low = [
+        (outer_cols(grad_down_low, w_down[j]) * gelu_slope(up_proj[j])).astype(BF16) for j in range(FFB)
+    ]
+    turned_up = [inner_rows(grad_up_low[j], hidden_low) for j in range(FFB)]
+    grad_bias_up = [jnp.sum(g.astype(F32), axis=0) for g in grad_up_low]
+    grad_hidden = grad_second + sum(outer_cols(grad_up_low[j], w_up[j]) for j in range(FFB))
+    grad_gain_one = jnp.sum(grad_hidden * normed_one, axis=0)
+    grad_shift_one = jnp.sum(grad_hidden, axis=0)
+    grad_first = norm_back(grad_hidden * gain_one, normed_one, rstd_one)
+    grad_attn_low = grad_first.astype(BF16)
+    turned_out = inner_rows(grad_attn_low, mixed_low)
+    grad_bias_out = jnp.sum(grad_attn_low.astype(F32), axis=0)
+    grad_mixed = (0.5 * outer_cols(grad_attn_low, w_out_relative)).astype(BF16)
+    zero_half = jnp.zeros((tok_count, WIDE - own_width), BF16)
+    grad_parts = exchange_unit(
+        [
+            jnp.concatenate([grad_mixed[:, k * own_width : (k + 1) * own_width], zero_half], axis=1)
+            for k in range(UNIT)
+        ]
+    )
+    sorted_grads = [sort_grads(orders[k], grad_parts[k]) for k in range(UNIT)]
+    sorted_back = attend_back(is_long, grouped, sorted_grads)
+    own_grads = [gather_grads(orders[k], sorted_back[k]) for k in range(UNIT)]
+    turned_qkv = sum(inner_rows(own_grads[k], unit_inputs[k]) for k in range(UNIT))
+    bias_qkv = sum(jnp.sum(own_grads[k].astype(F32), axis=0) for k in range(UNIT))
+    home_grads = exchange_unit(own_grads)
+    all_weights = jnp.stack(
+        [split_heads([b[:, m * own_width : (m + 1) * own_width] for b in block[:3]]) for m in range(UNIT)]
+    )
+    grad_inputs = grad_first + sum(
+        outer_cols(home_grads[k], pick(all_weights, member ^ k)) for k in range(UNIT)
+    )
+
+    bias_query, _, bias_value = join_heads(bias_qkv)
+    bias_rows = lax.dynamic_update_slice_in_dim(
+        jnp.zeros((2, D), F32), jnp.stack([bias_query, bias_value]), member * own_width, 1
+    )
+    vector_grads = jnp.concatenate(
+        [
+            jnp.stack([grad_gain_one, grad_shift_one, grad_gain_two, grad_shift_two]),
+            bias_rows,
+            jnp.stack([grad_bias_out, grad_bias_down] + grad_bias_up),
+        ],
+        axis=0,
+    )
+    vector_total = lax.psum(vector_grads, ("tok", "grp"))
+
+    piece = D // n_tok // n_grp
+    turned_out = jnp.concatenate(
+        [turned_out[:, (0) : own_width]]
+        + [turned_out[:, k * own_width : (k + 1) * own_width] for k in range(1, UNIT)],
+        axis=1,
+    )
+    turned_out = jnp.transpose(turned_out.reshape(D, UNIT, own_width), (1, 0, 2))
+    turned_out = jnp.concatenate([pick(turned_out, member ^ m) for m in range(UNIT)], axis=1)
+    rest = jnp.stack([turned_out] + turned_up + turned_down).astype(BF16)
+    rest = rest.reshape(blocks_all - 3, UNIT, n_tok // UNIT, n_grp, piece, D)
+    rest = jnp.transpose(rest, (2, 1, 3, 0, 4, 5)).reshape(n_tok * n_grp, blocks_all - 3, piece, D)
+    rest = lax.psum_scatter(rest, ("tok", "grp"), scatter_dimension=0, tiled=True)[0]
+    sent = jnp.stack(
+        [pick(rest, jnp.maximum(slot_block[s] - 3, 0)) for s in range(blocks_all)]
+    ).reshape(n_grp, slots, piece, D)
+    got = lax.all_to_all(sent, "grp", split_axis=0, concat_axis=0, tiled=True)
+    got = jnp.transpose(got, (1, 0, 2, 3)).reshape(slots, n_grp * piece, D).astype(F32)
+
+    turned_qkv = jnp.stack(join_heads(jnp.transpose(turned_qkv)))
+    turned_qkv = jnp.transpose(turned_qkv.astype(BF16).reshape(3, D, 2, own_width // 2), (2, 0, 3, 1))
+    keep = pick(turned_qkv, unit).astype(F32)
+    keep = (keep + swap(pick(turned_qkv, 1 - unit), "tok", UNIT).astype(F32)).astype(BF16)
+    keep = jnp.sum(lax.all_gather(keep, "grp", axis=0, tiled=False).astype(F32), axis=0)
+
+    mine = lax.dynamic_slice_in_dim(slot_block, grp * slots, slots, 0)
+    reduced = jnp.stack(
+        [
+            jnp.where(mine[s] < 3, pick(keep, jnp.minimum(mine[s], 2)), got[s]) for s in range(slots)
+        ]
+    )
+    left, right = bases[0], bases[1]
+    high = lax.Precision.HIGHEST
+    part = jnp.einsum("sia,sci->sac", left, reduced, precision=high)
+    part = turn_rows(part.astype(BF16), place).astype(F32)
+    rotated = jnp.einsum("sac,scb->sab", part, right, precision=high)
+    rotated = jnp.transpose(rotated, (1, 0, 2))
+    new_one = BETA_ONE * moment_one + (1.0 - BETA_ONE) * rotated
+    new_two = BETA_TWO * moment_two + (1.0 - BETA_TWO) * rotated * rotated
+    direction = new_one / (jnp.sqrt(new_two) + ADAM_EPS)
+    turned = jnp.einsum("asb,scb->sac", direction, right, precision=high)
+    turned = turn_columns(turned.astype(BF16), place).astype(F32)
+    change = jnp.einsum("sia,sac->sic", left, turned, precision=high)
+    change = turn_rows(change.astype(BF16), place).astype(F32)
+    new_master = master - RATE_MATRIX * jnp.transpose(change, (1, 0, 2))
+    new_vec_one = BETA_ONE * vector_one + (1.0 - BETA_ONE) * vector_total
+    new_vec_two = BETA_TWO * vector_two + (1.0 - BETA_TWO) * vector_total * vector_total
+    new_vectors = vectors - RATE_VECTOR * new_vec_one / (jnp.sqrt(new_vec_two) + ADAM_EPS)
+    return (
+        result[None],
+        grad_inputs[None],
+        new_one,
+        new_two,
+        new_master,
+        new_vec_one,
+        new_vec_two,
+        new_vectors,
+    )
+
+
+def general(
     tokens,
     cotangent,
     lengths,
@@ -76,7 +634,7 @@
     block_slot = jnp.argsort(slot_block, stable=True)
     slot_part = lax.all_gather(master.astype(jnp.bfloat16), "grp", axis=1, tiled=True)
     weights = lax.all_gather(slot_part, "tok", axis=0, tiled=True)
-    blocks = jnp.take(weights, block_slot, axis=1)
+    blocks = jnp.stack([pick(jnp.transpose(weights, (1, 0, 2)), block_slot[b]) for b in range(weights.shape[1])], axis=1)
     w_qkv = blocks[:, 0:3, :].reshape(D, 3 * D)
     w_out = blocks[:, 3, :]
     w_up = blocks[:, 4 : 4 + FF // D, :].reshape(D, FF)
@@ -97,9 +655,7 @@
         PAIRS * tok_count, 3 * HEAD
     )
     position = lax.axis_index("tok") * tok_count + jnp.arange(tok_count, dtype=jnp.int32)
-    item_lengths = lengths[0]
-    item_ends = jnp.cumsum(item_lengths)
-    item_starts = item_ends - item_lengths
+    item_starts = starts_of(lengths[0])
     item_start = jnp.max(
         jnp.where(item_starts[None, :] <= position[:, None], item_starts[None, :], 0), axis=1
     )
@@ -246,7 +802,8 @@
         ],
         axis=1,
     )
-    slot_grads = jnp.take(grad_blocks, slot_block, axis=1)
+    by_block = jnp.transpose(grad_blocks, (1, 0, 2))
+    slot_grads = jnp.stack([pick(by_block, slot_block[s]) for s in range(by_block.shape[0])], axis=1)
     vector_grads = jnp.concatenate(
         [
             jnp.stack(
@@ -309,8 +866,15 @@
         new_vectors,
     )
 
-
 def solution(mesh):
+    n_tok, n_grp = mesh.shape["tok"], mesh.shape["grp"]
+
+    def on_device(*args):
+        lengths, clusters = args[2], args[3]
+        unit = n_tok // (lengths.shape[1] - 1)
+        suits = unit == UNIT and n_tok == 2 * UNIT and n_grp == 4 and clusters.shape[2] == 1024
+        return (fast if suits else general)(*args)
+
     return jax.shard_map(
         on_device,
         mesh=mesh,

time: 2900 us -> 966 us (0.33)
  local copies, waits for them, and re-layouts: 1280 us -> 189 us
  waiting for transfers between devices: 1080 us -> 151 us
  Pallas kernels: 0 us -> 226 us
  other arithmetic: 159 us -> 55.2 us
  blocking collectives: 118 us -> 61.4 us
  matrix products: 217 us -> 175 us
  between operations: 15.2 us -> 50.7 us
    gather x11 -> x0, local copies, waits for them, and re-layouts: 1000 us -> none  [the longest x1 241 us: on_device(): sent_units = unit_ids[send_order].reshape(n_tok, slot_rows)]
    reduce_scatter x2 -> x1, waiting for transfers between devices: 470 us -> 0.01 us  [fast(): lax.psum_scatter(rest, ('tok', 'grp'), scatter_dimension=0, tiled=True)[0]]
    all_to_all x4, waiting for transfers between devices: 402 us -> 14.4 us  [the longest x1 5.2 us: fast(): got = lax.all_to_all(sent, 'grp', split_axis=0, concat_axis=0, tiled=True)]
    pallas_call x0 -> x18, Pallas kernels: none -> 226 us  [the longest x1 89.8 us: attend_back(): pl.pallas_call(attend_back_body, grid_spec=pltpu.PrefetchScalarGridSpec(n...]
    unnamed x8 -> x3, waiting for transfers between devices: 186 us -> 0.05 us
    reshape x14 -> x7, local copies, waits for them, and re-layouts: 143 us -> 11.8 us  [the longest x4 6.51 us: turn_rows(): value.reshape(slots, n_tok, rows // n_tok, width)]
    ppermute x0 -> x17, waiting for transfers between devices: none -> 101 us  [swap(): return lax.ppermute(value, axis, [(i, i ^ bit) for i in range(size)])]
    all_to_all x1 -> x0, blocking collectives: 74.9 us -> none  [on_device(): lax.all_to_all(sent_grad, 'tok', split_axis=0, concat_axis=0, tiled=True)]
  transfers between devices with their start and end apart: 10 -> 24, of which waited for: 8 -> 8; matrix products, arithmetic and copies ran while one was open for 19% -> 24% of each run, Pallas kernels for 0% -> 13%
where the time goes in v1:
time: 966 us; the launch traced here: 953 us
  Pallas kernels  226 us (23%)
  local copies, waits for them, and re-layouts  189 us (20%)
  matrix products  175 us (18%)
  waiting for transfers between devices  151 us (16%)
  blocking collectives  61.4 us (6%)
  other arithmetic  55.2 us (6%)
  between operations  50.7 us (5%)
  starting transfers between devices  44.4 us (5%)
    ppermute x17, waiting for transfers between devices, swap(): return lax.ppermute(value, axis, [(i, i ^ bit) for i in range(size)])  101 us
    unnamed x274, local copies, waits for them, and re-layouts  99.7 us
    pallas_call x1, Pallas kernels, attend_back(): pl.pallas_call(attend_back_body, grid_spec=pltpu.PrefetchScalarGridSpec(n...  89.8 us
    pallas_call x1, Pallas kernels, attend(): pl.pallas_call(attend_body, grid_spec=pltpu.PrefetchScalarGridSpec(num_sc...  69.9 us
    psum x1, blocking collectives, fast(): vector_total = lax.psum(vector_grads, ('tok', 'grp'))  61.4 us
    dot_general x13, matrix products, outer_cols(): lax.dot_general(left, right, (((1,), (1,)), ((), ())), preferred_element_...  50 us
    dot_general x4, matrix products, fast(): jnp.dot(hidden_low, w_up[j], preferred_element_type=F32) + vectors[8 + j]  36.3 us
    all_gather x1, waiting for transfers between devices, fast(): weights = lax.all_gather(local, ('tok', 'grp'), axis=0, tiled=False)  35.5 us
  transfers between devices with their start and end apart: 24, of which 8 were waited for; matrix products, arithmetic and copies ran while one was open for 24% of the time, Pallas kernels for 13%

profile of v1, /device:TPU:0, one launch (start us, length us, event | category | flops | bytes accessed | tf_op | source)
XLA Modules:
  0.0 953.1 jit_solution(5138076347314882338)
XLA Ops:
  22.8 29.4 %collective-permute-done.3 = bf16[1024,768]{0,1:T(8,128)(2,1)} collective-permute-done((bf16[1024,768]{0,1:T(8,128)(2,1)S(1)}, bf16[1024,768]{0,1:T(8,128)(2,1)}, u32[]{:S(2)}, u32[]{:S(2)}) %collective-permute-start.3) | collective-permute-done | bytes 1572896 | tf_op jit(solution)/shard_map/ppermute | solution.py:347
  55.2 20.6 %collective-permute-done.4 = bf16[1024,768]{0,1:T(8,128)(2,1)} collective-permute-done((bf16[1024,768]{0,1:T(8,128)(2,1)S(1)}, bf16[1024,768]{0,1:T(8,128)(2,1)}, u32[]{:S(2)}, u32[]{:S(2)}) %collective-permute-start.4) | collective-permute-done | bytes 1572896 | tf_op jit(solution)/shard_map/ppermute | solution.py:347
  85.6 23.9 %sort.48 = (s32[4,6,1024]{2,0,1:T(4,128)}, s32[4,6,1024]{2,0,1:T(4,128)S(1)}) sort(s32[4,6,1024]{2,0,1:T(4,128)S(1)} %pad_add_fusion, s32[4,6,1024]{2,0,1:T(4,128)S(1)} %iota.21), dimensions={2}, is_stable=true, to_apply=%region_0.1 | sort | flops 368640 | bytes 393216 | tf_op jit(solution)/shard_map/jit(argsort)/sort | solution.py:441
  111.0 35.5 %all-gather.5.cloned.1.call-done = bf16[96,96,768]{2,1,0:T(8,128)(2,1)} async-done(((bf16[3,96,768]{2,1,0:T(8,128)(2,1)}), bf16[96,96,768]{2,1,0:T(8,128)(2,1)}) %all-gather.5.cloned.1.call-update) | async-done | bytes 14155792 | tf_op jit(solution)/shard_map/all_gather | solution.py:454
  146.6 6.9 copy.228
  153.4 5.0 copy-done.22
  176.6 4.5 sort_rows.4.refs_0_
  185.1 4.3 sort_rows.6.refs_2_
  193.4 4.3 sort_rows.5.refs_1_
  199.5 4.7 sort_rows.7.refs_3_
  205.8 69.9 %attend.1 = (bf16[6,1024,128]{2,1,0:T(8,128)(2,1)S(1)}, bf16[6,1024,128]{2,1,0:T(8,128)(2,1)S(1)}, bf16[6,1024,128]{2,1,0:T(8,128)(2,1)S(1)}, bf16[6,1024,128]{2,1,0:T(8,128)(2,1)}) custom-call(s32[1]{0:T(128)} %bitcast.5.long_ref, bf16[6,1024,256]{2,1,0:T(8,128)(2,1)} %copy-done, bf16[6,1024,256]{2,1,0:T(8,128)(2,1)} %copy-done.2, ...), custom_call_target="tpu_custom_call" | custom-call | tf_op jit(solution)/shard_map/attend/pallas_call | solution.py:206
  279.5 4.0 mix.6
  287.3 6.7 collective-permute-start.9
  329.2 4.0 mix.4
  341.8 8.9 fusion.32
  350.7 9.3 fusion.29
  361.5 8.9 fusion.26
  371.9 9.1 fusion.23
  384.1 4.1 fusion.235
  433.6 6.6 multiply_reduce_fusion
  443.4 4.3 fusion.207
  461.5 4.8 copy.265
  534.8 4.6 sort_grads.4.refs_4_
  539.4 33.1 %collective-permute-done.12.rows_ref = bf16[1024,256]{1,0:T(8,128)(2,1)S(1)} collective-permute-done((bf16[1024,256]{1,0:T(8,128)(2,1)S(1)}, bf16[1024,256]{1,0:T(8,128)(2,1)S(1)}, u32[]{:S(2)}, u32[]{:S(2)}) %collective-permute-start.12) | collective-permute-done | bytes 524320 | tf_op jit(solution)/shard_map/ppermute | solution.py:347
  572.5 4.2 sort_grads.7.refs_7_
  577.8 4.2 sort_grads.6.refs_6_
  582.0 4.4 sort_grads.5.refs_5_
  586.4 89.8 %attend_back.1 = (bf16[6,1024,256]{2,1,0:T(8,128)(2,1)}, bf16[6,1024,256]{2,1,0:T(8,128)(2,1)}, bf16[6,1024,256]{2,1,0:T(8,128)(2,1)}, bf16[6,1024,256]{2,1,0:T(8,128)(2,1)}) custom-call(s32[1]{0:T(128)} %bitcast.5.long_ref, bf16[6,1024,256]{2,1,0:T(8,128)(2,1)} %copy-done, bf16[6,1024,256]{2,1,0:T(8,128)(2,1)} %copy-done.2, ...), custom_call_target="tpu_custom_call" | custom-call | tf_op jit(solution)/shard_map/attend_back/pallas_call | solution.py:251
  686.2 4.1 gather_grads.6
  707.2 18.3 %collective-permute-done.16 = bf16[3,96,768]{2,1,0:T(8,128)(2,1)S(1)} collective-permute-done((bf16[3,96,768]{2,1,0:T(8,128)(2,1)S(1)}, bf16[3,96,768]{2,1,0:T(8,128)(2,1)S(1)}, u32[]{:S(2)}, u32[]{:S(2)}) %collective-permute-start.16) | collective-permute-done | bytes 442400 | tf_op jit(solution)/shard_map/ppermute | solution.py:347
  726.4 4.4 pad_maximum_fusion
  749.6 4.1 all-to-all-start
  756.6 5.2 all-to-all-done
  763.2 7.9 fusion.111
  775.8 4.2 all-to-all-start.1
  780.4 61.4 %psum.7 = f32[12,768]{1,0:T(8,128)S(1)} all-reduce(f32[12,768]{1,0:T(8,128)S(1)} %concatenate.102), channel_id=1, replica_groups=mesh['tok'=8,'grp'=4] {'tok','grp'}, use_global_device_ids=true, to_apply=%region_29.30 | all-reduce | flops 9216 | bytes 73728 | tf_op jit(solution)/shard_map/psum | solution.py:555
  841.9 4.8 fusion.120
  857.3 6.2 fusion.170
  864.7 10.7 %fusion.105 = bf16[3,96,768]{2,1,0:T(8,128)(2,1)} fusion(f32[2,3,768,768]{3,2,1,0:T(8,128)} %param.18, f32[96,3,768]{2,0,1:T(8,128)S(1)} %get-tuple-element.134, f32[96,3,768]{2,0,1:T(8,128)S(1)} %get-tuple-element.133), kind=kOutput, calls=%fused_computation.182 | convolution fusion | flops 2039095296 | bytes 9289728 | tf_op jit(solution)/shard_map/asb,scb->sac/dot_general | solution.py:596
  877.9 4.8 fusion.229
  887.8 4.9 all-to-all-start.2
  893.4 4.8 fusion.116
  898.2 4.9 fusion.118
  903.2 4.4 all-to-all-done.2
  909.4 6.7 fusion.108
  918.0 4.2 all-to-all-start.3
  922.2 7.4 add_bitcast_fusion
  932.0 4.9 all-to-all-done.3
  (473 shorter events, 304.0 us)
Async XLA Ops:
  7.2 12.4 %copy-start.68 = (s32[12]{0:T(128)S(1)}, s32[12]{0:T(128)}, u32[]{:S(2)}) copy-start(s32[12]{0:T(128)} %param.16) | copy-start | bytes 148
  7.2 139.4 %all-gather.5.cloned.1.call-start = ((), (), s32[]{:S(2)}) async-start(), calls=%async_computation.6 | async-start | bytes 14598144 | tf_op jit(solution)/shard_map/all_gather | solution.py:454
  9.2 45.9 %copy-start.69 = (s32[1,3]{1,0:T(1,128)S(1)}, s32[1,3]{1,0:T(1,128)}, u32[]{:S(2)}) copy-start(s32[1,3]{1,0:T(1,128)} %param.14) | copy-start | bytes 40
  9.2 69.3 %copy-start.61 = (f32[12,768]{1,0:T(8,128)S(1)}, f32[12,768]{1,0:T(8,128)}, u32[]{:S(2)}) copy-start(f32[12,768]{1,0:T(8,128)} %param.21) | copy-start | bytes 110596
  9.2 730.4 %reduce-scatter.2.cloned.1.call-start = ((), (), s32[]{:S(2)}) async-start(), calls=%async_computation.5 | async-start | bytes 10948608 | tf_op jit(solution)/shard_map/reduce_scatter | solution.py:568
  11.0 98.5 %copy-start.32 = (bf16[1,1024,768]{1,2,0:T(8,128)(2,1)}, bf16[1,1024,768]{1,2,0:T(8,128)(2,1)S(1)}, u32[]{:S(2)}) copy-start(bf16[1,1024,768]{1,2,0:T(8,128)(2,1)S(1)} %copy.225) | copy-start | bytes 4718596
  11.0 41.2 %collective-permute-start.3 = (bf16[1024,768]{0,1:T(8,128)(2,1)S(1)}, bf16[1024,768]{0,1:T(8,128)(2,1)}, u32[]{:S(2)}, u32[]{:S(2)}) collective-permute-start(bf16[1024,768]{0,1:T(8,128)(2,1)S(1)} %bitcast.726), channel_id=1, source_target_pairs={{0,4},{4,0},{8,12},{12,8},{16,20},{20,16},{24,28},{28,24},{1,5},{5... | collective-permute-start | bytes 4718600 | tf_op jit(solution)/shard_map/ppermute | solution.py:347
  14.1 61.8 %collective-permute-start.4 = (bf16[1024,768]{0,1:T(8,128)(2,1)S(1)}, bf16[1024,768]{0,1:T(8,128)(2,1)}, u32[]{:S(2)}, u32[]{:S(2)}) collective-permute-start(bf16[1024,768]{0,1:T(8,128)(2,1)S(1)} %bitcast.727), channel_id=1, source_target_pairs={{0,8},{4,12},{8,0},{12,4},{16,24},{20,28},{24,16},{28,20},{1,9},{5... | collective-permute-start | bytes 4718600 | tf_op jit(solution)/shard_map/ppermute | solution.py:347
  15.9 69.5 %collective-permute-start = (s32[6,1024]{1,0:T(8,128)S(1)}, s32[6,1024]{1,0:T(8,128)S(1)}, u32[]{:S(2)}, u32[]{:S(2)}) collective-permute-start(s32[6,1024]{1,0:T(8,128)S(1)} %bitcast.797), channel_id=1, source_target_pairs={{0,4},{4,0},{8,12},{12,8},{16,20},{20,16},{24,28},{28,24},{1,5},{5... | collective-permute-start | bytes 73736 | tf_op jit(solution)/shard_map/ppermute | solution.py:347
  16.5 68.9 %collective-permute-start.1 = (s32[6,1024]{1,0:T(8,128)S(1)}, s32[6,1024]{1,0:T(8,128)S(1)}, u32[]{:S(2)}, u32[]{:S(2)}) collective-permute-start(s32[6,1024]{1,0:T(8,128)S(1)} %bitcast.798), channel_id=1, source_target_pairs={{0,8},{4,12},{8,0},{12,4},{16,24},{20,28},{24,16},{28,20},{1,9},{5... | collective-permute-start | bytes 73736 | tf_op jit(solution)/shard_map/ppermute | solution.py:347
  16.6 68.9 %collective-permute-start.2 = (s32[6,1024]{1,0:T(8,128)S(1)}, s32[6,1024]{1,0:T(8,128)S(1)}, u32[]{:S(2)}, u32[]{:S(2)}) collective-permute-start(s32[6,1024]{1,0:T(8,128)S(1)} %bitcast.799), channel_id=1, source_target_pairs={{0,12},{4,8},{8,4},{12,0},{16,28},{20,24},{24,20},{28,16},{1,13},{... | collective-permute-start | bytes 73736 | tf_op jit(solution)/shard_map/ppermute | solution.py:347
  53.4 56.2 %collective-permute-start.5 = (bf16[512,768]{0,1:T(8,128)(2,1)S(1)}, bf16[512,768]{0,1:T(8,128)(2,1)S(1)}, u32[]{:S(2)}, u32[]{:S(2)}) collective-permute-start(bf16[512,768]{0,1:T(8,128)(2,1)S(1)} %slice.685), channel_id=1, source_target_pairs={{0,8},{4,12},{8,0},{12,4},{16,24},{20,28},{24,16},{28,20},{1,9},{5... | collective-permute-start | bytes 2359304 | tf_op jit(solution)/shard_map/ppermute | solution.py:347
  77.9 31.8 %collective-permute-start.6 = (bf16[512,768]{0,1:T(8,128)(2,1)}, bf16[512,768]{0,1:T(8,128)(2,1)}, u32[]{:S(2)}, u32[]{:S(2)}) collective-permute-start(bf16[512,768]{0,1:T(8,128)(2,1)} %slice.686), channel_id=1, source_target_pairs={{0,4},{4,0},{8,12},{12,8},{16,20},{20,16},{24,28},{28,24},{1,5},{5... | collective-permute-start | bytes 2359304 | tf_op jit(solution)/shard_map/ppermute | solution.py:347
  109.6 462.9 %copy-start.13 = (s32[8,1024]{1,0:T(8,128)}, s32[8,1024]{1,0:T(8,128)S(1)}, u32[]{:S(2)}) copy-start(s32[8,1024]{1,0:T(8,128)S(1)} %get-tuple-element.151.order_ref) | copy-start | bytes 98308
  109.6 468.2 %copy-start.15 = (s32[8,1024]{1,0:T(8,128)}, s32[8,1024]{1,0:T(8,128)S(1)}, u32[]{:S(2)}) copy-start(s32[8,1024]{1,0:T(8,128)S(1)} %get-tuple-element.149.order_ref) | copy-start | bytes 98308
  109.6 472.4 %copy-start.17 = (s32[8,1024]{1,0:T(8,128)}, s32[8,1024]{1,0:T(8,128)S(1)}, u32[]{:S(2)}) copy-start(s32[8,1024]{1,0:T(8,128)S(1)} %get-tuple-element.150.order_ref) | copy-start | bytes 98308
  111.0 64.1 %copy-start.28 = (bf16[1024,768]{0,1:T(8,128)(2,1)}, bf16[1024,768]{0,1:T(8,128)(2,1)S(1)}, u32[]{:S(2)}) copy-start(bf16[1024,768]{0,1:T(8,128)(2,1)S(1)} %constant_dynamic-update-slice_fusion.12) | copy-start | bytes 4718596
  158.5 15.2 %copy-start.30 = (bf16[1,1024,768]{2,1,0:T(8,128)(2,1)S(1)}, bf16[1,1024,768]{2,1,0:T(8,128)(2,1)}, u32[]{:S(2)}) copy-start(bf16[1,1024,768]{2,1,0:T(8,128)(2,1)} %param.12) | copy-start | bytes 4718596
  287.3 47.7 %collective-permute-start.9 = (bf16[1024,256]{1,0:T(8,128)(2,1)S(1)}, bf16[1024,256]{1,0:T(8,128)(2,1)}, u32[]{:S(2)}, u32[]{:S(2)}) collective-permute-start(bf16[1024,256]{1,0:T(8,128)(2,1)S(1)} %mix.7), channel_id=1, source_target_pairs={{0,12},{4,8},{8,4},{12,0},{16,28},{20,24},{24,20},{28,16},{1,13},{... | collective-permute-start | bytes 1572872 | tf_op jit(solution)/shard_map/ppermute | solution.py:347
  294.0 41.0 %collective-permute-start.8 = (bf16[1024,256]{1,0:T(8,128)(2,1)S(1)}, bf16[1024,256]{1,0:T(8,128)(2,1)}, u32[]{:S(2)}, u32[]{:S(2)}) collective-permute-start(bf16[1024,256]{1,0:T(8,128)(2,1)S(1)} %mix.6), channel_id=1, source_target_pairs={{0,8},{4,12},{8,0},{12,4},{16,24},{20,28},{24,16},{28,20},{1,9},{5... | collective-permute-start | bytes 1572872 | tf_op jit(solution)/shard_map/ppermute | solution.py:347
  294.0 41.0 %collective-permute-start.7 = (bf16[1024,256]{1,0:T(8,128)(2,1)S(1)}, bf16[1024,256]{1,0:T(8,128)(2,1)}, u32[]{:S(2)}, u32[]{:S(2)}) collective-permute-start(bf16[1024,256]{1,0:T(8,128)(2,1)S(1)} %mix.5), channel_id=1, source_target_pairs={{0,4},{4,0},{8,12},{12,8},{16,20},{20,16},{24,28},{28,24},{1,5},{5... | collective-permute-start | bytes 1572872 | tf_op jit(solution)/shard_map/ppermute | solution.py:347
  339.5 32.3 %copy-start.34 = (bf16[1024,768]{0,1:T(8,128)(2,1)}, bf16[1024,768]{0,1:T(8,128)(2,1)S(1)}, u32[]{:S(2)}) copy-start(bf16[1024,768]{0,1:T(8,128)(2,1)S(1)} %fusion.85) | copy-start | bytes 4718596
  443.4 84.0 %copy-start.23 = (f32[1024,768]{0,1:T(8,128)}, f32[1024,768]{0,1:T(8,128)S(1)}, u32[]{:S(2)}) copy-start(f32[1024,768]{0,1:T(8,128)S(1)} %get-tuple-element.93) | copy-start | bytes 9437188
  466.3 287.5 %all-gather.7.cloned.1.call-start = ((), (), s32[]{:S(2)}) async-start(), calls=%async_computation.7 | async-start | bytes 2211840 | tf_op jit(solution)/shard_map/all_gather | solution.py:579
  497.6 14.9 %copy-start.51 = (bf16[768,192]{0,1:T(8,128)(2,1)S(1)}, bf16[768,192]{0,1:T(8,128)(2,1)}, u32[]{:S(2)}) copy-start(bf16[768,192]{0,1:T(8,128)(2,1)} %copy.254) | copy-start | bytes 884740
  497.6 15.5 %copy-start.50 = (bf16[768,192]{0,1:T(8,128)(2,1)S(1)}, bf16[768,192]{0,1:T(8,128)(2,1)}, u32[]{:S(2)}) copy-start(bf16[768,192]{0,1:T(8,128)(2,1)} %copy.255) | copy-start | bytes 884740
  497.6 16.8 %copy-start.47 = (bf16[768,192]{0,1:T(8,128)(2,1)S(1)}, bf16[768,192]{0,1:T(8,128)(2,1)}, u32[]{:S(2)}) copy-start(bf16[768,192]{0,1:T(8,128)(2,1)} %copy.256) | copy-start | bytes 884740
  497.6 22.0 %copy-start.49 = (bf16[768,192]{0,1:T(8,128)(2,1)S(1)}, bf16[768,192]{0,1:T(8,128)(2,1)}, u32[]{:S(2)}) copy-start(bf16[768,192]{0,1:T(8,128)(2,1)} %copy.245) | copy-start | bytes 884740
  497.6 22.7 %copy-start.48 = (bf16[768,192]{0,1:T(8,128)(2,1)S(1)}, bf16[768,192]{0,1:T(8,128)(2,1)}, u32[]{:S(2)}) copy-start(bf16[768,192]{0,1:T(8,128)(2,1)} %copy.246) | copy-start | bytes 884740
  497.6 24.0 %copy-start.46 = (bf16[768,192]{0,1:T(8,128)(2,1)S(1)}, bf16[768,192]{0,1:T(8,128)(2,1)}, u32[]{:S(2)}) copy-start(bf16[768,192]{0,1:T(8,128)(2,1)} %copy.247) | copy-start | bytes 884740
  503.2 24.2 %copy-start.54 = (bf16[192,768]{1,0:T(8,128)(2,1)S(1)}, bf16[192,768]{1,0:T(8,128)(2,1)}, u32[]{:S(2)}) copy-start(bf16[192,768]{1,0:T(8,128)(2,1)} %copy-done.53) | copy-start | bytes 884740
  503.2 24.2 %copy-start.56 = (bf16[192,768]{1,0:T(8,128)(2,1)S(1)}, bf16[192,768]{1,0:T(8,128)(2,1)}, u32[]{:S(2)}) copy-start(bf16[192,768]{1,0:T(8,128)(2,1)} %copy-done.55) | copy-start | bytes 884740
  503.2 24.2 %copy-start.58 = (bf16[192,768]{1,0:T(8,128)(2,1)S(1)}, bf16[192,768]{1,0:T(8,128)(2,1)}, u32[]{:S(2)}) copy-start(bf16[192,768]{1,0:T(8,128)(2,1)} %copy-done.57) | copy-start | bytes 884740
  503.2 24.2 %copy-start.60 = (bf16[192,768]{1,0:T(8,128)(2,1)S(1)}, bf16[192,768]{1,0:T(8,128)(2,1)}, u32[]{:S(2)}) copy-start(bf16[192,768]{1,0:T(8,128)(2,1)} %copy-done.59) | copy-start | bytes 884740
  529.6 52.4 %collective-permute-start.10 = (bf16[1024,256]{1,0:T(8,128)(2,1)S(1)}, bf16[1024,256]{1,0:T(8,128)(2,1)S(1)}, u32[]{:S(2)}, u32[]{:S(2)}) collective-permute-start(bf16[1024,256]{1,0:T(8,128)(2,1)S(1)} %concatenate.85), channel_id=1, source_target_pairs={{0,4},{4,0},{8,12},{12,8},{16,20},{20,16},{24,28},{28,24},{1,5},{5... | collective-permute-start | bytes 1572872 | tf_op jit(solution)/shard_map/ppermute | solution.py:347
  531.1 46.7 %collective-permute-start.11 = (bf16[1024,256]{1,0:T(8,128)(2,1)S(1)}, bf16[1024,256]{1,0:T(8,128)(2,1)S(1)}, u32[]{:S(2)}, u32[]{:S(2)}) collective-permute-start(bf16[1024,256]{1,0:T(8,128)(2,1)S(1)} %concatenate.86), channel_id=1, source_target_pairs={{0,8},{4,12},{8,0},{12,4},{16,24},{20,28},{24,16},{28,20},{1,9},{5... | collective-permute-start | bytes 1572872 | tf_op jit(solution)/shard_map/ppermute | solution.py:347
  533.1 39.4 %collective-permute-start.12 = (bf16[1024,256]{1,0:T(8,128)(2,1)S(1)}, bf16[1024,256]{1,0:T(8,128)(2,1)S(1)}, u32[]{:S(2)}, u32[]{:S(2)}) collective-permute-start(bf16[1024,256]{1,0:T(8,128)(2,1)S(1)} %concatenate.87), channel_id=1, source_target_pairs={{0,12},{4,8},{8,4},{12,0},{16,28},{20,24},{24,20},{28,16},{1,13},{... | collective-permute-start | bytes 1572872 | tf_op jit(solution)/shard_map/ppermute | solution.py:347
  703.5 22.0 %collective-permute-start.16 = (bf16[3,96,768]{2,1,0:T(8,128)(2,1)S(1)}, bf16[3,96,768]{2,1,0:T(8,128)(2,1)S(1)}, u32[]{:S(2)}, u32[]{:S(2)}) collective-permute-start(bf16[3,96,768]{2,1,0:T(8,128)(2,1)S(1)} %dynamic-slice_bitcast_fusion.3), channel_id=1, source_target_pairs={{0,16},{4,20},{8,24},{12,28},{16,0},{20,4},{24,8},{28,12},{1,17},{... | collective-permute-start | bytes 1327112 | tf_op jit(solution)/shard_map/ppermute | solution.py:347
  733.6 188.6 %collective-permute-start.15 = (bf16[1024,768]{1,0:T(8,128)(2,1)S(1)}, bf16[1024,768]{1,0:T(8,128)(2,1)}, u32[]{:S(2)}, u32[]{:S(2)}) collective-permute-start(bf16[1024,768]{1,0:T(8,128)(2,1)S(1)} %gather_grads.7), channel_id=1, source_target_pairs={{0,12},{4,8},{8,4},{12,0},{16,28},{20,24},{24,20},{28,16},{1,13},{... | collective-permute-start | bytes 4718600 | tf_op jit(solution)/shard_map/ppermute | solution.py:347
  733.6 159.8 %collective-permute-start.14 = (bf16[1024,768]{1,0:T(8,128)(2,1)}, bf16[1024,768]{1,0:T(8,128)(2,1)}, u32[]{:S(2)}, u32[]{:S(2)}) collective-permute-start(bf16[1024,768]{1,0:T(8,128)(2,1)} %copy-done.4), channel_id=1, source_target_pairs={{0,8},{4,12},{8,0},{12,4},{16,24},{20,28},{24,16},{28,20},{1,9},{5... | collective-permute-start | bytes 4718600 | tf_op jit(solution)/shard_map/ppermute | solution.py:347
  735.6 162.6 %collective-permute-start.13 = (bf16[1024,768]{1,0:T(8,128)(2,1)S(1)}, bf16[1024,768]{1,0:T(8,128)(2,1)}, u32[]{:S(2)}, u32[]{:S(2)}) collective-permute-start(bf16[1024,768]{1,0:T(8,128)(2,1)S(1)} %gather_grads.5), channel_id=1, source_target_pairs={{0,4},{4,0},{8,12},{12,8},{16,20},{20,16},{24,28},{28,24},{1,5},{5... | collective-permute-start | bytes 4718600 | tf_op jit(solution)/shard_map/ppermute | solution.py:347
  749.6 12.2 %all-to-all-start = ((bf16[4,3,24,768]{3,2,1,0:T(8,128)(2,1)}), bf16[4,3,24,768]{3,2,1,0:T(8,128)(2,1)}, u32[]{:S(2)}, u32[]{:S(2)}) async-start(bf16[4,3,24,768]{3,2,1,0:T(8,128)(2,1)} %bitcast.795), calls=%async_computation.1 | async-start | bytes 884736 | tf_op jit(solution)/shard_map/all_to_all | solution.py:572
  775.8 71.0 %all-to-all-start.1 = ((bf16[8,3,96,96]{3,2,1,0:T(8,128)(2,1)}), bf16[8,3,96,96]{3,2,1,0:T(8,128)(2,1)}, u32[]{:S(2)}, u32[]{:S(2)}) async-start(bf16[8,3,96,96]{3,2,1,0:T(8,128)(2,1)} %bitcast.724), calls=%async_computation.2 | async-start | bytes 1179648 | tf_op jit(solution)/shard_map/all_to_all | solution.py:375
  875.4 17.3 %copy-start.62 = (f32[12,768]{1,0:T(8,128)S(1)}, f32[12,768]{1,0:T(8,128)}, u32[]{:S(2)}) copy-start(f32[12,768]{1,0:T(8,128)} %param.21) | copy-start | bytes 110596
  875.4 17.3 %copy-start.64 = (f32[12,768]{1,0:T(8,128)S(1)}, f32[12,768]{1,0:T(8,128)}, u32[]{:S(2)}) copy-start(f32[12,768]{1,0:T(8,128)} %param.23) | copy-start | bytes 110596
  875.4 17.3 %copy-start.65 = (f32[12,768]{1,0:T(8,128)S(1)}, f32[12,768]{1,0:T(8,128)}, u32[]{:S(2)}) copy-start(f32[12,768]{1,0:T(8,128)} %param.22) | copy-start | bytes 110596
  887.8 19.8 %all-to-all-start.2 = ((bf16[8,3,96,96]{3,2,1,0:T(8,128)(2,1)}), bf16[8,3,96,96]{3,2,1,0:T(8,128)(2,1)}, u32[]{:S(2)}, u32[]{:S(2)}) async-start(bf16[8,3,96,96]{3,2,1,0:T(8,128)(2,1)} %constant_dynamic-update-slice_fusion.90), calls=%async_computation.3 | async-start | bytes 1179648 | tf_op jit(solution)/shard_map/all_to_all | solution.py:385
  918.0 18.9 %all-to-all-start.3 = ((bf16[8,3,96,96]{3,2,1,0:T(8,128)(2,1)}), bf16[8,3,96,96]{3,2,1,0:T(8,128)(2,1)}, u32[]{:S(2)}, u32[]{:S(2)}) async-start(bf16[8,3,96,96]{3,2,1,0:T(8,128)(2,1)} %bitcast.212), calls=%async_computation.4 | async-start | bytes 1179648 | tf_op jit(solution)/shard_map/all_to_all | solution.py:375
  (60 other events, 210.4 us)
Sparse Core Ops, SparseCore 0:
  11.5 135.0 all-gather.4
  466.5 163.2 reduce-scatter.1
  726.5 20.0 all-gather.6

commit v2 on v1

--- a/solution.py
+++ b/solution.py
@@ -106,7 +106,8 @@
 
 
 def sort_grads_body(order_ref, rows_ref, out_ref, column_ref):
-    count = rows_ref.shape[0]
+    count = order_ref.shape[1]
+    half = count // 2
 
     @pl.when(pl.program_id(0) == 0)
     def _():
@@ -120,9 +121,13 @@
 
         @pl.when(head == step)
         def _():
-            tile = rows_ref[:, (step // 2) * TILE : (step // 2 + 1) * TILE]
-            mask = low if step % 2 == 0 else jnp.logical_not(low)
-            tile = jnp.where(mask, tile.astype(F32), 0.0).astype(BF16)
+            if step < 2:
+                tile = rows_ref[0:count, :].astype(F32)
+                tile = jnp.where(low if step == 0 else jnp.logical_not(low), tile, 0.0).astype(BF16)
+            else:
+                both = rows_ref[count : count + half, :].astype(F32)
+                tile = jnp.concatenate([both, turn_half(both)], axis=0)
+                tile = jnp.where(low, tile, 0.0).astype(BF16)
             for turn in range(ROUNDS):
                 pair = step * ROUNDS + turn
                 for part in range(count // chunk):
@@ -134,13 +139,13 @@
 
 
 def sort_grads(order, rows):
-    count = rows.shape[0]
+    count = order.shape[1]
     return pl.pallas_call(
         sort_grads_body,
         grid=(HEADS_OWN,),
         in_specs=[
             pl.BlockSpec((8, count), lambda h: (0, 0)),
-            pl.BlockSpec((count, WIDE), lambda h: (0, 0)),
+            pl.BlockSpec(rows.shape, lambda h: (0, 0)),
         ],
         out_specs=pl.BlockSpec((ROUNDS, count, TILE), lambda h: (h, 0, 0)),
         out_shape=jax.ShapeDtypeStruct((LOCAL_PAIRS, count, TILE), BF16),
@@ -150,55 +155,62 @@
     )(order, rows)
 
 
-def clusters_of(count):
-    share_long = CLUSTER // UNIT
-    share_short = 2 * share_long
+def plans_of(count):
+    share = CLUSTER // UNIT
+    half = UNIT // 2
     return (
-        [(tuple(range(UNIT)), share_long, count // share_long)],
-        [
-            (tuple(range(half * UNIT // 2, (half + 1) * UNIT // 2)), share_short, count // share_short)
-            for half in range(2)
-        ],
-    )
-
-
-def for_each_cluster(is_long, count, unroll, work):
-    long_plan, short_plan = clusters_of(count)
-    for wanted, plan in ((1, long_plan), (0, short_plan)):
+        [(tuple(range(UNIT)), share)],
+        [(tuple(range(i * half, (i + 1) * half)), 2 * share) for i in range(2)],
+    )
+
+
+def for_each_batch(is_long, count, batch, work):
+    for wanted, plan in zip((1, 0), plans_of(count)):
 
         @pl.when(is_long == wanted)
         def _(plan=plan):
-            for runs, share, clusters in plan:
+            for runs, share in plan:
 
                 def step(group, carry, runs=runs, share=share):
-                    for inner in range(unroll):
-                        first = pl.multiple_of((group * unroll + inner) * share, share)
-                        work(runs, pl.ds(first, share), share)
+                    first = pl.multiple_of(group * (batch * share), batch * share)
+                    work(runs, pl.ds(first, batch * share), share)
                     return carry
 
-                lax.fori_loop(0, clusters // unroll, step, 0)
-
-
-def softmax(rows):
-    first, second = rows[:, :TILE], rows[:, TILE:]
-    scores = outer_cols(first, second) * (HEAD**-0.5)
-    peak = jnp.max(scores, axis=-1, keepdims=True)
-    expo = jnp.exp(scores - peak)
-    return first, second, expo / jnp.sum(expo, axis=-1, keepdims=True)
+                lax.fori_loop(0, count // share // batch, step, 0)
+
+
+def batch_of(refs, runs, where, share, width):
+    parts = [refs[r][0, where, :] for r in runs]
+    return jnp.concatenate([p.reshape(p.shape[0] // share, share, width) for p in parts], axis=1)
+
+
+def spread(refs, runs, where, share, columns, value):
+    for i, r in enumerate(runs):
+        part = value[:, i * share : (i + 1) * share]
+        refs[r][0, where, columns] = part.reshape(part.shape[0] * share, TILE)
+
+
+def products(form, left, right):
+    return jnp.einsum(form, left, right, preferred_element_type=F32)
+
+
+def softmax(first, second):
+    scores = products("ued,ucd->uec", second, first) * (HEAD**-0.5)
+    expo = jnp.exp(scores - jnp.max(scores, axis=1, keepdims=True))
+    return expo * (1.0 / jnp.sum(expo, axis=1, keepdims=True))
 
 
 def attend_body(long_ref, *refs):
     grouped, results = refs[:UNIT], refs[UNIT:]
-    count = grouped[0].shape[1]
 
     def work(runs, where, share):
-        rows = jnp.concatenate([grouped[r][0, where, :] for r in runs], axis=0)
-        first, _, probs = softmax(rows)
-        mixed = jnp.dot(probs.astype(BF16), first, preferred_element_type=F32).astype(BF16)
-        for i, r in enumerate(runs):
-            results[r][0, where, :] = mixed[i * share : (i + 1) * share]
-
-    for_each_cluster(long_ref[0], count, 4, work)
+        rows = batch_of(grouped, runs, where, share, WIDE)
+        first = rows[..., :TILE]
+        probs = softmax(first, rows[..., TILE:]).astype(BF16)
+        mixed = products("uce,ued->ucd", jnp.swapaxes(probs, 1, 2), first).astype(BF16)
+        spread(results, runs, where, share, slice(0, TILE), mixed)
+
+    for_each_batch(long_ref[0], grouped[0].shape[1], 8, work)
 
 
 def attend(is_long, grouped):
@@ -219,31 +231,29 @@
 
 def attend_back_body(long_ref, *refs):
     grouped, grads, results = refs[:UNIT], refs[UNIT : 2 * UNIT], refs[2 * UNIT :]
-    count = grouped[0].shape[1]
+    batch = 16
     odd = (pl.program_id(0) // ROUNDS) % 2
-    lane = lax.broadcasted_iota(jnp.int32, (CLUSTER, TILE), 1)
+    lane = lax.broadcasted_iota(jnp.int32, (batch, CLUSTER, TILE), 2)
     value_lane = (lane < HEAD) == (odd == 0)
     scale = HEAD**-0.5
 
     def work(runs, where, share):
-        rows = jnp.concatenate([grouped[r][0, where, :] for r in runs], axis=0)
-        grad = jnp.concatenate([grads[r][0, where, :] for r in runs], axis=0)
-        first, second, probs = softmax(rows)
-        probs_low = probs.astype(BF16)
-        grad_probs = outer_cols(grad, first)
-        centre = jnp.sum(probs * grad_probs, axis=-1, keepdims=True)
+        rows = batch_of(grouped, runs, where, share, WIDE)
+        grad = batch_of(grads, runs, where, share, TILE)
+        first, second = rows[..., :TILE], rows[..., TILE:]
+        probs = softmax(first, second)
+        grad_probs = products("ued,ucd->uec", first, grad)
+        centre = jnp.sum(probs * grad_probs, axis=1, keepdims=True)
         grad_scores = (probs * (grad_probs - centre)).astype(BF16)
-        grad_values = inner_rows(probs_low, grad)
-        grad_query = jnp.dot(grad_scores, second, preferred_element_type=F32) * scale
-        grad_keys = inner_rows(grad_scores, first) * scale
+        grad_values = products("uec,ucd->ued", probs.astype(BF16), grad)
+        grad_keys = products("uec,ucd->ued", grad_scores, first) * scale
+        grad_query = products("uce,ued->ucd", jnp.swapaxes(grad_scores, 1, 2), second) * scale
         tile_one = jnp.where(value_lane, grad_values, grad_query).astype(BF16)
         tile_two = jnp.where(value_lane, 0.0, grad_keys).astype(BF16)
-        for i, r in enumerate(runs):
-            part = slice(i * share, (i + 1) * share)
-            results[r][0, where, 0:TILE] = tile_one[part]
-            results[r][0, where, TILE:WIDE] = tile_two[part]
-
-    for_each_cluster(long_ref[0], count, 4, work)
+        spread(results, runs, where, share, slice(0, TILE), tile_one)
+        spread(results, runs, where, share, slice(TILE, WIDE), tile_two)
+
+    for_each_batch(long_ref[0], grouped[0].shape[1], batch, work)
 
 
 def attend_back(is_long, grouped, grads):
@@ -258,7 +268,7 @@
             out_specs=[pl.BlockSpec((1, count, WIDE), lambda p, _: (p, 0, 0))] * UNIT,
         ),
         out_shape=[jax.ShapeDtypeStruct((LOCAL_PAIRS, count, WIDE), BF16)] * UNIT,
-        compiler_params=pltpu.CompilerParams(vmem_limit_bytes=48 << 20),
+        compiler_params=pltpu.CompilerParams(vmem_limit_bytes=56 << 20),
         name="attend_back",
     )(is_long, *grouped, *grads)
 
@@ -278,27 +288,28 @@
 def mix_body(order_ref, rows_ref, out_ref):
     count = rows_ref.shape[1]
     chunk = 256
+    parts = count // chunk
     low = lax.broadcasted_iota(jnp.int32, (chunk, TILE), 1) < HEAD
     head = pl.program_id(0)
     for step in range(HEADS_OWN):
 
         @pl.when(head == step)
         def _():
-            for part in range(count // chunk):
+            means = [0.5 * unsorted(order_ref, step, rows_ref, part, chunk) for part in range(parts)]
+            for part in range(parts):
                 where = pl.ds(part * chunk, chunk)
-                mean = (0.5 * unsorted(order_ref, step, rows_ref, part, chunk)).astype(BF16)
                 if step == 0:
-                    out_ref[where, 0:TILE] = mean
+                    out_ref[where, :] = means[part].astype(BF16)
                 elif step == 1:
-                    out_ref[where, 0:TILE] = jnp.where(
-                        low, out_ref[where, 0:TILE].astype(F32), mean.astype(F32)
-                    ).astype(BF16)
-                else:
-                    out_ref[where, TILE:WIDE] = jnp.where(low, mean.astype(F32), 0.0).astype(BF16)
+                    out_ref[where, :] = jnp.where(low, out_ref[where, :].astype(F32), means[part]).astype(BF16)
+                elif part < parts // 2:
+                    both = jnp.where(low, means[part], turn_half(means[part + parts // 2]))
+                    out_ref[pl.ds(count + part * chunk, chunk), :] = both.astype(BF16)
 
 
 def mix(order, rows):
     count = rows.shape[1]
+    packed = (count + count // 2, TILE)
     return pl.pallas_call(
         mix_body,
         grid=(HEADS_OWN,),
@@ -306,8 +317,8 @@
             pl.BlockSpec((8, count), lambda h: (0, 0)),
             pl.BlockSpec((ROUNDS, count, TILE), lambda h: (h, 0, 0)),
         ],
-        out_specs=pl.BlockSpec((count, WIDE), lambda h: (0, 0)),
-        out_shape=jax.ShapeDtypeStruct((count, WIDE), BF16),
+        out_specs=pl.BlockSpec(packed, lambda h: (0, 0)),
+        out_shape=jax.ShapeDtypeStruct(packed, BF16),
         compiler_params=pltpu.CompilerParams(vmem_limit_bytes=48 << 20),
         name="mix",
     )(order, rows)
@@ -342,6 +353,242 @@
     )(order, rows)
 
 
+ERF_TOP = (0.00022905065861350646, 0.0034082910107109506, 0.050955695062380861, 0.18520832239976145, 1.128379143519084)
+ERF_BOTTOM = (
+    -1.1791602954361697e-7,
+    0.000023547966471313185,
+    0.0010179625278914885,
+    0.014070470171167667,
+    0.11098505178285362,
+    0.49746925110067538,
+    1.0,
+)
+
+
+def polynomial(value, factors):
+    total = jnp.full_like(value, factors[0])
+    for factor in factors[1:]:
+        total = total * value + factor
+    return total
+
+
+def error_function(value):
+    value = jnp.clip(value, -3.832506856900711, 3.832506856900711)
+    square = value * value
+    return value * polynomial(square, ERF_TOP) / polynomial(square, ERF_BOTTOM)
+
+
+VEC_ROWS = 16
+FFN_TILE = 256
+
+
+def turn_half(value):
+    return pltpu.roll(value, HEAD, 1)
+
+
+def layer_body(
+    n_shards,
+    table_ref,
+    *refs,
+):
+    shards, refs = refs[:n_shards], refs[n_shards:]
+    parts, refs = refs[:UNIT], refs[UNIT:]
+    x_ref, cot_ref, vec_ref, result_ref, first_ref, back_ref, sums_ref, pieces_ref = refs[:8]
+    w_ref, packed_ref, mixed_ref, hidden_ref, act_ref, down_ref, up_ref, attn_ref = refs[8:16]
+    slope_ref, stage_ref, weight_sem, part_sem, stage_sem = refs[16:]
+    count = x_ref.shape[0]
+    half = count // 2
+    n_weights, shard_rows = shards[0].shape[:2]
+    member = table_ref[0]
+    for k in range(UNIT):
+        pltpu.make_async_copy(parts[k], packed_ref.at[member ^ k], part_sem.at[k]).start()
+    for b in range(n_weights):
+        for n, shard in enumerate(shards):
+            row = pl.multiple_of(table_ref[6 + n], shard_rows)
+            pltpu.make_async_copy(
+                shard.at[b], w_ref.at[b, pl.ds(row, shard_rows), :], weight_sem.at[b]
+            ).start()
+    for k in range(UNIT):
+        pltpu.make_async_copy(parts[k], packed_ref.at[member ^ k], part_sem.at[k]).wait()
+    for b in range(n_weights):
+        pltpu.make_async_copy(w_ref.at[b], w_ref.at[b], weight_sem.at[b]).wait()
+
+    sums_ref[...] = jnp.zeros_like(sums_ref)
+    low = lax.broadcasted_iota(jnp.int32, (FFN_TILE, TILE), 1) < HEAD
+    vec = [vec_ref[i : i + 1, :] for i in range(8 + FFB)]
+    gain_one, shift_one, gain_two, shift_two = vec[:4]
+    bias_out, bias_down = vec[6], vec[7]
+
+    def add_sum(row, value):
+        sums_ref[row : row + 1, :] += jnp.sum(value, axis=0, keepdims=True)
+
+    def tile_step(i, carry):
+        rows = pl.ds(pl.multiple_of(i * FFN_TILE, FFN_TILE), FFN_TILE)
+        is_first = i * FFN_TILE < half
+        extra = pl.ds(pl.multiple_of(count + lax.rem(i * FFN_TILE, half), FFN_TILE), FFN_TILE)
+
+        def pair(m):
+            return packed_ref[m, rows, :].astype(F32)
+
+        def single(m):
+            value = packed_ref[m, extra, :].astype(F32)
+            return jnp.where(is_first, value, turn_half(value))
+
+        for m in (0, 2):
+            at = m * (HEADS_OWN * HEAD)
+            nxt = turn_half(pair(m + 1))
+            mixed_ref[rows, at : at + TILE] = pair(m).astype(BF16)
+            mixed_ref[rows, at + TILE : at + 2 * TILE] = jnp.where(low, single(m), nxt).astype(BF16)
+            mixed_ref[rows, at + 2 * TILE : at + 3 * TILE] = jnp.where(
+                low, nxt, turn_half(single(m + 1))
+            ).astype(BF16)
+        attention = jnp.dot(mixed_ref[rows, :], w_ref[0], preferred_element_type=F32) + bias_out
+        normed_one, rstd_one = normalize(x_ref[rows, :].astype(F32) + attention)
+        hidden = normed_one * gain_one + shift_one
+        hidden_low = hidden.astype(BF16)
+        hidden_ref[rows, :] = hidden_low
+        down = jnp.broadcast_to(bias_down, hidden.shape)
+        for j in range(FFB):
+            up = jnp.dot(hidden_low, w_ref[1 + j], preferred_element_type=F32) + vec[8 + j]
+            phi = 0.5 * (1.0 + error_function(up * SQRT_HALF))
+            slope_ref[j] = phi + up * jnp.exp(-0.5 * up * up) * INV_ROOT_TWO_PI
+            act = (up * phi).astype(BF16)
+            act_ref[j, rows, :] = act
+            down = down + jnp.dot(act, w_ref[1 + FFB + j], preferred_element_type=F32)
+        normed_two, rstd_two = normalize(hidden + down)
+        result_ref[rows, :] = (normed_two * gain_two + shift_two).astype(BF16)
+        grad_result = cot_ref[rows, :].astype(F32)
+        add_sum(2, grad_result * normed_two)
+        add_sum(3, grad_result)
+        grad_second = norm_back(grad_result * gain_two, normed_two, rstd_two)
+        grad_down = grad_second.astype(BF16)
+        down_ref[rows, :] = grad_down
+        add_sum(7, grad_down.astype(F32))
+        grad_hidden = grad_second
+        for j in range(FFB):
+            grad_up = (outer_cols(grad_down, w_ref[1 + FFB + j]) * slope_ref[j]).astype(BF16)
+            up_ref[j, rows, :] = grad_up
+            add_sum(8 + j, grad_up.astype(F32))
+            grad_hidden = grad_hidden + outer_cols(grad_up, w_ref[1 + j])
+        add_sum(0, grad_hidden * normed_one)
+        add_sum(1, grad_hidden)
+        grad_first = norm_back(grad_hidden * gain_one, normed_one, rstd_one)
+        first_ref[rows, :] = grad_first
+        grad_attn = grad_first.astype(BF16)
+        attn_ref[rows, :] = grad_attn
+        add_sum(6, grad_attn.astype(F32))
+        grad_mixed = (0.5 * outer_cols(grad_attn, w_ref[0])).astype(BF16).astype(F32)
+        for m in range(UNIT):
+            at = (m // 2) * 3 * TILE
+            tiles = [grad_mixed[:, at + n * TILE : at + (n + 1) * TILE] for n in range(3)]
+            if m % 2 == 0:
+                two, one = tiles[0], tiles[1]
+            else:
+                two, one = turn_half(jnp.where(low, tiles[2], tiles[1])), turn_half(tiles[2])
+            back_ref[member ^ m, rows, :] = two.astype(BF16)
+
+            @pl.when(is_first)
+            def _(one=one, m=m):
+                back_ref[member ^ m, extra, :] = jnp.where(low, one, 0.0).astype(BF16)
+
+            @pl.when(jnp.logical_not(is_first))
+            def _(one=one, m=m):
+                old = back_ref[member ^ m, extra, :].astype(F32)
+                back_ref[member ^ m, extra, :] = jnp.where(low, old, turn_half(one)).astype(BF16)
+
+        return carry
+
+    lax.fori_loop(0, count // FFN_TILE, tile_step, 0)
+
+    core, bits = table_ref[1], [table_ref[2 + d] for d in range(4)]
+    piece, half_columns = pieces_ref.shape[4:]
+    n_parts = pieces_ref.shape[1]
+
+    def copies(block, slot):
+        part = block // (n_weights // n_parts)
+        made = []
+        for index in range(2 * 16):
+            c = (index % 2) ^ core
+            x, zh, y, zl = ((index >> s) % 2 for s in (1, 2, 3, 4))
+            rel = {"x": x ^ bits[0], "y": y ^ bits[1], "zl": zl ^ bits[2], "zh": zh ^ bits[3]}
+            place = 0
+            for name in PART_ORDERS[part]:
+                place = place * 2 + rel[name]
+            made.append(
+                pltpu.make_async_copy(
+                    stage_ref.at[
+                        slot,
+                        pl.ds(index // 2 * piece, piece),
+                        pl.ds(index % 2 * half_columns, half_columns),
+                    ],
+                    pieces_ref.at[c, part, place, block % (n_weights // n_parts)],
+                    stage_sem.at[slot, index],
+                )
+            )
+        return made
+
+    plan = [(attn_ref, None, mixed_ref, None, 0)]
+    plan += [(down_ref, None, act_ref, j, 1 + FFB + j) for j in range(FFB)]
+    plan += [(up_ref, j, hidden_ref, None, 1 + j) for j in range(FFB)]
+    pending = [None, None]
+    for n, (left, lj, right, rj, block) in enumerate(plan):
+        slot = n % 2
+        if pending[slot] is not None:
+            for copy in pending[slot]:
+                copy.wait()
+        value = inner_rows(
+            left[...] if lj is None else left[lj], right[...] if rj is None else right[rj]
+        )
+        stage_ref[slot] = value.astype(BF16)
+        pending[slot] = copies(block, slot)
+        for copy in pending[slot]:
+            copy.start()
+    for group in pending:
+        for copy in group:
+            copy.wait()
+
+
+PART_ORDERS = (("x", "y", "zl", "zh"), ("y", "zl", "zh", "x"), ("zl", "zh", "x", "y"))
+
+
+def layer(table, shards, parts, inputs, cotangent, vectors):
+    count = inputs.shape[0]
+    n_weights = 1 + 2 * FFB
+    n_shards = len(shards)
+    anywhere = pl.BlockSpec(memory_space=pl.ANY)
+    inside = pl.BlockSpec(memory_space=pltpu.VMEM)
+    packed = parts[0].shape
+    return pl.pallas_call(
+        functools.partial(layer_body, n_shards),
+        in_specs=[pl.BlockSpec(memory_space=pltpu.SMEM)] + [anywhere] * (n_shards + UNIT) + [inside] * 3,
+        out_specs=[inside, inside, inside, inside, anywhere],
+        out_shape=[
+            jax.ShapeDtypeStruct((count, D), BF16),
+            jax.ShapeDtypeStruct((count, D), F32),
+            jax.ShapeDtypeStruct((UNIT, *packed), BF16),
+            jax.ShapeDtypeStruct((VEC_ROWS, D), F32),
+            jax.ShapeDtypeStruct((2, 3, 16, n_weights // 3, D // 16, D // 2), BF16),
+        ],
+        scratch_shapes=[
+            pltpu.VMEM((n_weights, D, D), BF16),
+            pltpu.VMEM((UNIT, *packed), BF16),
+            pltpu.VMEM((count, D), BF16),
+            pltpu.VMEM((count, D), BF16),
+            pltpu.VMEM((FFB, count, D), BF16),
+            pltpu.VMEM((count, D), BF16),
+            pltpu.VMEM((FFB, count, D), BF16),
+            pltpu.VMEM((count, D), BF16),
+            pltpu.VMEM((FFB, FFN_TILE, D), F32),
+            pltpu.VMEM((2, D, D), BF16),
+            pltpu.SemaphoreType.DMA((n_weights,)),
+            pltpu.SemaphoreType.DMA((UNIT,)),
+            pltpu.SemaphoreType.DMA((2, 32)),
+        ],
+        compiler_params=pltpu.CompilerParams(vmem_limit_bytes=60 << 20),
+        name="layer",
+    )(table, *shards, *parts, inputs, cotangent, vectors)
+
+
 def swap(value, axis, bit):
     size = lax.axis_size(axis)
     return lax.ppermute(value, axis, [(i, i ^ bit) for i in range(size)])
@@ -359,9 +606,33 @@
     return [parts[0]] + [swap(parts[k], "tok", k) for k in range(1, UNIT)]
 
 
+LINKS = {"x": ("grp", 2), "y": ("tok", 1), "zl": ("tok", 2), "zh": ("tok", 4)}
+
+
+def reduce_pieces(pieces):
+    other = swap(pieces[1], "grp", 1)
+    done = []
+    for part, names in enumerate(PART_ORDERS):
+        value = pieces[0, part].astype(F32) + other[part].astype(F32)
+        for name in names:
+            half = value.shape[0] // 2
+            value = value[:half] + swap(value[half:].astype(BF16), *LINKS[name]).astype(F32)
+        done.append(value[0].astype(BF16))
+    return jnp.concatenate(done, axis=0)
+
+
 def starts_of(lengths):
     index = jnp.arange(lengths.shape[0])
     return jnp.sum(jnp.where(index[None, :] < index[:, None], lengths[None, :], 0), axis=1)
+
+
+def total_of(value):
+    for axis in ("grp", "tok"):
+        bit = 1
+        while bit < lax.axis_size(axis):
+            value = value + swap(value, axis, bit)
+            bit *= 2
+    return value
 
 
 def pick(values, index):
@@ -449,20 +720,42 @@
 
     inputs = tokens[0]
     unit_inputs = gather_unit(inputs)
+    core, bit_x = grp % 2, grp // 2
 
     local = jnp.transpose(master.astype(BF16), (1, 0, 2))
-    weights = lax.all_gather(local, ("tok", "grp"), axis=0, tiled=False)
-    weights = weights.reshape(n_tok, n_grp * slots, rows_dev, D)
-    weights = jnp.transpose(weights, (1, 0, 2, 3)).reshape(blocks_all, D, D)
-    block = [pick(weights, block_slot[b]) for b in range(blocks_all)]
-    w_out = block[3]
-    w_up = block[4 : 4 + FFB]
-    w_down = block[4 + FFB :]
+    beside = swap(local, "grp", 1)
+    over = swap(local, "grp", 2)
+    by_slot = jnp.concatenate([local, beside, over, swap(over, "grp", 1)], axis=0)
+    at = [((block_slot[b] // slots) ^ grp) * slots + block_slot[b] % slots for b in range(blocks_all)]
+    rows_of = [pick(by_slot, at[b]) for b in range(blocks_all)]
 
     def columns_of(value, m):
         return lax.dynamic_slice_in_dim(value, m * own_width, own_width, value.ndim - 1)
 
-    own_weights = split_heads([columns_of(block[i], member) for i in range(3)])
+    by_owner = jnp.stack(
+        [split_heads([r[:, m * own_width : (m + 1) * own_width] for r in rows_of[:3]]) for m in range(UNIT)]
+    )
+    got = [pick(by_owner, member)]
+    got += [swap(pick(by_owner, member ^ (k % UNIT)), "tok", k) for k in range(1, n_tok)]
+    got = jnp.stack(got)
+    own_weights = jnp.concatenate([pick(got, tok ^ t) for t in range(n_tok)], axis=0)
+
+    part_rows = rows_dev // 2
+    rest_rows = jnp.stack(
+        [lax.dynamic_slice_in_dim(r, core * part_rows, part_rows, 0) for r in rows_of[3:]]
+    )
+    rest_rows, _ = lax.optimization_barrier((rest_rows, unit_inputs[3]))
+    shards, firsts = [], []
+    step = rest_rows
+    for k in range(n_tok // 2):
+        if k:
+            step = lax.ppermute(step, "tok", [(i, (i + 2) % n_tok) for i in range(n_tok)])
+        for flip, value in ((0, step), (1, swap(step, "tok", 1))):
+            source = (tok - 2 * k) % n_tok ^ flip
+            for other in range(2):
+                shards.append(swap(value, "grp", 1) if other else value)
+                firsts.append(source * rows_dev + (core ^ other) * part_rows)
+
     own_bias = split_heads(
         [columns_of(vectors[4], member), jnp.zeros((own_width,), F32), columns_of(vectors[5], member)]
     )
@@ -472,111 +765,44 @@
         grouped.append(sort_rows(orders[k], qkv, WIDE))
     sorted_out = attend(is_long, grouped)
     mixed_parts = exchange_unit([mix(orders[k], sorted_out[k]) for k in range(UNIT)])
-    mixed_low = jnp.concatenate([m[:, :own_width] for m in mixed_parts], axis=1)
-
-    def rows_relative(value):
-        return jnp.concatenate(
-            [
-                lax.dynamic_slice_in_dim(value, (member ^ k) * own_width, own_width, 0)
-                for k in range(UNIT)
-            ],
-            axis=0,
-        )
-
-    w_out_relative = rows_relative(w_out)
-    gain_one, shift_one, gain_two, shift_two = (vectors[i] for i in range(4))
-    attention = jnp.dot(mixed_low, w_out_relative, preferred_element_type=F32) + vectors[6]
-    first_sum = inputs.astype(F32) + attention
-    normed_one, rstd_one = normalize(first_sum)
-    hidden = normed_one * gain_one + shift_one
-    hidden_low = hidden.astype(BF16)
-    up_proj = [
-        jnp.dot(hidden_low, w_up[j], preferred_element_type=F32) + vectors[8 + j] for j in range(FFB)
-    ]
-    act_low = [jax.nn.gelu(u, approximate=False).astype(BF16) for u in up_proj]
-    down_proj = vectors[7] + sum(
-        jnp.dot(act_low[j], w_down[j], preferred_element_type=F32) for j in range(FFB)
-    )
-    second_sum = hidden + down_proj
-    normed_two, rstd_two = normalize(second_sum)
-    result = (normed_two * gain_two + shift_two).astype(BF16)
-    grad_result = cotangent[0].astype(F32)
-    grad_gain_two = jnp.sum(grad_result * normed_two, axis=0)
-    grad_shift_two = jnp.sum(grad_result, axis=0)
-    grad_second = norm_back(grad_result * gain_two, normed_two, rstd_two)
-    grad_down_low = grad_second.astype(BF16)
-    grad_bias_down = jnp.sum(grad_down_low.astype(F32), axis=0)
-    turned_down = [inner_rows(grad_down_low, act_low[j]) for j in range(FFB)]
-    grad_up_low = [
-        (outer_cols(grad_down_low, w_down[j]) * gelu_slope(up_proj[j])).astype(BF16) for j in range(FFB)
-    ]
-    turned_up = [inner_rows(grad_up_low[j], hidden_low) for j in range(FFB)]
-    grad_bias_up = [jnp.sum(g.astype(F32), axis=0) for g in grad_up_low]
-    grad_hidden = grad_second + sum(outer_cols(grad_up_low[j], w_up[j]) for j in range(FFB))
-    grad_gain_one = jnp.sum(grad_hidden * normed_one, axis=0)
-    grad_shift_one = jnp.sum(grad_hidden, axis=0)
-    grad_first = norm_back(grad_hidden * gain_one, normed_one, rstd_one)
-    grad_attn_low = grad_first.astype(BF16)
-    turned_out = inner_rows(grad_attn_low, mixed_low)
-    grad_bias_out = jnp.sum(grad_attn_low.astype(F32), axis=0)
-    grad_mixed = (0.5 * outer_cols(grad_attn_low, w_out_relative)).astype(BF16)
-    zero_half = jnp.zeros((tok_count, WIDE - own_width), BF16)
-    grad_parts = exchange_unit(
-        [
-            jnp.concatenate([grad_mixed[:, k * own_width : (k + 1) * own_width], zero_half], axis=1)
-            for k in range(UNIT)
-        ]
-    )
+    held_weights, *mixed_parts = lax.optimization_barrier((own_weights, *mixed_parts))
+    turned_weights = [swap(held_weights, "tok", k) for k in range(1, UNIT)]
+    table = jnp.stack([member, core, bit_x, tok % 2, tok // 2 % 2, tok // 4, *firsts]).astype(jnp.int32)
+    result, grad_first, back, sums, pieces = layer(
+        table, shards, mixed_parts, inputs, cotangent[0], vectors
+    )
+    grad_parts = exchange_unit([back[k] for k in range(UNIT)])
     sorted_grads = [sort_grads(orders[k], grad_parts[k]) for k in range(UNIT)]
+    rest = reduce_pieces(pieces)
     sorted_back = attend_back(is_long, grouped, sorted_grads)
     own_grads = [gather_grads(orders[k], sorted_back[k]) for k in range(UNIT)]
     turned_qkv = sum(inner_rows(own_grads[k], unit_inputs[k]) for k in range(UNIT))
     bias_qkv = sum(jnp.sum(own_grads[k].astype(F32), axis=0) for k in range(UNIT))
     home_grads = exchange_unit(own_grads)
-    all_weights = jnp.stack(
-        [split_heads([b[:, m * own_width : (m + 1) * own_width] for b in block[:3]]) for m in range(UNIT)]
-    )
     grad_inputs = grad_first + sum(
-        outer_cols(home_grads[k], pick(all_weights, member ^ k)) for k in range(UNIT)
+        outer_cols(home_grads[k], own_weights if k == 0 else turned_weights[k - 1]) for k in range(UNIT)
     )
 
     bias_query, _, bias_value = join_heads(bias_qkv)
     bias_rows = lax.dynamic_update_slice_in_dim(
         jnp.zeros((2, D), F32), jnp.stack([bias_query, bias_value]), member * own_width, 1
     )
-    vector_grads = jnp.concatenate(
-        [
-            jnp.stack([grad_gain_one, grad_shift_one, grad_gain_two, grad_shift_two]),
-            bias_rows,
-            jnp.stack([grad_bias_out, grad_bias_down] + grad_bias_up),
-        ],
-        axis=0,
-    )
-    vector_total = lax.psum(vector_grads, ("tok", "grp"))
-
-    piece = D // n_tok // n_grp
-    turned_out = jnp.concatenate(
-        [turned_out[:, (0) : own_width]]
-        + [turned_out[:, k * own_width : (k + 1) * own_width] for k in range(1, UNIT)],
-        axis=1,
-    )
-    turned_out = jnp.transpose(turned_out.reshape(D, UNIT, own_width), (1, 0, 2))
-    turned_out = jnp.concatenate([pick(turned_out, member ^ m) for m in range(UNIT)], axis=1)
-    rest = jnp.stack([turned_out] + turned_up + turned_down).astype(BF16)
-    rest = rest.reshape(blocks_all - 3, UNIT, n_tok // UNIT, n_grp, piece, D)
-    rest = jnp.transpose(rest, (2, 1, 3, 0, 4, 5)).reshape(n_tok * n_grp, blocks_all - 3, piece, D)
-    rest = lax.psum_scatter(rest, ("tok", "grp"), scatter_dimension=0, tiled=True)[0]
+    vector_grads = sums[: 8 + FFB] + jnp.pad(bias_rows, ((4, 2 + FFB), (0, 0)))
+    vector_total = total_of(vector_grads)
+
     sent = jnp.stack(
         [pick(rest, jnp.maximum(slot_block[s] - 3, 0)) for s in range(blocks_all)]
-    ).reshape(n_grp, slots, piece, D)
+    ).reshape(n_grp, slots, *rest.shape[1:])
     got = lax.all_to_all(sent, "grp", split_axis=0, concat_axis=0, tiled=True)
-    got = jnp.transpose(got, (1, 0, 2, 3)).reshape(slots, n_grp * piece, D).astype(F32)
+    got = jnp.transpose(got.reshape(2, 2, *got.shape[1:]), (2, 0, 3, 1, 4))
+    got = got.reshape(slots, D // n_tok, D).astype(F32)
 
     turned_qkv = jnp.stack(join_heads(jnp.transpose(turned_qkv)))
     turned_qkv = jnp.transpose(turned_qkv.astype(BF16).reshape(3, D, 2, own_width // 2), (2, 0, 3, 1))
     keep = pick(turned_qkv, unit).astype(F32)
-    keep = (keep + swap(pick(turned_qkv, 1 - unit), "tok", UNIT).astype(F32)).astype(BF16)
-    keep = jnp.sum(lax.all_gather(keep, "grp", axis=0, tiled=False).astype(F32), axis=0)
+    keep = keep + swap(pick(turned_qkv, 1 - unit), "tok", UNIT).astype(F32)
+    keep = keep + swap(keep.astype(BF16), "grp", 1).astype(F32)
+    keep = keep + swap(keep.astype(BF16), "grp", 2).astype(F32)
 
     mine = lax.dynamic_slice_in_dim(slot_block, grp * slots, slots, 0)
     reduced = jnp.stack(

time: 966 us -> 748 us (0.77)
  matrix products: 175 us -> 70.7 us
  local copies, waits for them, and re-layouts: 189 us -> 86.8 us
  waiting for transfers between devices: 151 us -> 233 us
  blocking collectives: 61.4 us -> 0 us
  Pallas kernels: 226 us -> 172 us
  starting transfers between devices: 44.4 us -> 85.6 us
  between operations: 50.7 us -> 38.3 us
    ppermute x17 -> x62, waiting for transfers between devices: 101 us -> 220 us  [swap(): return lax.ppermute(value, axis, [(i, i ^ bit) for i in range(size)])]
    pallas_call x1, Pallas kernels: 89.8 us -> 19.5 us  [attend_back(): pl.pallas_call(attend_back_body, grid_spec=pltpu.PrefetchScalarGridSpec(n...]
    pallas_call x0 -> x1, Pallas kernels: none -> 69.3 us  [layer(): pl.pallas_call(functools.partial(layer_body, n_shards), in_specs=[pl.Bloc...]
    unnamed x274 -> x202, local copies, waits for them, and re-layouts: 99.7 us -> 31.5 us
    psum x1 -> x0, blocking collectives: 61.4 us -> none  [fast(): vector_total = lax.psum(vector_grads, ('tok', 'grp'))]
    pallas_call x1, Pallas kernels: 69.9 us -> 16.9 us  [attend(): pl.pallas_call(attend_body, grid_spec=pltpu.PrefetchScalarGridSpec(num_sc...]
    dot_general x9 -> x0, matrix products: 49.8 us -> none  [the longest x4 36.3 us: fast(): jnp.dot(hidden_low, w_up[j], preferred_element_type=F32) + vectors[8 + j]]
    ppermute x17 -> x62, starting transfers between devices: 26.8 us -> 64.4 us  [swap(): return lax.ppermute(value, axis, [(i, i ^ bit) for i in range(size)])]
  transfers between devices with their start and end apart: 24 -> 69, of which waited for: 8 -> 28; matrix products, arithmetic and copies ran while one was open for 24% -> 22% of each run, Pallas kernels for 13% -> 14%
where the time goes in v2:
time: 748 us; the launch traced here: 739 us
  waiting for transfers between devices  233 us (31%)
  Pallas kernels  172 us (23%)
  local copies, waits for them, and re-layouts  86.8 us (12%)
  starting transfers between devices  85.6 us (11%)
  matrix products  70.7 us (9%)
  other arithmetic  53.3 us (7%)
  between operations  38.3 us (5%)
    ppermute x62, waiting for transfers between devices, swap(): return lax.ppermute(value, axis, [(i, i ^ bit) for i in range(size)])  220 us
    pallas_call x1, Pallas kernels, layer(): pl.pallas_call(functools.partial(layer_body, n_shards), in_specs=[pl.Bloc...  69.3 us
    ppermute x62, starting transfers between devices, swap(): return lax.ppermute(value, axis, [(i, i ^ bit) for i in range(size)])  64.4 us
    unnamed x202, local copies, waits for them, and re-layouts  31.5 us
    sort x1, other arithmetic, fast(): jnp.argsort(jnp.stack(own_clusters), axis=-1, stable=True).astype(jnp.int32)  23.9 us
    pallas_call x1, Pallas kernels, attend_back(): pl.pallas_call(attend_back_body, grid_spec=pltpu.PrefetchScalarGridSpec(n...  19.5 us
    dot_general x4, matrix products, outer_cols(): lax.dot_general(left, right, (((1,), (1,)), ((), ())), preferred_element_...  17.6 us
    pallas_call x4, Pallas kernels, sort_rows(): pl.pallas_call(sort_body, grid=(HEADS_OWN,), in_specs=[pl.BlockSpec((8, c...  17.4 us
  transfers between devices with their start and end apart: 69, of which 28 were waited for; matrix products, arithmetic and copies ran while one was open for 22% of the time, Pallas kernels for 14%

profile of v2, /device:TPU:0, one launch (start us, length us, event | category | flops | bytes accessed | tf_op | source)
XLA Modules:
  0.0 739.4 jit_solution(11164423595996887662)
XLA Ops:
  43.4 23.9 %sort.50 = (s32[4,6,1024]{2,0,1:T(4,128)}, s32[4,6,1024]{2,0,1:T(4,128)S(1)}) sort(s32[4,6,1024]{2,0,1:T(4,128)S(1)} %pad_add_fusion, s32[4,6,1024]{2,0,1:T(4,128)S(1)} %iota.23), dimensions={2}, is_stable=true, to_apply=%region_2.3 | sort | flops 368640 | bytes 393216 | tf_op jit(solution)/shard_map/jit(argsort)/sort | solution.py:712
  76.1 9.1 %collective-permute-done.22 = bf16[96,768]{0,1:T(8,128)(2,1)S(1)} collective-permute-done((bf16[96,768]{0,1:T(8,128)(2,1)S(1)}, bf16[96,768]{0,1:T(8,128)(2,1)S(1)}, u32[]{:S(2)}, u32[]{:S(2)}) %collective-permute-start.22) | collective-permute-done | bytes 147488 | tf_op jit(solution)/shard_map/ppermute | solution.py:594
  89.7 9.4 %collective-permute-done.24 = bf16[96,768]{0,1:T(8,128)(2,1)S(1)} collective-permute-done((bf16[96,768]{0,1:T(8,128)(2,1)S(1)}, bf16[96,768]{0,1:T(8,128)(2,1)S(1)}, u32[]{:S(2)}, u32[]{:S(2)}) %collective-permute-start.24) | collective-permute-done | bytes 147488 | tf_op jit(solution)/shard_map/ppermute | solution.py:594
  99.7 11.4 %collective-permute-done.25 = bf16[96,768]{0,1:T(8,128)(2,1)S(1)} collective-permute-done((bf16[96,768]{0,1:T(8,128)(2,1)S(1)}, bf16[96,768]{0,1:T(8,128)(2,1)S(1)}, u32[]{:S(2)}, u32[]{:S(2)}) %collective-permute-start.25) | collective-permute-done | bytes 147488 | tf_op jit(solution)/shard_map/ppermute | solution.py:594
  124.9 11.3 %collective-permute-done.4 = bf16[512,768]{1,0:T(8,128)(2,1)S(1)} collective-permute-done((bf16[512,768]{1,0:T(8,128)(2,1)}, bf16[512,768]{1,0:T(8,128)(2,1)S(1)}, u32[]{:S(2)}, u32[]{:S(2)}) %collective-permute-start.4) | collective-permute-done | bytes 786464 | tf_op jit(solution)/shard_map/ppermute | solution.py:594
  142.3 4.3 sort_rows.4.refs_0_
  150.6 7.5 %collective-permute-done.10.refs_4_ = bf16[9,48,768]{2,1,0:T(8,128)(2,1)S(1)} collective-permute-done((bf16[9,48,768]{2,1,0:T(8,128)(2,1)S(1)}, bf16[9,48,768]{2,1,0:T(8,128)(2,1)S(1)}, u32[]{:S(2)}, u32[]{:S(2)}) %collective-permute-start.10) | collective-permute-done | bytes 663584 | tf_op jit(solution)/shard_map/ppermute | solution.py:752
  161.2 4.5 sort_rows.5.refs_1_
  167.3 4.3 sort_rows.6.refs_2_
  173.2 4.3 sort_rows.7.refs_3_
  179.2 16.9 %attend.1 = (bf16[6,1024,128]{2,1,0:T(8,128)(2,1)S(1)}, bf16[6,1024,128]{2,1,0:T(8,128)(2,1)S(1)}, bf16[6,1024,128]{2,1,0:T(8,128)(2,1)S(1)}, bf16[6,1024,128]{2,1,0:T(8,128)(2,1)}) custom-call(s32[1]{0:T(128)} %bitcast.138.long_ref, bf16[6,1024,256]{2,1,0:T(8,128)(2,1)} %copy-done, bf16[6,1024,256]{2,1,0:T(8,128)(2,1)} %copy-done.1, ...), custom_call_target="tpu_custom_call" | custom-call | tf_op jit(solution)/shard_map/attend/pallas_call | solution.py:218
  216.1 18.5 %collective-permute-done.33.refs_18_ = bf16[1536,128]{1,0:T(8,128)(2,1)S(1)} collective-permute-done((bf16[1536,128]{1,0:T(8,128)(2,1)S(1)}, bf16[1536,128]{1,0:T(8,128)(2,1)S(1)}, u32[]{:S(2)}, u32[]{:S(2)}) %collective-permute-start.33) | collective-permute-done | bytes 393248 | tf_op jit(solution)/shard_map/ppermute | solution.py:594
  238.4 14.1 %collective-permute-done.12.refs_6_ = bf16[9,48,768]{2,1,0:T(8,128)(2,1)} collective-permute-done((bf16[9,48,768]{2,1,0:T(8,128)(2,1)S(1)}, bf16[9,48,768]{2,1,0:T(8,128)(2,1)}, u32[]{:S(2)}, u32[]{:S(2)}) %collective-permute-start.12) | collective-permute-done | bytes 663584 | tf_op jit(solution)/shard_map/ppermute | solution.py:594
  253.4 13.2 %collective-permute-done.16.refs_10_ = bf16[9,48,768]{2,1,0:T(8,128)(2,1)S(1)} collective-permute-done((bf16[9,48,768]{2,1,0:T(8,128)(2,1)}, bf16[9,48,768]{2,1,0:T(8,128)(2,1)S(1)}, u32[]{:S(2)}, u32[]{:S(2)}) %collective-permute-start.16) | collective-permute-done | bytes 663584 | tf_op jit(solution)/shard_map/ppermute | solution.py:594
  266.6 13.2 %collective-permute-done.20.refs_14_ = bf16[9,48,768]{2,1,0:T(8,128)(2,1)} collective-permute-done((bf16[9,48,768]{2,1,0:T(8,128)(2,1)}, bf16[9,48,768]{2,1,0:T(8,128)(2,1)}, u32[]{:S(2)}, u32[]{:S(2)}) %collective-permute-start.20) | collective-permute-done | bytes 663584 | tf_op jit(solution)/shard_map/ppermute | solution.py:594
  286.2 69.3 %layer.1 = (bf16[1024,768]{1,0:T(8,128)(2,1)}, f32[1024,768]{1,0:T(8,128)}, bf16[4,1536,128]{2,1,0:T(8,128)(2,1)}, f32[16,768]{1,0:T(8,128)}, bf16[2,3,16,3,48,384]{5,4,3,2,1,0:T(8,128)(2,1)}) custom-call(s32[22]{0:T(128)} %stack.207.table_ref, bf16[9,48,768]{2,1,0:T(8,128)(2,1)} %copy-done.31, bf16[9,48,768]{2,1,0:T(8,128)(2,1)} %copy-done.34, ...), custom_call_target="tpu_custom_call" | custom-call | tf_op jit(solution)/shard_map/layer/pallas_call | solution.py:561
  355.5 5.5 slice_bitcast_fusion
  378.3 4.2 sort_grads.4.refs_4_
  383.8 4.2 sort_grads.6.refs_6_
  389.1 4.2 sort_grads.7.refs_7_
  394.5 4.4 sort_grads.5.refs_5_
  400.1 19.5 %attend_back.1 = (bf16[6,1024,256]{2,1,0:T(8,128)(2,1)}, bf16[6,1024,256]{2,1,0:T(8,128)(2,1)}, bf16[6,1024,256]{2,1,0:T(8,128)(2,1)}, bf16[6,1024,256]{2,1,0:T(8,128)(2,1)}) custom-call(s32[1]{0:T(128)} %bitcast.138.long_ref, bf16[6,1024,256]{2,1,0:T(8,128)(2,1)} %copy-done, bf16[6,1024,256]{2,1,0:T(8,128)(2,1)} %copy-done.1, ...), custom_call_target="tpu_custom_call" | custom-call | tf_op jit(solution)/shard_map/attend_back/pallas_call | solution.py:261
  425.4 4.3 gather_grads.5
  433.7 4.1 gather_grads.7
  451.2 5.2 convert_add_fusion.2
  460.6 8.9 %collective-permute-done.44 = bf16[3,96,768]{2,1,0:T(8,128)(2,1)S(1)} collective-permute-done((bf16[3,96,768]{2,1,0:T(8,128)(2,1)S(1)}, bf16[3,96,768]{2,1,0:T(8,128)(2,1)S(1)}, u32[]{:S(2)}, u32[]{:S(2)}) %collective-permute-start.44) | collective-permute-done | bytes 442400 | tf_op jit(solution)/shard_map/ppermute | solution.py:594
  482.0 12.7 %collective-permute-done.52 = bf16[8,3,48,384]{3,2,1,0:T(8,128)(2,1)S(1)} collective-permute-done((bf16[8,3,48,384]{3,2,1,0:T(8,128)(2,1)S(1)}, bf16[8,3,48,384]{3,2,1,0:T(8,128)(2,1)S(1)}, u32[]{:S(2)}, u32[]{:S(2)}) %collective-permute-start.52) | collective-permute-done | bytes 884768 | tf_op jit(solution)/shard_map/ppermute | solution.py:594
  498.4 5.4 collective-permute-done.49
  504.0 10.9 %collective-permute-done.53 = bf16[4,3,48,384]{3,2,1,0:T(8,128)(2,1)S(1)} collective-permute-done((bf16[4,3,48,384]{3,2,1,0:T(8,128)(2,1)S(1)}, bf16[4,3,48,384]{3,2,1,0:T(8,128)(2,1)S(1)}, u32[]{:S(2)}, u32[]{:S(2)}) %collective-permute-start.53) | collective-permute-done | bytes 442400 | tf_op jit(solution)/shard_map/ppermute | solution.py:594
  515.1 6.4 collective-permute-done.57
  523.0 8.0 %collective-permute-done.54 = bf16[2,3,48,384]{3,2,1,0:T(8,128)(2,1)S(1)} collective-permute-done((bf16[2,3,48,384]{3,2,1,0:T(8,128)(2,1)S(1)}, bf16[2,3,48,384]{3,2,1,0:T(8,128)(2,1)S(1)}, u32[]{:S(2)}, u32[]{:S(2)}) %collective-permute-start.54) | collective-permute-done | bytes 221216 | tf_op jit(solution)/shard_map/ppermute | solution.py:594
  538.9 4.3 all-to-all-start
  545.8 5.4 all-to-all-done
  559.9 7.9 %fusion.31 = bf16[3,768,96]{1,2,0:T(8,128)(2,1)} fusion(f32[2,3,768,768]{3,2,1,0:T(8,128)} %param.18, f32[1,96,768]{2,1,0:T(8,128)S(1)} %get-tuple-element.85, f32[1,96,768]{2,1,0:T(8,128)S(1)} %get-tuple-element.86, f32[1,96,768]{2,1,0:T(8,128)S(1)} %get-tuple-element.84), kind=kOutput, calls=%fused_computation.47 | convolution fusion | flops 2039095296 | bytes 8404992 | tf_op jit(solution)/shard_map/sia,sci->sac/dot_general | solution.py:815
  572.5 5.9 all-to-all-start.1
  592.0 4.8 fusion.79
  597.0 21.7 %collective-permute-done.63 = f32[12,768]{1,0:T(8,128)S(1)} collective-permute-done((f32[12,768]{1,0:T(8,128)S(1)}, f32[12,768]{1,0:T(8,128)S(1)}, u32[]{:S(2)}, u32[]{:S(2)}) %collective-permute-start.63) | collective-permute-done | bytes 36896 | tf_op jit(solution)/shard_map/ppermute | solution.py:594
  630.3 6.2 fusion.34
  637.7 10.6 %fusion.25 = bf16[3,96,768]{2,1,0:T(8,128)(2,1)} fusion(f32[2,3,768,768]{3,2,1,0:T(8,128)} %param.18, f32[96,3,768]{2,0,1:T(8,128)S(1)} %get-tuple-element.83, f32[96,3,768]{2,0,1:T(8,128)S(1)} %get-tuple-element.82), kind=kOutput, calls=%fused_computation.45 | convolution fusion | flops 2039095296 | bytes 9289728 | tf_op jit(solution)/shard_map/asb,scb->sac/dot_general | solution.py:822
  650.8 4.9 fusion.71
  664.7 4.2 all-to-all-start.2
  668.9 17.5 %collective-permute-done.64 = f32[12,768]{1,0:T(8,128)S(1)} collective-permute-done((f32[12,768]{1,0:T(8,128)S(1)}, f32[12,768]{1,0:T(8,128)S(1)}, u32[]{:S(2)}, u32[]{:S(2)}) %collective-permute-start.64) | collective-permute-done | bytes 36896 | tf_op jit(solution)/shard_map/ppermute | solution.py:594
  686.4 4.6 collective-permute-start.43
  691.7 4.8 fusion.80
  696.4 4.8 fusion.81
  703.1 6.7 fusion.28
  715.2 11.3 %collective-permute-done.43 = bf16[768,768]{0,1:T(8,128)(2,1)} collective-permute-done((bf16[768,768]{0,1:T(8,128)(2,1)}, bf16[768,768]{0,1:T(8,128)(2,1)}, u32[]{:S(2)}, u32[]{:S(2)}) %collective-permute-start.43) | collective-permute-done | bytes 1179680 | tf_op jit(solution)/shard_map/ppermute | solution.py:594
  730.2 5.9 add_bitcast_fusion
  (464 shorter events, 226.5 us)
Async XLA Ops:
  4.9 62.5 %collective-permute-start = (bf16[3,96,768]{2,1,0:T(8,128)(2,1)S(1)}, bf16[3,96,768]{2,1,0:T(8,128)(2,1)S(1)}, u32[]{:S(2)}, u32[]{:S(2)}) collective-permute-start(bf16[3,96,768]{2,1,0:T(8,128)(2,1)S(1)} %convert_bitcast_fusion), channel_id=1, source_target_pairs={{0,1},{1,0},{2,3},{3,2},{4,5},{5,4},{6,7},{7,6},{8,9},{9,8},{10,11... | collective-permute-start | bytes 1327112 | tf_op jit(solution)/shard_map/ppermute | solution.py:594
  6.0 33.7 %collective-permute-start.29 = (s32[6,1024]{1,0:T(8,128)S(1)}, s32[6,1024]{1,0:T(8,128)S(1)}, u32[]{:S(2)}, u32[]{:S(2)}) collective-permute-start(s32[6,1024]{1,0:T(8,128)S(1)} %bitcast.653), channel_id=1, source_target_pairs={{0,4},{4,0},{8,12},{12,8},{16,20},{20,16},{24,28},{28,24},{1,5},{5... | collective-permute-start | bytes 73736 | tf_op jit(solution)/shard_map/ppermute | solution.py:594
  7.6 33.9 %collective-permute-start.30 = (s32[6,1024]{1,0:T(8,128)S(1)}, s32[6,1024]{1,0:T(8,128)S(1)}, u32[]{:S(2)}, u32[]{:S(2)}) collective-permute-start(s32[6,1024]{1,0:T(8,128)S(1)} %bitcast.652), channel_id=1, source_target_pairs={{0,8},{4,12},{8,0},{12,4},{16,24},{20,28},{24,16},{28,20},{1,9},{5... | collective-permute-start | bytes 73736 | tf_op jit(solution)/shard_map/ppermute | solution.py:594
  9.3 34.0 %collective-permute-start.31 = (s32[6,1024]{1,0:T(8,128)S(1)}, s32[6,1024]{1,0:T(8,128)S(1)}, u32[]{:S(2)}, u32[]{:S(2)}) collective-permute-start(s32[6,1024]{1,0:T(8,128)S(1)} %bitcast.651), channel_id=1, source_target_pairs={{0,12},{4,8},{8,4},{12,0},{16,28},{20,24},{24,20},{28,16},{1,13},{... | collective-permute-start | bytes 73736 | tf_op jit(solution)/shard_map/ppermute | solution.py:594
  15.1 52.3 %collective-permute-start.2 = (bf16[3,96,768]{2,1,0:T(8,128)(2,1)S(1)}, bf16[3,96,768]{2,1,0:T(8,128)(2,1)}, u32[]{:S(2)}, u32[]{:S(2)}) collective-permute-start(bf16[3,96,768]{2,1,0:T(8,128)(2,1)S(1)} %collective-permute-done.1), channel_id=1, source_target_pairs={{0,1},{1,0},{2,3},{3,2},{4,5},{5,4},{6,7},{7,6},{8,9},{9,8},{10,11... | collective-permute-start | bytes 1327112 | tf_op jit(solution)/shard_map/ppermute | solution.py:594
  39.8 72.2 %collective-permute-start.3 = (bf16[1024,768]{1,0:T(8,128)(2,1)}, bf16[1024,768]{1,0:T(8,128)(2,1)}, u32[]{:S(2)}, u32[]{:S(2)}) collective-permute-start(bf16[1024,768]{1,0:T(8,128)(2,1)} %bitcast.50.refs_20_), channel_id=1, source_target_pairs={{0,4},{4,0},{8,12},{12,8},{16,20},{20,16},{24,28},{28,24},{1,5},{5... | collective-permute-start | bytes 4718600 | tf_op jit(solution)/shard_map/ppermute | solution.py:594
  41.6 72.5 %collective-permute-start.5 = (bf16[1024,768]{1,0:T(8,128)(2,1)}, bf16[1024,768]{1,0:T(8,128)(2,1)}, u32[]{:S(2)}, u32[]{:S(2)}) collective-permute-start(bf16[1024,768]{1,0:T(8,128)(2,1)} %bitcast.50.refs_20_), channel_id=1, source_target_pairs={{0,8},{4,12},{8,0},{12,4},{16,24},{20,28},{24,16},{28,20},{1,9},{5... | collective-permute-start | bytes 4718600 | tf_op jit(solution)/shard_map/ppermute | solution.py:594
  71.8 46.1 %collective-permute-start.26 = (bf16[96,768]{0,1:T(8,128)(2,1)S(1)}, bf16[96,768]{0,1:T(8,128)(2,1)S(1)}, u32[]{:S(2)}, u32[]{:S(2)}) collective-permute-start(bf16[96,768]{0,1:T(8,128)(2,1)S(1)} %get-tuple-element.94), channel_id=1, source_target_pairs={{0,20},{4,16},{8,28},{12,24},{16,4},{20,0},{24,12},{28,8},{1,21},{... | collective-permute-start | bytes 442376 | tf_op jit(solution)/shard_map/ppermute | solution.py:594
  85.3 32.7 %collective-permute-start.27 = (bf16[96,768]{0,1:T(8,128)(2,1)S(1)}, bf16[96,768]{0,1:T(8,128)(2,1)S(1)}, u32[]{:S(2)}, u32[]{:S(2)}) collective-permute-start(bf16[96,768]{0,1:T(8,128)(2,1)S(1)} %get-tuple-element.93), channel_id=1, source_target_pairs={{0,24},{4,28},{8,16},{12,20},{16,8},{20,12},{24,0},{28,4},{1,25},{... | collective-permute-start | bytes 442376 | tf_op jit(solution)/shard_map/ppermute | solution.py:594
  114.1 22.1 %collective-permute-start.4 = (bf16[512,768]{1,0:T(8,128)(2,1)}, bf16[512,768]{1,0:T(8,128)(2,1)S(1)}, u32[]{:S(2)}, u32[]{:S(2)}) collective-permute-start(bf16[512,768]{1,0:T(8,128)(2,1)} %slice.730), channel_id=1, source_target_pairs={{0,8},{4,12},{8,0},{12,4},{16,24},{20,28},{24,16},{28,20},{1,9},{5... | collective-permute-start | bytes 2359304 | tf_op jit(solution)/shard_map/ppermute | solution.py:594
  116.2 21.6 %collective-permute-start.6 = (bf16[512,768]{1,0:T(8,128)(2,1)}, bf16[512,768]{1,0:T(8,128)(2,1)}, u32[]{:S(2)}, u32[]{:S(2)}) collective-permute-start(bf16[512,768]{1,0:T(8,128)(2,1)} %slice.731), channel_id=1, source_target_pairs={{0,4},{4,0},{8,12},{12,8},{16,20},{20,16},{24,28},{28,24},{1,5},{5... | collective-permute-start | bytes 2359304 | tf_op jit(solution)/shard_map/ppermute | solution.py:594
  138.9 19.1 %collective-permute-start.10 = (bf16[9,48,768]{2,1,0:T(8,128)(2,1)S(1)}, bf16[9,48,768]{2,1,0:T(8,128)(2,1)S(1)}, u32[]{:S(2)}, u32[]{:S(2)}) collective-permute-start(bf16[9,48,768]{2,1,0:T(8,128)(2,1)S(1)} %constant_dynamic-update-slice_fusion.refs_0_), channel_id=1, source_target_pairs={{0,8},{4,12},{8,16},{12,20},{16,24},{20,28},{24,0},{28,4},{1,9},{5... | collective-permute-start | bytes 1990664 | tf_op jit(solution)/shard_map/ppermute | solution.py:752
  158.1 44.3 %collective-permute-start.14 = (bf16[9,48,768]{2,1,0:T(8,128)(2,1)S(1)}, bf16[9,48,768]{2,1,0:T(8,128)(2,1)}, u32[]{:S(2)}, u32[]{:S(2)}) collective-permute-start(bf16[9,48,768]{2,1,0:T(8,128)(2,1)S(1)} %collective-permute-done.10.refs_4_), channel_id=1, source_target_pairs={{0,8},{4,12},{8,16},{12,20},{16,24},{20,28},{24,0},{28,4},{1,9},{5... | collective-permute-start | bytes 1990664 | tf_op jit(solution)/shard_map/ppermute | solution.py:752
  201.4 34.4 %collective-permute-start.8 = (bf16[9,48,768]{2,1,0:T(8,128)(2,1)S(1)}, bf16[9,48,768]{2,1,0:T(8,128)(2,1)S(1)}, u32[]{:S(2)}, u32[]{:S(2)}) collective-permute-start(bf16[9,48,768]{2,1,0:T(8,128)(2,1)S(1)} %constant_dynamic-update-slice_fusion.refs_0_), channel_id=1, source_target_pairs={{0,4},{4,0},{8,12},{12,8},{16,20},{20,16},{24,28},{28,24},{1,5},{5... | collective-permute-start | bytes 1990664 | tf_op jit(solution)/shard_map/ppermute | solution.py:594
  202.3 34.0 %collective-permute-start.7 = (bf16[9,48,768]{2,1,0:T(8,128)(2,1)S(1)}, bf16[9,48,768]{2,1,0:T(8,128)(2,1)S(1)}, u32[]{:S(2)}, u32[]{:S(2)}) collective-permute-start(bf16[9,48,768]{2,1,0:T(8,128)(2,1)S(1)} %constant_dynamic-update-slice_fusion.refs_0_), channel_id=1, source_target_pairs={{0,1},{1,0},{2,3},{3,2},{4,5},{5,4},{6,7},{7,6},{8,9},{9,8},{10,11... | collective-permute-start | bytes 1990664 | tf_op jit(solution)/shard_map/ppermute | solution.py:594
  202.3 34.9 %collective-permute-start.18 = (bf16[9,48,768]{2,1,0:T(8,128)(2,1)}, bf16[9,48,768]{2,1,0:T(8,128)(2,1)}, u32[]{:S(2)}, u32[]{:S(2)}) collective-permute-start(bf16[9,48,768]{2,1,0:T(8,128)(2,1)} %collective-permute-done.14.refs_8_), channel_id=1, source_target_pairs={{0,8},{4,12},{8,16},{12,20},{16,24},{20,28},{24,0},{28,4},{1,9},{5... | collective-permute-start | bytes 1990664 | tf_op jit(solution)/shard_map/ppermute | solution.py:752
  208.8 25.8 %collective-permute-start.33 = (bf16[1536,128]{1,0:T(8,128)(2,1)S(1)}, bf16[1536,128]{1,0:T(8,128)(2,1)S(1)}, u32[]{:S(2)}, u32[]{:S(2)}) collective-permute-start(bf16[1536,128]{1,0:T(8,128)(2,1)S(1)} %mix.6), channel_id=1, source_target_pairs={{0,8},{4,12},{8,0},{12,4},{16,24},{20,28},{24,16},{28,20},{1,9},{5... | collective-permute-start | bytes 1179656 | tf_op jit(solution)/shard_map/ppermute | solution.py:594
  215.5 20.3 %collective-permute-start.32 = (bf16[1536,128]{1,0:T(8,128)(2,1)S(1)}, bf16[1536,128]{1,0:T(8,128)(2,1)S(1)}, u32[]{:S(2)}, u32[]{:S(2)}) collective-permute-start(bf16[1536,128]{1,0:T(8,128)(2,1)S(1)} %mix.5), channel_id=1, source_target_pairs={{0,4},{4,0},{8,12},{12,8},{16,20},{20,16},{24,28},{28,24},{1,5},{5... | collective-permute-start | bytes 1179656 | tf_op jit(solution)/shard_map/ppermute | solution.py:594
  236.4 30.2 %collective-permute-start.16 = (bf16[9,48,768]{2,1,0:T(8,128)(2,1)}, bf16[9,48,768]{2,1,0:T(8,128)(2,1)S(1)}, u32[]{:S(2)}, u32[]{:S(2)}) collective-permute-start(bf16[9,48,768]{2,1,0:T(8,128)(2,1)} %collective-permute-done.14.refs_8_), channel_id=1, source_target_pairs={{0,4},{4,0},{8,12},{12,8},{16,20},{20,16},{24,28},{28,24},{1,5},{5... | collective-permute-start | bytes 1990664 | tf_op jit(solution)/shard_map/ppermute | solution.py:594
  237.2 42.6 %collective-permute-start.20 = (bf16[9,48,768]{2,1,0:T(8,128)(2,1)}, bf16[9,48,768]{2,1,0:T(8,128)(2,1)}, u32[]{:S(2)}, u32[]{:S(2)}) collective-permute-start(bf16[9,48,768]{2,1,0:T(8,128)(2,1)} %collective-permute-done.18.refs_12_), channel_id=1, source_target_pairs={{0,4},{4,0},{8,12},{12,8},{16,20},{20,16},{24,28},{28,24},{1,5},{5... | collective-permute-start | bytes 1990664 | tf_op jit(solution)/shard_map/ppermute | solution.py:594
  252.5 32.8 %collective-permute-start.15 = (bf16[9,48,768]{2,1,0:T(8,128)(2,1)}, bf16[9,48,768]{2,1,0:T(8,128)(2,1)}, u32[]{:S(2)}, u32[]{:S(2)}) collective-permute-start(bf16[9,48,768]{2,1,0:T(8,128)(2,1)} %collective-permute-done.14.refs_8_), channel_id=1, source_target_pairs={{0,1},{1,0},{2,3},{3,2},{4,5},{5,4},{6,7},{7,6},{8,9},{9,8},{10,11... | collective-permute-start | bytes 1990664 | tf_op jit(solution)/shard_map/ppermute | solution.py:594
  252.5 32.8 %collective-permute-start.13 = (bf16[9,48,768]{2,1,0:T(8,128)(2,1)}, bf16[9,48,768]{2,1,0:T(8,128)(2,1)S(1)}, u32[]{:S(2)}, u32[]{:S(2)}) collective-permute-start(bf16[9,48,768]{2,1,0:T(8,128)(2,1)} %collective-permute-done.12.refs_6_), channel_id=1, source_target_pairs={{0,1},{1,0},{2,3},{3,2},{4,5},{5,4},{6,7},{7,6},{8,9},{9,8},{10,11... | collective-permute-start | bytes 1990664 | tf_op jit(solution)/shard_map/ppermute | solution.py:594
  253.1 32.2 %collective-permute-start.19 = (bf16[9,48,768]{2,1,0:T(8,128)(2,1)}, bf16[9,48,768]{2,1,0:T(8,128)(2,1)}, u32[]{:S(2)}, u32[]{:S(2)}) collective-permute-start(bf16[9,48,768]{2,1,0:T(8,128)(2,1)} %collective-permute-done.18.refs_12_), channel_id=1, source_target_pairs={{0,1},{1,0},{2,3},{3,2},{4,5},{5,4},{6,7},{7,6},{8,9},{9,8},{10,11... | collective-permute-start | bytes 1990664 | tf_op jit(solution)/shard_map/ppermute | solution.py:594
  266.6 18.7 %collective-permute-start.17 = (bf16[9,48,768]{2,1,0:T(8,128)(2,1)S(1)}, bf16[9,48,768]{2,1,0:T(8,128)(2,1)}, u32[]{:S(2)}, u32[]{:S(2)}) collective-permute-start(bf16[9,48,768]{2,1,0:T(8,128)(2,1)S(1)} %collective-permute-done.16.refs_10_), channel_id=1, source_target_pairs={{0,1},{1,0},{2,3},{3,2},{4,5},{5,4},{6,7},{7,6},{8,9},{9,8},{10,11... | collective-permute-start | bytes 1990664 | tf_op jit(solution)/shard_map/ppermute | solution.py:594
  361.0 88.8 %collective-permute-start.47 = (bf16[3,16,3,48,384]{4,3,2,1,0:T(8,128)(2,1)}, bf16[3,16,3,48,384]{4,3,2,1,0:T(8,128)(2,1)}, u32[]{:S(2)}, u32[]{:S(2)}) collective-permute-start(bf16[3,16,3,48,384]{4,3,2,1,0:T(8,128)(2,1)} %slice_bitcast_fusion), channel_id=1, source_target_pairs={{0,1},{1,0},{2,3},{3,2},{4,5},{5,4},{6,7},{7,6},{8,9},{9,8},{10,11... | collective-permute-start | bytes 15925256 | tf_op jit(solution)/shard_map/ppermute | solution.py:594
  361.6 22.1 %collective-permute-start.36 = (bf16[1536,128]{1,0:T(8,128)(2,1)S(1)}, bf16[1536,128]{1,0:T(8,128)(2,1)S(1)}, u32[]{:S(2)}, u32[]{:S(2)}) collective-permute-start(bf16[1536,128]{1,0:T(8,128)(2,1)S(1)} %get-tuple-element.62), channel_id=1, source_target_pairs={{0,8},{4,12},{8,0},{12,4},{16,24},{20,28},{24,16},{28,20},{1,9},{5... | collective-permute-start | bytes 1179656 | tf_op jit(solution)/shard_map/ppermute | solution.py:594
  361.7 27.4 %collective-permute-start.37 = (bf16[1536,128]{1,0:T(8,128)(2,1)S(1)}, bf16[1536,128]{1,0:T(8,128)(2,1)S(1)}, u32[]{:S(2)}, u32[]{:S(2)}) collective-permute-start(bf16[1536,128]{1,0:T(8,128)(2,1)S(1)} %get-tuple-element.61), channel_id=1, source_target_pairs={{0,12},{4,8},{8,4},{12,0},{16,28},{20,24},{24,20},{28,16},{1,13},{... | collective-permute-start | bytes 1179656 | tf_op jit(solution)/shard_map/ppermute | solution.py:594
  364.2 30.4 %collective-permute-start.35 = (bf16[1536,128]{1,0:T(8,128)(2,1)S(1)}, bf16[1536,128]{1,0:T(8,128)(2,1)S(1)}, u32[]{:S(2)}, u32[]{:S(2)}) collective-permute-start(bf16[1536,128]{1,0:T(8,128)(2,1)S(1)} %get-tuple-element.63), channel_id=1, source_target_pairs={{0,4},{4,0},{8,12},{12,8},{16,20},{20,16},{24,28},{28,24},{1,5},{5... | collective-permute-start | bytes 1179656 | tf_op jit(solution)/shard_map/ppermute | solution.py:594
  448.6 20.8 %collective-permute-start.44 = (bf16[3,96,768]{2,1,0:T(8,128)(2,1)S(1)}, bf16[3,96,768]{2,1,0:T(8,128)(2,1)S(1)}, u32[]{:S(2)}, u32[]{:S(2)}) collective-permute-start(bf16[3,96,768]{2,1,0:T(8,128)(2,1)S(1)} %dynamic-slice_bitcast_fusion), channel_id=1, source_target_pairs={{0,16},{4,20},{8,24},{12,28},{16,0},{20,4},{24,8},{28,12},{1,17},{... | collective-permute-start | bytes 1327112 | tf_op jit(solution)/shard_map/ppermute | solution.py:594
  459.1 20.4 %collective-permute-start.48 = (bf16[8,3,48,384]{3,2,1,0:T(8,128)(2,1)}, bf16[8,3,48,384]{3,2,1,0:T(8,128)(2,1)}, u32[]{:S(2)}, u32[]{:S(2)}) collective-permute-start(bf16[8,3,48,384]{3,2,1,0:T(8,128)(2,1)} %slice.1116), channel_id=1, source_target_pairs={{0,2},{1,3},{2,0},{3,1},{4,6},{5,7},{6,4},{7,5},{8,10},{9,11},{10,... | collective-permute-start | bytes 2654216 | tf_op jit(solution)/shard_map/ppermute | solution.py:594
  472.2 22.5 %collective-permute-start.52 = (bf16[8,3,48,384]{3,2,1,0:T(8,128)(2,1)S(1)}, bf16[8,3,48,384]{3,2,1,0:T(8,128)(2,1)S(1)}, u32[]{:S(2)}, u32[]{:S(2)}) collective-permute-start(bf16[8,3,48,384]{3,2,1,0:T(8,128)(2,1)S(1)} %slice.1115), channel_id=1, source_target_pairs={{0,4},{4,0},{8,12},{12,8},{16,20},{20,16},{24,28},{28,24},{1,5},{5... | collective-permute-start | bytes 2654216 | tf_op jit(solution)/shard_map/ppermute | solution.py:594
  475.1 21.8 %collective-permute-start.56 = (bf16[8,3,48,384]{3,2,1,0:T(8,128)(2,1)S(1)}, bf16[8,3,48,384]{3,2,1,0:T(8,128)(2,1)S(1)}, u32[]{:S(2)}, u32[]{:S(2)}) collective-permute-start(bf16[8,3,48,384]{3,2,1,0:T(8,128)(2,1)S(1)} %slice.1114), channel_id=1, source_target_pairs={{0,8},{4,12},{8,0},{12,4},{16,24},{20,28},{24,16},{28,20},{1,9},{5... | collective-permute-start | bytes 2654216 | tf_op jit(solution)/shard_map/ppermute | solution.py:594
  477.2 66.1 %collective-permute-start.46 = (bf16[3,96,768]{2,1,0:T(8,128)(2,1)}, bf16[3,96,768]{2,1,0:T(8,128)(2,1)}, u32[]{:S(2)}, u32[]{:S(2)}) collective-permute-start(bf16[3,96,768]{2,1,0:T(8,128)(2,1)} %fusion.44), channel_id=1, source_target_pairs={{0,2},{1,3},{2,0},{3,1},{4,6},{5,7},{6,4},{7,5},{8,10},{9,11},{10,... | collective-permute-start | bytes 1327112 | tf_op jit(solution)/shard_map/ppermute | solution.py:594
  481.0 22.8 %collective-permute-start.49 = (bf16[4,3,48,384]{3,2,1,0:T(8,128)(2,1)S(1)}, bf16[4,3,48,384]{3,2,1,0:T(8,128)(2,1)S(1)}, u32[]{:S(2)}, u32[]{:S(2)}) collective-permute-start(bf16[4,3,48,384]{3,2,1,0:T(8,128)(2,1)S(1)} %slice.1119), channel_id=1, source_target_pairs={{0,4},{4,0},{8,12},{12,8},{16,20},{20,16},{24,28},{28,24},{1,5},{5... | collective-permute-start | bytes 1327112 | tf_op jit(solution)/shard_map/ppermute | solution.py:594
  494.9 20.0 %collective-permute-start.53 = (bf16[4,3,48,384]{3,2,1,0:T(8,128)(2,1)S(1)}, bf16[4,3,48,384]{3,2,1,0:T(8,128)(2,1)S(1)}, u32[]{:S(2)}, u32[]{:S(2)}) collective-permute-start(bf16[4,3,48,384]{3,2,1,0:T(8,128)(2,1)S(1)} %slice.1118), channel_id=1, source_target_pairs={{0,8},{4,12},{8,0},{12,4},{16,24},{20,28},{24,16},{28,20},{1,9},{5... | collective-permute-start | bytes 1327112 | tf_op jit(solution)/shard_map/ppermute | solution.py:594
  497.1 24.4 %collective-permute-start.57 = (bf16[4,3,48,384]{3,2,1,0:T(8,128)(2,1)S(1)}, bf16[4,3,48,384]{3,2,1,0:T(8,128)(2,1)S(1)}, u32[]{:S(2)}, u32[]{:S(2)}) collective-permute-start(bf16[4,3,48,384]{3,2,1,0:T(8,128)(2,1)S(1)} %slice.1117), channel_id=1, source_target_pairs={{0,16},{4,20},{8,24},{12,28},{16,0},{20,4},{24,8},{28,12},{1,17},{... | collective-permute-start | bytes 1327112 | tf_op jit(solution)/shard_map/ppermute | solution.py:594
  503.9 18.8 %collective-permute-start.50 = (bf16[2,3,48,384]{3,2,1,0:T(8,128)(2,1)S(1)}, bf16[2,3,48,384]{3,2,1,0:T(8,128)(2,1)S(1)}, u32[]{:S(2)}, u32[]{:S(2)}) collective-permute-start(bf16[2,3,48,384]{3,2,1,0:T(8,128)(2,1)S(1)} %slice.1122), channel_id=1, source_target_pairs={{0,8},{4,12},{8,0},{12,4},{16,24},{20,28},{24,16},{28,20},{1,9},{5... | collective-permute-start | bytes 663560 | tf_op jit(solution)/shard_map/ppermute | solution.py:594
  572.5 47.3 %all-to-all-start.1 = ((bf16[8,3,96,96]{3,2,1,0:T(8,128)(2,1)}), bf16[8,3,96,96]{3,2,1,0:T(8,128)(2,1)}, u32[]{:S(2)}, u32[]{:S(2)}) async-start(bf16[8,3,96,96]{3,2,1,0:T(8,128)(2,1)} %bitcast.602), calls=%async_computation.1 | async-start | bytes 1179648 | tf_op jit(solution)/shard_map/all_to_all | solution.py:646
  586.7 73.6 %collective-permute-start.39 = (bf16[768,768]{0,1:T(8,128)(2,1)}, bf16[768,768]{0,1:T(8,128)(2,1)}, u32[]{:S(2)}, u32[]{:S(2)}) collective-permute-start(bf16[768,768]{0,1:T(8,128)(2,1)} %copy-done.30), channel_id=1, source_target_pairs={{0,4},{4,0},{8,12},{12,8},{16,20},{20,16},{24,28},{28,24},{1,5},{5... | collective-permute-start | bytes 3538952 | tf_op jit(solution)/shard_map/ppermute | solution.py:594
  586.7 109.7 %collective-permute-start.41 = (bf16[768,768]{0,1:T(8,128)(2,1)}, bf16[768,768]{0,1:T(8,128)(2,1)}, u32[]{:S(2)}, u32[]{:S(2)}) collective-permute-start(bf16[768,768]{0,1:T(8,128)(2,1)} %copy-done.30), channel_id=1, source_target_pairs={{0,8},{4,12},{8,0},{12,4},{16,24},{20,28},{24,16},{28,20},{1,9},{5... | collective-permute-start | bytes 3538952 | tf_op jit(solution)/shard_map/ppermute | solution.py:594
  588.6 103.1 %collective-permute-start.38 = (bf16[1024,768]{1,0:T(8,128)(2,1)}, bf16[1024,768]{1,0:T(8,128)(2,1)}, u32[]{:S(2)}, u32[]{:S(2)}) collective-permute-start(bf16[1024,768]{1,0:T(8,128)(2,1)} %copy-done.4), channel_id=1, source_target_pairs={{0,4},{4,0},{8,12},{12,8},{16,20},{20,16},{24,28},{28,24},{1,5},{5... | collective-permute-start | bytes 4718600 | tf_op jit(solution)/shard_map/ppermute | solution.py:594
  590.1 28.6 %collective-permute-start.63 = (f32[12,768]{1,0:T(8,128)S(1)}, f32[12,768]{1,0:T(8,128)S(1)}, u32[]{:S(2)}, u32[]{:S(2)}) collective-permute-start(f32[12,768]{1,0:T(8,128)S(1)} %add.655), channel_id=1, source_target_pairs={{0,8},{4,12},{8,0},{12,4},{16,24},{20,28},{24,16},{28,20},{1,9},{5... | collective-permute-start | bytes 110600 | tf_op jit(solution)/shard_map/ppermute | solution.py:594
  596.8 99.7 %collective-permute-start.40 = (bf16[1024,768]{1,0:T(8,128)(2,1)S(1)}, bf16[1024,768]{1,0:T(8,128)(2,1)}, u32[]{:S(2)}, u32[]{:S(2)}) collective-permute-start(bf16[1024,768]{1,0:T(8,128)(2,1)S(1)} %gather_grads.6), channel_id=1, source_target_pairs={{0,8},{4,12},{8,0},{12,4},{16,24},{20,28},{24,16},{28,20},{1,9},{5... | collective-permute-start | bytes 4718600 | tf_op jit(solution)/shard_map/ppermute | solution.py:594
  618.7 107.8 %collective-permute-start.42 = (bf16[1024,768]{1,0:T(8,128)(2,1)S(1)}, bf16[1024,768]{1,0:T(8,128)(2,1)}, u32[]{:S(2)}, u32[]{:S(2)}) collective-permute-start(bf16[1024,768]{1,0:T(8,128)(2,1)S(1)} %gather_grads.7), channel_id=1, source_target_pairs={{0,12},{4,8},{8,4},{12,0},{16,28},{20,24},{24,20},{28,16},{1,13},{... | collective-permute-start | bytes 4718600 | tf_op jit(solution)/shard_map/ppermute | solution.py:594
  660.3 26.1 %collective-permute-start.64 = (f32[12,768]{1,0:T(8,128)S(1)}, f32[12,768]{1,0:T(8,128)S(1)}, u32[]{:S(2)}, u32[]{:S(2)}) collective-permute-start(f32[12,768]{1,0:T(8,128)S(1)} %add.656), channel_id=1, source_target_pairs={{0,16},{4,20},{8,24},{12,28},{16,0},{20,4},{24,8},{28,12},{1,17},{... | collective-permute-start | bytes 110600 | tf_op jit(solution)/shard_map/ppermute | solution.py:594
  664.7 36.6 %all-to-all-start.2 = ((bf16[8,3,96,96]{3,2,1,0:T(8,128)(2,1)}), bf16[8,3,96,96]{3,2,1,0:T(8,128)(2,1)}, u32[]{:S(2)}, u32[]{:S(2)}) async-start(bf16[8,3,96,96]{3,2,1,0:T(8,128)(2,1)} %constant_dynamic-update-slice_fusion.87), calls=%async_computation.2 | async-start | bytes 1179648 | tf_op jit(solution)/shard_map/all_to_all | solution.py:656
  686.4 40.1 %collective-permute-start.43 = (bf16[768,768]{0,1:T(8,128)(2,1)}, bf16[768,768]{0,1:T(8,128)(2,1)}, u32[]{:S(2)}, u32[]{:S(2)}) collective-permute-start(bf16[768,768]{0,1:T(8,128)(2,1)} %copy-done.30), channel_id=1, source_target_pairs={{0,12},{4,8},{8,4},{12,0},{16,28},{20,24},{24,20},{28,16},{1,13},{... | collective-permute-start | bytes 3538952 | tf_op jit(solution)/shard_map/ppermute | solution.py:594
  711.6 24.4 %all-to-all-start.3 = ((bf16[8,3,96,96]{3,2,1,0:T(8,128)(2,1)}), bf16[8,3,96,96]{3,2,1,0:T(8,128)(2,1)S(1)}, u32[]{:S(2)}, u32[]{:S(2)}) async-start(bf16[8,3,96,96]{3,2,1,0:T(8,128)(2,1)} %bitcast.230), calls=%async_computation.3 | async-start | bytes 1179648 | tf_op jit(solution)/shard_map/all_to_all | solution.py:646
  (75 other events, 973.9 us)

commit v3 on v2

--- a/solution.py
+++ b/solution.py
@@ -33,6 +33,7 @@
 LOCAL_PAIRS = ROUNDS * HEADS_OWN
 TILE = 128
 WIDE = 2 * TILE
+SMALL = pl.CostEstimate(flops=0, transcendentals=0, bytes_accessed=0)
 
 
 def inner_rows(left, right):
@@ -64,8 +65,73 @@
     )
 
 
-def sort_body(order_ref, rows_ref, out_ref, column_ref):
-    count = rows_ref.shape[0]
+def turn_half(value):
+    return pltpu.roll(value, HEAD, 1)
+
+
+def arrange_body(rows_ref, out_ref):
+    count = rows_ref.shape[1]
+    low = lax.broadcasted_iota(jnp.int32, (count, TILE), 1) < HEAD
+
+    def half(part, head, high):
+        at = head // 2 * TILE
+        tile = rows_ref[part, :, at : at + TILE].astype(F32)
+        return tile if head % 2 == high else turn_half(tile)
+
+    for head in range(H):
+        own = head % HEADS_OWN
+        odd = own % 2
+        value = half(2, head, odd)
+        query = half(0, head, 1 - odd)
+        keys = half(1, head, 1 - odd)
+        one = jnp.where(low, query, value) if odd else jnp.where(low, value, query)
+        two = jnp.where(low, keys, 0.0) if odd else jnp.where(low, 0.0, keys)
+        out_ref[head // HEADS_OWN, :, own * WIDE : own * WIDE + TILE] = one.astype(BF16)
+        out_ref[head // HEADS_OWN, :, own * WIDE + TILE : (own + 1) * WIDE] = two.astype(BF16)
+
+
+def arrange(rows):
+    return pl.pallas_call(
+        arrange_body,
+        out_shape=jax.ShapeDtypeStruct((UNIT, rows.shape[1], HEADS_OWN * WIDE), BF16),
+        cost_estimate=SMALL,
+        name="arrange",
+    )(rows)
+
+
+def assemble_body(table_ref, *refs):
+    shards, out_ref, sem = refs[:-2], refs[-2], refs[-1]
+    rows = shards[0].shape[1]
+    copies = []
+    for shard in shards:
+        for i in range(shard.shape[0]):
+            n = len(copies)
+            first = pl.multiple_of(table_ref[n], rows)
+            copies.append(
+                pltpu.make_async_copy(shard.at[i], out_ref.at[pl.ds(first, rows), :], sem.at[n])
+            )
+    for copy in copies:
+        copy.start()
+    for copy in copies:
+        copy.wait()
+
+
+def assemble(table, shards):
+    pieces = sum(s.shape[0] for s in shards)
+    anywhere = pl.BlockSpec(memory_space=pl.ANY)
+    return pl.pallas_call(
+        assemble_body,
+        in_specs=[pl.BlockSpec(memory_space=pltpu.SMEM)] + [anywhere] * len(shards),
+        out_specs=anywhere,
+        out_shape=jax.ShapeDtypeStruct((pieces * shards[0].shape[1], shards[0].shape[2]), BF16),
+        scratch_shapes=[pltpu.SemaphoreType.DMA((pieces,))],
+        cost_estimate=SMALL,
+        name="assemble",
+    )(table, *shards)
+
+
+def sort_body(order_ref, x_ref, weight_ref, bias_ref, out_ref, column_ref, rows_ref):
+    count = x_ref.shape[0]
 
     @pl.when(pl.program_id(0) == 0)
     def _():
@@ -74,6 +140,9 @@
     head = pl.program_id(0)
     chunk = 256
     lane = lax.broadcasted_iota(jnp.int32, (chunk, count), 1)
+    rows_ref[...] = (
+        jnp.dot(x_ref[...], weight_ref[...], preferred_element_type=F32) + bias_ref[...]
+    ).astype(BF16)
     for step in range(HEADS_OWN):
 
         @pl.when(head == step)
@@ -88,21 +157,24 @@
                     ).astype(BF16)
 
 
-def sort_rows(order, rows, width):
-    count = rows.shape[0]
+def sort_rows(order, inputs, weights, bias):
+    count = inputs.shape[0]
     return pl.pallas_call(
         sort_body,
         grid=(HEADS_OWN,),
         in_specs=[
             pl.BlockSpec((8, count), lambda h: (0, 0)),
-            pl.BlockSpec((count, width), lambda h: (0, h)),
+            pl.BlockSpec((count, D), lambda h: (0, 0)),
+            pl.BlockSpec((D, WIDE), lambda h: (0, h)),
+            pl.BlockSpec((1, WIDE), lambda h: (0, h)),
         ],
-        out_specs=pl.BlockSpec((ROUNDS, count, width), lambda h: (h, 0, 0)),
-        out_shape=jax.ShapeDtypeStruct((LOCAL_PAIRS, count, width), BF16),
-        scratch_shapes=[pltpu.VMEM((count, 8), jnp.int32)],
+        out_specs=pl.BlockSpec((ROUNDS, count, WIDE), lambda h: (h, 0, 0)),
+        out_shape=jax.ShapeDtypeStruct((LOCAL_PAIRS, count, WIDE), BF16),
+        scratch_shapes=[pltpu.VMEM((count, 8), jnp.int32), pltpu.VMEM((count, WIDE), BF16)],
         compiler_params=pltpu.CompilerParams(vmem_limit_bytes=48 << 20),
+        cost_estimate=SMALL,
         name="sort_rows",
-    )(order, rows)
+    )(order, inputs, weights, bias)
 
 
 def sort_grads_body(order_ref, rows_ref, out_ref, column_ref):
@@ -151,6 +223,7 @@
         out_shape=jax.ShapeDtypeStruct((LOCAL_PAIRS, count, TILE), BF16),
         scratch_shapes=[pltpu.VMEM((count, 8), jnp.int32)],
         compiler_params=pltpu.CompilerParams(vmem_limit_bytes=48 << 20),
+        cost_estimate=SMALL,
         name="sort_grads",
     )(order, rows)
 
@@ -225,6 +298,7 @@
         ),
         out_shape=[jax.ShapeDtypeStruct((LOCAL_PAIRS, count, TILE), BF16)] * UNIT,
         compiler_params=pltpu.CompilerParams(vmem_limit_bytes=48 << 20),
+        cost_estimate=SMALL,
         name="attend",
     )(is_long, *grouped)
 
@@ -269,6 +343,7 @@
         ),
         out_shape=[jax.ShapeDtypeStruct((LOCAL_PAIRS, count, WIDE), BF16)] * UNIT,
         compiler_params=pltpu.CompilerParams(vmem_limit_bytes=56 << 20),
+        cost_estimate=SMALL,
         name="attend_back",
     )(is_long, *grouped, *grads)
 
@@ -320,6 +395,7 @@
         out_specs=pl.BlockSpec(packed, lambda h: (0, 0)),
         out_shape=jax.ShapeDtypeStruct(packed, BF16),
         compiler_params=pltpu.CompilerParams(vmem_limit_bytes=48 << 20),
+        cost_estimate=SMALL,
         name="mix",
     )(order, rows)
 
@@ -349,6 +425,7 @@
         out_specs=pl.BlockSpec((count, WIDE), lambda h: (0, h)),
         out_shape=jax.ShapeDtypeStruct((count, HEADS_OWN * WIDE), BF16),
         compiler_params=pltpu.CompilerParams(vmem_limit_bytes=48 << 20),
+        cost_estimate=SMALL,
         name="gather_grads",
     )(order, rows)
 
@@ -382,10 +459,6 @@
 FFN_TILE = 256
 
 
-def turn_half(value):
-    return pltpu.roll(value, HEAD, 1)
-
-
 def layer_body(
     n_shards,
     table_ref,
@@ -393,20 +466,20 @@
 ):
     shards, refs = refs[:n_shards], refs[n_shards:]
     parts, refs = refs[:UNIT], refs[UNIT:]
-    x_ref, cot_ref, vec_ref, result_ref, first_ref, back_ref, sums_ref, pieces_ref = refs[:8]
-    w_ref, packed_ref, mixed_ref, hidden_ref, act_ref, down_ref, up_ref, attn_ref = refs[8:16]
-    slope_ref, stage_ref, weight_sem, part_sem, stage_sem = refs[16:]
+    x_ref, cot_ref, vec_ref, result_ref, first_ref, back_ref, sums_ref, kept_ref, sent_ref = refs[:9]
+    w_ref, packed_ref, mixed_ref, hidden_ref, act_ref, down_ref, up_ref, attn_ref = refs[9:17]
+    slope_ref, stage_ref, weight_sem, part_sem, stage_sem = refs[17:]
     count = x_ref.shape[0]
     half = count // 2
-    n_weights, shard_rows = shards[0].shape[:2]
+    per_shard, n_weights, shard_rows = shards[0].shape[:3]
     member = table_ref[0]
     for k in range(UNIT):
         pltpu.make_async_copy(parts[k], packed_ref.at[member ^ k], part_sem.at[k]).start()
     for b in range(n_weights):
-        for n, shard in enumerate(shards):
+        for n in range(n_shards * per_shard):
             row = pl.multiple_of(table_ref[6 + n], shard_rows)
             pltpu.make_async_copy(
-                shard.at[b], w_ref.at[b, pl.ds(row, shard_rows), :], weight_sem.at[b]
+                shards[n // per_shard].at[n % per_shard, b], w_ref.at[b, pl.ds(row, shard_rows), :], weight_sem.at[b]
             ).start()
     for k in range(UNIT):
         pltpu.make_async_copy(parts[k], packed_ref.at[member ^ k], part_sem.at[k]).wait()
@@ -501,15 +574,15 @@
     lax.fori_loop(0, count // FFN_TILE, tile_step, 0)
 
     core, bits = table_ref[1], [table_ref[2 + d] for d in range(4)]
-    piece, half_columns = pieces_ref.shape[4:]
-    n_parts = pieces_ref.shape[1]
-
-    def copies(block, slot):
-        part = block // (n_weights // n_parts)
+    piece, half_columns = kept_ref.shape[3:]
+    n_parts = kept_ref.shape[0]
+    per_part = n_weights // n_parts
+
+    def copies(block, slot, half, target):
+        part = block // per_part
         made = []
-        for index in range(2 * 16):
-            c = (index % 2) ^ core
-            x, zh, y, zl = ((index >> s) % 2 for s in (1, 2, 3, 4))
+        for index in range(16):
+            x, zh, y, zl = ((index >> s) % 2 for s in range(4))
             rel = {"x": x ^ bits[0], "y": y ^ bits[1], "zl": zl ^ bits[2], "zh": zh ^ bits[3]}
             place = 0
             for name in PART_ORDERS[part]:
@@ -517,35 +590,46 @@
             made.append(
                 pltpu.make_async_copy(
                     stage_ref.at[
-                        slot,
-                        pl.ds(index // 2 * piece, piece),
-                        pl.ds(index % 2 * half_columns, half_columns),
+                        slot, pl.ds(index * piece, piece), pl.ds(half * half_columns, half_columns)
                     ],
-                    pieces_ref.at[c, part, place, block % (n_weights // n_parts)],
-                    stage_sem.at[slot, index],
+                    target.at[part, place, block % per_part],
+                    stage_sem.at[slot, half * 16 + index],
                 )
             )
         return made
 
+    def send(block, slot):
+        for half in range(2):
+
+            @pl.when(core == half)
+            def _(half=half):
+                for copy in copies(block, slot, half, kept_ref):
+                    copy.start()
+
+            @pl.when(core != half)
+            def _(half=half):
+                for copy in copies(block, slot, half, sent_ref):
+                    copy.start()
+
+    def sent(block, slot):
+        for half in range(2):
+            for copy in copies(block, slot, half, kept_ref):
+                copy.wait()
+
     plan = [(attn_ref, None, mixed_ref, None, 0)]
     plan += [(down_ref, None, act_ref, j, 1 + FFB + j) for j in range(FFB)]
     plan += [(up_ref, j, hidden_ref, None, 1 + j) for j in range(FFB)]
-    pending = [None, None]
     for n, (left, lj, right, rj, block) in enumerate(plan):
         slot = n % 2
-        if pending[slot] is not None:
-            for copy in pending[slot]:
-                copy.wait()
+        if n >= 2:
+            sent(plan[n - 2][4], slot)
         value = inner_rows(
             left[...] if lj is None else left[lj], right[...] if rj is None else right[rj]
         )
         stage_ref[slot] = value.astype(BF16)
-        pending[slot] = copies(block, slot)
-        for copy in pending[slot]:
-            copy.start()
-    for group in pending:
-        for copy in group:
-            copy.wait()
+        send(block, slot)
+    for n in (len(plan) - 2, len(plan) - 1):
+        sent(plan[n][4], n % 2)
 
 
 PART_ORDERS = (("x", "y", "zl", "zh"), ("y", "zl", "zh", "x"), ("zl", "zh", "x", "y"))
@@ -561,13 +645,14 @@
     return pl.pallas_call(
         functools.partial(layer_body, n_shards),
         in_specs=[pl.BlockSpec(memory_space=pltpu.SMEM)] + [anywhere] * (n_shards + UNIT) + [inside] * 3,
-        out_specs=[inside, inside, inside, inside, anywhere],
+        out_specs=[inside, inside, inside, inside, anywhere, anywhere],
         out_shape=[
             jax.ShapeDtypeStruct((count, D), BF16),
             jax.ShapeDtypeStruct((count, D), F32),
             jax.ShapeDtypeStruct((UNIT, *packed), BF16),
             jax.ShapeDtypeStruct((VEC_ROWS, D), F32),
-            jax.ShapeDtypeStruct((2, 3, 16, n_weights // 3, D // 16, D // 2), BF16),
+            jax.ShapeDtypeStruct((3, 16, n_weights // 3, D // 16, D // 2), BF16),
+            jax.ShapeDtypeStruct((3, 16, n_weights // 3, D // 16, D // 2), BF16),
         ],
         scratch_shapes=[
             pltpu.VMEM((n_weights, D, D), BF16),
@@ -585,6 +670,7 @@
             pltpu.SemaphoreType.DMA((2, 32)),
         ],
         compiler_params=pltpu.CompilerParams(vmem_limit_bytes=60 << 20),
+        cost_estimate=SMALL,
         name="layer",
     )(table, *shards, *parts, inputs, cotangent, vectors)
 
@@ -594,31 +680,11 @@
     return lax.ppermute(value, axis, [(i, i ^ bit) for i in range(size)])
 
 
-def gather_unit(rows):
-    near = swap(rows, "tok", 1)
-    far = swap(rows, "tok", 2)
-    half = rows.shape[0] // 2
-    across = jnp.concatenate([swap(near[:half], "tok", 2), swap(far[half:], "tok", 1)], axis=0)
-    return [rows, near, far, across]
-
-
 def exchange_unit(parts):
     return [parts[0]] + [swap(parts[k], "tok", k) for k in range(1, UNIT)]
 
 
 LINKS = {"x": ("grp", 2), "y": ("tok", 1), "zl": ("tok", 2), "zh": ("tok", 4)}
-
-
-def reduce_pieces(pieces):
-    other = swap(pieces[1], "grp", 1)
-    done = []
-    for part, names in enumerate(PART_ORDERS):
-        value = pieces[0, part].astype(F32) + other[part].astype(F32)
-        for name in names:
-            half = value.shape[0] // 2
-            value = value[:half] + swap(value[half:].astype(BF16), *LINKS[name]).astype(F32)
-        done.append(value[0].astype(BF16))
-    return jnp.concatenate(done, axis=0)
 
 
 def starts_of(lengths):
@@ -658,21 +724,34 @@
 
 
 def split_heads(columns):
-    query, keys, values = (c.reshape(*c.shape[:-1], HEADS_OWN, HEAD) for c in columns)
-    zero = jnp.zeros_like(query[..., 0, :])
+    query, keys, values = (c.reshape(HEADS_OWN, HEAD) for c in columns)
+    zero = jnp.zeros((HEAD,), query.dtype)
     tiles = []
     for h in range(HEADS_OWN):
-        q, k, v = query[..., h, :], keys[..., h, :], values[..., h, :]
-        tiles += [v, q, zero, k] if h % 2 == 0 else [q, v, k, zero]
-    return jnp.concatenate(tiles, axis=-1)
+        tiles += [values[h], query[h], zero, keys[h]] if h % 2 == 0 else [query[h], values[h], keys[h], zero]
+    return jnp.concatenate(tiles)
 
 
 def join_heads(tiles):
-    parts = tiles.reshape(*tiles.shape[:-1], HEADS_OWN, 4, HEAD)
-    query = [parts[..., h, 1 if h % 2 == 0 else 0, :] for h in range(HEADS_OWN)]
-    keys = [parts[..., h, 3 if h % 2 == 0 else 2, :] for h in range(HEADS_OWN)]
-    values = [parts[..., h, 0 if h % 2 == 0 else 1, :] for h in range(HEADS_OWN)]
-    return tuple(jnp.concatenate(p, axis=-1) for p in (query, keys, values))
+    parts = tiles.reshape(HEADS_OWN, 4, HEAD, *tiles.shape[1:])
+    at = [(1, 0), (3, 2), (0, 1)]
+    return jnp.stack(
+        [jnp.concatenate([parts[h, at[i][h % 2]] for h in range(HEADS_OWN)], axis=0) for i in range(3)]
+    )
+
+
+def doubled(value):
+    high = value.astype(BF16)
+    return high, (value - high.astype(F32)).astype(BF16)
+
+
+def twice(form, left, right):
+    return products(form, left, right[0]) + products(form, left, right[1])
+
+
+def together(*groups):
+    flat, tree = jax.tree.flatten(groups)
+    return jax.tree.unflatten(tree, lax.optimization_barrier(flat))
 
 
 def fast(
@@ -705,104 +784,155 @@
     slot_block = jnp.argsort(owners, stable=True).astype(jnp.int32)
     block_slot = jnp.argsort(slot_block, stable=True).astype(jnp.int32)
 
-    by_member = jnp.transpose(
-        clusters[0].reshape(ROUNDS, UNIT, HEADS_OWN, tok_count), (1, 2, 0, 3)
-    ).reshape(UNIT, LOCAL_PAIRS, tok_count)
-    own_clusters = exchange_unit([pick(by_member, member ^ k) for k in range(UNIT)])
-    order = jnp.argsort(jnp.stack(own_clusters), axis=-1, stable=True).astype(jnp.int32)
-    order = jnp.pad(order, ((0, 0), (0, 8 - LOCAL_PAIRS), (0, 0)))
-    orders = [order[k] for k in range(UNIT)]
+    core, bit_x = grp % 2, grp // 2
+    inputs = tokens[0]
+
+    near, far = swap(inputs, "tok", 1), swap(inputs, "tok", 2)
+    local = jnp.transpose(master.astype(BF16), (1, 0, 2))
+    beside, over = swap(local, "grp", 1), swap(local, "grp", 2)
+    across = swap(over, "grp", 1)
+
+    order = jnp.argsort(clusters[0], axis=-1, stable=True).astype(jnp.int32)
+    by_member = jnp.transpose(order.reshape(ROUNDS, UNIT, HEADS_OWN, tok_count), (1, 2, 0, 3))
+    by_member = by_member.reshape(UNIT, LOCAL_PAIRS, tok_count)
+    orders = exchange_unit([pick(by_member, member ^ k) for k in range(UNIT)])
+    orders = [jnp.pad(o, ((0, 8 - LOCAL_PAIRS), (0, 0))) for o in orders]
     item_starts = starts_of(lengths[0])
     unit_start = unit * UNIT * tok_count
     middle = unit_start + UNIT // 2 * tok_count
     start_of_middle = jnp.max(jnp.where(item_starts <= middle, item_starts, 0))
     is_long = (start_of_middle <= unit_start).astype(jnp.int32).reshape(1)
 
-    inputs = tokens[0]
-    unit_inputs = gather_unit(inputs)
-    core, bit_x = grp % 2, grp // 2
-
-    local = jnp.transpose(master.astype(BF16), (1, 0, 2))
-    beside = swap(local, "grp", 1)
-    over = swap(local, "grp", 2)
-    by_slot = jnp.concatenate([local, beside, over, swap(over, "grp", 1)], axis=0)
+    left, right = doubled(bases[0]), doubled(bases[1])
+    (near, far, beside, over, across, left, right) = together(near, far, beside, over, across, left, right)
+    by_slot = jnp.concatenate([local, beside, over, across], axis=0)
     at = [((block_slot[b] // slots) ^ grp) * slots + block_slot[b] % slots for b in range(blocks_all)]
-    rows_of = [pick(by_slot, at[b]) for b in range(blocks_all)]
+    part_rows = rows_dev // 2
+
+    def own_half(b):
+        return lax.dynamic_slice(by_slot, (at[b], core * part_rows, 0), (1, part_rows, D))[0]
+
+    by_owner = arrange(jnp.stack([own_half(b) for b in range(3)]))
+    theirs = exchange_unit([pick(by_owner, member ^ k) for k in range(UNIT)])
+    half = tok_count // 2
+    third = (swap(near[:half], "tok", 2), swap(far[half:], "tok", 1))
+    theirs = jnp.stack(theirs)
+    theirs_far = swap(theirs, "tok", UNIT)
+    mine_all = jnp.concatenate([theirs, theirs_far], axis=0)
+    others_all = swap(mine_all, "grp", 1)
+    sources = [tok ^ k ^ (UNIT * f) for f in range(2) for k in range(UNIT)]
+    firsts = [t * rows_dev + c * part_rows for c in (core, 1 - core) for t in sources]
+    own_weights = assemble(jnp.stack(firsts).astype(jnp.int32), [mine_all, others_all])
 
     def columns_of(value, m):
         return lax.dynamic_slice_in_dim(value, m * own_width, own_width, value.ndim - 1)
 
-    by_owner = jnp.stack(
-        [split_heads([r[:, m * own_width : (m + 1) * own_width] for r in rows_of[:3]]) for m in range(UNIT)]
-    )
-    got = [pick(by_owner, member)]
-    got += [swap(pick(by_owner, member ^ (k % UNIT)), "tok", k) for k in range(1, n_tok)]
-    got = jnp.stack(got)
-    own_weights = jnp.concatenate([pick(got, tok ^ t) for t in range(n_tok)], axis=0)
-
-    part_rows = rows_dev // 2
-    rest_rows = jnp.stack(
-        [lax.dynamic_slice_in_dim(r, core * part_rows, part_rows, 0) for r in rows_of[3:]]
-    )
-    rest_rows, _ = lax.optimization_barrier((rest_rows, unit_inputs[3]))
-    shards, firsts = [], []
-    step = rest_rows
-    for k in range(n_tok // 2):
-        if k:
-            step = lax.ppermute(step, "tok", [(i, (i + 2) % n_tok) for i in range(n_tok)])
-        for flip, value in ((0, step), (1, swap(step, "tok", 1))):
-            source = (tok - 2 * k) % n_tok ^ flip
-            for other in range(2):
-                shards.append(swap(value, "grp", 1) if other else value)
-                firsts.append(source * rows_dev + (core ^ other) * part_rows)
-
     own_bias = split_heads(
         [columns_of(vectors[4], member), jnp.zeros((own_width,), F32), columns_of(vectors[5], member)]
-    )
-    grouped = []
-    for k in range(UNIT):
-        qkv = (jnp.dot(unit_inputs[k], own_weights, preferred_element_type=F32) + own_bias).astype(BF16)
-        grouped.append(sort_rows(orders[k], qkv, WIDE))
+    ).reshape(1, -1)
+    grouped = [
+        sort_rows(orders[k], value, own_weights, own_bias) for k, value in enumerate((inputs, near, far))
+    ]
+    (third, grouped) = together(third, grouped)
+    unit_inputs = [inputs, near, far, jnp.concatenate(third, axis=0)]
+    grouped.append(sort_rows(orders[3], unit_inputs[3], own_weights, own_bias))
+
+    (rest_rows, _) = together(jnp.stack([own_half(b) for b in range(3, blocks_all)]), third)
+    ring = [(i, (i + 2) % n_tok) for i in range(n_tok)]
+    depth = n_tok // 2
+    steps, flips = [rest_rows], []
+    steps.append(lax.ppermute(steps[0], "tok", ring))
+    flips.append(swap(steps[0], "tok", 1))
     sorted_out = attend(is_long, grouped)
-    mixed_parts = exchange_unit([mix(orders[k], sorted_out[k]) for k in range(UNIT)])
-    held_weights, *mixed_parts = lax.optimization_barrier((own_weights, *mixed_parts))
+    (sorted_out, steps[1], flips[0]) = together(sorted_out, steps[1], flips[0])
+    mixed = [None] * UNIT
+    mixed[3] = mix(orders[3], sorted_out[3])
+    mixed[2] = mix(orders[2], sorted_out[2])
+    mixed[1] = mix(orders[1], sorted_out[1])
+    mixed_parts = exchange_unit(mixed)
+    steps.append(lax.ppermute(steps[1], "tok", ring))
+    flips.append(swap(steps[1], "tok", 1))
+    (steps[2], flips[1], mixed_parts[1:]) = together(steps[2], flips[1], mixed_parts[1:])
+    steps.append(lax.ppermute(steps[2], "tok", ring))
+    flips.append(swap(steps[2], "tok", 1))
+    flips.append(swap(steps[3], "tok", 1))
+    mixed_parts[0] = mix(orders[0], sorted_out[0])
+    mine_rest = [jnp.stack([steps[k], flips[k]]) for k in range(depth)]
+    shards = mine_rest + [swap(m, "grp", 1) for m in mine_rest]
+    firsts = [
+        ((tok - 2 * k) % n_tok ^ flip) * rows_dev + c * part_rows
+        for c in (core, 1 - core)
+        for k in range(depth)
+        for flip in range(2)
+    ]
+
+    held_weights, *shards = lax.optimization_barrier((own_weights, *shards))
     turned_weights = [swap(held_weights, "tok", k) for k in range(1, UNIT)]
     table = jnp.stack([member, core, bit_x, tok % 2, tok // 2 % 2, tok // 4, *firsts]).astype(jnp.int32)
-    result, grad_first, back, sums, pieces = layer(
+    result, grad_first, back, sums, kept, sent_pieces = layer(
         table, shards, mixed_parts, inputs, cotangent[0], vectors
     )
+    (turned_weights, kept, sent_pieces, back) = together(turned_weights, kept, sent_pieces, back)
+
     grad_parts = exchange_unit([back[k] for k in range(UNIT)])
-    sorted_grads = [sort_grads(orders[k], grad_parts[k]) for k in range(UNIT)]
-    rest = reduce_pieces(pieces)
+    other = swap(sent_pieces, "grp", 1)
+    sums_of = [kept[p].astype(F32) + other[p].astype(F32) for p in range(3)]
+
+    def halves(values):
+        return [v[: v.shape[0] // 2] for v in values], [v[v.shape[0] // 2 :].astype(BF16) for v in values]
+
+    def exchanged(sent_now, stage):
+        return [swap(v, *LINKS[PART_ORDERS[p][stage]]) for p, v in enumerate(sent_now)]
+
+    def joined(kept_now, got_now):
+        return [k + g.astype(F32) for k, g in zip(kept_now, got_now)]
+
+    sorted_grads = [sort_grads(orders[0], grad_parts[0])]
+    kept_now, sent_now = halves(sums_of)
+    (sent_now, sorted_grads, grad_parts) = together(sent_now, sorted_grads, grad_parts)
+    got_now = exchanged(sent_now, 0)
+    sorted_grads += [sort_grads(orders[k], grad_parts[k]) for k in range(1, UNIT)]
     sorted_back = attend_back(is_long, grouped, sorted_grads)
-    own_grads = [gather_grads(orders[k], sorted_back[k]) for k in range(UNIT)]
-    turned_qkv = sum(inner_rows(own_grads[k], unit_inputs[k]) for k in range(UNIT))
+    kept_now, sent_now = halves(joined(kept_now, got_now))
+    (sent_now, sorted_back) = together(sent_now, sorted_back)
+    got_now = exchanged(sent_now, 1)
+    own_grads = [None] * UNIT
+    for k in (3, 2):
+        own_grads[k] = gather_grads(orders[k], sorted_back[k])
+    turned_qkv = sum(inner_rows(own_grads[k], unit_inputs[k]) for k in (3, 2))
+    kept_now, sent_now = halves(joined(kept_now, got_now))
+    (sent_now, turned_qkv, sorted_back, own_grads[3]) = together(
+        sent_now, turned_qkv, sorted_back, own_grads[3]
+    )
+    got_now = exchanged(sent_now, 2)
+    home_grads = [None, None, None, swap(own_grads[3], "tok", 3)]
+    for k in (1, 0):
+        own_grads[k] = gather_grads(orders[k], sorted_back[k])
+    turned_qkv = turned_qkv + sum(inner_rows(own_grads[k], unit_inputs[k]) for k in (1, 0))
+    kept_now, sent_now = halves(joined(kept_now, got_now))
+    turned_qkv = join_heads(turned_qkv).astype(BF16).reshape(3, 2, own_width // 2, D)
+    turned_qkv = (pick(jnp.swapaxes(turned_qkv, 0, 1), unit), pick(jnp.swapaxes(turned_qkv, 0, 1), 1 - unit))
+    (sent_now, turned_qkv, own_grads) = together(sent_now, turned_qkv, own_grads)
+    got_now = exchanged(sent_now, 3)
     bias_qkv = sum(jnp.sum(own_grads[k].astype(F32), axis=0) for k in range(UNIT))
-    home_grads = exchange_unit(own_grads)
-    grad_inputs = grad_first + sum(
-        outer_cols(home_grads[k], own_weights if k == 0 else turned_weights[k - 1]) for k in range(UNIT)
-    )
 
     bias_query, _, bias_value = join_heads(bias_qkv)
     bias_rows = lax.dynamic_update_slice_in_dim(
         jnp.zeros((2, D), F32), jnp.stack([bias_query, bias_value]), member * own_width, 1
     )
     vector_grads = sums[: 8 + FFB] + jnp.pad(bias_rows, ((4, 2 + FFB), (0, 0)))
+    keep = turned_qkv[0].astype(F32) + swap(turned_qkv[1], "tok", UNIT).astype(F32)
+    keep = keep + swap(keep.astype(BF16), "grp", 1).astype(F32)
     vector_total = total_of(vector_grads)
-
+    rest = jnp.concatenate([v[0].astype(BF16) for v in joined(kept_now, got_now)], axis=0)
+    (rest, home_grads[3]) = together(rest, home_grads[3])
     sent = jnp.stack(
         [pick(rest, jnp.maximum(slot_block[s] - 3, 0)) for s in range(blocks_all)]
     ).reshape(n_grp, slots, *rest.shape[1:])
     got = lax.all_to_all(sent, "grp", split_axis=0, concat_axis=0, tiled=True)
+    keep = (keep + swap(keep.astype(BF16), "grp", 2).astype(F32)).astype(BF16)
     got = jnp.transpose(got.reshape(2, 2, *got.shape[1:]), (2, 0, 3, 1, 4))
-    got = got.reshape(slots, D // n_tok, D).astype(F32)
-
-    turned_qkv = jnp.stack(join_heads(jnp.transpose(turned_qkv)))
-    turned_qkv = jnp.transpose(turned_qkv.astype(BF16).reshape(3, D, 2, own_width // 2), (2, 0, 3, 1))
-    keep = pick(turned_qkv, unit).astype(F32)
-    keep = keep + swap(pick(turned_qkv, 1 - unit), "tok", UNIT).astype(F32)
-    keep = keep + swap(keep.astype(BF16), "grp", 1).astype(F32)
-    keep = keep + swap(keep.astype(BF16), "grp", 2).astype(F32)
+    got = got.reshape(slots, D // n_tok, D)
 
     mine = lax.dynamic_slice_in_dim(slot_block, grp * slots, slots, 0)
     reduced = jnp.stack(
@@ -810,19 +940,23 @@
             jnp.where(mine[s] < 3, pick(keep, jnp.minimum(mine[s], 2)), got[s]) for s in range(slots)
         ]
     )
-    left, right = bases[0], bases[1]
-    high = lax.Precision.HIGHEST
-    part = jnp.einsum("sia,sci->sac", left, reduced, precision=high)
-    part = turn_rows(part.astype(BF16), place).astype(F32)
-    rotated = jnp.einsum("sac,scb->sab", part, right, precision=high)
+    part = products("sia,sci->sac", left[0], reduced) + products("sia,sci->sac", left[1], reduced)
+    part = turn_rows(part.astype(BF16), place)
+    (part, own_grads[:3], vector_total) = together(part, own_grads[:3], vector_total)
+    home_grads[:3] = [own_grads[0]] + [swap(own_grads[k], "tok", k) for k in (1, 2)]
+    rotated = twice("sac,scb->sab", part, right)
     rotated = jnp.transpose(rotated, (1, 0, 2))
     new_one = BETA_ONE * moment_one + (1.0 - BETA_ONE) * rotated
     new_two = BETA_TWO * moment_two + (1.0 - BETA_TWO) * rotated * rotated
-    direction = new_one / (jnp.sqrt(new_two) + ADAM_EPS)
-    turned = jnp.einsum("asb,scb->sac", direction, right, precision=high)
-    turned = turn_columns(turned.astype(BF16), place).astype(F32)
-    change = jnp.einsum("sia,sac->sic", left, turned, precision=high)
+    direction = (new_one / (jnp.sqrt(new_two) + ADAM_EPS)).astype(BF16)
+    turned = twice("asb,scb->sac", direction, right)
+    (turned, home_grads[:3]) = together(turned.astype(BF16), home_grads[:3])
+    turned = turn_columns(turned, place)
+    change = products("sia,sac->sic", left[0], turned) + products("sia,sac->sic", left[1], turned)
     change = turn_rows(change.astype(BF16), place).astype(F32)
+    grad_inputs = grad_first + sum(
+        outer_cols(home_grads[k], own_weights if k == 0 else turned_weights[k - 1]) for k in range(UNIT)
+    )
     new_master = master - RATE_MATRIX * jnp.transpose(change, (1, 0, 2))
     new_vec_one = BETA_ONE * vector_one + (1.0 - BETA_ONE) * vector_total
     new_vec_two = BETA_TWO * vector_two + (1.0 - BETA_TWO) * vector_total * vector_total

time: 748 us -> 736 us (0.984)
  waiting for transfers between devices: 233 us -> 181 us
  Pallas kernels: 172 us -> 218 us
  matrix products: 70.7 us -> 40.9 us
  between operations: 38.3 us -> 51.4 us
  local copies, waits for them, and re-layouts: 86.8 us -> 97.4 us
    ppermute x62 -> x56, waiting for transfers between devices: 220 us -> 151 us  [swap(): return lax.ppermute(value, axis, [(i, i ^ bit) for i in range(size)])]
    pallas_call x0 -> x2, Pallas kernels: none -> 39.4 us  [the longest x1 37.7 us: assemble(): pl.pallas_call(assemble_body, in_specs=[pl.BlockSpec(memory_space=pltpu.S...]
    dot_general x8, matrix products: 42.7 us -> 13.2 us  [products(): return jnp.einsum(form, left, right, preferred_element_type=F32)]
    sort x1 -> x0, other arithmetic: 23.9 us -> none  [fast(): jnp.argsort(jnp.stack(own_clusters), axis=-1, stable=True).astype(jnp.int32)]
    convert_element_type x4 -> x6, other arithmetic: 2.08 us -> 19.2 us  [the longest x1 15.9 us: doubled(): return (high, (value - high.astype(F32)).astype(BF16))]
    unnamed x202 -> x203, local copies, waits for them, and re-layouts: 31.5 us -> 48.6 us
    ppermute x3, waiting for transfers between devices: 7.48 us -> 17.7 us  [the longest x1 17.7 us: fast(): steps.append(lax.ppermute(steps[2], 'tok', ring))]
    ppermute x62 -> x56, starting transfers between devices: 64.4 us -> 57.8 us  [swap(): return lax.ppermute(value, axis, [(i, i ^ bit) for i in range(size)])]
  transfers between devices with their start and end apart: 69 -> 63, of which waited for: 28 -> 25; matrix products, arithmetic and copies ran while one was open for 22% -> 14% of each run, Pallas kernels for 14% -> 30%
where the time goes in v3:
time: 736 us; the launch traced here: 724 us
  Pallas kernels  218 us (30%)
  waiting for transfers between devices  181 us (25%)
  local copies, waits for them, and re-layouts  97.4 us (13%)
  starting transfers between devices  79.7 us (11%)
  other arithmetic  54.8 us (7%)
  between operations  51.4 us (7%)
  matrix products  40.9 us (6%)
    ppermute x56, waiting for transfers between devices, swap(): return lax.ppermute(value, axis, [(i, i ^ bit) for i in range(size)])  151 us
    pallas_call x1, Pallas kernels, layer(): pl.pallas_call(functools.partial(layer_body, n_shards), in_specs=[pl.Bloc...  69.8 us
    ppermute x56, starting transfers between devices, swap(): return lax.ppermute(value, axis, [(i, i ^ bit) for i in range(size)])  57.8 us
    unnamed x203, local copies, waits for them, and re-layouts  48.6 us
    pallas_call x1, Pallas kernels, assemble(): pl.pallas_call(assemble_body, in_specs=[pl.BlockSpec(memory_space=pltpu.S...  37.7 us
    pallas_call x4, Pallas kernels, sort_rows(): pl.pallas_call(sort_body, grid=(HEADS_OWN,), in_specs=[pl.BlockSpec((8, c...  24.4 us
    pallas_call x1, Pallas kernels, attend_back(): pl.pallas_call(attend_back_body, grid_spec=pltpu.PrefetchScalarGridSpec(n...  19.7 us
    ppermute x1, waiting for transfers between devices, fast(): steps.append(lax.ppermute(steps[2], 'tok', ring))  17.7 us
  transfers between devices with their start and end apart: 63, of which 25 were waited for; matrix products, arithmetic and copies ran while one was open for 14% of the time, Pallas kernels for 30%

profile of v3, /device:TPU:0, one launch (start us, length us, event | category | flops | bytes accessed | tf_op | source)
XLA Modules:
  0.0 723.9 jit_solution(11950015095711166209)
XLA Ops:
  7.2 3.0 collective-permute-start
  43.3 15.9 %fusion = (bf16[3,768,768]{2,1,0:T(8,128)(2,1)}, bf16[3,768,768]{2,1,0:T(8,128)(2,1)}, bf16[3,768,768]{2,1,0:T(8,128)(2,1)}, bf16[3,768,768]{2,1,0:T(8,128)(2,1)}) fusion(f32[2,3,768,768]{3,2,1,0:T(8,128)} %param.18), kind=kLoop, calls=%fused_computation.2 | loop fusion | flops 10616832 | bytes 35389440 | tf_op jit(solution)/shard_map/convert_element_type | solution.py:745
  83.8 16.2 %collective-permute-done.8 = bf16[4,48,768]{2,1,0:T(8,128)(2,1)S(1)} collective-permute-done((bf16[4,48,768]{2,1,0:T(8,128)(2,1)S(1)}, bf16[4,48,768]{2,1,0:T(8,128)(2,1)S(1)}, u32[]{:S(2)}, u32[]{:S(2)}) %collective-permute-start.8) | collective-permute-done | bytes 294944 | tf_op jit(solution)/shard_map/ppermute | solution.py:680
  102.2 3.2 sort.52.cloned.1.call-done
  107.5 4.3 collective-permute-start.13
  113.7 37.7 %assemble.1.weight_ref = bf16[768,768]{1,0:T(8,128)(2,1)} custom-call(s32[16]{0:T(128)} %stack.265.table_ref, bf16[8,48,768]{2,1,0:T(8,128)(2,1)} %constant_dynamic-update-slice_fusion.refs_0_, bf16[8,48,768]{2,1,0:T(8,128)(2,1)} %collective-permute-done.9.refs_1_), custom_call_target="tpu_custom_call" | custom-call | tf_op jit(solution)/shard_map/assemble/pallas_call | solution.py:122
  152.6 6.0 sort_rows.4.refs_0_
  160.3 6.0 sort_rows.5.refs_1_
  168.0 6.4 sort_rows.6.refs_2_
  181.2 14.2 %collective-permute-done.14 = s32[6,1024]{1,0:T(8,128)S(1)} collective-permute-done((s32[6,1024]{1,0:T(8,128)S(1)}, s32[6,1024]{1,0:T(8,128)S(1)}, u32[]{:S(2)}, u32[]{:S(2)}) %collective-permute-start.14) | collective-permute-done | bytes 24608 | tf_op jit(solution)/shard_map/ppermute | solution.py:680
  197.8 6.0 sort_rows.7.refs_3_
  205.4 16.5 %attend.1 = (bf16[6,1024,128]{2,1,0:T(8,128)(2,1)S(1)}, bf16[6,1024,128]{2,1,0:T(8,128)(2,1)S(1)}, bf16[6,1024,128]{2,1,0:T(8,128)(2,1)S(1)}, bf16[6,1024,128]{2,1,0:T(8,128)(2,1)}) custom-call(s32[1]{0:T(128)} %bitcast.95.long_ref, bf16[6,1024,256]{2,1,0:T(8,128)(2,1)} %copy-done.2, bf16[6,1024,256]{2,1,0:T(8,128)(2,1)} %copy-done.3, ...), custom_call_target="tpu_custom_call" | custom-call | tf_op jit(solution)/shard_map/attend/pallas_call | solution.py:291
  223.3 4.0 mix.4
  228.2 3.9 mix.5
  233.2 3.9 mix.6
  238.7 8.8 %collective-permute-done.19.refs_9_ = bf16[1536,128]{1,0:T(8,128)(2,1)S(1)} collective-permute-done((bf16[1536,128]{1,0:T(8,128)(2,1)S(1)}, bf16[1536,128]{1,0:T(8,128)(2,1)S(1)}, u32[]{:S(2)}, u32[]{:S(2)}) %collective-permute-start.19) | collective-permute-done | bytes 393248 | tf_op jit(solution)/shard_map/ppermute | solution.py:680
  249.4 8.9 %collective-permute-done.21.refs_11_ = bf16[1536,128]{1,0:T(8,128)(2,1)S(1)} collective-permute-done((bf16[1536,128]{1,0:T(8,128)(2,1)S(1)}, bf16[1536,128]{1,0:T(8,128)(2,1)S(1)}, u32[]{:S(2)}, u32[]{:S(2)}) %collective-permute-start.21) | collective-permute-done | bytes 393248 | tf_op jit(solution)/shard_map/ppermute | solution.py:680
  259.3 17.7 %collective-permute-done.23 = bf16[9,48,768]{2,1,0:T(8,128)(2,1)S(1)} collective-permute-done((bf16[9,48,768]{2,1,0:T(8,128)(2,1)S(1)}, bf16[9,48,768]{2,1,0:T(8,128)(2,1)S(1)}, u32[]{:S(2)}, u32[]{:S(2)}) %collective-permute-start.23) | collective-permute-done | bytes 663584 | tf_op jit(solution)/shard_map/ppermute | solution.py:856
  281.8 11.2 %collective-permute-done.24 = bf16[9,48,768]{2,1,0:T(8,128)(2,1)S(1)} collective-permute-done((bf16[9,48,768]{2,1,0:T(8,128)(2,1)S(1)}, bf16[9,48,768]{2,1,0:T(8,128)(2,1)S(1)}, u32[]{:S(2)}, u32[]{:S(2)}) %collective-permute-start.24) | collective-permute-done | bytes 663584 | tf_op jit(solution)/shard_map/ppermute | solution.py:680
  300.4 3.9 mix.7.refs_8_
  305.1 69.8 %layer.1 = (bf16[1024,768]{1,0:T(8,128)(2,1)}, f32[1024,768]{1,0:T(8,128)}, bf16[4,1536,128]{2,1,0:T(8,128)(2,1)}, f32[16,768]{1,0:T(8,128)}, bf16[3,16,3,48,384...) custom-call(s32[22]{0:T(128)} %stack.248.table_ref, bf16[2,9,48,768]{3,2,1,0:T(8,128)(2,1)} %copy-done.40, ...), custom_call_target="tpu_custom_call" | custom-call | tf_op jit(solution)/shard_map/layer/pallas_call | solution.py:645
  376.4 4.2 sort_grads.4.refs_4_
  384.2 4.6 convert_add_fusion
  393.5 8.3 %collective-permute-done.35.rows_ref = bf16[1536,128]{1,0:T(8,128)(2,1)S(1)} collective-permute-done((bf16[1536,128]{1,0:T(8,128)(2,1)S(1)}, bf16[1536,128]{1,0:T(8,128)(2,1)S(1)}, u32[]{:S(2)}, u32[]{:S(2)}) %collective-permute-start.35) | collective-permute-done | bytes 393248 | tf_op jit(solution)/shard_map/ppermute | solution.py:680
  416.5 4.2 sort_grads.5.refs_5_
  421.9 4.6 sort_grads.6.refs_6_
  427.6 4.2 sort_grads.7.refs_7_
  433.0 19.7 %attend_back.1 = (bf16[6,1024,256]{2,1,0:T(8,128)(2,1)}, bf16[6,1024,256]{2,1,0:T(8,128)(2,1)}, bf16[6,1024,256]{2,1,0:T(8,128)(2,1)}, bf16[6,1024,256]{2,1,0:T(8,128)(2,1)}) custom-call(s32[1]{0:T(128)} %bitcast.95.long_ref, bf16[6,1024,256]{2,1,0:T(8,128)(2,1)} %copy-done.2, bf16[6,1024,256]{2,1,0:T(8,128)(2,1)} %copy-done.3, ...), custom_call_target="tpu_custom_call" | custom-call | tf_op jit(solution)/shard_map/attend_back/pallas_call | solution.py:335
  462.9 3.9 gather_grads.5
  469.7 3.9 gather_grads.4
  473.6 4.5 convolution_add_fusion
  488.2 4.1 gather_grads.6
  495.2 3.9 gather_grads.7
  514.5 33.4 %collective-permute-done.45 = bf16[3,96,768]{2,1,0:T(8,128)(2,1)S(1)} collective-permute-done((bf16[3,96,768]{2,1,0:T(8,128)(2,1)S(1)}, bf16[3,96,768]{2,1,0:T(8,128)(2,1)S(1)}, u32[]{:S(2)}, u32[]{:S(2)}) %collective-permute-start.45) | collective-permute-done | bytes 442400 | tf_op jit(solution)/shard_map/ppermute | solution.py:680
  553.6 4.5 all-to-all-start
  558.2 5.9 collective-permute-done.47
  580.2 5.3 all-to-all-start.1
  587.7 3.6 collective-permute-done.53
  598.1 3.3 collective-permute-done.55
  603.4 3.6 collective-permute-done.56
  618.2 4.8 fusion.49
  630.9 18.1 %collective-permute-done.57 = bf16[1024,768]{1,0:T(8,128)(2,1)S(1)} collective-permute-done((bf16[1024,768]{1,0:T(8,128)(2,1)}, bf16[1024,768]{1,0:T(8,128)(2,1)S(1)}, u32[]{:S(2)}, u32[]{:S(2)}) %collective-permute-start.57) | collective-permute-done | bytes 1572896 | tf_op jit(solution)/shard_map/ppermute | solution.py:680
  658.4 5.6 all-to-all-start.2
  667.7 4.9 fusion.48
  672.7 4.4 all-to-all-done.2
  689.1 4.2 all-to-all-start.3
  693.3 3.3 fusion.47
  700.8 6.6 all-to-all-done.3
  (441 shorter events, 223.6 us)
Async XLA Ops:
  7.2 52.0 %collective-permute-start = (bf16[1024,768]{1,0:T(8,128)(2,1)}, bf16[1024,768]{1,0:T(8,128)(2,1)S(1)}, u32[]{:S(2)}, u32[]{:S(2)}) collective-permute-start(bf16[1024,768]{1,0:T(8,128)(2,1)} %bitcast.389), channel_id=1, source_target_pairs={{0,4},{4,0},{8,12},{12,8},{16,20},{20,16},{24,28},{28,24},{1,5},{5... | collective-permute-start | bytes 4718600 | tf_op jit(solution)/shard_map/ppermute | solution.py:680
  10.2 49.0 %collective-permute-start.1 = (bf16[1024,768]{1,0:T(8,128)(2,1)}, bf16[1024,768]{1,0:T(8,128)(2,1)S(1)}, u32[]{:S(2)}, u32[]{:S(2)}) collective-permute-start(bf16[1024,768]{1,0:T(8,128)(2,1)} %bitcast.390), channel_id=1, source_target_pairs={{0,8},{4,12},{8,0},{12,4},{16,24},{20,28},{24,16},{28,20},{1,9},{5... | collective-permute-start | bytes 4718600 | tf_op jit(solution)/shard_map/ppermute | solution.py:680
  13.8 28.9 %collective-permute-start.3 = (bf16[3,96,768]{2,1,0:T(8,128)(2,1)}, bf16[3,96,768]{2,1,0:T(8,128)(2,1)}, u32[]{:S(2)}, u32[]{:S(2)}) collective-permute-start(bf16[3,96,768]{2,1,0:T(8,128)(2,1)} %convert_bitcast_fusion), channel_id=1, source_target_pairs={{0,2},{1,3},{2,0},{3,1},{4,6},{5,7},{6,4},{7,5},{8,10},{9,11},{10,... | collective-permute-start | bytes 1327112 | tf_op jit(solution)/shard_map/ppermute | solution.py:680
  15.3 43.9 %collective-permute-start.2 = (bf16[3,96,768]{2,1,0:T(8,128)(2,1)}, bf16[3,96,768]{2,1,0:T(8,128)(2,1)}, u32[]{:S(2)}, u32[]{:S(2)}) collective-permute-start(bf16[3,96,768]{2,1,0:T(8,128)(2,1)} %convert_bitcast_fusion), channel_id=1, source_target_pairs={{0,1},{1,0},{2,3},{3,2},{4,5},{5,4},{6,7},{7,6},{8,9},{9,8},{10,11... | collective-permute-start | bytes 1327112 | tf_op jit(solution)/shard_map/ppermute | solution.py:680
  42.7 16.5 %collective-permute-start.4 = (bf16[3,96,768]{2,1,0:T(8,128)(2,1)}, bf16[3,96,768]{2,1,0:T(8,128)(2,1)S(1)}, u32[]{:S(2)}, u32[]{:S(2)}) collective-permute-start(bf16[3,96,768]{2,1,0:T(8,128)(2,1)} %collective-permute-done.3), channel_id=1, source_target_pairs={{0,1},{1,0},{2,3},{3,2},{4,5},{5,4},{6,7},{7,6},{8,9},{9,8},{10,11... | collective-permute-start | bytes 1327112 | tf_op jit(solution)/shard_map/ppermute | solution.py:680
  76.0 100.1 %collective-permute-start.10 = (bf16[512,768]{1,0:T(8,128)(2,1)}, bf16[512,768]{1,0:T(8,128)(2,1)}, u32[]{:S(2)}, u32[]{:S(2)}) collective-permute-start(bf16[512,768]{1,0:T(8,128)(2,1)} %slice.419), channel_id=1, source_target_pairs={{0,8},{4,12},{8,0},{12,4},{16,24},{20,28},{24,16},{28,20},{1,9},{5... | collective-permute-start | bytes 2359304 | tf_op jit(solution)/shard_map/ppermute | solution.py:680
  77.4 98.7 %collective-permute-start.11 = (bf16[512,768]{1,0:T(8,128)(2,1)}, bf16[512,768]{1,0:T(8,128)(2,1)}, u32[]{:S(2)}, u32[]{:S(2)}) collective-permute-start(bf16[512,768]{1,0:T(8,128)(2,1)} %slice.420), channel_id=1, source_target_pairs={{0,4},{4,0},{8,12},{12,8},{16,20},{20,16},{24,28},{28,24},{1,5},{5... | collective-permute-start | bytes 2359304 | tf_op jit(solution)/shard_map/ppermute | solution.py:680
  79.2 20.8 %collective-permute-start.8 = (bf16[4,48,768]{2,1,0:T(8,128)(2,1)S(1)}, bf16[4,48,768]{2,1,0:T(8,128)(2,1)S(1)}, u32[]{:S(2)}, u32[]{:S(2)}) collective-permute-start(bf16[4,48,768]{2,1,0:T(8,128)(2,1)S(1)} %pad_maximum_fusion.8), channel_id=1, source_target_pairs={{0,16},{4,20},{8,24},{12,28},{16,0},{20,4},{24,8},{28,12},{1,17},{... | collective-permute-start | bytes 884744 | tf_op jit(solution)/shard_map/ppermute | solution.py:680
  100.7 13.0 %collective-permute-start.9 = (bf16[8,48,768]{2,1,0:T(8,128)(2,1)}, bf16[8,48,768]{2,1,0:T(8,128)(2,1)}, u32[]{:S(2)}, u32[]{:S(2)}) collective-permute-start(bf16[8,48,768]{2,1,0:T(8,128)(2,1)} %constant_dynamic-update-slice_fusion.refs_0_), channel_id=1, source_target_pairs={{0,1},{1,0},{2,3},{3,2},{4,5},{5,4},{6,7},{7,6},{8,9},{9,8},{10,11... | collective-permute-start | bytes 1769480 | tf_op jit(solution)/shard_map/ppermute | solution.py:680
  176.1 45.8 %collective-permute-start.15 = (bf16[9,48,768]{2,1,0:T(8,128)(2,1)}, bf16[9,48,768]{2,1,0:T(8,128)(2,1)}, u32[]{:S(2)}, u32[]{:S(2)}) collective-permute-start(bf16[9,48,768]{2,1,0:T(8,128)(2,1)} %get-tuple-element.117), channel_id=1, source_target_pairs={{0,8},{4,12},{8,16},{12,20},{16,24},{20,28},{24,0},{28,4},{1,9},{5... | collective-permute-start | bytes 1990664 | tf_op jit(solution)/shard_map/ppermute | solution.py:844
  178.2 43.8 %collective-permute-start.16 = (bf16[9,48,768]{2,1,0:T(8,128)(2,1)}, bf16[9,48,768]{2,1,0:T(8,128)(2,1)}, u32[]{:S(2)}, u32[]{:S(2)}) collective-permute-start(bf16[9,48,768]{2,1,0:T(8,128)(2,1)} %get-tuple-element.117), channel_id=1, source_target_pairs={{0,4},{4,0},{8,12},{12,8},{16,20},{20,16},{24,28},{28,24},{1,5},{5... | collective-permute-start | bytes 1990664 | tf_op jit(solution)/shard_map/ppermute | solution.py:680
  179.2 16.2 %collective-permute-start.14 = (s32[6,1024]{1,0:T(8,128)S(1)}, s32[6,1024]{1,0:T(8,128)S(1)}, u32[]{:S(2)}, u32[]{:S(2)}) collective-permute-start(s32[6,1024]{1,0:T(8,128)S(1)} %bitcast.416), channel_id=1, source_target_pairs={{0,12},{4,8},{8,4},{12,0},{16,28},{20,24},{24,20},{28,16},{1,13},{... | collective-permute-start | bytes 73736 | tf_op jit(solution)/shard_map/ppermute | solution.py:680
  222.0 36.4 %collective-permute-start.17 = (bf16[9,48,768]{2,1,0:T(8,128)(2,1)}, bf16[9,48,768]{2,1,0:T(8,128)(2,1)S(1)}, u32[]{:S(2)}, u32[]{:S(2)}) collective-permute-start(bf16[9,48,768]{2,1,0:T(8,128)(2,1)} %collective-permute-done.15), channel_id=1, source_target_pairs={{0,8},{4,12},{8,16},{12,20},{16,24},{20,28},{24,0},{28,4},{1,9},{5... | collective-permute-start | bytes 1990664 | tf_op jit(solution)/shard_map/ppermute | solution.py:853
  222.1 36.3 %collective-permute-start.18 = (bf16[9,48,768]{2,1,0:T(8,128)(2,1)}, bf16[9,48,768]{2,1,0:T(8,128)(2,1)S(1)}, u32[]{:S(2)}, u32[]{:S(2)}) collective-permute-start(bf16[9,48,768]{2,1,0:T(8,128)(2,1)} %collective-permute-done.15), channel_id=1, source_target_pairs={{0,4},{4,0},{8,12},{12,8},{16,20},{20,16},{24,28},{28,24},{1,5},{5... | collective-permute-start | bytes 1990664 | tf_op jit(solution)/shard_map/ppermute | solution.py:680
  227.3 20.3 %collective-permute-start.19 = (bf16[1536,128]{1,0:T(8,128)(2,1)S(1)}, bf16[1536,128]{1,0:T(8,128)(2,1)S(1)}, u32[]{:S(2)}, u32[]{:S(2)}) collective-permute-start(bf16[1536,128]{1,0:T(8,128)(2,1)S(1)} %mix.4), channel_id=1, source_target_pairs={{0,4},{4,0},{8,12},{12,8},{16,20},{20,16},{24,28},{28,24},{1,5},{5... | collective-permute-start | bytes 1179656 | tf_op jit(solution)/shard_map/ppermute | solution.py:680
  232.1 17.3 %collective-permute-start.20 = (bf16[1536,128]{1,0:T(8,128)(2,1)S(1)}, bf16[1536,128]{1,0:T(8,128)(2,1)S(1)}, u32[]{:S(2)}, u32[]{:S(2)}) collective-permute-start(bf16[1536,128]{1,0:T(8,128)(2,1)S(1)} %mix.5), channel_id=1, source_target_pairs={{0,8},{4,12},{8,0},{12,4},{16,24},{20,28},{24,16},{28,20},{1,9},{5... | collective-permute-start | bytes 1179656 | tf_op jit(solution)/shard_map/ppermute | solution.py:680
  237.1 21.2 %collective-permute-start.21 = (bf16[1536,128]{1,0:T(8,128)(2,1)S(1)}, bf16[1536,128]{1,0:T(8,128)(2,1)S(1)}, u32[]{:S(2)}, u32[]{:S(2)}) collective-permute-start(bf16[1536,128]{1,0:T(8,128)(2,1)S(1)} %mix.6), channel_id=1, source_target_pairs={{0,12},{4,8},{8,4},{12,0},{16,28},{20,24},{24,20},{28,16},{1,13},{... | collective-permute-start | bytes 1179656 | tf_op jit(solution)/shard_map/ppermute | solution.py:680
  258.3 18.7 %collective-permute-start.23 = (bf16[9,48,768]{2,1,0:T(8,128)(2,1)S(1)}, bf16[9,48,768]{2,1,0:T(8,128)(2,1)S(1)}, u32[]{:S(2)}, u32[]{:S(2)}) collective-permute-start(bf16[9,48,768]{2,1,0:T(8,128)(2,1)S(1)} %collective-permute-done.17), channel_id=1, source_target_pairs={{0,8},{4,12},{8,16},{12,20},{16,24},{20,28},{24,0},{28,4},{1,9},{5... | collective-permute-start | bytes 1990664 | tf_op jit(solution)/shard_map/ppermute | solution.py:856
  258.4 22.8 %collective-permute-start.22 = (bf16[9,48,768]{2,1,0:T(8,128)(2,1)S(1)}, bf16[9,48,768]{2,1,0:T(8,128)(2,1)S(1)}, u32[]{:S(2)}, u32[]{:S(2)}) collective-permute-start(bf16[9,48,768]{2,1,0:T(8,128)(2,1)S(1)} %collective-permute-done.17), channel_id=1, source_target_pairs={{0,4},{4,0},{8,12},{12,8},{16,20},{20,16},{24,28},{28,24},{1,5},{5... | collective-permute-start | bytes 1990664 | tf_op jit(solution)/shard_map/ppermute | solution.py:680
  277.0 16.0 %collective-permute-start.24 = (bf16[9,48,768]{2,1,0:T(8,128)(2,1)S(1)}, bf16[9,48,768]{2,1,0:T(8,128)(2,1)S(1)}, u32[]{:S(2)}, u32[]{:S(2)}) collective-permute-start(bf16[9,48,768]{2,1,0:T(8,128)(2,1)S(1)} %collective-permute-done.23), channel_id=1, source_target_pairs={{0,4},{4,0},{8,12},{12,8},{16,20},{20,16},{24,28},{28,24},{1,5},{5... | collective-permute-start | bytes 1990664 | tf_op jit(solution)/shard_map/ppermute | solution.py:680
  279.3 13.9 %collective-permute-start.25 = (bf16[2,9,48,768]{3,2,1,0:T(8,128)(2,1)S(1)}, bf16[2,9,48,768]{3,2,1,0:T(8,128)(2,1)S(1)}, u32[]{:S(2)}, u32[]{:S(2)}) collective-permute-start(bf16[2,9,48,768]{3,2,1,0:T(8,128)(2,1)S(1)} %pad_maximum_fusion.1.refs_0_), channel_id=1, source_target_pairs={{0,1},{1,0},{2,3},{3,2},{4,5},{5,4},{6,7},{7,6},{8,9},{9,8},{10,11... | collective-permute-start | bytes 3981320 | tf_op jit(solution)/shard_map/ppermute | solution.py:680
  281.0 12.2 %collective-permute-start.26 = (bf16[2,9,48,768]{3,2,1,0:T(8,128)(2,1)S(1)}, bf16[2,9,48,768]{3,2,1,0:T(8,128)(2,1)S(1)}, u32[]{:S(2)}, u32[]{:S(2)}) collective-permute-start(bf16[2,9,48,768]{3,2,1,0:T(8,128)(2,1)S(1)} %pad_maximum_fusion.2.refs_1_), channel_id=1, source_target_pairs={{0,1},{1,0},{2,3},{3,2},{4,5},{5,4},{6,7},{7,6},{8,9},{9,8},{10,11... | collective-permute-start | bytes 3981320 | tf_op jit(solution)/shard_map/ppermute | solution.py:680
  296.3 78.6 %collective-permute-start.29 = (bf16[768,768]{1,0:T(8,128)(2,1)S(1)}, bf16[768,768]{1,0:T(8,128)(2,1)}, u32[]{:S(2)}, u32[]{:S(2)}) collective-permute-start(bf16[768,768]{1,0:T(8,128)(2,1)S(1)} %copy-done.1), channel_id=1, source_target_pairs={{0,4},{4,0},{8,12},{12,8},{16,20},{20,16},{24,28},{28,24},{1,5},{5... | collective-permute-start | bytes 3538952 | tf_op jit(solution)/shard_map/ppermute | solution.py:680
  297.1 77.7 %collective-permute-start.30 = (bf16[768,768]{1,0:T(8,128)(2,1)S(1)}, bf16[768,768]{1,0:T(8,128)(2,1)}, u32[]{:S(2)}, u32[]{:S(2)}) collective-permute-start(bf16[768,768]{1,0:T(8,128)(2,1)S(1)} %copy-done.1), channel_id=1, source_target_pairs={{0,8},{4,12},{8,0},{12,4},{16,24},{20,28},{24,16},{28,20},{1,9},{5... | collective-permute-start | bytes 3538952 | tf_op jit(solution)/shard_map/ppermute | solution.py:680
  297.3 77.5 %collective-permute-start.31 = (bf16[768,768]{1,0:T(8,128)(2,1)S(1)}, bf16[768,768]{1,0:T(8,128)(2,1)}, u32[]{:S(2)}, u32[]{:S(2)}) collective-permute-start(bf16[768,768]{1,0:T(8,128)(2,1)S(1)} %copy-done.1), channel_id=1, source_target_pairs={{0,12},{4,8},{8,4},{12,0},{16,28},{20,24},{24,20},{28,16},{1,13},{... | collective-permute-start | bytes 3538952 | tf_op jit(solution)/shard_map/ppermute | solution.py:680
  380.6 12.5 %collective-permute-start.33 = (bf16[1536,128]{1,0:T(8,128)(2,1)S(1)}, bf16[1536,128]{1,0:T(8,128)(2,1)S(1)}, u32[]{:S(2)}, u32[]{:S(2)}) collective-permute-start(bf16[1536,128]{1,0:T(8,128)(2,1)S(1)} %get-tuple-element.229), channel_id=1, source_target_pairs={{0,4},{4,0},{8,12},{12,8},{16,20},{20,16},{24,28},{28,24},{1,5},{5... | collective-permute-start | bytes 1179656 | tf_op jit(solution)/shard_map/ppermute | solution.py:680
  381.5 12.0 %collective-permute-start.34 = (bf16[1536,128]{1,0:T(8,128)(2,1)S(1)}, bf16[1536,128]{1,0:T(8,128)(2,1)S(1)}, u32[]{:S(2)}, u32[]{:S(2)}) collective-permute-start(bf16[1536,128]{1,0:T(8,128)(2,1)S(1)} %get-tuple-element.228), channel_id=1, source_target_pairs={{0,8},{4,12},{8,0},{12,4},{16,24},{20,28},{24,16},{28,20},{1,9},{5... | collective-permute-start | bytes 1179656 | tf_op jit(solution)/shard_map/ppermute | solution.py:680
  381.6 20.2 %collective-permute-start.35 = (bf16[1536,128]{1,0:T(8,128)(2,1)S(1)}, bf16[1536,128]{1,0:T(8,128)(2,1)S(1)}, u32[]{:S(2)}, u32[]{:S(2)}) collective-permute-start(bf16[1536,128]{1,0:T(8,128)(2,1)S(1)} %get-tuple-element.227), channel_id=1, source_target_pairs={{0,12},{4,8},{8,4},{12,0},{16,28},{20,24},{24,20},{28,16},{1,13},{... | collective-permute-start | bytes 1179656 | tf_op jit(solution)/shard_map/ppermute | solution.py:680
  401.8 50.9 %collective-permute-start.36 = (bf16[8,3,48,384]{3,2,1,0:T(8,128)(2,1)}, bf16[8,3,48,384]{3,2,1,0:T(8,128)(2,1)}, u32[]{:S(2)}, u32[]{:S(2)}) collective-permute-start(bf16[8,3,48,384]{3,2,1,0:T(8,128)(2,1)} %fusion.10), channel_id=1, source_target_pairs={{0,2},{1,3},{2,0},{3,1},{4,6},{5,7},{6,4},{7,5},{8,10},{9,11},{10,... | collective-permute-start | bytes 2654216 | tf_op jit(solution)/shard_map/ppermute | solution.py:680
  402.3 52.5 %collective-permute-start.37 = (bf16[8,3,48,384]{3,2,1,0:T(8,128)(2,1)}, bf16[8,3,48,384]{3,2,1,0:T(8,128)(2,1)}, u32[]{:S(2)}, u32[]{:S(2)}) collective-permute-start(bf16[8,3,48,384]{3,2,1,0:T(8,128)(2,1)} %fusion.11), channel_id=1, source_target_pairs={{0,4},{4,0},{8,12},{12,8},{16,20},{20,16},{24,28},{28,24},{1,5},{5... | collective-permute-start | bytes 2654216 | tf_op jit(solution)/shard_map/ppermute | solution.py:680
  403.6 54.5 %collective-permute-start.38 = (bf16[8,3,48,384]{3,2,1,0:T(8,128)(2,1)}, bf16[8,3,48,384]{3,2,1,0:T(8,128)(2,1)}, u32[]{:S(2)}, u32[]{:S(2)}) collective-permute-start(bf16[8,3,48,384]{3,2,1,0:T(8,128)(2,1)} %fusion.12), channel_id=1, source_target_pairs={{0,8},{4,12},{8,0},{12,4},{16,24},{20,28},{24,16},{28,20},{1,9},{5... | collective-permute-start | bytes 2654216 | tf_op jit(solution)/shard_map/ppermute | solution.py:680
  460.4 17.8 %collective-permute-start.39 = (bf16[4,3,48,384]{3,2,1,0:T(8,128)(2,1)S(1)}, bf16[4,3,48,384]{3,2,1,0:T(8,128)(2,1)}, u32[]{:S(2)}, u32[]{:S(2)}) collective-permute-start(bf16[4,3,48,384]{3,2,1,0:T(8,128)(2,1)S(1)} %slice.721), channel_id=1, source_target_pairs={{0,4},{4,0},{8,12},{12,8},{16,20},{20,16},{24,28},{28,24},{1,5},{5... | collective-permute-start | bytes 1327112 | tf_op jit(solution)/shard_map/ppermute | solution.py:680
  461.2 18.2 %collective-permute-start.40 = (bf16[4,3,48,384]{3,2,1,0:T(8,128)(2,1)}, bf16[4,3,48,384]{3,2,1,0:T(8,128)(2,1)}, u32[]{:S(2)}, u32[]{:S(2)}) collective-permute-start(bf16[4,3,48,384]{3,2,1,0:T(8,128)(2,1)} %slice.720), channel_id=1, source_target_pairs={{0,8},{4,12},{8,0},{12,4},{16,24},{20,28},{24,16},{28,20},{1,9},{5... | collective-permute-start | bytes 1327112 | tf_op jit(solution)/shard_map/ppermute | solution.py:680
  462.9 20.8 %collective-permute-start.41 = (bf16[4,3,48,384]{3,2,1,0:T(8,128)(2,1)}, bf16[4,3,48,384]{3,2,1,0:T(8,128)(2,1)}, u32[]{:S(2)}, u32[]{:S(2)}) collective-permute-start(bf16[4,3,48,384]{3,2,1,0:T(8,128)(2,1)} %slice.719), channel_id=1, source_target_pairs={{0,16},{4,20},{8,24},{12,28},{16,0},{20,4},{24,8},{28,12},{1,17},{... | collective-permute-start | bytes 1327112 | tf_op jit(solution)/shard_map/ppermute | solution.py:680
  486.4 18.9 %collective-permute-start.42 = (bf16[2,3,48,384]{3,2,1,0:T(8,128)(2,1)S(1)}, bf16[2,3,48,384]{3,2,1,0:T(8,128)(2,1)}, u32[]{:S(2)}, u32[]{:S(2)}) collective-permute-start(bf16[2,3,48,384]{3,2,1,0:T(8,128)(2,1)S(1)} %slice.724), channel_id=1, source_target_pairs={{0,8},{4,12},{8,0},{12,4},{16,24},{20,28},{24,16},{28,20},{1,9},{5... | collective-permute-start | bytes 663560 | tf_op jit(solution)/shard_map/ppermute | solution.py:680
  486.4 20.9 %collective-permute-start.43 = (bf16[2,3,48,384]{3,2,1,0:T(8,128)(2,1)S(1)}, bf16[2,3,48,384]{3,2,1,0:T(8,128)(2,1)}, u32[]{:S(2)}, u32[]{:S(2)}) collective-permute-start(bf16[2,3,48,384]{3,2,1,0:T(8,128)(2,1)S(1)} %slice.723), channel_id=1, source_target_pairs={{0,16},{4,20},{8,24},{12,28},{16,0},{20,4},{24,8},{28,12},{1,17},{... | collective-permute-start | bytes 663560 | tf_op jit(solution)/shard_map/ppermute | solution.py:680
  487.3 21.1 %collective-permute-start.44 = (bf16[2,3,48,384]{3,2,1,0:T(8,128)(2,1)}, bf16[2,3,48,384]{3,2,1,0:T(8,128)(2,1)S(1)}, u32[]{:S(2)}, u32[]{:S(2)}) collective-permute-start(bf16[2,3,48,384]{3,2,1,0:T(8,128)(2,1)} %slice.722), channel_id=1, source_target_pairs={{0,2},{1,3},{2,0},{3,1},{4,6},{5,7},{6,4},{7,5},{8,10},{9,11},{10,... | collective-permute-start | bytes 663560 | tf_op jit(solution)/shard_map/ppermute | solution.py:680
  502.7 49.0 %collective-permute-start.51 = (bf16[1024,768]{1,0:T(8,128)(2,1)S(1)}, bf16[1024,768]{1,0:T(8,128)(2,1)S(1)}, u32[]{:S(2)}, u32[]{:S(2)}) collective-permute-start(bf16[1024,768]{1,0:T(8,128)(2,1)S(1)} %gather_grads.4), channel_id=1, source_target_pairs={{0,12},{4,8},{8,4},{12,0},{16,28},{20,24},{24,20},{28,16},{1,13},{... | collective-permute-start | bytes 4718600 | tf_op jit(solution)/shard_map/ppermute | solution.py:680
  509.7 38.4 %collective-permute-start.49 = (bf16[1,3,48,384]{3,2,1,0:T(8,128)(2,1)S(1)}, bf16[1,3,48,384]{3,2,1,0:T(8,128)(2,1)S(1)}, u32[]{:S(2)}, u32[]{:S(2)}) collective-permute-start(bf16[1,3,48,384]{3,2,1,0:T(8,128)(2,1)S(1)} %slice.726), channel_id=1, source_target_pairs={{0,2},{1,3},{2,0},{3,1},{4,6},{5,7},{6,4},{7,5},{8,10},{9,11},{10,... | collective-permute-start | bytes 331784 | tf_op jit(solution)/shard_map/ppermute | solution.py:680
  510.4 37.7 %collective-permute-start.48 = (bf16[1,3,48,384]{3,2,1,0:T(8,128)(2,1)S(1)}, bf16[1,3,48,384]{3,2,1,0:T(8,128)(2,1)S(1)}, u32[]{:S(2)}, u32[]{:S(2)}) collective-permute-start(bf16[1,3,48,384]{3,2,1,0:T(8,128)(2,1)S(1)} %slice.727), channel_id=1, source_target_pairs={{0,16},{4,20},{8,24},{12,28},{16,0},{20,4},{24,8},{28,12},{1,17},{... | collective-permute-start | bytes 331784 | tf_op jit(solution)/shard_map/ppermute | solution.py:680
  512.8 35.1 %collective-permute-start.45 = (bf16[3,96,768]{2,1,0:T(8,128)(2,1)S(1)}, bf16[3,96,768]{2,1,0:T(8,128)(2,1)S(1)}, u32[]{:S(2)}, u32[]{:S(2)}) collective-permute-start(bf16[3,96,768]{2,1,0:T(8,128)(2,1)S(1)} %get-tuple-element.180), channel_id=1, source_target_pairs={{0,16},{4,20},{8,24},{12,28},{16,0},{20,4},{24,8},{28,12},{1,17},{... | collective-permute-start | bytes 1327112 | tf_op jit(solution)/shard_map/ppermute | solution.py:680
  550.8 13.3 %collective-permute-start.47 = (bf16[3,96,768]{2,1,0:T(8,128)(2,1)}, bf16[3,96,768]{2,1,0:T(8,128)(2,1)}, u32[]{:S(2)}, u32[]{:S(2)}) collective-permute-start(bf16[3,96,768]{2,1,0:T(8,128)(2,1)} %fusion.14), channel_id=1, source_target_pairs={{0,2},{1,3},{2,0},{3,1},{4,6},{5,7},{6,4},{7,5},{8,10},{9,11},{10,... | collective-permute-start | bytes 1327112 | tf_op jit(solution)/shard_map/ppermute | solution.py:680
  553.6 14.4 %all-to-all-start = ((bf16[4,3,48,384]{3,2,1,0:T(8,128)(2,1)}), bf16[4,3,48,384]{3,2,1,0:T(8,128)(2,1)}, u32[]{:S(2)}, u32[]{:S(2)}) async-start(bf16[4,3,48,384]{3,2,1,0:T(8,128)(2,1)} %bitcast.407), calls=%async_computation | async-start | bytes 884736 | tf_op jit(solution)/shard_map/all_to_all | solution.py:932
  580.2 26.8 %all-to-all-start.1 = ((bf16[8,3,96,96]{3,2,1,0:T(8,128)(2,1)}), bf16[8,3,96,96]{3,2,1,0:T(8,128)(2,1)}, u32[]{:S(2)}, u32[]{:S(2)}) async-start(bf16[8,3,96,96]{3,2,1,0:T(8,128)(2,1)} %bitcast.394), calls=%async_computation.1 | async-start | bytes 1179648 | tf_op jit(solution)/shard_map/all_to_all | solution.py:712
  616.8 32.1 %collective-permute-start.57 = (bf16[1024,768]{1,0:T(8,128)(2,1)}, bf16[1024,768]{1,0:T(8,128)(2,1)S(1)}, u32[]{:S(2)}, u32[]{:S(2)}) collective-permute-start(bf16[1024,768]{1,0:T(8,128)(2,1)} %copy-done.10), channel_id=1, source_target_pairs={{0,4},{4,0},{8,12},{12,8},{16,20},{20,16},{24,28},{28,24},{1,5},{5... | collective-permute-start | bytes 4718600 | tf_op jit(solution)/shard_map/ppermute | solution.py:680
  618.0 32.2 %collective-permute-start.58 = (bf16[1024,768]{1,0:T(8,128)(2,1)S(1)}, bf16[1024,768]{1,0:T(8,128)(2,1)}, u32[]{:S(2)}, u32[]{:S(2)}) collective-permute-start(bf16[1024,768]{1,0:T(8,128)(2,1)S(1)} %gather_grads.5), channel_id=1, source_target_pairs={{0,8},{4,12},{8,0},{12,4},{16,24},{20,28},{24,16},{28,20},{1,9},{5... | collective-permute-start | bytes 4718600 | tf_op jit(solution)/shard_map/ppermute | solution.py:680
  658.4 18.7 %all-to-all-start.2 = ((bf16[8,3,96,96]{3,2,1,0:T(8,128)(2,1)}), bf16[8,3,96,96]{3,2,1,0:T(8,128)(2,1)}, u32[]{:S(2)}, u32[]{:S(2)}) async-start(bf16[8,3,96,96]{3,2,1,0:T(8,128)(2,1)} %constant_dynamic-update-slice_fusion.36), calls=%async_computation.2 | async-start | bytes 1179648 | tf_op jit(solution)/shard_map/all_to_all | solution.py:722
  689.1 18.3 %all-to-all-start.3 = ((bf16[8,3,96,96]{3,2,1,0:T(8,128)(2,1)}), bf16[8,3,96,96]{3,2,1,0:T(8,128)(2,1)}, u32[]{:S(2)}, u32[]{:S(2)}) async-start(bf16[8,3,96,96]{3,2,1,0:T(8,128)(2,1)} %bitcast.395), calls=%async_computation.3 | async-start | bytes 1179648 | tf_op jit(solution)/shard_map/all_to_all | solution.py:712
  (93 other events, 815.8 us)
Sparse Core Ops, SparseCore 0:
  101.5 3.5 sort.54.cloned.1.call-done
  (1 shorter events, 0.0 us)

commit v4 on v3

--- a/solution.py
+++ b/solution.py
@@ -67,6 +67,31 @@
 
 def turn_half(value):
     return pltpu.roll(value, HEAD, 1)
+
+
+def places_body(share_ref, clusters_ref, out_ref):
+    pairs, count = clusters_ref.shape
+    share = share_ref[0]
+    kinds = UNIT * count // CLUSTER
+    kind = lax.broadcasted_iota(jnp.int32, (kinds, count), 0)
+    earlier = lax.broadcasted_iota(jnp.int32, (count, count), 0) < lax.broadcasted_iota(jnp.int32, (count, count), 1)
+    earlier = earlier.astype(F32).astype(BF16)
+    for pair in range(pairs):
+        cluster = clusters_ref[pair : pair + 1, :]
+        same = (kind == cluster).astype(F32)
+        before = jnp.dot(same.astype(BF16), earlier, preferred_element_type=F32)
+        rank = jnp.sum(same * before, axis=0, keepdims=True).astype(jnp.int32)
+        out_ref[pair : pair + 1, :] = cluster * share + rank
+
+
+def places(share, clusters):
+    return pl.pallas_call(
+        places_body,
+        in_specs=[pl.BlockSpec(memory_space=pltpu.SMEM), pl.BlockSpec(memory_space=pltpu.VMEM)],
+        out_shape=jax.ShapeDtypeStruct(clusters.shape, jnp.int32),
+        cost_estimate=SMALL,
+        name="places",
+    )(share, clusters)
 
 
 def arrange_body(rows_ref, out_ref):
@@ -122,7 +147,7 @@
     return pl.pallas_call(
         assemble_body,
         in_specs=[pl.BlockSpec(memory_space=pltpu.SMEM)] + [anywhere] * len(shards),
-        out_specs=anywhere,
+        out_specs=pl.BlockSpec(memory_space=pltpu.VMEM),
         out_shape=jax.ShapeDtypeStruct((pieces * shards[0].shape[1], shards[0].shape[2]), BF16),
         scratch_shapes=[pltpu.SemaphoreType.DMA((pieces,))],
         cost_estimate=SMALL,
@@ -130,16 +155,11 @@
     )(table, *shards)
 
 
-def sort_body(order_ref, x_ref, weight_ref, bias_ref, out_ref, column_ref, rows_ref):
+def sort_body(place_ref, x_ref, weight_ref, bias_ref, out_ref, rows_ref):
     count = x_ref.shape[0]
-
-    @pl.when(pl.program_id(0) == 0)
-    def _():
-        column_ref[...] = jnp.transpose(order_ref[...])
-
     head = pl.program_id(0)
     chunk = 256
-    lane = lax.broadcasted_iota(jnp.int32, (chunk, count), 1)
+    row = lax.broadcasted_iota(jnp.int32, (chunk, count), 0)
     rows_ref[...] = (
         jnp.dot(x_ref[...], weight_ref[...], preferred_element_type=F32) + bias_ref[...]
     ).astype(BF16)
@@ -151,7 +171,8 @@
                 pair = step * ROUNDS + turn
                 for part in range(count // chunk):
                     where = pl.ds(part * chunk, chunk)
-                    picked = (column_ref[where, pair : pair + 1] == lane).astype(F32).astype(BF16)
+                    picked = place_ref[pair : pair + 1, :] == row + part * chunk
+                    picked = picked.astype(F32).astype(BF16)
                     out_ref[turn, where, :] = jnp.dot(
                         picked, rows_ref[...], preferred_element_type=F32
                     ).astype(BF16)
@@ -170,24 +191,19 @@
         ],
         out_specs=pl.BlockSpec((ROUNDS, count, WIDE), lambda h: (h, 0, 0)),
         out_shape=jax.ShapeDtypeStruct((LOCAL_PAIRS, count, WIDE), BF16),
-        scratch_shapes=[pltpu.VMEM((count, 8), jnp.int32), pltpu.VMEM((count, WIDE), BF16)],
+        scratch_shapes=[pltpu.VMEM((count, WIDE), BF16)],
         compiler_params=pltpu.CompilerParams(vmem_limit_bytes=48 << 20),
         cost_estimate=SMALL,
         name="sort_rows",
     )(order, inputs, weights, bias)
 
 
-def sort_grads_body(order_ref, rows_ref, out_ref, column_ref):
-    count = order_ref.shape[1]
+def sort_grads_body(place_ref, rows_ref, out_ref):
+    count = place_ref.shape[1]
     half = count // 2
-
-    @pl.when(pl.program_id(0) == 0)
-    def _():
-        column_ref[...] = jnp.transpose(order_ref[...])
-
     head = pl.program_id(0)
     chunk = 256
-    lane = lax.broadcasted_iota(jnp.int32, (chunk, count), 1)
+    row = lax.broadcasted_iota(jnp.int32, (chunk, count), 0)
     low = lax.broadcasted_iota(jnp.int32, (count, TILE), 1) < HEAD
     for step in range(HEADS_OWN):
 
@@ -204,7 +220,8 @@
                 pair = step * ROUNDS + turn
                 for part in range(count // chunk):
                     where = pl.ds(part * chunk, chunk)
-                    picked = (column_ref[where, pair : pair + 1] == lane).astype(F32).astype(BF16)
+                    picked = place_ref[pair : pair + 1, :] == row + part * chunk
+                    picked = picked.astype(F32).astype(BF16)
                     out_ref[turn, where, :] = jnp.dot(
                         picked, tile, preferred_element_type=F32
                     ).astype(BF16)
@@ -221,7 +238,6 @@
         ],
         out_specs=pl.BlockSpec((ROUNDS, count, TILE), lambda h: (h, 0, 0)),
         out_shape=jax.ShapeDtypeStruct((LOCAL_PAIRS, count, TILE), BF16),
-        scratch_shapes=[pltpu.VMEM((count, 8), jnp.int32)],
         compiler_params=pltpu.CompilerParams(vmem_limit_bytes=48 << 20),
         cost_estimate=SMALL,
         name="sort_grads",
@@ -348,19 +364,24 @@
     )(is_long, *grouped, *grads)
 
 
-def unsorted(order_ref, step, rows_ref, part, chunk):
+def unsorted(column_ref, step, rows_ref, part, chunk):
     count = rows_ref.shape[1]
-    row = lax.broadcasted_iota(jnp.int32, (chunk, count), 0) + part * chunk
+    where = pl.ds(part * chunk, chunk)
+    lane = lax.broadcasted_iota(jnp.int32, (chunk, count), 1)
     total = None
     for turn in range(ROUNDS):
         pair = step * ROUNDS + turn
-        picked = (order_ref[pair : pair + 1, :] == row).astype(F32).astype(BF16)
+        picked = (column_ref[where, pair : pair + 1] == lane).astype(F32).astype(BF16)
         more = jnp.dot(picked, rows_ref[turn], preferred_element_type=F32)
         total = more if total is None else total + more
     return total
 
 
-def mix_body(order_ref, rows_ref, out_ref):
+def mix_body(place_ref, rows_ref, out_ref, column_ref):
+    @pl.when(pl.program_id(0) == 0)
+    def _():
+        column_ref[...] = jnp.transpose(place_ref[...])
+
     count = rows_ref.shape[1]
     chunk = 256
     parts = count // chunk
@@ -370,7 +391,7 @@
 
         @pl.when(head == step)
         def _():
-            means = [0.5 * unsorted(order_ref, step, rows_ref, part, chunk) for part in range(parts)]
+            means = [0.5 * unsorted(column_ref, step, rows_ref, part, chunk) for part in range(parts)]
             for part in range(parts):
                 where = pl.ds(part * chunk, chunk)
                 if step == 0:
@@ -394,13 +415,18 @@
         ],
         out_specs=pl.BlockSpec(packed, lambda h: (0, 0)),
         out_shape=jax.ShapeDtypeStruct(packed, BF16),
+        scratch_shapes=[pltpu.VMEM((count, 8), jnp.int32)],
         compiler_params=pltpu.CompilerParams(vmem_limit_bytes=48 << 20),
         cost_estimate=SMALL,
         name="mix",
     )(order, rows)
 
 
-def gather_grads_body(order_ref, rows_ref, out_ref):
+def gather_grads_body(place_ref, rows_ref, out_ref, column_ref):
+    @pl.when(pl.program_id(0) == 0)
+    def _():
+        column_ref[...] = jnp.transpose(place_ref[...])
+
     count = rows_ref.shape[1]
     chunk = 256
     head = pl.program_id(0)
@@ -410,7 +436,7 @@
         def _():
             for part in range(count // chunk):
                 where = pl.ds(part * chunk, chunk)
-                out_ref[where, :] = unsorted(order_ref, step, rows_ref, part, chunk).astype(BF16)
+                out_ref[where, :] = unsorted(column_ref, step, rows_ref, part, chunk).astype(BF16)
 
 
 def gather_grads(order, rows):
@@ -424,6 +450,7 @@
         ],
         out_specs=pl.BlockSpec((count, WIDE), lambda h: (0, h)),
         out_shape=jax.ShapeDtypeStruct((count, HEADS_OWN * WIDE), BF16),
+        scratch_shapes=[pltpu.VMEM((count, 8), jnp.int32)],
         compiler_params=pltpu.CompilerParams(vmem_limit_bytes=48 << 20),
         cost_estimate=SMALL,
         name="gather_grads",
@@ -675,6 +702,131 @@
     )(table, *shards, *parts, inputs, cotangent, vectors)
 
 
+def rotate_in_body(mine_ref, keep_ref, got_ref, high_ref, low_ref, out_ref, grad_ref):
+    slots, n_tok = got_ref.shape[1], out_ref.shape[0]
+    rows, columns = got_ref.shape[2:]
+    width = out_ref.shape[3]
+    for s in range(slots):
+        block = mine_ref[s]
+
+        @pl.when(block < 3)
+        def _(s=s, block=block):
+            grad_ref[...] = keep_ref[jnp.minimum(block, 2)]
+
+        @pl.when(block >= 3)
+        def _(s=s):
+            for g in range(got_ref.shape[0]):
+                x, c = g // 2, g % 2
+                grad_ref[x * rows : (x + 1) * rows, c * columns : (c + 1) * columns] = got_ref[g, s]
+
+        grad = grad_ref[...]
+        part = jnp.dot(grad, high_ref[s], preferred_element_type=F32)
+        part = jnp.transpose(part + jnp.dot(grad, low_ref[s], preferred_element_type=F32))
+        for r in range(n_tok):
+            out_ref[r, s] = part[r * width : (r + 1) * width].astype(BF16)
+
+
+def rotate_in(mine, keep, got, left, n_tok):
+    slots, width = got.shape[1], keep.shape[1]
+    inside = pl.BlockSpec(memory_space=pltpu.VMEM)
+    return pl.pallas_call(
+        rotate_in_body,
+        in_specs=[pl.BlockSpec(memory_space=pltpu.SMEM)] + [inside] * 4,
+        out_specs=inside,
+        out_shape=jax.ShapeDtypeStruct((n_tok, slots, width, width), BF16),
+        scratch_shapes=[pltpu.VMEM(keep.shape[1:], BF16)],
+        compiler_params=pltpu.CompilerParams(vmem_limit_bytes=48 << 20),
+        cost_estimate=SMALL,
+        name="rotate_in",
+    )(mine, keep, got, *left)
+
+
+def moments_body(place, got_ref, high_ref, low_ref, one_ref, two_ref, new_one_ref, new_two_ref, out_ref):
+    n_tok, slots, width = got_ref.shape[:3]
+    for s in range(slots):
+        rotated = jnp.zeros(one_ref.shape[1:], F32)
+        for t in range(n_tok):
+            at = slice(place[t] * width, (place[t] + 1) * width)
+            part = got_ref[t, s]
+            rotated = rotated + jnp.dot(part, high_ref[s, at], preferred_element_type=F32)
+            rotated = rotated + jnp.dot(part, low_ref[s, at], preferred_element_type=F32)
+        new_one = BETA_ONE * one_ref[s] + (1.0 - BETA_ONE) * rotated
+        new_two = BETA_TWO * two_ref[s] + (1.0 - BETA_TWO) * rotated * rotated
+        new_one_ref[s] = new_one
+        new_two_ref[s] = new_two
+        direction = (new_one / (jnp.sqrt(new_two) + ADAM_EPS)).astype(BF16)
+        for t in range(n_tok):
+            at = slice(place[t] * width, (place[t] + 1) * width)
+            turned = outer_cols(direction, high_ref[s, at]) + outer_cols(direction, low_ref[s, at])
+            out_ref[t, s] = turned.astype(BF16)
+
+
+def moments(place, got, right, one, two):
+    n_tok, slots, width = got.shape[:3]
+    inside = pl.BlockSpec(memory_space=pltpu.VMEM)
+    return pl.pallas_call(
+        functools.partial(moments_body, tuple(place)),
+        in_specs=[inside] * 5,
+        out_specs=[inside] * 3,
+        out_shape=[
+            jax.ShapeDtypeStruct(one.shape, F32),
+            jax.ShapeDtypeStruct(one.shape, F32),
+            jax.ShapeDtypeStruct(got.shape, BF16),
+        ],
+        compiler_params=pltpu.CompilerParams(vmem_limit_bytes=48 << 20),
+        cost_estimate=SMALL,
+        name="moments",
+    )(got, *right, one, two)
+
+
+def rotate_out_body(got_ref, high_ref, low_ref, out_ref, rows_ref):
+    n_tok, slots, width = got_ref.shape[:3]
+    for s in range(slots):
+        for r in range(n_tok):
+            rows_ref[r * width : (r + 1) * width, :] = got_ref[r, s]
+        rows = rows_ref[...]
+        change = jnp.dot(high_ref[s], rows, preferred_element_type=F32)
+        change = change + jnp.dot(low_ref[s], rows, preferred_element_type=F32)
+        for r in range(n_tok):
+            out_ref[r, s] = change[r * width : (r + 1) * width].astype(BF16)
+
+
+def rotate_out(got, left):
+    n_tok, slots, width = got.shape[:3]
+    inside = pl.BlockSpec(memory_space=pltpu.VMEM)
+    return pl.pallas_call(
+        rotate_out_body,
+        in_specs=[inside] * 3,
+        out_specs=inside,
+        out_shape=jax.ShapeDtypeStruct(got.shape, BF16),
+        scratch_shapes=[pltpu.VMEM((n_tok * width, width), BF16)],
+        compiler_params=pltpu.CompilerParams(vmem_limit_bytes=48 << 20),
+        cost_estimate=SMALL,
+        name="rotate_out",
+    )(got, *left)
+
+
+def apply_body(place, got_ref, master_ref, out_ref):
+    n_tok, slots, width = got_ref.shape[:3]
+    for s in range(slots):
+        for t in range(n_tok):
+            at = slice(place[t] * width, (place[t] + 1) * width)
+            out_ref[s, :, at] = master_ref[s, :, at] - RATE_MATRIX * got_ref[t, s].astype(F32)
+
+
+def apply_change(place, got, master):
+    inside = pl.BlockSpec(memory_space=pltpu.VMEM)
+    return pl.pallas_call(
+        functools.partial(apply_body, tuple(place)),
+        in_specs=[inside] * 2,
+        out_specs=inside,
+        out_shape=jax.ShapeDtypeStruct(master.shape, F32),
+        compiler_params=pltpu.CompilerParams(vmem_limit_bytes=48 << 20),
+        cost_estimate=SMALL,
+        name="apply_change",
+    )(got, master)
+
+
 def swap(value, axis, bit):
     size = lax.axis_size(axis)
     return lax.ppermute(value, axis, [(i, i ^ bit) for i in range(size)])
@@ -682,6 +834,14 @@
 
 def exchange_unit(parts):
     return [parts[0]] + [swap(parts[k], "tok", k) for k in range(1, UNIT)]
+
+
+LINKS = {"x": ("grp", 2), "y": ("tok", 1), "zl": ("tok", 2), "zh": ("tok", 4)}
+
+
+def starts_of(lengths):
+    index = jnp.arange(lengths.shape[0])
+    return jnp.sum(jnp.where(index[None, :] < index[:, None], lengths[None, :], 0), axis=1)
 
 
 LINKS = {"x": ("grp", 2), "y": ("tok", 1), "zl": ("tok", 2), "zh": ("tok", 4)}
@@ -705,24 +865,6 @@
     return lax.dynamic_index_in_dim(values, index, 0, keepdims=False)
 
 
-def turn_rows(value, place):
-    n_tok = lax.axis_size("tok")
-    slots, rows, width = value.shape
-    parts = jnp.transpose(value.reshape(slots, n_tok, rows // n_tok, width), (1, 0, 2, 3))
-    got = lax.all_to_all(parts, "tok", split_axis=0, concat_axis=0, tiled=True)
-    got = jnp.stack([got[place.index(c)] for c in range(n_tok)], axis=2)
-    return got.reshape(slots, rows // n_tok, n_tok * width)
-
-
-def turn_columns(value, place):
-    n_tok = lax.axis_size("tok")
-    slots, rows, width = value.shape
-    parts = value.reshape(slots, rows, n_tok, width // n_tok)
-    parts = jnp.stack([parts[:, :, place[t]] for t in range(n_tok)], axis=0)
-    got = lax.all_to_all(parts, "tok", split_axis=0, concat_axis=0, tiled=True)
-    return jnp.transpose(got, (1, 0, 2, 3)).reshape(slots, n_tok * rows, width // n_tok)
-
-
 def split_heads(columns):
     query, keys, values = (c.reshape(HEADS_OWN, HEAD) for c in columns)
     zero = jnp.zeros((HEAD,), query.dtype)
@@ -743,10 +885,6 @@
 def doubled(value):
     high = value.astype(BF16)
     return high, (value - high.astype(F32)).astype(BF16)
-
-
-def twice(form, left, right):
-    return products(form, left, right[0]) + products(form, left, right[1])
 
 
 def together(*groups):
@@ -790,38 +928,42 @@
     near, far = swap(inputs, "tok", 1), swap(inputs, "tok", 2)
     local = jnp.transpose(master.astype(BF16), (1, 0, 2))
     beside, over = swap(local, "grp", 1), swap(local, "grp", 2)
-    across = swap(over, "grp", 1)
-
-    order = jnp.argsort(clusters[0], axis=-1, stable=True).astype(jnp.int32)
-    by_member = jnp.transpose(order.reshape(ROUNDS, UNIT, HEADS_OWN, tok_count), (1, 2, 0, 3))
-    by_member = by_member.reshape(UNIT, LOCAL_PAIRS, tok_count)
-    orders = exchange_unit([pick(by_member, member ^ k) for k in range(UNIT)])
-    orders = [jnp.pad(o, ((0, 8 - LOCAL_PAIRS), (0, 0))) for o in orders]
+
     item_starts = starts_of(lengths[0])
     unit_start = unit * UNIT * tok_count
     middle = unit_start + UNIT // 2 * tok_count
     start_of_middle = jnp.max(jnp.where(item_starts <= middle, item_starts, 0))
     is_long = (start_of_middle <= unit_start).astype(jnp.int32).reshape(1)
-
+    order = places(CLUSTER // UNIT * (2 - is_long), clusters[0])
+    by_member = jnp.transpose(order.reshape(ROUNDS, UNIT, HEADS_OWN, tok_count), (1, 2, 0, 3))
+    by_member = by_member.reshape(UNIT, LOCAL_PAIRS, tok_count)
+    by_member = jnp.pad(by_member, ((0, 0), (0, 8 - LOCAL_PAIRS), (0, 0)))
+    orders = exchange_unit([pick(by_member, member ^ k) for k in range(UNIT)])
     left, right = doubled(bases[0]), doubled(bases[1])
-    (near, far, beside, over, across, left, right) = together(near, far, beside, over, across, left, right)
+    (over, left, right) = together(over, left, right)
+    across = swap(over, "grp", 1)
+
+    (near, far, beside, over, across) = together(near, far, beside, over, across)
     by_slot = jnp.concatenate([local, beside, over, across], axis=0)
     at = [((block_slot[b] // slots) ^ grp) * slots + block_slot[b] % slots for b in range(blocks_all)]
     part_rows = rows_dev // 2
 
-    def own_half(b):
-        return lax.dynamic_slice(by_slot, (at[b], core * part_rows, 0), (1, part_rows, D))[0]
-
-    by_owner = arrange(jnp.stack([own_half(b) for b in range(3)]))
+    def own_half(source, b):
+        return lax.dynamic_slice(source, (at[b], core * part_rows, 0), (1, part_rows, D))[0]
+
+    by_owner = arrange(jnp.stack([own_half(by_slot, b) for b in range(3)]))
     theirs = exchange_unit([pick(by_owner, member ^ k) for k in range(UNIT)])
     half = tok_count // 2
     third = (swap(near[:half], "tok", 2), swap(far[half:], "tok", 1))
+    (theirs, by_slot) = together(theirs, by_slot)
     theirs = jnp.stack(theirs)
     theirs_far = swap(theirs, "tok", UNIT)
     mine_all = jnp.concatenate([theirs, theirs_far], axis=0)
     others_all = swap(mine_all, "grp", 1)
     sources = [tok ^ k ^ (UNIT * f) for f in range(2) for k in range(UNIT)]
     firsts = [t * rows_dev + c * part_rows for c in (core, 1 - core) for t in sources]
+    rest_rows = jnp.stack([own_half(by_slot, b) for b in range(3, blocks_all)])
+    (third, others_all, rest_rows, orders) = together(third, others_all, rest_rows, orders)
     own_weights = assemble(jnp.stack(firsts).astype(jnp.int32), [mine_all, others_all])
 
     def columns_of(value, m):
@@ -833,28 +975,27 @@
     grouped = [
         sort_rows(orders[k], value, own_weights, own_bias) for k, value in enumerate((inputs, near, far))
     ]
-    (third, grouped) = together(third, grouped)
     unit_inputs = [inputs, near, far, jnp.concatenate(third, axis=0)]
     grouped.append(sort_rows(orders[3], unit_inputs[3], own_weights, own_bias))
 
-    (rest_rows, _) = together(jnp.stack([own_half(b) for b in range(3, blocks_all)]), third)
     ring = [(i, (i + 2) % n_tok) for i in range(n_tok)]
     depth = n_tok // 2
     steps, flips = [rest_rows], []
     steps.append(lax.ppermute(steps[0], "tok", ring))
     flips.append(swap(steps[0], "tok", 1))
+    (grouped, steps[1], flips[0]) = together(grouped, steps[1], flips[0])
+    steps.append(lax.ppermute(steps[1], "tok", ring))
+    flips.append(swap(steps[1], "tok", 1))
     sorted_out = attend(is_long, grouped)
-    (sorted_out, steps[1], flips[0]) = together(sorted_out, steps[1], flips[0])
+    (sorted_out, steps[2], flips[1]) = together(sorted_out, steps[2], flips[1])
     mixed = [None] * UNIT
     mixed[3] = mix(orders[3], sorted_out[3])
     mixed[2] = mix(orders[2], sorted_out[2])
     mixed[1] = mix(orders[1], sorted_out[1])
     mixed_parts = exchange_unit(mixed)
-    steps.append(lax.ppermute(steps[1], "tok", ring))
-    flips.append(swap(steps[1], "tok", 1))
-    (steps[2], flips[1], mixed_parts[1:]) = together(steps[2], flips[1], mixed_parts[1:])
     steps.append(lax.ppermute(steps[2], "tok", ring))
     flips.append(swap(steps[2], "tok", 1))
+    (steps[3], flips[2], mixed_parts[1:]) = together(steps[3], flips[2], mixed_parts[1:])
     flips.append(swap(steps[3], "tok", 1))
     mixed_parts[0] = mix(orders[0], sorted_out[0])
     mine_rest = [jnp.stack([steps[k], flips[k]]) for k in range(depth)]
@@ -887,11 +1028,10 @@
     def joined(kept_now, got_now):
         return [k + g.astype(F32) for k, g in zip(kept_now, got_now)]
 
-    sorted_grads = [sort_grads(orders[0], grad_parts[0])]
     kept_now, sent_now = halves(sums_of)
-    (sent_now, sorted_grads, grad_parts) = together(sent_now, sorted_grads, grad_parts)
+    (sent_now, grad_parts) = together(sent_now, grad_parts)
     got_now = exchanged(sent_now, 0)
-    sorted_grads += [sort_grads(orders[k], grad_parts[k]) for k in range(1, UNIT)]
+    sorted_grads = [sort_grads(orders[k], grad_parts[k]) for k in range(UNIT)]
     sorted_back = attend_back(is_long, grouped, sorted_grads)
     kept_now, sent_now = halves(joined(kept_now, got_now))
     (sent_now, sorted_back) = together(sent_now, sorted_back)
@@ -901,63 +1041,74 @@
         own_grads[k] = gather_grads(orders[k], sorted_back[k])
     turned_qkv = sum(inner_rows(own_grads[k], unit_inputs[k]) for k in (3, 2))
     kept_now, sent_now = halves(joined(kept_now, got_now))
-    (sent_now, turned_qkv, sorted_back, own_grads[3]) = together(
-        sent_now, turned_qkv, sorted_back, own_grads[3]
-    )
+    (sent_now, turned_qkv, sorted_back) = together(sent_now, turned_qkv, sorted_back)
     got_now = exchanged(sent_now, 2)
-    home_grads = [None, None, None, swap(own_grads[3], "tok", 3)]
     for k in (1, 0):
         own_grads[k] = gather_grads(orders[k], sorted_back[k])
     turned_qkv = turned_qkv + sum(inner_rows(own_grads[k], unit_inputs[k]) for k in (1, 0))
     kept_now, sent_now = halves(joined(kept_now, got_now))
-    turned_qkv = join_heads(turned_qkv).astype(BF16).reshape(3, 2, own_width // 2, D)
-    turned_qkv = (pick(jnp.swapaxes(turned_qkv, 0, 1), unit), pick(jnp.swapaxes(turned_qkv, 0, 1), 1 - unit))
-    (sent_now, turned_qkv, own_grads) = together(sent_now, turned_qkv, own_grads)
+    turned_qkv = join_heads(turned_qkv).astype(BF16).reshape(3, 2, own_width // 2, 2, D // 2)
+    turned_qkv = jnp.transpose(turned_qkv, (3, 1, 0, 2, 4))
+    (sent_now, turned_qkv) = together(sent_now, turned_qkv)
     got_now = exchanged(sent_now, 3)
+
     bias_qkv = sum(jnp.sum(own_grads[k].astype(F32), axis=0) for k in range(UNIT))
-
     bias_query, _, bias_value = join_heads(bias_qkv)
     bias_rows = lax.dynamic_update_slice_in_dim(
         jnp.zeros((2, D), F32), jnp.stack([bias_query, bias_value]), member * own_width, 1
     )
-    vector_grads = sums[: 8 + FFB] + jnp.pad(bias_rows, ((4, 2 + FFB), (0, 0)))
-    keep = turned_qkv[0].astype(F32) + swap(turned_qkv[1], "tok", UNIT).astype(F32)
-    keep = keep + swap(keep.astype(BF16), "grp", 1).astype(F32)
-    vector_total = total_of(vector_grads)
+    total = sums[: 8 + FFB] + jnp.pad(bias_rows, ((4, 2 + FFB), (0, 0)))
+
+    core_got = swap(pick(turned_qkv, 1 - core), "grp", 1)
+    more = swap(total, "grp", 1)
+    keep = pick(turned_qkv, core).astype(F32) + core_got.astype(F32)
+    (keep, more) = together(keep, more)
+    total = total + more
+    more = swap(total, "grp", 2)
+    unit_got = swap(pick(keep, 1 - unit).astype(BF16), "tok", UNIT)
+    home_grads = [own_grads[0], swap(own_grads[1], "tok", 1), None, None]
     rest = jnp.concatenate([v[0].astype(BF16) for v in joined(kept_now, got_now)], axis=0)
-    (rest, home_grads[3]) = together(rest, home_grads[3])
     sent = jnp.stack(
         [pick(rest, jnp.maximum(slot_block[s] - 3, 0)) for s in range(blocks_all)]
     ).reshape(n_grp, slots, *rest.shape[1:])
     got = lax.all_to_all(sent, "grp", split_axis=0, concat_axis=0, tiled=True)
-    keep = (keep + swap(keep.astype(BF16), "grp", 2).astype(F32)).astype(BF16)
-    got = jnp.transpose(got.reshape(2, 2, *got.shape[1:]), (2, 0, 3, 1, 4))
-    got = got.reshape(slots, D // n_tok, D)
-
+    keep = pick(keep, unit) + unit_got.astype(F32)
+    (keep, more, own_grads[2]) = together(keep, more, own_grads[2])
+    total = total + more
+    more = swap(total, "tok", 1)
+    keep = keep + swap(keep.astype(BF16), "grp", 2).astype(F32)
+    (keep, more) = together(keep.astype(BF16), more)
+    total = total + more
+    more = swap(total, "tok", 2)
+    home_grads[2] = swap(own_grads[2], "tok", 2)
+    kept_core = (keep, swap(keep, "grp", 1))
+    keep = jnp.concatenate(
+        [jnp.where(core == 0, kept_core[0], kept_core[1]), jnp.where(core == 0, kept_core[1], kept_core[0])],
+        axis=-1,
+    )
     mine = lax.dynamic_slice_in_dim(slot_block, grp * slots, slots, 0)
-    reduced = jnp.stack(
-        [
-            jnp.where(mine[s] < 3, pick(keep, jnp.minimum(mine[s], 2)), got[s]) for s in range(slots)
-        ]
-    )
-    part = products("sia,sci->sac", left[0], reduced) + products("sia,sci->sac", left[1], reduced)
-    part = turn_rows(part.astype(BF16), place)
-    (part, own_grads[:3], vector_total) = together(part, own_grads[:3], vector_total)
-    home_grads[:3] = [own_grads[0]] + [swap(own_grads[k], "tok", k) for k in (1, 2)]
-    rotated = twice("sac,scb->sab", part, right)
-    rotated = jnp.transpose(rotated, (1, 0, 2))
-    new_one = BETA_ONE * moment_one + (1.0 - BETA_ONE) * rotated
-    new_two = BETA_TWO * moment_two + (1.0 - BETA_TWO) * rotated * rotated
-    direction = (new_one / (jnp.sqrt(new_two) + ADAM_EPS)).astype(BF16)
-    turned = twice("asb,scb->sac", direction, right)
-    (turned, home_grads[:3]) = together(turned.astype(BF16), home_grads[:3])
-    turned = turn_columns(turned, place)
-    change = products("sia,sac->sic", left[0], turned) + products("sia,sac->sic", left[1], turned)
-    change = turn_rows(change.astype(BF16), place).astype(F32)
+
+    def to_tok(value):
+        return lax.all_to_all(value, "tok", split_axis=0, concat_axis=0, tiled=True)
+
+    part = to_tok(rotate_in(mine, keep, got, left, n_tok))
+    (part, more, home_grads[1], own_grads[3]) = together(part, more, home_grads[1], own_grads[3])
+    total = total + more
+    more = swap(total, "tok", 4)
+    home_grads[3] = swap(own_grads[3], "tok", 3)
+    by_slot_of = lambda value: jnp.transpose(value, (1, 0, 2))
+    new_one, new_two, turned = moments(
+        place, part, right, by_slot_of(moment_one), by_slot_of(moment_two)
+    )
+    turned = to_tok(turned)
+    (turned, more, home_grads[2]) = together(turned, more, home_grads[2])
+    vector_total = total + more
+    change = to_tok(rotate_out(turned, left))
+    new_master = by_slot_of(apply_change(place, change, by_slot_of(master)))
+    new_one, new_two = by_slot_of(new_one), by_slot_of(new_two)
     grad_inputs = grad_first + sum(
         outer_cols(home_grads[k], own_weights if k == 0 else turned_weights[k - 1]) for k in range(UNIT)
     )
-    new_master = master - RATE_MATRIX * jnp.transpose(change, (1, 0, 2))
     new_vec_one = BETA_ONE * vector_one + (1.0 - BETA_ONE) * vector_total
     new_vec_two = BETA_TWO * vector_two + (1.0 - BETA_TWO) * vector_total * vector_total
     new_vectors = vectors - RATE_VECTOR * new_vec_one / (jnp.sqrt(new_vec_two) + ADAM_EPS)

time: 736 us -> 678 us (0.921)
  waiting for transfers between devices: 181 us -> 145 us
  between operations: 51.4 us -> 33.8 us
  matrix products: 40.9 us -> 32.7 us
    pallas_call x1, Pallas kernels: 37.7 us -> 3.25 us  [assemble(): pl.pallas_call(assemble_body, in_specs=[pl.BlockSpec(memory_space=pltpu.S...]
    pallas_call x0 -> x5, Pallas kernels: none -> 25.4 us  [the longest x1 8.89 us: moments(): pl.pallas_call(functools.partial(moments_body, tuple(place)), in_specs=[i...]
    ppermute x1, waiting for transfers between devices: 17.7 us -> 0.01 us  [fast(): steps.append(lax.ppermute(steps[2], 'tok', ring))]
    ppermute x56 -> x57, waiting for transfers between devices: 151 us -> 135 us  [swap(): return lax.ppermute(value, axis, [(i, i ^ bit) for i in range(size)])]
    reshape x8 -> x0, local copies, waits for them, and re-layouts: 14.4 us -> none  [the longest x4 7.52 us: turn_rows(): value.reshape(slots, n_tok, rows // n_tok, width)]
    dot_general x8 -> x0, matrix products: 13.2 us -> none  [products(): return jnp.einsum(form, left, right, preferred_element_type=F32)]
    unnamed x203 -> x224, local copies, waits for them, and re-layouts: 48.6 us -> 60.2 us
    ppermute x56 -> x57, starting transfers between devices: 57.8 us -> 57.8 us  [swap(): return lax.ppermute(value, axis, [(i, i ^ bit) for i in range(size)])]
  transfers between devices with their start and end apart: 63 -> 64, of which waited for: 25 -> 17; matrix products, arithmetic and copies ran while one was open for 14% -> 20% of each run, Pallas kernels for 30% -> 31%
where the time goes in v4:
time: 678 us; the launch traced here: 667 us
  Pallas kernels  220 us (32%)
  waiting for transfers between devices  145 us (21%)
  local copies, waits for them, and re-layouts  98.1 us (14%)
  starting transfers between devices  79.9 us (12%)
  other arithmetic  58.1 us (9%)
  between operations  33.8 us (5%)
  matrix products  32.7 us (5%)
    ppermute x57, waiting for transfers between devices, swap(): return lax.ppermute(value, axis, [(i, i ^ bit) for i in range(size)])  135 us
    pallas_call x1, Pallas kernels, layer(): pl.pallas_call(functools.partial(layer_body, n_shards), in_specs=[pl.Bloc...  69.3 us
    unnamed x224, local copies, waits for them, and re-layouts  60.2 us
    ppermute x57, starting transfers between devices, swap(): return lax.ppermute(value, axis, [(i, i ^ bit) for i in range(size)])  57.8 us
    pallas_call x4, Pallas kernels, sort_rows(): pl.pallas_call(sort_body, grid=(HEADS_OWN,), in_specs=[pl.BlockSpec((8, c...  27.7 us
    pallas_call x4, Pallas kernels, gather_grads(): pl.pallas_call(gather_grads_body, grid=(HEADS_OWN,), in_specs=[pl.BlockSp...  20.3 us
    pallas_call x1, Pallas kernels, attend_back(): pl.pallas_call(attend_back_body, grid_spec=pltpu.PrefetchScalarGridSpec(n...  19.1 us
    pallas_call x4, Pallas kernels, mix(): pl.pallas_call(mix_body, grid=(HEADS_OWN,), in_specs=[pl.BlockSpec((8, co...  19.1 us
  transfers between devices with their start and end apart: 64, of which 17 were waited for; matrix products, arithmetic and copies ran while one was open for 20% of the time, Pallas kernels for 31%

profile of v4, /device:TPU:0, one launch (start us, length us, event | category | flops | bytes accessed | tf_op | source)
XLA Modules:
  0.0 667.4 jit_solution(5874131379552758892)
XLA Ops:
  8.8 14.7 %fusion = (bf16[3,768,768]{2,1,0:T(8,128)(2,1)}, bf16[3,768,768]{2,1,0:T(8,128)(2,1)}, bf16[3,768,768]{2,1,0:T(8,128)(2,1)}, bf16[3,768,768]{2,1,0:T(8,128)(2,1)S(1)}) fusion(f32[2,3,768,768]{3,2,1,0:T(8,128)} %param.18), kind=kLoop, calls=%fused_computation.2 | loop fusion | flops 10616832 | bytes 35389440 | tf_op jit(solution)/shard_map/convert_element_type | solution.py:887
  34.3 6.9 %places.1 = s32[24,1024]{1,0:T(8,128)} custom-call(s32[1]{0:T(128)S(6)} %mul.213.share_ref, s32[24,1024]{1,0:T(8,128)} %bitcast.281), custom_call_target="tpu_custom_call" | custom-call | tf_op jit(solution)/shard_map/places/pallas_call | solution.py:88
  95.6 9.8 %collective-permute-done.8 = bf16[4,48,768]{2,1,0:T(8,128)(2,1)S(1)} collective-permute-done((bf16[4,48,768]{2,1,0:T(8,128)(2,1)S(1)}, bf16[4,48,768]{2,1,0:T(8,128)(2,1)S(1)}, u32[]{:S(2)}, u32[]{:S(2)}) %collective-permute-start.8) | collective-permute-done | bytes 294944 | tf_op jit(solution)/shard_map/ppermute | solution.py:832
  113.2 4.5 collective-permute-start.14
  133.2 6.5 sort_rows.4.refs_0_
  141.4 7.1 %sort_rows.5.refs_1_ = bf16[6,1024,256]{2,1,0:T(8,128)(2,1)S(1)} custom-call(s32[8,1024]{1,0:T(8,128)} %collective-permute-done.12.place_ref, bf16[1024,768]{1,0:T(8,128)(2,1)} %collective-permute-done.x_ref, bf16[768,768]{1,0:T(8,128)(2,1)} %assemble.1.weight_ref, f32[1,768]{1,0:T(1,128)S(1)} %reshape.232.bias_ref), custom_call_target="tpu_custom_call" | custom-call | tf_op jit(solution)/shard_map/sort_rows/pallas_call | solution.py:183
  150.2 7.1 %sort_rows.6.refs_2_ = bf16[6,1024,256]{2,1,0:T(8,128)(2,1)S(1)} custom-call(s32[8,1024]{1,0:T(8,128)} %collective-permute-done.13.place_ref, bf16[1024,768]{1,0:T(8,128)(2,1)} %collective-permute-done.1.x_ref, bf16[768,768]{1,0:T(8,128)(2,1)} %assemble.1.weight_ref, f32[1,768]{1,0:T(1,128)S(1)} %reshape.232.bias_ref), custom_call_target="tpu_custom_call" | custom-call | tf_op jit(solution)/shard_map/sort_rows/pallas_call | solution.py:183
  161.4 6.9 %sort_rows.7.refs_3_ = bf16[6,1024,256]{2,1,0:T(8,128)(2,1)S(1)} custom-call(s32[8,1024]{1,0:T(8,128)S(1)} %copy-done.36, bf16[1024,768]{1,0:T(8,128)(2,1)S(1)} %constant_dynamic-update-slice_fusion.5.x_ref, bf16[768,768]{1,0:T(8,128)(2,1)} %assemble.1.weight_ref, f32[1,768]{1,0:T(1,128)S(1)} %reshape.232.bias_ref), custom_call_target="tpu_custom_call" | custom-call | tf_op jit(solution)/shard_map/sort_rows/pallas_call | solution.py:183
  170.9 16.5 %attend.1 = (bf16[6,1024,128]{2,1,0:T(8,128)(2,1)S(1)}, bf16[6,1024,128]{2,1,0:T(8,128)(2,1)S(1)}, bf16[6,1024,128]{2,1,0:T(8,128)(2,1)S(1)}, bf16[6,1024,128]{2,1,0:T(8,128)(2,1)}) custom-call(s32[1]{0:T(128)} %bitcast.87.long_ref, bf16[6,1024,256]{2,1,0:T(8,128)(2,1)} %copy-done, bf16[6,1024,256]{2,1,0:T(8,128)(2,1)} %copy-done.1, ...), custom_call_target="tpu_custom_call" | custom-call | tf_op jit(solution)/shard_map/attend/pallas_call | solution.py:307
  190.2 5.2 mix.4
  196.0 5.0 mix.5
  203.6 4.6 mix.6
  208.7 3.7 collective-permute-done.21.refs_9_
  214.3 8.9 %collective-permute-done.23.refs_11_ = bf16[1536,128]{1,0:T(8,128)(2,1)S(1)} collective-permute-done((bf16[1536,128]{1,0:T(8,128)(2,1)S(1)}, bf16[1536,128]{1,0:T(8,128)(2,1)S(1)}, u32[]{:S(2)}, u32[]{:S(2)}) %collective-permute-start.23) | collective-permute-done | bytes 393248 | tf_op jit(solution)/shard_map/ppermute | solution.py:832
  227.7 12.3 %collective-permute-done.24 = bf16[9,48,768]{2,1,0:T(8,128)(2,1)S(1)} collective-permute-done((bf16[9,48,768]{2,1,0:T(8,128)(2,1)S(1)}, bf16[9,48,768]{2,1,0:T(8,128)(2,1)S(1)}, u32[]{:S(2)}, u32[]{:S(2)}) %collective-permute-start.24) | collective-permute-done | bytes 663584 | tf_op jit(solution)/shard_map/ppermute | solution.py:832
  249.6 4.2 mix.7.refs_8_
  254.6 69.3 %layer.1 = (bf16[1024,768]{1,0:T(8,128)(2,1)}, f32[1024,768]{1,0:T(8,128)}, bf16[4,1536,128]{2,1,0:T(8,128)(2,1)}, f32[16,768]{1,0:T(8,128)}, bf16[3,16,3,48,384...) custom-call(s32[22]{0:T(128)} %stack.235.table_ref, bf16[2,9,48,768]{3,2,1,0:T(8,128)(2,1)} %copy-done.56, ...), custom_call_target="tpu_custom_call" | custom-call | tf_op jit(solution)/shard_map/layer/pallas_call | solution.py:672
  342.1 5.3 collective-permute-done.35.rows_ref
  359.8 3.8 sort_grads.4.refs_4_
  364.9 4.7 sort_grads.5.refs_5_
  370.7 5.0 sort_grads.6.refs_6_
  376.8 3.8 sort_grads.7.refs_7_
  381.8 19.1 %attend_back.1 = (bf16[6,1024,256]{2,1,0:T(8,128)(2,1)}, bf16[6,1024,256]{2,1,0:T(8,128)(2,1)}, bf16[6,1024,256]{2,1,0:T(8,128)(2,1)}, bf16[6,1024,256]{2,1,0:T(8,128)(2,1)}) custom-call(s32[1]{0:T(128)} %bitcast.87.long_ref, bf16[6,1024,256]{2,1,0:T(8,128)(2,1)} %copy-done, bf16[6,1024,256]{2,1,0:T(8,128)(2,1)} %copy-done.1, ...), custom_call_target="tpu_custom_call" | custom-call | tf_op jit(solution)/shard_map/attend_back/pallas_call | solution.py:351
  410.5 5.3 gather_grads.5
  415.9 4.9 fusion.29
  420.8 4.4 gather_grads.4
  425.1 5.1 convolution_add_fusion
  435.1 4.6 gather_grads.6
  442.2 6.0 gather_grads.7
  456.6 3.3 add_convert_fusion
  485.1 3.8 collective-permute-done.54
  490.7 6.1 collective-permute-done.52
  497.8 10.6 %collective-permute-done.47 = bf16[3,96,384]{2,1,0:T(8,128)(2,1)S(1)} collective-permute-done((bf16[3,96,384]{2,1,0:T(8,128)(2,1)S(1)}, bf16[3,96,384]{2,1,0:T(8,128)(2,1)S(1)}, u32[]{:S(2)}, u32[]{:S(2)}) %collective-permute-start.47) | collective-permute-done | bytes 221216 | tf_op jit(solution)/shard_map/ppermute | solution.py:832
  508.8 7.2 %collective-permute-done.49 = bf16[3,96,384]{2,1,0:T(8,128)(2,1)S(1)} collective-permute-done((bf16[3,96,384]{2,1,0:T(8,128)(2,1)S(1)}, bf16[3,96,384]{2,1,0:T(8,128)(2,1)S(1)}, u32[]{:S(2)}, u32[]{:S(2)}) %collective-permute-start.49) | collective-permute-done | bytes 221216 | tf_op jit(solution)/shard_map/ppermute | solution.py:832
  518.1 4.1 all-to-all-start
  524.2 6.0 all-to-all-done.got_ref
  531.2 4.1 rotate_in.1
  536.2 4.2 all-to-all-start.1
  543.8 25.9 %collective-permute-done.55 = f32[12,768]{1,0:T(8,128)S(1)} collective-permute-done((f32[12,768]{1,0:T(8,128)S(1)}, f32[12,768]{1,0:T(8,128)S(1)}, u32[]{:S(2)}, u32[]{:S(2)}) %collective-permute-start.55) | collective-permute-done | bytes 36896 | tf_op jit(solution)/shard_map/ppermute | solution.py:832
  572.7 8.9 %moments.1 = (f32[3,96,768]{2,1,0:T(8,128)}, f32[3,96,768]{2,1,0:T(8,128)}, bf16[8,3,96,96]{3,2,1,0:T(8,128)(2,1)S(1)}) custom-call(bf16[8,3,96,96]{3,2,1,0:T(8,128)(2,1)} %all-to-all-done.1.got_ref, bf16[3,768,768]{2,1,0:T(8,128)(2,1)} %get-tuple-element.219.high_ref, bf16[3,768,768]{2,1,0:T(8,128)(2,1)} %get-tuple-element.220.low_ref, ...), custom_call_target="tpu_custom_call" | custom-call | tf_op jit(solution)/shard_map/moments/pallas_call | solution.py:767
  582.4 4.2 all-to-all-start.2
  592.7 4.8 fusion.30
  597.5 33.9 %collective-permute-done.57 = f32[12,768]{1,0:T(8,128)S(1)} collective-permute-done((f32[12,768]{1,0:T(8,128)S(1)}, f32[12,768]{1,0:T(8,128)S(1)}, u32[]{:S(2)}, u32[]{:S(2)}) %collective-permute-start.57) | collective-permute-done | bytes 36896 | tf_op jit(solution)/shard_map/ppermute | solution.py:832
  632.0 4.2 rotate_out.1
  637.1 6.6 all-to-all-start.3
  643.8 4.9 fusion.31
  649.4 4.9 fusion.32
  654.3 3.9 all-to-all-done.3.got_ref
  (439 shorter events, 216.5 us)
Async XLA Ops:
  0.6 43.8 %collective-permute-start = (bf16[1024,768]{1,0:T(8,128)(2,1)}, bf16[1024,768]{1,0:T(8,128)(2,1)}, u32[]{:S(2)}, u32[]{:S(2)}) collective-permute-start(bf16[1024,768]{1,0:T(8,128)(2,1)} %bitcast.258), channel_id=1, source_target_pairs={{0,4},{4,0},{8,12},{12,8},{16,20},{20,16},{24,28},{28,24},{1,5},{5... | collective-permute-start | bytes 4718600 | tf_op jit(solution)/shard_map/ppermute | solution.py:832
  3.7 40.8 %collective-permute-start.1 = (bf16[1024,768]{1,0:T(8,128)(2,1)}, bf16[1024,768]{1,0:T(8,128)(2,1)}, u32[]{:S(2)}, u32[]{:S(2)}) collective-permute-start(bf16[1024,768]{1,0:T(8,128)(2,1)} %bitcast.259), channel_id=1, source_target_pairs={{0,8},{4,12},{8,0},{12,4},{16,24},{20,28},{24,16},{28,20},{1,9},{5... | collective-permute-start | bytes 4718600 | tf_op jit(solution)/shard_map/ppermute | solution.py:832
  7.2 37.2 %collective-permute-start.2 = (bf16[3,96,768]{2,1,0:T(8,128)(2,1)}, bf16[3,96,768]{2,1,0:T(8,128)(2,1)}, u32[]{:S(2)}, u32[]{:S(2)}) collective-permute-start(bf16[3,96,768]{2,1,0:T(8,128)(2,1)} %convert_bitcast_fusion), channel_id=1, source_target_pairs={{0,1},{1,0},{2,3},{3,2},{4,5},{5,4},{6,7},{7,6},{8,9},{9,8},{10,11... | collective-permute-start | bytes 1327112 | tf_op jit(solution)/shard_map/ppermute | solution.py:832
  7.2 16.3 %collective-permute-start.3 = (bf16[3,96,768]{2,1,0:T(8,128)(2,1)}, bf16[3,96,768]{2,1,0:T(8,128)(2,1)}, u32[]{:S(2)}, u32[]{:S(2)}) collective-permute-start(bf16[3,96,768]{2,1,0:T(8,128)(2,1)} %convert_bitcast_fusion), channel_id=1, source_target_pairs={{0,2},{1,3},{2,0},{3,1},{4,6},{5,7},{6,4},{7,5},{8,10},{9,11},{10,... | collective-permute-start | bytes 1327112 | tf_op jit(solution)/shard_map/ppermute | solution.py:832
  23.5 20.9 %collective-permute-start.4 = (bf16[3,96,768]{2,1,0:T(8,128)(2,1)}, bf16[3,96,768]{2,1,0:T(8,128)(2,1)}, u32[]{:S(2)}, u32[]{:S(2)}) collective-permute-start(bf16[3,96,768]{2,1,0:T(8,128)(2,1)} %collective-permute-done.3), channel_id=1, source_target_pairs={{0,1},{1,0},{2,3},{3,2},{4,5},{5,4},{6,7},{7,6},{8,9},{9,8},{10,11... | collective-permute-start | bytes 1327112 | tf_op jit(solution)/shard_map/ppermute | solution.py:832
  51.5 30.0 %collective-permute-start.5 = (bf16[48,768]{1,0:T(8,128)(2,1)}, bf16[48,768]{1,0:T(8,128)(2,1)}, u32[]{:S(2)}, u32[]{:S(2)}) collective-permute-start(bf16[48,768]{1,0:T(8,128)(2,1)} %get-tuple-element.264), channel_id=1, source_target_pairs={{0,4},{4,0},{8,12},{12,8},{16,20},{20,16},{24,28},{28,24},{1,5},{5... | collective-permute-start | bytes 221192 | tf_op jit(solution)/shard_map/ppermute | solution.py:832
  52.0 31.1 %collective-permute-start.6 = (bf16[48,768]{1,0:T(8,128)(2,1)}, bf16[48,768]{1,0:T(8,128)(2,1)}, u32[]{:S(2)}, u32[]{:S(2)}) collective-permute-start(bf16[48,768]{1,0:T(8,128)(2,1)} %get-tuple-element.263), channel_id=1, source_target_pairs={{0,8},{4,12},{8,0},{12,4},{16,24},{20,28},{24,16},{28,20},{1,9},{5... | collective-permute-start | bytes 221192 | tf_op jit(solution)/shard_map/ppermute | solution.py:832
  52.5 32.2 %collective-permute-start.7 = (bf16[48,768]{1,0:T(8,128)(2,1)}, bf16[48,768]{1,0:T(8,128)(2,1)}, u32[]{:S(2)}, u32[]{:S(2)}) collective-permute-start(bf16[48,768]{1,0:T(8,128)(2,1)} %get-tuple-element.262), channel_id=1, source_target_pairs={{0,12},{4,8},{8,4},{12,0},{16,28},{20,24},{24,20},{28,16},{1,13},{... | collective-permute-start | bytes 221192 | tf_op jit(solution)/shard_map/ppermute | solution.py:832
  57.4 55.8 %collective-permute-start.12 = (s32[8,1024]{1,0:T(8,128)}, s32[8,1024]{1,0:T(8,128)}, u32[]{:S(2)}, u32[]{:S(2)}) collective-permute-start(s32[8,1024]{1,0:T(8,128)} %bitcast.256), channel_id=1, source_target_pairs={{0,4},{4,0},{8,12},{12,8},{16,20},{20,16},{24,28},{28,24},{1,5},{5... | collective-permute-start | bytes 98312 | tf_op jit(solution)/shard_map/ppermute | solution.py:832
  58.5 60.6 %collective-permute-start.13 = (s32[8,1024]{1,0:T(8,128)}, s32[8,1024]{1,0:T(8,128)}, u32[]{:S(2)}, u32[]{:S(2)}) collective-permute-start(s32[8,1024]{1,0:T(8,128)} %bitcast.255), channel_id=1, source_target_pairs={{0,8},{4,12},{8,0},{12,4},{16,24},{20,28},{24,16},{28,20},{1,9},{5... | collective-permute-start | bytes 98312 | tf_op jit(solution)/shard_map/ppermute | solution.py:832
  81.5 38.7 %collective-permute-start.9 = (bf16[512,768]{1,0:T(8,128)(2,1)S(1)}, bf16[512,768]{1,0:T(8,128)(2,1)}, u32[]{:S(2)}, u32[]{:S(2)}) collective-permute-start(bf16[512,768]{1,0:T(8,128)(2,1)S(1)} %slice.314), channel_id=1, source_target_pairs={{0,8},{4,12},{8,0},{12,4},{16,24},{20,28},{24,16},{28,20},{1,9},{5... | collective-permute-start | bytes 2359304 | tf_op jit(solution)/shard_map/ppermute | solution.py:832
  83.2 37.1 %collective-permute-start.10 = (bf16[512,768]{1,0:T(8,128)(2,1)S(1)}, bf16[512,768]{1,0:T(8,128)(2,1)}, u32[]{:S(2)}, u32[]{:S(2)}) collective-permute-start(bf16[512,768]{1,0:T(8,128)(2,1)S(1)} %slice.315), channel_id=1, source_target_pairs={{0,4},{4,0},{8,12},{12,8},{16,20},{20,16},{24,28},{28,24},{1,5},{5... | collective-permute-start | bytes 2359304 | tf_op jit(solution)/shard_map/ppermute | solution.py:832
  87.5 17.9 %collective-permute-start.8 = (bf16[4,48,768]{2,1,0:T(8,128)(2,1)S(1)}, bf16[4,48,768]{2,1,0:T(8,128)(2,1)S(1)}, u32[]{:S(2)}, u32[]{:S(2)}) collective-permute-start(bf16[4,48,768]{2,1,0:T(8,128)(2,1)S(1)} %pad_maximum_fusion.7), channel_id=1, source_target_pairs={{0,16},{4,20},{8,24},{12,28},{16,0},{20,4},{24,8},{28,12},{1,17},{... | collective-permute-start | bytes 884744 | tf_op jit(solution)/shard_map/ppermute | solution.py:832
  105.4 14.8 %collective-permute-start.11 = (bf16[8,48,768]{2,1,0:T(8,128)(2,1)S(1)}, bf16[8,48,768]{2,1,0:T(8,128)(2,1)S(1)}, u32[]{:S(2)}, u32[]{:S(2)}) collective-permute-start(bf16[8,48,768]{2,1,0:T(8,128)(2,1)S(1)} %constant_dynamic-update-slice_fusion.refs_0_), channel_id=1, source_target_pairs={{0,1},{1,0},{2,3},{3,2},{4,5},{5,4},{6,7},{7,6},{8,9},{9,8},{10,11... | collective-permute-start | bytes 1769480 | tf_op jit(solution)/shard_map/ppermute | solution.py:832
  121.1 48.9 %collective-permute-start.15 = (bf16[9,48,768]{2,1,0:T(8,128)(2,1)}, bf16[9,48,768]{2,1,0:T(8,128)(2,1)}, u32[]{:S(2)}, u32[]{:S(2)}) collective-permute-start(bf16[9,48,768]{2,1,0:T(8,128)(2,1)} %dynamic-slice_dynamic-update-slice_fusion), channel_id=1, source_target_pairs={{0,8},{4,12},{8,16},{12,20},{16,24},{20,28},{24,0},{28,4},{1,9},{5... | collective-permute-start | bytes 1990664 | tf_op jit(solution)/shard_map/ppermute | solution.py:984
  123.4 46.5 %collective-permute-start.16 = (bf16[9,48,768]{2,1,0:T(8,128)(2,1)}, bf16[9,48,768]{2,1,0:T(8,128)(2,1)}, u32[]{:S(2)}, u32[]{:S(2)}) collective-permute-start(bf16[9,48,768]{2,1,0:T(8,128)(2,1)} %dynamic-slice_dynamic-update-slice_fusion), channel_id=1, source_target_pairs={{0,4},{4,0},{8,12},{12,8},{16,20},{20,16},{24,28},{28,24},{1,5},{5... | collective-permute-start | bytes 1990664 | tf_op jit(solution)/shard_map/ppermute | solution.py:832
  169.9 18.6 %collective-permute-start.17 = (bf16[9,48,768]{2,1,0:T(8,128)(2,1)}, bf16[9,48,768]{2,1,0:T(8,128)(2,1)S(1)}, u32[]{:S(2)}, u32[]{:S(2)}) collective-permute-start(bf16[9,48,768]{2,1,0:T(8,128)(2,1)} %collective-permute-done.15), channel_id=1, source_target_pairs={{0,8},{4,12},{8,16},{12,20},{16,24},{20,28},{24,0},{28,4},{1,9},{5... | collective-permute-start | bytes 1990664 | tf_op jit(solution)/shard_map/ppermute | solution.py:987
  170.4 18.2 %collective-permute-start.18 = (bf16[9,48,768]{2,1,0:T(8,128)(2,1)}, bf16[9,48,768]{2,1,0:T(8,128)(2,1)S(1)}, u32[]{:S(2)}, u32[]{:S(2)}) collective-permute-start(bf16[9,48,768]{2,1,0:T(8,128)(2,1)} %collective-permute-done.15), channel_id=1, source_target_pairs={{0,4},{4,0},{8,12},{12,8},{16,20},{20,16},{24,28},{28,24},{1,5},{5... | collective-permute-start | bytes 1990664 | tf_op jit(solution)/shard_map/ppermute | solution.py:832
  188.6 34.6 %collective-permute-start.19 = (bf16[9,48,768]{2,1,0:T(8,128)(2,1)S(1)}, bf16[9,48,768]{2,1,0:T(8,128)(2,1)S(1)}, u32[]{:S(2)}, u32[]{:S(2)}) collective-permute-start(bf16[9,48,768]{2,1,0:T(8,128)(2,1)S(1)} %collective-permute-done.17), channel_id=1, source_target_pairs={{0,8},{4,12},{8,16},{12,20},{16,24},{20,28},{24,0},{28,4},{1,9},{5... | collective-permute-start | bytes 1990664 | tf_op jit(solution)/shard_map/ppermute | solution.py:996
  188.7 34.5 %collective-permute-start.20 = (bf16[9,48,768]{2,1,0:T(8,128)(2,1)S(1)}, bf16[9,48,768]{2,1,0:T(8,128)(2,1)S(1)}, u32[]{:S(2)}, u32[]{:S(2)}) collective-permute-start(bf16[9,48,768]{2,1,0:T(8,128)(2,1)S(1)} %collective-permute-done.17), channel_id=1, source_target_pairs={{0,4},{4,0},{8,12},{12,8},{16,20},{20,16},{24,28},{28,24},{1,5},{5... | collective-permute-start | bytes 1990664 | tf_op jit(solution)/shard_map/ppermute | solution.py:832
  195.4 17.0 %collective-permute-start.21 = (bf16[1536,128]{1,0:T(8,128)(2,1)S(1)}, bf16[1536,128]{1,0:T(8,128)(2,1)S(1)}, u32[]{:S(2)}, u32[]{:S(2)}) collective-permute-start(bf16[1536,128]{1,0:T(8,128)(2,1)S(1)} %mix.4), channel_id=1, source_target_pairs={{0,4},{4,0},{8,12},{12,8},{16,20},{20,16},{24,28},{28,24},{1,5},{5... | collective-permute-start | bytes 1179656 | tf_op jit(solution)/shard_map/ppermute | solution.py:832
  208.2 15.0 %collective-permute-start.23 = (bf16[1536,128]{1,0:T(8,128)(2,1)S(1)}, bf16[1536,128]{1,0:T(8,128)(2,1)S(1)}, u32[]{:S(2)}, u32[]{:S(2)}) collective-permute-start(bf16[1536,128]{1,0:T(8,128)(2,1)S(1)} %mix.6), channel_id=1, source_target_pairs={{0,12},{4,8},{8,4},{12,0},{16,28},{20,24},{24,20},{28,16},{1,13},{... | collective-permute-start | bytes 1179656 | tf_op jit(solution)/shard_map/ppermute | solution.py:832
  223.2 16.8 %collective-permute-start.24 = (bf16[9,48,768]{2,1,0:T(8,128)(2,1)S(1)}, bf16[9,48,768]{2,1,0:T(8,128)(2,1)S(1)}, u32[]{:S(2)}, u32[]{:S(2)}) collective-permute-start(bf16[9,48,768]{2,1,0:T(8,128)(2,1)S(1)} %collective-permute-done.19), channel_id=1, source_target_pairs={{0,4},{4,0},{8,12},{12,8},{16,20},{20,16},{24,28},{28,24},{1,5},{5... | collective-permute-start | bytes 1990664 | tf_op jit(solution)/shard_map/ppermute | solution.py:832
  225.2 15.1 %collective-permute-start.25 = (bf16[2,9,48,768]{3,2,1,0:T(8,128)(2,1)S(1)}, bf16[2,9,48,768]{3,2,1,0:T(8,128)(2,1)S(1)}, u32[]{:S(2)}, u32[]{:S(2)}) collective-permute-start(bf16[2,9,48,768]{3,2,1,0:T(8,128)(2,1)S(1)} %pad_maximum_fusion.1.refs_0_), channel_id=1, source_target_pairs={{0,1},{1,0},{2,3},{3,2},{4,5},{5,4},{6,7},{7,6},{8,9},{9,8},{10,11... | collective-permute-start | bytes 3981320 | tf_op jit(solution)/shard_map/ppermute | solution.py:832
  243.3 80.6 %collective-permute-start.29 = (bf16[768,768]{1,0:T(8,128)(2,1)}, bf16[768,768]{1,0:T(8,128)(2,1)}, u32[]{:S(2)}, u32[]{:S(2)}) collective-permute-start(bf16[768,768]{1,0:T(8,128)(2,1)} %assemble.1.weight_ref), channel_id=1, source_target_pairs={{0,4},{4,0},{8,12},{12,8},{16,20},{20,16},{24,28},{28,24},{1,5},{5... | collective-permute-start | bytes 3538952 | tf_op jit(solution)/shard_map/ppermute | solution.py:832
  243.6 80.4 %collective-permute-start.30 = (bf16[768,768]{1,0:T(8,128)(2,1)}, bf16[768,768]{1,0:T(8,128)(2,1)}, u32[]{:S(2)}, u32[]{:S(2)}) collective-permute-start(bf16[768,768]{1,0:T(8,128)(2,1)} %assemble.1.weight_ref), channel_id=1, source_target_pairs={{0,8},{4,12},{8,0},{12,4},{16,24},{20,28},{24,16},{28,20},{1,9},{5... | collective-permute-start | bytes 3538952 | tf_op jit(solution)/shard_map/ppermute | solution.py:832
  244.4 79.6 %collective-permute-start.31 = (bf16[768,768]{1,0:T(8,128)(2,1)}, bf16[768,768]{1,0:T(8,128)(2,1)}, u32[]{:S(2)}, u32[]{:S(2)}) collective-permute-start(bf16[768,768]{1,0:T(8,128)(2,1)} %assemble.1.weight_ref), channel_id=1, source_target_pairs={{0,12},{4,8},{8,4},{12,0},{16,28},{20,24},{24,20},{28,16},{1,13},{... | collective-permute-start | bytes 3538952 | tf_op jit(solution)/shard_map/ppermute | solution.py:832
  326.3 14.3 %collective-permute-start.33 = (bf16[1536,128]{1,0:T(8,128)(2,1)S(1)}, bf16[1536,128]{1,0:T(8,128)(2,1)S(1)}, u32[]{:S(2)}, u32[]{:S(2)}) collective-permute-start(bf16[1536,128]{1,0:T(8,128)(2,1)S(1)} %get-tuple-element.249), channel_id=1, source_target_pairs={{0,4},{4,0},{8,12},{12,8},{16,20},{20,16},{24,28},{28,24},{1,5},{5... | collective-permute-start | bytes 1179656 | tf_op jit(solution)/shard_map/ppermute | solution.py:832
  326.5 14.8 %collective-permute-start.34 = (bf16[1536,128]{1,0:T(8,128)(2,1)S(1)}, bf16[1536,128]{1,0:T(8,128)(2,1)S(1)}, u32[]{:S(2)}, u32[]{:S(2)}) collective-permute-start(bf16[1536,128]{1,0:T(8,128)(2,1)S(1)} %get-tuple-element.248), channel_id=1, source_target_pairs={{0,8},{4,12},{8,0},{12,4},{16,24},{20,28},{24,16},{28,20},{1,9},{5... | collective-permute-start | bytes 1179656 | tf_op jit(solution)/shard_map/ppermute | solution.py:832
  327.3 20.1 %collective-permute-start.35 = (bf16[1536,128]{1,0:T(8,128)(2,1)S(1)}, bf16[1536,128]{1,0:T(8,128)(2,1)S(1)}, u32[]{:S(2)}, u32[]{:S(2)}) collective-permute-start(bf16[1536,128]{1,0:T(8,128)(2,1)S(1)} %get-tuple-element.247), channel_id=1, source_target_pairs={{0,12},{4,8},{8,4},{12,0},{16,28},{20,24},{24,20},{28,16},{1,13},{... | collective-permute-start | bytes 1179656 | tf_op jit(solution)/shard_map/ppermute | solution.py:832
  348.1 52.8 %collective-permute-start.36 = (bf16[8,3,48,384]{3,2,1,0:T(8,128)(2,1)}, bf16[8,3,48,384]{3,2,1,0:T(8,128)(2,1)}, u32[]{:S(2)}, u32[]{:S(2)}) collective-permute-start(bf16[8,3,48,384]{3,2,1,0:T(8,128)(2,1)} %fusion.5), channel_id=1, source_target_pairs={{0,2},{1,3},{2,0},{3,1},{4,6},{5,7},{6,4},{7,5},{8,10},{9,11},{10,... | collective-permute-start | bytes 2654216 | tf_op jit(solution)/shard_map/ppermute | solution.py:832
  348.6 53.9 %collective-permute-start.37 = (bf16[8,3,48,384]{3,2,1,0:T(8,128)(2,1)}, bf16[8,3,48,384]{3,2,1,0:T(8,128)(2,1)}, u32[]{:S(2)}, u32[]{:S(2)}) collective-permute-start(bf16[8,3,48,384]{3,2,1,0:T(8,128)(2,1)} %fusion.6), channel_id=1, source_target_pairs={{0,4},{4,0},{8,12},{12,8},{16,20},{20,16},{24,28},{28,24},{1,5},{5... | collective-permute-start | bytes 2654216 | tf_op jit(solution)/shard_map/ppermute | solution.py:832
  348.9 56.6 %collective-permute-start.38 = (bf16[8,3,48,384]{3,2,1,0:T(8,128)(2,1)}, bf16[8,3,48,384]{3,2,1,0:T(8,128)(2,1)}, u32[]{:S(2)}, u32[]{:S(2)}) collective-permute-start(bf16[8,3,48,384]{3,2,1,0:T(8,128)(2,1)} %fusion.7), channel_id=1, source_target_pairs={{0,8},{4,12},{8,0},{12,4},{16,24},{20,28},{24,16},{28,20},{1,9},{5... | collective-permute-start | bytes 2654216 | tf_op jit(solution)/shard_map/ppermute | solution.py:832
  407.5 23.3 %collective-permute-start.39 = (bf16[4,3,48,384]{3,2,1,0:T(8,128)(2,1)S(1)}, bf16[4,3,48,384]{3,2,1,0:T(8,128)(2,1)S(1)}, u32[]{:S(2)}, u32[]{:S(2)}) collective-permute-start(bf16[4,3,48,384]{3,2,1,0:T(8,128)(2,1)S(1)} %slice.520), channel_id=1, source_target_pairs={{0,4},{4,0},{8,12},{12,8},{16,20},{20,16},{24,28},{28,24},{1,5},{5... | collective-permute-start | bytes 1327112 | tf_op jit(solution)/shard_map/ppermute | solution.py:832
  408.8 23.8 %collective-permute-start.40 = (bf16[4,3,48,384]{3,2,1,0:T(8,128)(2,1)S(1)}, bf16[4,3,48,384]{3,2,1,0:T(8,128)(2,1)S(1)}, u32[]{:S(2)}, u32[]{:S(2)}) collective-permute-start(bf16[4,3,48,384]{3,2,1,0:T(8,128)(2,1)S(1)} %slice.519), channel_id=1, source_target_pairs={{0,8},{4,12},{8,0},{12,4},{16,24},{20,28},{24,16},{28,20},{1,9},{5... | collective-permute-start | bytes 1327112 | tf_op jit(solution)/shard_map/ppermute | solution.py:832
  410.5 22.8 %collective-permute-start.41 = (bf16[4,3,48,384]{3,2,1,0:T(8,128)(2,1)S(1)}, bf16[4,3,48,384]{3,2,1,0:T(8,128)(2,1)S(1)}, u32[]{:S(2)}, u32[]{:S(2)}) collective-permute-start(bf16[4,3,48,384]{3,2,1,0:T(8,128)(2,1)S(1)} %slice.518), channel_id=1, source_target_pairs={{0,16},{4,20},{8,24},{12,28},{16,0},{20,4},{24,8},{28,12},{1,17},{... | collective-permute-start | bytes 1327112 | tf_op jit(solution)/shard_map/ppermute | solution.py:832
  450.4 119.9 %collective-permute-start.56 = (bf16[1024,768]{1,0:T(8,128)(2,1)}, bf16[1024,768]{1,0:T(8,128)(2,1)}, u32[]{:S(2)}, u32[]{:S(2)}) collective-permute-start(bf16[1024,768]{1,0:T(8,128)(2,1)} %gather_grads.7), channel_id=1, source_target_pairs={{0,4},{4,0},{8,12},{12,8},{16,20},{20,16},{24,28},{28,24},{1,5},{5... | collective-permute-start | bytes 4718600 | tf_op jit(solution)/shard_map/ppermute | solution.py:832
  450.8 29.5 %collective-permute-start.42 = (bf16[2,3,48,384]{3,2,1,0:T(8,128)(2,1)}, bf16[2,3,48,384]{3,2,1,0:T(8,128)(2,1)}, u32[]{:S(2)}, u32[]{:S(2)}) collective-permute-start(bf16[2,3,48,384]{3,2,1,0:T(8,128)(2,1)} %slice.523), channel_id=1, source_target_pairs={{0,8},{4,12},{8,0},{12,4},{16,24},{20,28},{24,16},{28,20},{1,9},{5... | collective-permute-start | bytes 663560 | tf_op jit(solution)/shard_map/ppermute | solution.py:832
  451.7 29.7 %collective-permute-start.43 = (bf16[2,3,48,384]{3,2,1,0:T(8,128)(2,1)}, bf16[2,3,48,384]{3,2,1,0:T(8,128)(2,1)}, u32[]{:S(2)}, u32[]{:S(2)}) collective-permute-start(bf16[2,3,48,384]{3,2,1,0:T(8,128)(2,1)} %slice.522), channel_id=1, source_target_pairs={{0,16},{4,20},{8,24},{12,28},{16,0},{20,4},{24,8},{28,12},{1,17},{... | collective-permute-start | bytes 663560 | tf_op jit(solution)/shard_map/ppermute | solution.py:832
  454.4 28.0 %collective-permute-start.44 = (bf16[2,3,48,384]{3,2,1,0:T(8,128)(2,1)}, bf16[2,3,48,384]{3,2,1,0:T(8,128)(2,1)}, u32[]{:S(2)}, u32[]{:S(2)}) collective-permute-start(bf16[2,3,48,384]{3,2,1,0:T(8,128)(2,1)} %slice.521), channel_id=1, source_target_pairs={{0,2},{1,3},{2,0},{3,1},{4,6},{5,7},{6,4},{7,5},{8,10},{9,11},{10,... | collective-permute-start | bytes 663560 | tf_op jit(solution)/shard_map/ppermute | solution.py:832
  479.0 18.1 %collective-permute-start.46 = (f32[12,768]{1,0:T(8,128)}, f32[12,768]{1,0:T(8,128)S(1)}, u32[]{:S(2)}, u32[]{:S(2)}) collective-permute-start(f32[12,768]{1,0:T(8,128)} %pad_add_fusion), channel_id=1, source_target_pairs={{0,1},{1,0},{2,3},{3,2},{4,5},{5,4},{6,7},{7,6},{8,9},{9,8},{10,11... | collective-permute-start | bytes 110600 | tf_op jit(solution)/shard_map/ppermute | solution.py:832
  522.2 109.8 %collective-permute-start.58 = (bf16[1024,768]{1,0:T(8,128)(2,1)}, bf16[1024,768]{1,0:T(8,128)(2,1)}, u32[]{:S(2)}, u32[]{:S(2)}) collective-permute-start(bf16[1024,768]{1,0:T(8,128)(2,1)} %copy-done.7), channel_id=1, source_target_pairs={{0,8},{4,12},{8,0},{12,4},{16,24},{20,28},{24,16},{28,20},{1,9},{5... | collective-permute-start | bytes 4718600 | tf_op jit(solution)/shard_map/ppermute | solution.py:832
  536.2 34.1 %all-to-all-start.1 = ((bf16[8,3,96,96]{3,2,1,0:T(8,128)(2,1)}), bf16[8,3,96,96]{3,2,1,0:T(8,128)(2,1)}, u32[]{:S(2)}, u32[]{:S(2)}) async-start(bf16[8,3,96,96]{3,2,1,0:T(8,128)(2,1)} %copy-done.20), calls=%async_computation.1 | async-start | bytes 1179648 | tf_op jit(solution)/shard_map/all_to_all | solution.py:1092
  541.9 27.8 %collective-permute-start.55 = (f32[12,768]{1,0:T(8,128)S(1)}, f32[12,768]{1,0:T(8,128)S(1)}, u32[]{:S(2)}, u32[]{:S(2)}) collective-permute-start(f32[12,768]{1,0:T(8,128)S(1)} %add.600), channel_id=1, source_target_pairs={{0,8},{4,12},{8,0},{12,4},{16,24},{20,28},{24,16},{28,20},{1,9},{5... | collective-permute-start | bytes 110600 | tf_op jit(solution)/shard_map/ppermute | solution.py:832
  582.4 49.6 %all-to-all-start.2 = ((bf16[8,3,96,96]{3,2,1,0:T(8,128)(2,1)}), bf16[8,3,96,96]{3,2,1,0:T(8,128)(2,1)}, u32[]{:S(2)}, u32[]{:S(2)}) async-start(bf16[8,3,96,96]{3,2,1,0:T(8,128)(2,1)} %copy-done.34), calls=%async_computation.2 | async-start | bytes 1179648 | tf_op jit(solution)/shard_map/all_to_all | solution.py:1092
  586.6 72.8 %collective-permute-start.59 = (bf16[1024,768]{1,0:T(8,128)(2,1)}, bf16[1024,768]{1,0:T(8,128)(2,1)}, u32[]{:S(2)}, u32[]{:S(2)}) collective-permute-start(bf16[1024,768]{1,0:T(8,128)(2,1)} %copy-done.6), channel_id=1, source_target_pairs={{0,12},{4,8},{8,4},{12,0},{16,28},{20,24},{24,20},{28,16},{1,13},{... | collective-permute-start | bytes 4718600 | tf_op jit(solution)/shard_map/ppermute | solution.py:832
  590.2 41.2 %collective-permute-start.57 = (f32[12,768]{1,0:T(8,128)S(1)}, f32[12,768]{1,0:T(8,128)S(1)}, u32[]{:S(2)}, u32[]{:S(2)}) collective-permute-start(f32[12,768]{1,0:T(8,128)S(1)} %add.602), channel_id=1, source_target_pairs={{0,16},{4,20},{8,24},{12,28},{16,0},{20,4},{24,8},{28,12},{1,17},{... | collective-permute-start | bytes 110600 | tf_op jit(solution)/shard_map/ppermute | solution.py:832
  637.1 21.1 %all-to-all-start.3 = ((bf16[8,3,96,96]{3,2,1,0:T(8,128)(2,1)}), bf16[8,3,96,96]{3,2,1,0:T(8,128)(2,1)S(1)}, u32[]{:S(2)}, u32[]{:S(2)}) async-start(bf16[8,3,96,96]{3,2,1,0:T(8,128)(2,1)} %copy-done.21), calls=%async_computation.3 | async-start | bytes 1179648 | tf_op jit(solution)/shard_map/all_to_all | solution.py:1092
  (114 other events, 617.7 us)

commit v5 on v4

--- a/solution.py
+++ b/solution.py
@@ -69,38 +69,63 @@
     return pltpu.roll(value, HEAD, 1)
 
 
-def places_body(share_ref, clusters_ref, out_ref):
+def places_body(scalars_ref, clusters_ref, *refs):
+    outs, all_ref = refs[:UNIT], refs[UNIT]
     pairs, count = clusters_ref.shape
-    share = share_ref[0]
+    share, member = scalars_ref[0], scalars_ref[1]
     kinds = UNIT * count // CLUSTER
     kind = lax.broadcasted_iota(jnp.int32, (kinds, count), 0)
     earlier = lax.broadcasted_iota(jnp.int32, (count, count), 0) < lax.broadcasted_iota(jnp.int32, (count, count), 1)
     earlier = earlier.astype(F32).astype(BF16)
+    all_ref[...] = jnp.zeros_like(all_ref)
     for pair in range(pairs):
+        turn, head = pair // H, pair % H
         cluster = clusters_ref[pair : pair + 1, :]
         same = (kind == cluster).astype(F32)
         before = jnp.dot(same.astype(BF16), earlier, preferred_element_type=F32)
         rank = jnp.sum(same * before, axis=0, keepdims=True).astype(jnp.int32)
-        out_ref[pair : pair + 1, :] = cluster * share + rank
-
-
-def places(share, clusters):
+        own = head % HEADS_OWN * ROUNDS + turn
+        all_ref[head // HEADS_OWN, own : own + 1, :] = cluster * share + rank
+    for k in range(UNIT):
+        outs[k][...] = all_ref[member ^ k]
+
+
+def places(scalars, clusters):
+    count = clusters.shape[1]
+    inside = pl.BlockSpec(memory_space=pltpu.VMEM)
     return pl.pallas_call(
         places_body,
-        in_specs=[pl.BlockSpec(memory_space=pltpu.SMEM), pl.BlockSpec(memory_space=pltpu.VMEM)],
-        out_shape=jax.ShapeDtypeStruct(clusters.shape, jnp.int32),
+        in_specs=[pl.BlockSpec(memory_space=pltpu.SMEM), inside],
+        out_specs=[inside] * UNIT,
+        out_shape=[jax.ShapeDtypeStruct((8, count), jnp.int32)] * UNIT,
+        scratch_shapes=[pltpu.VMEM((UNIT, 8, count), jnp.int32)],
         cost_estimate=SMALL,
         name="places",
-    )(share, clusters)
-
-
-def arrange_body(rows_ref, out_ref):
-    count = rows_ref.shape[1]
+    )(scalars, clusters)
+
+
+def arrange_body(slots, scalars_ref, *refs):
+    sources, outs, rest_ref, tiles_ref = refs[:4], refs[4 : 4 + UNIT], refs[4 + UNIT], refs[5 + UNIT]
+    n_rest, count = rest_ref.shape[:2]
+    n_blocks = n_rest + 3
+    group, core, member = (scalars_ref[n_blocks + i] for i in range(3))
+    first = pl.multiple_of(core * count, count)
+
+    def rows_of(block):
+        slot = scalars_ref[block]
+        owner = lax.div(slot, slots)
+        near, inner = owner ^ group, lax.rem(slot, slots)
+        found = [source[inner, pl.ds(first, count), :].astype(F32) for source in sources]
+        low = jnp.where(near % 2 == 0, found[0], found[1])
+        high = jnp.where(near % 2 == 0, found[2], found[3])
+        return jnp.where(near < 2, low, high)
+
     low = lax.broadcasted_iota(jnp.int32, (count, TILE), 1) < HEAD
+    parts = [rows_of(i) for i in range(3)]
 
     def half(part, head, high):
         at = head // 2 * TILE
-        tile = rows_ref[part, :, at : at + TILE].astype(F32)
+        tile = parts[part][:, at : at + TILE]
         return tile if head % 2 == high else turn_half(tile)
 
     for head in range(H):
@@ -111,17 +136,30 @@
         keys = half(1, head, 1 - odd)
         one = jnp.where(low, query, value) if odd else jnp.where(low, value, query)
         two = jnp.where(low, keys, 0.0) if odd else jnp.where(low, 0.0, keys)
-        out_ref[head // HEADS_OWN, :, own * WIDE : own * WIDE + TILE] = one.astype(BF16)
-        out_ref[head // HEADS_OWN, :, own * WIDE + TILE : (own + 1) * WIDE] = two.astype(BF16)
-
-
-def arrange(rows):
+        tiles_ref[head // HEADS_OWN, :, own * WIDE : own * WIDE + TILE] = one.astype(BF16)
+        tiles_ref[head // HEADS_OWN, :, own * WIDE + TILE : (own + 1) * WIDE] = two.astype(BF16)
+    for k in range(UNIT):
+        outs[k][...] = tiles_ref[member ^ k]
+    for b in range(n_rest):
+        rest_ref[b] = rows_of(3 + b).astype(BF16)
+
+
+def arrange(scalars, sources, n_blocks):
+    slots, rows = sources[0].shape[:2]
+    count = rows // 2
+    width = HEADS_OWN * WIDE
+    inside = pl.BlockSpec(memory_space=pltpu.VMEM)
     return pl.pallas_call(
-        arrange_body,
-        out_shape=jax.ShapeDtypeStruct((UNIT, rows.shape[1], HEADS_OWN * WIDE), BF16),
+        functools.partial(arrange_body, slots),
+        in_specs=[pl.BlockSpec(memory_space=pltpu.SMEM)] + [inside] * 4,
+        out_specs=[inside] * (UNIT + 1),
+        out_shape=[jax.ShapeDtypeStruct((count, width), BF16)] * UNIT
+        + [jax.ShapeDtypeStruct((n_blocks - 3, count, D), BF16)],
+        scratch_shapes=[pltpu.VMEM((UNIT, count, width), BF16)],
+        compiler_params=pltpu.CompilerParams(vmem_limit_bytes=32 << 20),
         cost_estimate=SMALL,
         name="arrange",
-    )(rows)
+    )(scalars, *sources)
 
 
 def assemble_body(table_ref, *refs):
@@ -493,9 +531,10 @@
 ):
     shards, refs = refs[:n_shards], refs[n_shards:]
     parts, refs = refs[:UNIT], refs[UNIT:]
-    x_ref, cot_ref, vec_ref, result_ref, first_ref, back_ref, sums_ref, kept_ref, sent_ref = refs[:9]
-    w_ref, packed_ref, mixed_ref, hidden_ref, act_ref, down_ref, up_ref, attn_ref = refs[9:17]
-    slope_ref, stage_ref, weight_sem, part_sem, stage_sem = refs[17:]
+    x_ref, cot_ref, vec_ref, result_ref, first_ref, sums_ref, kept_ref, sent_ref = refs[:8]
+    backs, refs = refs[8 : 8 + UNIT], refs[8 + UNIT :]
+    w_ref, packed_ref, mixed_ref, hidden_ref, act_ref, down_ref, up_ref, attn_ref, back_ref = refs[:9]
+    slope_ref, stage_ref, weight_sem, part_sem, stage_sem = refs[9:]
     count = x_ref.shape[0]
     half = count // 2
     per_shard, n_weights, shard_rows = shards[0].shape[:3]
@@ -599,6 +638,8 @@
         return carry
 
     lax.fori_loop(0, count // FFN_TILE, tile_step, 0)
+    for k in range(UNIT):
+        backs[k][...] = back_ref[k]
 
     core, bits = table_ref[1], [table_ref[2 + d] for d in range(4)]
     piece, half_columns = kept_ref.shape[3:]
@@ -672,15 +713,15 @@
     return pl.pallas_call(
         functools.partial(layer_body, n_shards),
         in_specs=[pl.BlockSpec(memory_space=pltpu.SMEM)] + [anywhere] * (n_shards + UNIT) + [inside] * 3,
-        out_specs=[inside, inside, inside, inside, anywhere, anywhere],
+        out_specs=[inside, inside, inside, anywhere, anywhere] + [inside] * UNIT,
         out_shape=[
             jax.ShapeDtypeStruct((count, D), BF16),
             jax.ShapeDtypeStruct((count, D), F32),
-            jax.ShapeDtypeStruct((UNIT, *packed), BF16),
             jax.ShapeDtypeStruct((VEC_ROWS, D), F32),
             jax.ShapeDtypeStruct((3, 16, n_weights // 3, D // 16, D // 2), BF16),
             jax.ShapeDtypeStruct((3, 16, n_weights // 3, D // 16, D // 2), BF16),
-        ],
+        ]
+        + [jax.ShapeDtypeStruct(packed, BF16)] * UNIT,
         scratch_shapes=[
             pltpu.VMEM((n_weights, D, D), BF16),
             pltpu.VMEM((UNIT, *packed), BF16),
@@ -690,6 +731,7 @@
             pltpu.VMEM((count, D), BF16),
             pltpu.VMEM((FFB, count, D), BF16),
             pltpu.VMEM((count, D), BF16),
+            pltpu.VMEM((UNIT, *packed), BF16),
             pltpu.VMEM((FFB, FFN_TILE, D), F32),
             pltpu.VMEM((2, D, D), BF16),
             pltpu.SemaphoreType.DMA((n_weights,)),
@@ -700,6 +742,79 @@
         cost_estimate=SMALL,
         name="layer",
     )(table, *shards, *parts, inputs, cotangent, vectors)
+
+
+def qkv_back_body(scalars_ref, *refs):
+    grads, inputs, kept_ref, sent_ref, bias_ref, all_ref = refs[:4], refs[4:8], *refs[8:]
+    core, unit = scalars_ref[0], scalars_ref[1]
+    columns = all_ref.shape[4]
+    step = 32
+    per_unit = all_ref.shape[3]
+    bias_ref[...] = jnp.zeros_like(bias_ref)
+    for head in range(HEADS_OWN):
+        at = slice(head * WIDE, (head + 1) * WIDE)
+        total = inner_rows(grads[0][:, at], inputs[0][...])
+        bias = jnp.sum(grads[0][:, at].astype(F32), axis=0, keepdims=True)
+        for k in range(1, UNIT):
+            total = total + inner_rows(grads[k][:, at], inputs[k][...])
+            bias = bias + jnp.sum(grads[k][:, at].astype(F32), axis=0, keepdims=True)
+        bias_ref[0:1, at] = bias
+        firsts = (HEAD, 3 * HEAD, 0) if head % 2 == 0 else (0, 2 * HEAD, HEAD)
+        for block, first in enumerate(firsts):
+            for i in range(HEAD // step):
+                row = head * HEAD + i * step
+                rows = total[first + i * step : first + (i + 1) * step]
+                for c in range(2):
+                    all_ref[
+                        c ^ core, row // per_unit ^ unit, block, row % per_unit : row % per_unit + step, :
+                    ] = rows[:, c * columns : (c + 1) * columns].astype(BF16)
+    kept_ref[...] = all_ref[0]
+    sent_ref[...] = all_ref[1]
+
+
+def qkv_back(scalars, grads, inputs):
+    inside = pl.BlockSpec(memory_space=pltpu.VMEM)
+    shape = (2, 3, HEADS_OWN * HEAD // 2, D // 2)
+    return pl.pallas_call(
+        qkv_back_body,
+        in_specs=[pl.BlockSpec(memory_space=pltpu.SMEM)] + [inside] * (2 * UNIT),
+        out_specs=[inside] * 3,
+        out_shape=[
+            jax.ShapeDtypeStruct(shape, BF16),
+            jax.ShapeDtypeStruct(shape, BF16),
+            jax.ShapeDtypeStruct((8, HEADS_OWN * WIDE), F32),
+        ],
+        scratch_shapes=[pltpu.VMEM((2, *shape), BF16)],
+        compiler_params=pltpu.CompilerParams(vmem_limit_bytes=56 << 20),
+        cost_estimate=SMALL,
+        name="qkv_back",
+    )(scalars, *grads, *inputs)
+
+
+def pack_body(slot_block_ref, *refs):
+    half = (len(refs) - 2) // 2
+    kept, got, out_ref, all_ref = refs[:half], refs[half : 2 * half], refs[-2], refs[-1]
+    per_part = kept[0].shape[1]
+    for p in range(half):
+        for b in range(per_part):
+            all_ref[p * per_part + b] = (kept[p][0, b] + got[p][0, b].astype(F32)).astype(BF16)
+    for s in range(out_ref.shape[0] * out_ref.shape[1]):
+        out_ref[s // out_ref.shape[1], s % out_ref.shape[1]] = all_ref[jnp.maximum(slot_block_ref[s] - 3, 0)]
+
+
+def pack(slot_block, kept, got, n_grp, slots):
+    shape = kept[0].shape[2:]
+    inside = pl.BlockSpec(memory_space=pltpu.VMEM)
+    return pl.pallas_call(
+        pack_body,
+        in_specs=[pl.BlockSpec(memory_space=pltpu.SMEM)] + [inside] * (2 * len(kept)),
+        out_specs=inside,
+        out_shape=jax.ShapeDtypeStruct((n_grp, slots, *shape), BF16),
+        scratch_shapes=[pltpu.VMEM((len(kept) * kept[0].shape[1], *shape), BF16)],
+        compiler_params=pltpu.CompilerParams(vmem_limit_bytes=32 << 20),
+        cost_estimate=SMALL,
+        name="pack",
+    )(slot_block, *kept, *got)
 
 
 def rotate_in_body(mine_ref, keep_ref, got_ref, high_ref, low_ref, out_ref, grad_ref):
@@ -914,15 +1029,15 @@
     rows_dev = master.shape[0]
     slots = master.shape[1]
     blocks_all = slots * n_grp
-    member = tok % UNIT
-    unit = tok // UNIT
+    member = tok & (UNIT - 1)
+    unit = tok >> 2
     place = [2 * (t % UNIT) + t // UNIT for t in range(n_tok)]
     own_width = HEADS_OWN * HEAD
 
     slot_block = jnp.argsort(owners, stable=True).astype(jnp.int32)
     block_slot = jnp.argsort(slot_block, stable=True).astype(jnp.int32)
 
-    core, bit_x = grp % 2, grp // 2
+    core, bit_x = grp & 1, grp >> 1
     inputs = tokens[0]
 
     near, far = swap(inputs, "tok", 1), swap(inputs, "tok", 2)
@@ -934,37 +1049,29 @@
     middle = unit_start + UNIT // 2 * tok_count
     start_of_middle = jnp.max(jnp.where(item_starts <= middle, item_starts, 0))
     is_long = (start_of_middle <= unit_start).astype(jnp.int32).reshape(1)
-    order = places(CLUSTER // UNIT * (2 - is_long), clusters[0])
-    by_member = jnp.transpose(order.reshape(ROUNDS, UNIT, HEADS_OWN, tok_count), (1, 2, 0, 3))
-    by_member = by_member.reshape(UNIT, LOCAL_PAIRS, tok_count)
-    by_member = jnp.pad(by_member, ((0, 0), (0, 8 - LOCAL_PAIRS), (0, 0)))
-    orders = exchange_unit([pick(by_member, member ^ k) for k in range(UNIT)])
+    share = CLUSTER // UNIT * (2 - is_long)
+    orders = exchange_unit(places(jnp.concatenate([share, member.reshape(1)]), clusters[0]))
     left, right = doubled(bases[0]), doubled(bases[1])
     (over, left, right) = together(over, left, right)
     across = swap(over, "grp", 1)
 
     (near, far, beside, over, across) = together(near, far, beside, over, across)
-    by_slot = jnp.concatenate([local, beside, over, across], axis=0)
-    at = [((block_slot[b] // slots) ^ grp) * slots + block_slot[b] % slots for b in range(blocks_all)]
     part_rows = rows_dev // 2
 
-    def own_half(source, b):
-        return lax.dynamic_slice(source, (at[b], core * part_rows, 0), (1, part_rows, D))[0]
-
-    by_owner = arrange(jnp.stack([own_half(by_slot, b) for b in range(3)]))
-    theirs = exchange_unit([pick(by_owner, member ^ k) for k in range(UNIT)])
+    scalars = jnp.concatenate([block_slot, jnp.stack([grp, core, member])]).astype(jnp.int32)
+    *by_owner, rest_rows = arrange(scalars, [local, beside, over, across], blocks_all)
+    theirs = exchange_unit(by_owner)
     half = tok_count // 2
     third = (swap(near[:half], "tok", 2), swap(far[half:], "tok", 1))
-    (theirs, by_slot) = together(theirs, by_slot)
     theirs = jnp.stack(theirs)
     theirs_far = swap(theirs, "tok", UNIT)
     mine_all = jnp.concatenate([theirs, theirs_far], axis=0)
     others_all = swap(mine_all, "grp", 1)
-    sources = [tok ^ k ^ (UNIT * f) for f in range(2) for k in range(UNIT)]
-    firsts = [t * rows_dev + c * part_rows for c in (core, 1 - core) for t in sources]
-    rest_rows = jnp.stack([own_half(by_slot, b) for b in range(3, blocks_all)])
+    sources = tok ^ jnp.arange(2 * UNIT, dtype=jnp.int32)
+    cores = core ^ jnp.arange(2, dtype=jnp.int32)
+    firsts = (sources[None, :] * rows_dev + cores[:, None] * part_rows).reshape(-1)
     (third, others_all, rest_rows, orders) = together(third, others_all, rest_rows, orders)
-    own_weights = assemble(jnp.stack(firsts).astype(jnp.int32), [mine_all, others_all])
+    own_weights = assemble(firsts, [mine_all, others_all])
 
     def columns_of(value, m):
         return lax.dynamic_slice_in_dim(value, m * own_width, own_width, value.ndim - 1)
@@ -1000,22 +1107,20 @@
     mixed_parts[0] = mix(orders[0], sorted_out[0])
     mine_rest = [jnp.stack([steps[k], flips[k]]) for k in range(depth)]
     shards = mine_rest + [swap(m, "grp", 1) for m in mine_rest]
-    firsts = [
-        ((tok - 2 * k) % n_tok ^ flip) * rows_dev + c * part_rows
-        for c in (core, 1 - core)
-        for k in range(depth)
-        for flip in range(2)
-    ]
+    sources = (tok + n_tok - 2 * jnp.arange(depth, dtype=jnp.int32)) & (n_tok - 1)
+    sources = (sources[:, None] ^ jnp.arange(2, dtype=jnp.int32)[None, :]).reshape(-1)
+    firsts = (sources[None, :] * rows_dev + cores[:, None] * part_rows).reshape(-1)
 
     held_weights, *shards = lax.optimization_barrier((own_weights, *shards))
     turned_weights = [swap(held_weights, "tok", k) for k in range(1, UNIT)]
-    table = jnp.stack([member, core, bit_x, tok % 2, tok // 2 % 2, tok // 4, *firsts]).astype(jnp.int32)
-    result, grad_first, back, sums, kept, sent_pieces = layer(
+    place_bits = jnp.stack([member, core, bit_x, tok & 1, (tok >> 1) & 1, tok >> 2]).astype(jnp.int32)
+    table = jnp.concatenate([place_bits, firsts])
+    result, grad_first, sums, kept, sent_pieces, *back = layer(
         table, shards, mixed_parts, inputs, cotangent[0], vectors
     )
     (turned_weights, kept, sent_pieces, back) = together(turned_weights, kept, sent_pieces, back)
 
-    grad_parts = exchange_unit([back[k] for k in range(UNIT)])
+    grad_parts = exchange_unit(back)
     other = swap(sent_pieces, "grp", 1)
     sums_of = [kept[p].astype(F32) + other[p].astype(F32) for p in range(3)]
 
@@ -1037,50 +1142,43 @@
     (sent_now, sorted_back) = together(sent_now, sorted_back)
     got_now = exchanged(sent_now, 1)
     own_grads = [None] * UNIT
-    for k in (3, 2):
-        own_grads[k] = gather_grads(orders[k], sorted_back[k])
-    turned_qkv = sum(inner_rows(own_grads[k], unit_inputs[k]) for k in (3, 2))
+    own_grads[3] = gather_grads(orders[3], sorted_back[3])
+    home_grads = [None, None, None, swap(own_grads[3], "tok", 3)]
+    own_grads[2] = gather_grads(orders[2], sorted_back[2])
     kept_now, sent_now = halves(joined(kept_now, got_now))
-    (sent_now, turned_qkv, sorted_back) = together(sent_now, turned_qkv, sorted_back)
+    (sent_now, own_grads[2], sorted_back) = together(sent_now, own_grads[2], sorted_back)
     got_now = exchanged(sent_now, 2)
     for k in (1, 0):
         own_grads[k] = gather_grads(orders[k], sorted_back[k])
-    turned_qkv = turned_qkv + sum(inner_rows(own_grads[k], unit_inputs[k]) for k in (1, 0))
+    kept_qkv, sent_qkv, bias_qkv = qkv_back(jnp.stack([core, unit]).astype(jnp.int32), own_grads, unit_inputs)
     kept_now, sent_now = halves(joined(kept_now, got_now))
-    turned_qkv = join_heads(turned_qkv).astype(BF16).reshape(3, 2, own_width // 2, 2, D // 2)
-    turned_qkv = jnp.transpose(turned_qkv, (3, 1, 0, 2, 4))
-    (sent_now, turned_qkv) = together(sent_now, turned_qkv)
+    (sent_now, sent_qkv, home_grads[3]) = together(sent_now, sent_qkv, home_grads[3])
     got_now = exchanged(sent_now, 3)
 
-    bias_qkv = sum(jnp.sum(own_grads[k].astype(F32), axis=0) for k in range(UNIT))
-    bias_query, _, bias_value = join_heads(bias_qkv)
+    bias_query, _, bias_value = join_heads(bias_qkv[0])
     bias_rows = lax.dynamic_update_slice_in_dim(
         jnp.zeros((2, D), F32), jnp.stack([bias_query, bias_value]), member * own_width, 1
     )
     total = sums[: 8 + FFB] + jnp.pad(bias_rows, ((4, 2 + FFB), (0, 0)))
 
-    core_got = swap(pick(turned_qkv, 1 - core), "grp", 1)
     more = swap(total, "grp", 1)
-    keep = pick(turned_qkv, core).astype(F32) + core_got.astype(F32)
+    keep = kept_qkv.astype(F32) + swap(sent_qkv, "grp", 1).astype(F32)
     (keep, more) = together(keep, more)
     total = total + more
     more = swap(total, "grp", 2)
-    unit_got = swap(pick(keep, 1 - unit).astype(BF16), "tok", UNIT)
-    home_grads = [own_grads[0], swap(own_grads[1], "tok", 1), None, None]
-    rest = jnp.concatenate([v[0].astype(BF16) for v in joined(kept_now, got_now)], axis=0)
-    sent = jnp.stack(
-        [pick(rest, jnp.maximum(slot_block[s] - 3, 0)) for s in range(blocks_all)]
-    ).reshape(n_grp, slots, *rest.shape[1:])
+    unit_got = swap(keep[1].astype(BF16), "tok", UNIT)
+    home_grads[1] = swap(own_grads[1], "tok", 1)
+    home_grads[2] = swap(own_grads[2], "tok", 2)
+    sent = pack(slot_block, kept_now, got_now, n_grp, slots)
     got = lax.all_to_all(sent, "grp", split_axis=0, concat_axis=0, tiled=True)
-    keep = pick(keep, unit) + unit_got.astype(F32)
-    (keep, more, own_grads[2]) = together(keep, more, own_grads[2])
+    keep = keep[0] + unit_got.astype(F32)
+    (keep, more) = together(keep, more)
     total = total + more
     more = swap(total, "tok", 1)
     keep = keep + swap(keep.astype(BF16), "grp", 2).astype(F32)
     (keep, more) = together(keep.astype(BF16), more)
     total = total + more
     more = swap(total, "tok", 2)
-    home_grads[2] = swap(own_grads[2], "tok", 2)
     kept_core = (keep, swap(keep, "grp", 1))
     keep = jnp.concatenate(
         [jnp.where(core == 0, kept_core[0], kept_core[1]), jnp.where(core == 0, kept_core[1], kept_core[0])],
@@ -1092,16 +1190,15 @@
         return lax.all_to_all(value, "tok", split_axis=0, concat_axis=0, tiled=True)
 
     part = to_tok(rotate_in(mine, keep, got, left, n_tok))
-    (part, more, home_grads[1], own_grads[3]) = together(part, more, home_grads[1], own_grads[3])
+    (part, more, home_grads) = together(part, more, [own_grads[0]] + home_grads[1:])
     total = total + more
     more = swap(total, "tok", 4)
-    home_grads[3] = swap(own_grads[3], "tok", 3)
     by_slot_of = lambda value: jnp.transpose(value, (1, 0, 2))
     new_one, new_two, turned = moments(
         place, part, right, by_slot_of(moment_one), by_slot_of(moment_two)
     )
     turned = to_tok(turned)
-    (turned, more, home_grads[2]) = together(turned, more, home_grads[2])
+    (turned, more) = together(turned, more)
     vector_total = total + more
     change = to_tok(rotate_out(turned, left))
     new_master = by_slot_of(apply_change(place, change, by_slot_of(master)))

time: 678 us -> 612 us (0.903)
  local copies, waits for them, and re-layouts: 98.1 us -> 54.3 us
  between operations: 33.8 us -> 2.54 us
  Pallas kernels: 220 us -> 236 us
  matrix products: 32.7 us -> 19.6 us
  waiting for transfers between devices: 145 us -> 152 us
    unnamed x224 -> x153, local copies, waits for them, and re-layouts: 60.2 us -> 31.3 us
    dot_general x4 -> x0, matrix products: 14.7 us -> none  [inner_rows(): lax.dot_general(left, right, (((0,), (0,)), ((), ())), preferred_element_...]
    another operation x11 -> x2, local copies, waits for them, and re-layouts: 12.6 us -> 0.08 us  [the longest x1 0.08 us: join_heads(): parts = tiles.reshape(HEADS_OWN, 4, HEAD, *tiles.shape[1:])]
    pallas_call x1 -> x3, Pallas kernels: 1.78 us -> 13.9 us  [the longest x1 10.8 us: qkv_back(): pl.pallas_call(qkv_back_body, in_specs=[pl.BlockSpec(memory_space=pltpu.S...]
    all_to_all x3, waiting for transfers between devices: 3.89 us -> 11 us  [to_tok(): return lax.all_to_all(value, 'tok', split_axis=0, concat_axis=0, tiled=True)]
  transfers between devices with their start and end apart: 64 -> 64, of which waited for: 17 -> 22; matrix products, arithmetic and copies ran while one was open for 20% -> 16% of each run, Pallas kernels for 31% -> 36%
where the time goes in v5:
time: 612 us; the launch traced here: 602 us
  Pallas kernels  236 us (39%)
  waiting for transfers between devices  152 us (25%)
  starting transfers between devices  82.6 us (13%)
  other arithmetic  55.4 us (9%)
  local copies, waits for them, and re-layouts  54.3 us (9%)
  matrix products  19.6 us (3%)
    ppermute x57, waiting for transfers between devices, swap(): return lax.ppermute(value, axis, [(i, i ^ bit) for i in range(size)])  135 us
    pallas_call x1, Pallas kernels, layer(): pl.pallas_call(functools.partial(layer_body, n_shards), in_specs=[pl.Bloc...  69.4 us
    ppermute x57, starting transfers between devices, swap(): return lax.ppermute(value, axis, [(i, i ^ bit) for i in range(size)])  63 us
    unnamed x153, local copies, waits for them, and re-layouts  31.3 us
    pallas_call x4, Pallas kernels, sort_rows(): pl.pallas_call(sort_body, grid=(HEADS_OWN,), in_specs=[pl.BlockSpec((8, c...  27.7 us
    pallas_call x4, Pallas kernels, gather_grads(): pl.pallas_call(gather_grads_body, grid=(HEADS_OWN,), in_specs=[pl.BlockSp...  22.7 us
    pallas_call x4, Pallas kernels, mix(): pl.pallas_call(mix_body, grid=(HEADS_OWN,), in_specs=[pl.BlockSpec((8, co...  19.9 us
    dot_general x4, matrix products, outer_cols(): lax.dot_general(left, right, (((1,), (1,)), ((), ())), preferred_element_...  19.6 us
  transfers between devices with their start and end apart: 64, of which 22 were waited for; matrix products, arithmetic and copies ran while one was open for 16% of the time, Pallas kernels for 36%

profile of v5, /device:TPU:0, one launch (start us, length us, event | category | flops | bytes accessed | tf_op | source)
XLA Modules:
  0.0 602.2 jit_solution(1030696060697738419)
XLA Ops:
  8.8 14.8 %fusion = (bf16[3,768,768]{2,1,0:T(8,128)(2,1)}, bf16[3,768,768]{2,1,0:T(8,128)(2,1)}, bf16[3,768,768]{2,1,0:T(8,128)(2,1)}, bf16[3,768,768]{2,1,0:T(8,128)(2,1)S(1)}) fusion(f32[2,3,768,768]{3,2,1,0:T(8,128)} %param.18), kind=kLoop, calls=%fused_computation.2 | loop fusion | flops 10616832 | bytes 35389440 | tf_op jit(solution)/shard_map/convert_element_type | solution.py:1002
  27.8 10.6 %collective-permute-done.x_ref.refs_5_ = bf16[1024,768]{1,0:T(8,128)(2,1)} collective-permute-done((bf16[1024,768]{1,0:T(8,128)(2,1)}, bf16[1024,768]{1,0:T(8,128)(2,1)}, u32[]{:S(2)}, u32[]{:S(2)}) %collective-permute-start) | collective-permute-done | bytes 1572896 | tf_op jit(solution)/shard_map/ppermute | solution.py:947
  57.0 14.1 %collective-permute-done.8 = bf16[4,48,768]{2,1,0:T(8,128)(2,1)S(1)} collective-permute-done((bf16[4,48,768]{2,1,0:T(8,128)(2,1)S(1)}, bf16[4,48,768]{2,1,0:T(8,128)(2,1)S(1)}, u32[]{:S(2)}, u32[]{:S(2)}) %collective-permute-start.8) | collective-permute-done | bytes 294944 | tf_op jit(solution)/shard_map/ppermute | solution.py:947
  72.4 6.9 %places.1 = (s32[8,1024]{1,0:T(8,128)}, s32[8,1024]{1,0:T(8,128)}, s32[8,1024]{1,0:T(8,128)}, s32[8,1024]{1,0:T(8,128)}) custom-call(s32[2]{0:T(128)} %get-tuple-element.290.scalars_ref, s32[24,1024]{1,0:T(8,128)} %bitcast.127), custom_call_target="tpu_custom_call" | custom-call | tf_op jit(solution)/shard_map/places/pallas_call | solution.py:96
  80.0 4.0 collective-permute-start.13
  103.1 6.5 %sort_rows.4.refs_0_ = bf16[6,1024,256]{2,1,0:T(8,128)(2,1)S(1)} custom-call(s32[8,1024]{1,0:T(8,128)S(1)} %copy-done.29, bf16[1024,768]{1,0:T(8,128)(2,1)S(1)} %bitcast.111, bf16[768,768]{1,0:T(8,128)(2,1)} %assemble.1.weight_ref, f32[1,768]{1,0:T(1,128)S(1)} %reshape.107.bias_ref), custom_call_target="tpu_custom_call" | custom-call | tf_op jit(solution)/shard_map/sort_rows/pallas_call | solution.py:221
  111.4 7.1 %sort_rows.5.refs_1_ = bf16[6,1024,256]{2,1,0:T(8,128)(2,1)S(1)} custom-call(s32[8,1024]{1,0:T(8,128)} %collective-permute-done.12.place_ref, bf16[1024,768]{1,0:T(8,128)(2,1)} %collective-permute-done.x_ref.refs_5_, bf16[768,768]{1,0:T(8,128)(2,1)} %assemble.1.weight_ref, f32[1,768]{1,0:T(1,128)S(1)} %reshape.107.bias_ref), custom_call_target="tpu_custom_call" | custom-call | tf_op jit(solution)/shard_map/sort_rows/pallas_call | solution.py:221
  120.2 7.1 %sort_rows.6.refs_2_ = bf16[6,1024,256]{2,1,0:T(8,128)(2,1)S(1)} custom-call(s32[8,1024]{1,0:T(8,128)} %collective-permute-done.13.place_ref, bf16[1024,768]{1,0:T(8,128)(2,1)} %collective-permute-done.1.x_ref.refs_6_, bf16[768,768]{1,0:T(8,128)(2,1)} %assemble.1.weight_ref, f32[1,768]{1,0:T(1,128)S(1)} %reshape.107.bias_ref), custom_call_target="tpu_custom_call" | custom-call | tf_op jit(solution)/shard_map/sort_rows/pallas_call | solution.py:221
  131.5 6.9 %sort_rows.7.refs_3_ = bf16[6,1024,256]{2,1,0:T(8,128)(2,1)S(1)} custom-call(s32[8,1024]{1,0:T(8,128)} %collective-permute-done.14.place_ref, bf16[1024,768]{1,0:T(8,128)(2,1)S(1)} %constant_dynamic-update-slice_fusion.5.x_ref.refs_7_, bf16[768,768]{1,0:T(8,128)(2,1)} %assemble.1.weight_ref, f32[1,768]{1,0:T(1,128)S(1)} %reshape.107.bias_ref), custom_call_target="tpu_custom_call" | custom-call | tf_op jit(solution)/shard_map/sort_rows/pallas_call | solution.py:221
  141.6 16.5 %attend.1 = (bf16[6,1024,128]{2,1,0:T(8,128)(2,1)S(1)}, bf16[6,1024,128]{2,1,0:T(8,128)(2,1)S(1)}, bf16[6,1024,128]{2,1,0:T(8,128)(2,1)S(1)}, bf16[6,1024,128]{2,1,0:T(8,128)(2,1)}) custom-call(s32[1]{0:T(128)} %bitcast.16.long_ref, bf16[6,1024,256]{2,1,0:T(8,128)(2,1)} %copy-done, bf16[6,1024,256]{2,1,0:T(8,128)(2,1)} %copy-done.1, ...), custom_call_target="tpu_custom_call" | custom-call | tf_op jit(solution)/shard_map/attend/pallas_call | solution.py:345
  159.9 5.5 mix.4
  167.0 5.0 mix.5
  173.9 5.2 mix.6
  184.3 7.8 %collective-permute-done.23.refs_11_ = bf16[1536,128]{1,0:T(8,128)(2,1)S(1)} collective-permute-done((bf16[1536,128]{1,0:T(8,128)(2,1)S(1)}, bf16[1536,128]{1,0:T(8,128)(2,1)S(1)}, u32[]{:S(2)}, u32[]{:S(2)}) %collective-permute-start.23) | collective-permute-done | bytes 393248 | tf_op jit(solution)/shard_map/ppermute | solution.py:947
  198.1 10.9 %collective-permute-done.24 = bf16[9,48,768]{2,1,0:T(8,128)(2,1)S(1)} collective-permute-done((bf16[9,48,768]{2,1,0:T(8,128)(2,1)S(1)}, bf16[9,48,768]{2,1,0:T(8,128)(2,1)S(1)}, u32[]{:S(2)}, u32[]{:S(2)}) %collective-permute-start.24) | collective-permute-done | bytes 663584 | tf_op jit(solution)/shard_map/ppermute | solution.py:947
  218.7 4.2 mix.7.refs_8_
  223.7 69.4 %layer.1 = (bf16[1024,768]{1,0:T(8,128)(2,1)}, f32[1024,768]{1,0:T(8,128)}, f32[16,768]{1,0:T(8,128)}, bf16[3,16,3,48,384]{4,3,2,1,0:T(8,128)(2,1)}, bf16[3,16,3...) custom-call(s32[22]{0:T(128)} %concatenate.28.table_ref, ...), custom_call_target="tpu_custom_call" | custom-call | tf_op jit(solution)/shard_map/layer/pallas_call | solution.py:713
  296.7 5.4 collective-permute-done.32
  307.7 6.9 %collective-permute-done.35.rows_ref = bf16[1536,128]{1,0:T(8,128)(2,1)S(1)} collective-permute-done((bf16[1536,128]{1,0:T(8,128)(2,1)}, bf16[1536,128]{1,0:T(8,128)(2,1)S(1)}, u32[]{:S(2)}, u32[]{:S(2)}) %collective-permute-start.35) | collective-permute-done | bytes 393248 | tf_op jit(solution)/shard_map/ppermute | solution.py:947
  318.0 3.8 sort_grads.4.refs_4_
  323.1 4.6 sort_grads.5.refs_5_
  328.8 4.8 sort_grads.6.refs_6_
  334.7 4.6 sort_grads.7.refs_7_
  340.5 18.9 %attend_back.1 = (bf16[6,1024,256]{2,1,0:T(8,128)(2,1)}, bf16[6,1024,256]{2,1,0:T(8,128)(2,1)}, bf16[6,1024,256]{2,1,0:T(8,128)(2,1)}, bf16[6,1024,256]{2,1,0:T(8,128)(2,1)}) custom-call(s32[1]{0:T(128)} %bitcast.16.long_ref, bf16[6,1024,256]{2,1,0:T(8,128)(2,1)} %copy-done, bf16[6,1024,256]{2,1,0:T(8,128)(2,1)} %copy-done.1, ...), custom_call_target="tpu_custom_call" | custom-call | tf_op jit(solution)/shard_map/attend_back/pallas_call | solution.py:389
  369.4 6.1 %gather_grads.4.refs_2_ = bf16[1024,768]{1,0:T(8,128)(2,1)} custom-call(s32[8,1024]{1,0:T(8,128)} %collective-permute-done.13.place_ref, bf16[6,1024,256]{2,1,0:T(8,128)(2,1)S(1)} %copy-done.15), custom_call_target="tpu_custom_call" | custom-call | tf_op jit(solution)/shard_map/gather_grads/pallas_call | solution.py:482
  375.5 6.0 %gather_grads.7.refs_3_ = bf16[1024,768]{1,0:T(8,128)(2,1)} custom-call(s32[8,1024]{1,0:T(8,128)} %collective-permute-done.14.place_ref, bf16[6,1024,256]{2,1,0:T(8,128)(2,1)S(1)} %copy-done.14), custom_call_target="tpu_custom_call" | custom-call | tf_op jit(solution)/shard_map/gather_grads/pallas_call | solution.py:482
  383.8 6.5 %collective-permute-done.40 = bf16[4,3,48,384]{3,2,1,0:T(8,128)(2,1)} collective-permute-done((bf16[4,3,48,384]{3,2,1,0:T(8,128)(2,1)}, bf16[4,3,48,384]{3,2,1,0:T(8,128)(2,1)}, u32[]{:S(2)}, u32[]{:S(2)}) %collective-permute-start.40) | collective-permute-done | bytes 442400 | tf_op jit(solution)/shard_map/ppermute | solution.py:947
  396.5 4.4 gather_grads.5.refs_0_
  402.1 6.3 %gather_grads.6.refs_1_ = bf16[1024,768]{1,0:T(8,128)(2,1)} custom-call(s32[8,1024]{1,0:T(8,128)} %collective-permute-done.12.place_ref, bf16[6,1024,256]{2,1,0:T(8,128)(2,1)S(1)} %copy-done.12), custom_call_target="tpu_custom_call" | custom-call | tf_op jit(solution)/shard_map/gather_grads/pallas_call | solution.py:482
  408.3 10.8 %qkv_back.1 = (bf16[2,3,96,384]{3,2,1,0:T(8,128)(2,1)}, bf16[2,3,96,384]{3,2,1,0:T(8,128)(2,1)}, f32[8,768]{1,0:T(8,128)}) custom-call(s32[2]{0:T(128)} %get-tuple-element.291.scalars_ref, bf16[1024,768]{1,0:T(8,128)(2,1)} %copy-done.6, bf16[1024,768]{1,0:T(8,128)(2,1)} %gather_grads.6.refs_1_, bf16[1024,768]{1,0:T(8,128)(2,1)} %gather_grads.4.refs_2_, ...), custom_call_target="tpu_custom_call" | custom-call | tf_op jit(solution)/shard_map/qkv_back/pallas_call | solution.py:778
  420.0 11.4 %collective-permute-done.42 = bf16[2,3,48,384]{3,2,1,0:T(8,128)(2,1)} collective-permute-done((bf16[2,3,48,384]{3,2,1,0:T(8,128)(2,1)}, bf16[2,3,48,384]{3,2,1,0:T(8,128)(2,1)}, u32[]{:S(2)}, u32[]{:S(2)}) %collective-permute-start.42) | collective-permute-done | bytes 221216 | tf_op jit(solution)/shard_map/ppermute | solution.py:947
  441.3 11.2 %collective-permute-done.48 = bf16[3,96,384]{2,1,0:T(8,128)(2,1)S(1)} collective-permute-done((bf16[3,96,384]{2,1,0:T(8,128)(2,1)S(1)}, bf16[3,96,384]{2,1,0:T(8,128)(2,1)S(1)}, u32[]{:S(2)}, u32[]{:S(2)}) %collective-permute-start.48) | collective-permute-done | bytes 221216 | tf_op jit(solution)/shard_map/ppermute | solution.py:947
  460.7 29.8 %collective-permute-done.51 = f32[12,768]{1,0:T(8,128)S(1)} collective-permute-done((f32[12,768]{1,0:T(8,128)S(1)}, f32[12,768]{1,0:T(8,128)S(1)}, u32[]{:S(2)}, u32[]{:S(2)}) %collective-permute-start.51) | collective-permute-done | bytes 36896 | tf_op jit(solution)/shard_map/ppermute | solution.py:947
  500.9 4.1 all-to-all-start
  506.9 6.1 %all-to-all-done.got_ref = bf16[4,3,48,384]{3,2,1,0:T(8,128)(2,1)} async-done(((bf16[4,3,48,384]{3,2,1,0:T(8,128)(2,1)}), bf16[4,3,48,384]{3,2,1,0:T(8,128)(2,1)}, u32[]{:S(2)}, u32[]{:S(2)}) %all-to-all-start) | async-done | bytes 442400 | tf_op jit(solution)/shard_map/all_to_all | solution.py:1173
  514.1 4.3 rotate_in.1
  519.2 4.2 all-to-all-start.1
  526.8 7.3 %collective-permute-done.56 = f32[12,768]{1,0:T(8,128)} collective-permute-done((f32[12,768]{1,0:T(8,128)S(1)}, f32[12,768]{1,0:T(8,128)}, u32[]{:S(2)}, u32[]{:S(2)}) %collective-permute-start.56) | collective-permute-done | bytes 36896 | tf_op jit(solution)/shard_map/ppermute | solution.py:947
  534.1 5.3 all-to-all-done.1.got_ref
  539.4 5.0 fusion.19
  544.4 8.9 %moments.1 = (f32[3,96,768]{2,1,0:T(8,128)}, f32[3,96,768]{2,1,0:T(8,128)}, bf16[8,3,96,96]{3,2,1,0:T(8,128)(2,1)S(1)}) custom-call(bf16[8,3,96,96]{3,2,1,0:T(8,128)(2,1)} %all-to-all-done.1.got_ref, bf16[3,768,768]{2,1,0:T(8,128)(2,1)} %get-tuple-element.252.high_ref, bf16[3,768,768]{2,1,0:T(8,128)(2,1)} %get-tuple-element.253.low_ref, ...), custom_call_target="tpu_custom_call" | custom-call | tf_op jit(solution)/shard_map/moments/pallas_call | solution.py:882
  554.1 4.2 all-to-all-start.2
  562.0 4.8 fusion.22
  566.9 4.9 fusion.21
  571.7 4.8 fusion.20
  576.6 4.2 rotate_out.1
  585.3 8.3 %add_bitcast_fusion = f32[1,1024,768]{2,1,0:T(8,128)} fusion(f32[1024,768]{1,0:T(8,128)} %get-tuple-element.189, f32[1024,768]{1,0:T(8,128)} %fusion.22, f32[1024,768]{1,0:T(8,128)} %fusion.21, f32[1024,768]{1,0:T(8,128)} %fusion.19, f32[1024,768]{1,0:T(8,128)} %fusion.20), kind=kLoop, calls=%fused_computation.9 | loop fusion | flops 3145728 | bytes 18874368 | tf_op jit(solution)/shard_map/broadcast_in_dim | solution.py:1214
  595.1 5.7 all-to-all-done.3.got_ref
  (346 shorter events, 173.8 us)
Async XLA Ops:
  0.6 37.7 %collective-permute-start = (bf16[1024,768]{1,0:T(8,128)(2,1)}, bf16[1024,768]{1,0:T(8,128)(2,1)}, u32[]{:S(2)}, u32[]{:S(2)}) collective-permute-start(bf16[1024,768]{1,0:T(8,128)(2,1)} %bitcast.107), channel_id=1, source_target_pairs={{0,4},{4,0},{8,12},{12,8},{16,20},{20,16},{24,28},{28,24},{1,5},{5... | collective-permute-start | bytes 4718600 | tf_op jit(solution)/shard_map/ppermute | solution.py:947
  3.7 36.2 %collective-permute-start.1 = (bf16[1024,768]{1,0:T(8,128)(2,1)}, bf16[1024,768]{1,0:T(8,128)(2,1)}, u32[]{:S(2)}, u32[]{:S(2)}) collective-permute-start(bf16[1024,768]{1,0:T(8,128)(2,1)} %bitcast.108), channel_id=1, source_target_pairs={{0,8},{4,12},{8,0},{12,4},{16,24},{20,28},{24,16},{28,20},{1,9},{5... | collective-permute-start | bytes 4718600 | tf_op jit(solution)/shard_map/ppermute | solution.py:947
  7.2 20.6 %collective-permute-start.2 = (bf16[3,96,768]{2,1,0:T(8,128)(2,1)}, bf16[3,96,768]{2,1,0:T(8,128)(2,1)}, u32[]{:S(2)}, u32[]{:S(2)}) collective-permute-start(bf16[3,96,768]{2,1,0:T(8,128)(2,1)} %convert_bitcast_fusion.refs_0_), channel_id=1, source_target_pairs={{0,1},{1,0},{2,3},{3,2},{4,5},{5,4},{6,7},{7,6},{8,9},{9,8},{10,11... | collective-permute-start | bytes 1327112 | tf_op jit(solution)/shard_map/ppermute | solution.py:947
  7.2 16.3 %collective-permute-start.3 = (bf16[3,96,768]{2,1,0:T(8,128)(2,1)}, bf16[3,96,768]{2,1,0:T(8,128)(2,1)}, u32[]{:S(2)}, u32[]{:S(2)}) collective-permute-start(bf16[3,96,768]{2,1,0:T(8,128)(2,1)} %convert_bitcast_fusion.refs_0_), channel_id=1, source_target_pairs={{0,2},{1,3},{2,0},{3,1},{4,6},{5,7},{6,4},{7,5},{8,10},{9,11},{10,... | collective-permute-start | bytes 1327112 | tf_op jit(solution)/shard_map/ppermute | solution.py:947
  48.2 41.6 %collective-permute-start.9 = (bf16[512,768]{1,0:T(8,128)(2,1)}, bf16[512,768]{1,0:T(8,128)(2,1)}, u32[]{:S(2)}, u32[]{:S(2)}) collective-permute-start(bf16[512,768]{1,0:T(8,128)(2,1)} %slice.189), channel_id=1, source_target_pairs={{0,8},{4,12},{8,0},{12,4},{16,24},{20,28},{24,16},{28,20},{1,9},{5... | collective-permute-start | bytes 2359304 | tf_op jit(solution)/shard_map/ppermute | solution.py:947
  51.8 38.0 %collective-permute-start.10 = (bf16[512,768]{1,0:T(8,128)(2,1)}, bf16[512,768]{1,0:T(8,128)(2,1)}, u32[]{:S(2)}, u32[]{:S(2)}) collective-permute-start(bf16[512,768]{1,0:T(8,128)(2,1)} %slice.190), channel_id=1, source_target_pairs={{0,4},{4,0},{8,12},{12,8},{16,20},{20,16},{24,28},{28,24},{1,5},{5... | collective-permute-start | bytes 2359304 | tf_op jit(solution)/shard_map/ppermute | solution.py:947
  52.4 18.7 %collective-permute-start.8 = (bf16[4,48,768]{2,1,0:T(8,128)(2,1)S(1)}, bf16[4,48,768]{2,1,0:T(8,128)(2,1)S(1)}, u32[]{:S(2)}, u32[]{:S(2)}) collective-permute-start(bf16[4,48,768]{2,1,0:T(8,128)(2,1)S(1)} %pad_maximum_fusion.5), channel_id=1, source_target_pairs={{0,16},{4,20},{8,24},{12,28},{16,0},{20,4},{24,8},{28,12},{1,17},{... | collective-permute-start | bytes 884744 | tf_op jit(solution)/shard_map/ppermute | solution.py:947
  71.8 18.0 %collective-permute-start.11 = (bf16[8,48,768]{2,1,0:T(8,128)(2,1)}, bf16[8,48,768]{2,1,0:T(8,128)(2,1)}, u32[]{:S(2)}, u32[]{:S(2)}) collective-permute-start(bf16[8,48,768]{2,1,0:T(8,128)(2,1)} %constant_dynamic-update-slice_fusion.refs_0_), channel_id=1, source_target_pairs={{0,1},{1,0},{2,3},{3,2},{4,5},{5,4},{6,7},{7,6},{8,9},{9,8},{10,11... | collective-permute-start | bytes 1769480 | tf_op jit(solution)/shard_map/ppermute | solution.py:947
  89.8 50.2 %collective-permute-start.15 = (bf16[9,48,768]{2,1,0:T(8,128)(2,1)}, bf16[9,48,768]{2,1,0:T(8,128)(2,1)}, u32[]{:S(2)}, u32[]{:S(2)}) collective-permute-start(bf16[9,48,768]{2,1,0:T(8,128)(2,1)} %copy-done.26), channel_id=1, source_target_pairs={{0,8},{4,12},{8,16},{12,20},{16,24},{20,28},{24,0},{28,4},{1,9},{5... | collective-permute-start | bytes 1990664 | tf_op jit(solution)/shard_map/ppermute | solution.py:1091
  93.1 46.9 %collective-permute-start.16 = (bf16[9,48,768]{2,1,0:T(8,128)(2,1)}, bf16[9,48,768]{2,1,0:T(8,128)(2,1)}, u32[]{:S(2)}, u32[]{:S(2)}) collective-permute-start(bf16[9,48,768]{2,1,0:T(8,128)(2,1)} %copy-done.26), channel_id=1, source_target_pairs={{0,4},{4,0},{8,12},{12,8},{16,20},{20,16},{24,28},{28,24},{1,5},{5... | collective-permute-start | bytes 1990664 | tf_op jit(solution)/shard_map/ppermute | solution.py:947
  140.0 19.3 %collective-permute-start.17 = (bf16[9,48,768]{2,1,0:T(8,128)(2,1)}, bf16[9,48,768]{2,1,0:T(8,128)(2,1)S(1)}, u32[]{:S(2)}, u32[]{:S(2)}) collective-permute-start(bf16[9,48,768]{2,1,0:T(8,128)(2,1)} %collective-permute-done.15), channel_id=1, source_target_pairs={{0,8},{4,12},{8,16},{12,20},{16,24},{20,28},{24,0},{28,4},{1,9},{5... | collective-permute-start | bytes 1990664 | tf_op jit(solution)/shard_map/ppermute | solution.py:1094
  140.1 19.2 %collective-permute-start.18 = (bf16[9,48,768]{2,1,0:T(8,128)(2,1)}, bf16[9,48,768]{2,1,0:T(8,128)(2,1)S(1)}, u32[]{:S(2)}, u32[]{:S(2)}) collective-permute-start(bf16[9,48,768]{2,1,0:T(8,128)(2,1)} %collective-permute-done.15), channel_id=1, source_target_pairs={{0,4},{4,0},{8,12},{12,8},{16,20},{20,16},{24,28},{28,24},{1,5},{5... | collective-permute-start | bytes 1990664 | tf_op jit(solution)/shard_map/ppermute | solution.py:947
  159.3 32.8 %collective-permute-start.19 = (bf16[9,48,768]{2,1,0:T(8,128)(2,1)S(1)}, bf16[9,48,768]{2,1,0:T(8,128)(2,1)S(1)}, u32[]{:S(2)}, u32[]{:S(2)}) collective-permute-start(bf16[9,48,768]{2,1,0:T(8,128)(2,1)S(1)} %collective-permute-done.17), channel_id=1, source_target_pairs={{0,8},{4,12},{8,16},{12,20},{16,24},{20,28},{24,0},{28,4},{1,9},{5... | collective-permute-start | bytes 1990664 | tf_op jit(solution)/shard_map/ppermute | solution.py:1103
  159.4 33.4 %collective-permute-start.20 = (bf16[9,48,768]{2,1,0:T(8,128)(2,1)S(1)}, bf16[9,48,768]{2,1,0:T(8,128)(2,1)S(1)}, u32[]{:S(2)}, u32[]{:S(2)}) collective-permute-start(bf16[9,48,768]{2,1,0:T(8,128)(2,1)S(1)} %collective-permute-done.17), channel_id=1, source_target_pairs={{0,4},{4,0},{8,12},{12,8},{16,20},{20,16},{24,28},{28,24},{1,5},{5... | collective-permute-start | bytes 1990664 | tf_op jit(solution)/shard_map/ppermute | solution.py:947
  165.4 16.6 %collective-permute-start.21 = (bf16[1536,128]{1,0:T(8,128)(2,1)S(1)}, bf16[1536,128]{1,0:T(8,128)(2,1)S(1)}, u32[]{:S(2)}, u32[]{:S(2)}) collective-permute-start(bf16[1536,128]{1,0:T(8,128)(2,1)S(1)} %mix.4), channel_id=1, source_target_pairs={{0,4},{4,0},{8,12},{12,8},{16,20},{20,16},{24,28},{28,24},{1,5},{5... | collective-permute-start | bytes 1179656 | tf_op jit(solution)/shard_map/ppermute | solution.py:947
  172.0 12.3 %collective-permute-start.22 = (bf16[1536,128]{1,0:T(8,128)(2,1)S(1)}, bf16[1536,128]{1,0:T(8,128)(2,1)S(1)}, u32[]{:S(2)}, u32[]{:S(2)}) collective-permute-start(bf16[1536,128]{1,0:T(8,128)(2,1)S(1)} %mix.5), channel_id=1, source_target_pairs={{0,8},{4,12},{8,0},{12,4},{16,24},{20,28},{24,16},{28,20},{1,9},{5... | collective-permute-start | bytes 1179656 | tf_op jit(solution)/shard_map/ppermute | solution.py:947
  179.1 13.0 %collective-permute-start.23 = (bf16[1536,128]{1,0:T(8,128)(2,1)S(1)}, bf16[1536,128]{1,0:T(8,128)(2,1)S(1)}, u32[]{:S(2)}, u32[]{:S(2)}) collective-permute-start(bf16[1536,128]{1,0:T(8,128)(2,1)S(1)} %mix.6), channel_id=1, source_target_pairs={{0,12},{4,8},{8,4},{12,0},{16,28},{20,24},{24,20},{28,16},{1,13},{... | collective-permute-start | bytes 1179656 | tf_op jit(solution)/shard_map/ppermute | solution.py:947
  192.9 16.2 %collective-permute-start.24 = (bf16[9,48,768]{2,1,0:T(8,128)(2,1)S(1)}, bf16[9,48,768]{2,1,0:T(8,128)(2,1)S(1)}, u32[]{:S(2)}, u32[]{:S(2)}) collective-permute-start(bf16[9,48,768]{2,1,0:T(8,128)(2,1)S(1)} %collective-permute-done.19), channel_id=1, source_target_pairs={{0,4},{4,0},{8,12},{12,8},{16,20},{20,16},{24,28},{28,24},{1,5},{5... | collective-permute-start | bytes 1990664 | tf_op jit(solution)/shard_map/ppermute | solution.py:947
  195.6 13.6 %collective-permute-start.25 = (bf16[2,9,48,768]{3,2,1,0:T(8,128)(2,1)S(1)}, bf16[2,9,48,768]{3,2,1,0:T(8,128)(2,1)S(1)}, u32[]{:S(2)}, u32[]{:S(2)}) collective-permute-start(bf16[2,9,48,768]{3,2,1,0:T(8,128)(2,1)S(1)} %pad_maximum_fusion.refs_0_), channel_id=1, source_target_pairs={{0,1},{1,0},{2,3},{3,2},{4,5},{5,4},{6,7},{7,6},{8,9},{9,8},{10,11... | collective-permute-start | bytes 3981320 | tf_op jit(solution)/shard_map/ppermute | solution.py:947
  197.3 11.9 %collective-permute-start.26 = (bf16[2,9,48,768]{3,2,1,0:T(8,128)(2,1)S(1)}, bf16[2,9,48,768]{3,2,1,0:T(8,128)(2,1)S(1)}, u32[]{:S(2)}, u32[]{:S(2)}) collective-permute-start(bf16[2,9,48,768]{3,2,1,0:T(8,128)(2,1)S(1)} %pad_maximum_fusion.1.refs_1_), channel_id=1, source_target_pairs={{0,1},{1,0},{2,3},{3,2},{4,5},{5,4},{6,7},{7,6},{8,9},{9,8},{10,11... | collective-permute-start | bytes 3981320 | tf_op jit(solution)/shard_map/ppermute | solution.py:947
  212.3 80.8 %collective-permute-start.29 = (bf16[768,768]{1,0:T(8,128)(2,1)}, bf16[768,768]{1,0:T(8,128)(2,1)}, u32[]{:S(2)}, u32[]{:S(2)}) collective-permute-start(bf16[768,768]{1,0:T(8,128)(2,1)} %assemble.1.weight_ref), channel_id=1, source_target_pairs={{0,4},{4,0},{8,12},{12,8},{16,20},{20,16},{24,28},{28,24},{1,5},{5... | collective-permute-start | bytes 3538952 | tf_op jit(solution)/shard_map/ppermute | solution.py:947
  214.0 79.1 %collective-permute-start.30 = (bf16[768,768]{1,0:T(8,128)(2,1)}, bf16[768,768]{1,0:T(8,128)(2,1)}, u32[]{:S(2)}, u32[]{:S(2)}) collective-permute-start(bf16[768,768]{1,0:T(8,128)(2,1)} %assemble.1.weight_ref), channel_id=1, source_target_pairs={{0,8},{4,12},{8,0},{12,4},{16,24},{20,28},{24,16},{28,20},{1,9},{5... | collective-permute-start | bytes 3538952 | tf_op jit(solution)/shard_map/ppermute | solution.py:947
  214.0 79.1 %collective-permute-start.31 = (bf16[768,768]{1,0:T(8,128)(2,1)}, bf16[768,768]{1,0:T(8,128)(2,1)}, u32[]{:S(2)}, u32[]{:S(2)}) collective-permute-start(bf16[768,768]{1,0:T(8,128)(2,1)} %assemble.1.weight_ref), channel_id=1, source_target_pairs={{0,12},{4,8},{8,4},{12,0},{16,28},{20,24},{24,20},{28,16},{1,13},{... | collective-permute-start | bytes 3538952 | tf_op jit(solution)/shard_map/ppermute | solution.py:947
  293.2 14.5 %collective-permute-start.33 = (bf16[1536,128]{1,0:T(8,128)(2,1)}, bf16[1536,128]{1,0:T(8,128)(2,1)S(1)}, u32[]{:S(2)}, u32[]{:S(2)}) collective-permute-start(bf16[1536,128]{1,0:T(8,128)(2,1)} %get-tuple-element.200), channel_id=1, source_target_pairs={{0,4},{4,0},{8,12},{12,8},{16,20},{20,16},{24,28},{28,24},{1,5},{5... | collective-permute-start | bytes 1179656 | tf_op jit(solution)/shard_map/ppermute | solution.py:947
  295.0 12.7 %collective-permute-start.34 = (bf16[1536,128]{1,0:T(8,128)(2,1)}, bf16[1536,128]{1,0:T(8,128)(2,1)S(1)}, u32[]{:S(2)}, u32[]{:S(2)}) collective-permute-start(bf16[1536,128]{1,0:T(8,128)(2,1)} %get-tuple-element.201), channel_id=1, source_target_pairs={{0,8},{4,12},{8,0},{12,4},{16,24},{20,28},{24,16},{28,20},{1,9},{5... | collective-permute-start | bytes 1179656 | tf_op jit(solution)/shard_map/ppermute | solution.py:947
  295.1 19.5 %collective-permute-start.35 = (bf16[1536,128]{1,0:T(8,128)(2,1)}, bf16[1536,128]{1,0:T(8,128)(2,1)S(1)}, u32[]{:S(2)}, u32[]{:S(2)}) collective-permute-start(bf16[1536,128]{1,0:T(8,128)(2,1)} %get-tuple-element.202), channel_id=1, source_target_pairs={{0,12},{4,8},{8,4},{12,0},{16,28},{20,24},{24,20},{28,16},{1,13},{... | collective-permute-start | bytes 1179656 | tf_op jit(solution)/shard_map/ppermute | solution.py:947
  314.5 44.8 %collective-permute-start.36 = (bf16[8,3,48,384]{3,2,1,0:T(8,128)(2,1)}, bf16[8,3,48,384]{3,2,1,0:T(8,128)(2,1)}, u32[]{:S(2)}, u32[]{:S(2)}) collective-permute-start(bf16[8,3,48,384]{3,2,1,0:T(8,128)(2,1)} %fusion.5), channel_id=1, source_target_pairs={{0,2},{1,3},{2,0},{3,1},{4,6},{5,7},{6,4},{7,5},{8,10},{9,11},{10,... | collective-permute-start | bytes 2654216 | tf_op jit(solution)/shard_map/ppermute | solution.py:947
  316.0 46.3 %collective-permute-start.37 = (bf16[8,3,48,384]{3,2,1,0:T(8,128)(2,1)}, bf16[8,3,48,384]{3,2,1,0:T(8,128)(2,1)}, u32[]{:S(2)}, u32[]{:S(2)}) collective-permute-start(bf16[8,3,48,384]{3,2,1,0:T(8,128)(2,1)} %fusion.6), channel_id=1, source_target_pairs={{0,4},{4,0},{8,12},{12,8},{16,20},{20,16},{24,28},{28,24},{1,5},{5... | collective-permute-start | bytes 2654216 | tf_op jit(solution)/shard_map/ppermute | solution.py:947
  317.8 46.8 %collective-permute-start.38 = (bf16[8,3,48,384]{3,2,1,0:T(8,128)(2,1)S(1)}, bf16[8,3,48,384]{3,2,1,0:T(8,128)(2,1)}, u32[]{:S(2)}, u32[]{:S(2)}) collective-permute-start(bf16[8,3,48,384]{3,2,1,0:T(8,128)(2,1)S(1)} %fusion.7), channel_id=1, source_target_pairs={{0,8},{4,12},{8,0},{12,4},{16,24},{20,28},{24,16},{28,20},{1,9},{5... | collective-permute-start | bytes 2654216 | tf_op jit(solution)/shard_map/ppermute | solution.py:947
  367.4 16.3 %collective-permute-start.39 = (bf16[4,3,48,384]{3,2,1,0:T(8,128)(2,1)}, bf16[4,3,48,384]{3,2,1,0:T(8,128)(2,1)S(1)}, u32[]{:S(2)}, u32[]{:S(2)}) collective-permute-start(bf16[4,3,48,384]{3,2,1,0:T(8,128)(2,1)} %slice.333), channel_id=1, source_target_pairs={{0,4},{4,0},{8,12},{12,8},{16,20},{20,16},{24,28},{28,24},{1,5},{5... | collective-permute-start | bytes 1327112 | tf_op jit(solution)/shard_map/ppermute | solution.py:947
  368.1 22.1 %collective-permute-start.40 = (bf16[4,3,48,384]{3,2,1,0:T(8,128)(2,1)}, bf16[4,3,48,384]{3,2,1,0:T(8,128)(2,1)}, u32[]{:S(2)}, u32[]{:S(2)}) collective-permute-start(bf16[4,3,48,384]{3,2,1,0:T(8,128)(2,1)} %slice.332), channel_id=1, source_target_pairs={{0,8},{4,12},{8,0},{12,4},{16,24},{20,28},{24,16},{28,20},{1,9},{5... | collective-permute-start | bytes 1327112 | tf_op jit(solution)/shard_map/ppermute | solution.py:947
  369.4 23.4 %collective-permute-start.41 = (bf16[4,3,48,384]{3,2,1,0:T(8,128)(2,1)}, bf16[4,3,48,384]{3,2,1,0:T(8,128)(2,1)}, u32[]{:S(2)}, u32[]{:S(2)}) collective-permute-start(bf16[4,3,48,384]{3,2,1,0:T(8,128)(2,1)} %slice.331), channel_id=1, source_target_pairs={{0,16},{4,20},{8,24},{12,28},{16,0},{20,4},{24,8},{28,12},{1,17},{... | collective-permute-start | bytes 1327112 | tf_op jit(solution)/shard_map/ppermute | solution.py:947
  381.5 55.3 %collective-permute-start.45 = (bf16[1024,768]{1,0:T(8,128)(2,1)}, bf16[1024,768]{1,0:T(8,128)(2,1)}, u32[]{:S(2)}, u32[]{:S(2)}) collective-permute-start(bf16[1024,768]{1,0:T(8,128)(2,1)} %gather_grads.7.refs_3_), channel_id=1, source_target_pairs={{0,12},{4,8},{8,4},{12,0},{16,28},{20,24},{24,20},{28,16},{1,13},{... | collective-permute-start | bytes 4718600 | tf_op jit(solution)/shard_map/ppermute | solution.py:947
  394.7 36.6 %collective-permute-start.42 = (bf16[2,3,48,384]{3,2,1,0:T(8,128)(2,1)}, bf16[2,3,48,384]{3,2,1,0:T(8,128)(2,1)}, u32[]{:S(2)}, u32[]{:S(2)}) collective-permute-start(bf16[2,3,48,384]{3,2,1,0:T(8,128)(2,1)} %slice.336), channel_id=1, source_target_pairs={{0,8},{4,12},{8,0},{12,4},{16,24},{20,28},{24,16},{28,20},{1,9},{5... | collective-permute-start | bytes 663560 | tf_op jit(solution)/shard_map/ppermute | solution.py:947
  394.7 38.5 %collective-permute-start.43 = (bf16[2,3,48,384]{3,2,1,0:T(8,128)(2,1)}, bf16[2,3,48,384]{3,2,1,0:T(8,128)(2,1)}, u32[]{:S(2)}, u32[]{:S(2)}) collective-permute-start(bf16[2,3,48,384]{3,2,1,0:T(8,128)(2,1)} %slice.335), channel_id=1, source_target_pairs={{0,16},{4,20},{8,24},{12,28},{16,0},{20,4},{24,8},{28,12},{1,17},{... | collective-permute-start | bytes 663560 | tf_op jit(solution)/shard_map/ppermute | solution.py:947
  396.0 39.1 %collective-permute-start.44 = (bf16[2,3,48,384]{3,2,1,0:T(8,128)(2,1)}, bf16[2,3,48,384]{3,2,1,0:T(8,128)(2,1)}, u32[]{:S(2)}, u32[]{:S(2)}) collective-permute-start(bf16[2,3,48,384]{3,2,1,0:T(8,128)(2,1)} %slice.334), channel_id=1, source_target_pairs={{0,2},{1,3},{2,0},{3,1},{4,6},{5,7},{6,4},{7,5},{8,10},{9,11},{10,... | collective-permute-start | bytes 663560 | tf_op jit(solution)/shard_map/ppermute | solution.py:947
  440.4 12.2 %collective-permute-start.48 = (bf16[3,96,384]{2,1,0:T(8,128)(2,1)S(1)}, bf16[3,96,384]{2,1,0:T(8,128)(2,1)S(1)}, u32[]{:S(2)}, u32[]{:S(2)}) collective-permute-start(bf16[3,96,384]{2,1,0:T(8,128)(2,1)S(1)} %fusion.8), channel_id=1, source_target_pairs={{0,16},{4,20},{8,24},{12,28},{16,0},{20,4},{24,8},{28,12},{1,17},{... | collective-permute-start | bytes 663560 | tf_op jit(solution)/shard_map/ppermute | solution.py:947
  440.8 11.8 %collective-permute-start.49 = (f32[12,768]{1,0:T(8,128)S(1)}, f32[12,768]{1,0:T(8,128)S(1)}, u32[]{:S(2)}, u32[]{:S(2)}) collective-permute-start(f32[12,768]{1,0:T(8,128)S(1)} %add.164), channel_id=1, source_target_pairs={{0,2},{1,3},{2,0},{3,1},{4,6},{5,7},{6,4},{7,5},{8,10},{9,11},{10,... | collective-permute-start | bytes 110600 | tf_op jit(solution)/shard_map/ppermute | solution.py:947
  453.2 73.5 %collective-permute-start.57 = (bf16[1024,768]{1,0:T(8,128)(2,1)}, bf16[1024,768]{1,0:T(8,128)(2,1)}, u32[]{:S(2)}, u32[]{:S(2)}) collective-permute-start(bf16[1024,768]{1,0:T(8,128)(2,1)} %gather_grads.6.refs_1_), channel_id=1, source_target_pairs={{0,4},{4,0},{8,12},{12,8},{16,20},{20,16},{24,28},{28,24},{1,5},{5... | collective-permute-start | bytes 4718600 | tf_op jit(solution)/shard_map/ppermute | solution.py:947
  454.7 72.0 %collective-permute-start.58 = (bf16[1024,768]{1,0:T(8,128)(2,1)}, bf16[1024,768]{1,0:T(8,128)(2,1)}, u32[]{:S(2)}, u32[]{:S(2)}) collective-permute-start(bf16[1024,768]{1,0:T(8,128)(2,1)} %gather_grads.4.refs_2_), channel_id=1, source_target_pairs={{0,8},{4,12},{8,0},{12,4},{16,24},{20,28},{24,16},{28,20},{1,9},{5... | collective-permute-start | bytes 4718600 | tf_op jit(solution)/shard_map/ppermute | solution.py:947
  454.7 37.3 %collective-permute-start.53 = (bf16[1,3,48,384]{3,2,1,0:T(8,128)(2,1)S(1)}, bf16[1,3,48,384]{3,2,1,0:T(8,128)(2,1)S(1)}, u32[]{:S(2)}, u32[]{:S(2)}) collective-permute-start(bf16[1,3,48,384]{3,2,1,0:T(8,128)(2,1)S(1)} %copy-done.67), channel_id=1, source_target_pairs={{0,16},{4,20},{8,24},{12,28},{16,0},{20,4},{24,8},{28,12},{1,17},{... | collective-permute-start | bytes 331784 | tf_op jit(solution)/shard_map/ppermute | solution.py:947
  456.7 33.8 %collective-permute-start.51 = (f32[12,768]{1,0:T(8,128)S(1)}, f32[12,768]{1,0:T(8,128)S(1)}, u32[]{:S(2)}, u32[]{:S(2)}) collective-permute-start(f32[12,768]{1,0:T(8,128)S(1)} %add.166), channel_id=1, source_target_pairs={{0,4},{4,0},{8,12},{12,8},{16,20},{20,16},{24,28},{28,24},{1,5},{5... | collective-permute-start | bytes 110600 | tf_op jit(solution)/shard_map/ppermute | solution.py:947
  490.6 14.5 %collective-permute-start.52 = (bf16[3,96,384]{2,1,0:T(8,128)(2,1)}, bf16[3,96,384]{2,1,0:T(8,128)(2,1)}, u32[]{:S(2)}, u32[]{:S(2)}) collective-permute-start(bf16[3,96,384]{2,1,0:T(8,128)(2,1)} %add_convert_fusion), channel_id=1, source_target_pairs={{0,1},{1,0},{2,3},{3,2},{4,5},{5,4},{6,7},{7,6},{8,9},{9,8},{10,11... | collective-permute-start | bytes 663560 | tf_op jit(solution)/shard_map/ppermute | solution.py:947
  500.9 12.2 %all-to-all-start = ((bf16[4,3,48,384]{3,2,1,0:T(8,128)(2,1)}), bf16[4,3,48,384]{3,2,1,0:T(8,128)(2,1)}, u32[]{:S(2)}, u32[]{:S(2)}) async-start(bf16[4,3,48,384]{3,2,1,0:T(8,128)(2,1)} %copy-done.18), calls=%async_computation | async-start | bytes 884736 | tf_op jit(solution)/shard_map/all_to_all | solution.py:1173
  519.2 20.2 %all-to-all-start.1 = ((bf16[8,3,96,96]{3,2,1,0:T(8,128)(2,1)}), bf16[8,3,96,96]{3,2,1,0:T(8,128)(2,1)}, u32[]{:S(2)}, u32[]{:S(2)}) async-start(bf16[8,3,96,96]{3,2,1,0:T(8,128)(2,1)} %copy-done.16), calls=%async_computation.1 | async-start | bytes 1179648 | tf_op jit(solution)/shard_map/all_to_all | solution.py:1190
  554.1 22.4 %all-to-all-start.2 = ((bf16[8,3,96,96]{3,2,1,0:T(8,128)(2,1)}), bf16[8,3,96,96]{3,2,1,0:T(8,128)(2,1)}, u32[]{:S(2)}, u32[]{:S(2)}) async-start(bf16[8,3,96,96]{3,2,1,0:T(8,128)(2,1)} %copy-done.28), calls=%async_computation.2 | async-start | bytes 1179648 | tf_op jit(solution)/shard_map/all_to_all | solution.py:1190
  559.2 17.4 %collective-permute-start.59 = (f32[12,768]{1,0:T(8,128)S(1)}, f32[12,768]{1,0:T(8,128)}, u32[]{:S(2)}, u32[]{:S(2)}) collective-permute-start(f32[12,768]{1,0:T(8,128)S(1)} %add.172), channel_id=1, source_target_pairs={{0,16},{4,20},{8,24},{12,28},{16,0},{20,4},{24,8},{28,12},{1,17},{... | collective-permute-start | bytes 110600 | tf_op jit(solution)/shard_map/ppermute | solution.py:947
  581.6 19.2 %all-to-all-start.3 = ((bf16[8,3,96,96]{3,2,1,0:T(8,128)(2,1)}), bf16[8,3,96,96]{3,2,1,0:T(8,128)(2,1)S(1)}, u32[]{:S(2)}, u32[]{:S(2)}) async-start(bf16[8,3,96,96]{3,2,1,0:T(8,128)(2,1)} %copy-done.17), calls=%async_computation.3 | async-start | bytes 1179648 | tf_op jit(solution)/shard_map/all_to_all | solution.py:1190
  (90 other events, 569.6 us)

commit v6 on v5

--- a/solution.py
+++ b/solution.py
@@ -1050,12 +1050,13 @@
     start_of_middle = jnp.max(jnp.where(item_starts <= middle, item_starts, 0))
     is_long = (start_of_middle <= unit_start).astype(jnp.int32).reshape(1)
     share = CLUSTER // UNIT * (2 - is_long)
-    orders = exchange_unit(places(jnp.concatenate([share, member.reshape(1)]), clusters[0]))
+    placed = places(jnp.concatenate([share, member.reshape(1)]), clusters[0])
     left, right = doubled(bases[0]), doubled(bases[1])
-    (over, left, right) = together(over, left, right)
+    (over, left, right, placed) = together(over, left, right, placed)
     across = swap(over, "grp", 1)
 
-    (near, far, beside, over, across) = together(near, far, beside, over, across)
+    orders = exchange_unit(placed)
+    (near, far, beside, over, across, orders) = together(near, far, beside, over, across, orders)
     part_rows = rows_dev // 2
 
     scalars = jnp.concatenate([block_slot, jnp.stack([grp, core, member])]).astype(jnp.int32)
@@ -1070,7 +1071,7 @@
     sources = tok ^ jnp.arange(2 * UNIT, dtype=jnp.int32)
     cores = core ^ jnp.arange(2, dtype=jnp.int32)
     firsts = (sources[None, :] * rows_dev + cores[:, None] * part_rows).reshape(-1)
-    (third, others_all, rest_rows, orders) = together(third, others_all, rest_rows, orders)
+    (third, others_all, rest_rows) = together(third, others_all, rest_rows)
     own_weights = assemble(firsts, [mine_all, others_all])
 
     def columns_of(value, m):
@@ -1079,39 +1080,51 @@
     own_bias = split_heads(
         [columns_of(vectors[4], member), jnp.zeros((own_width,), F32), columns_of(vectors[5], member)]
     ).reshape(1, -1)
-    grouped = [
-        sort_rows(orders[k], value, own_weights, own_bias) for k, value in enumerate((inputs, near, far))
-    ]
+    ring = [(i, (i + 2) % n_tok) for i in range(n_tok)]
+    depth = n_tok // 2
+    steps, flips, mine_rest, other_rest = [rest_rows], [], [], []
+
+    def advance():
+        if len(steps) < depth:
+            steps.append(lax.ppermute(steps[-1], "tok", ring))
+        flips.append(swap(steps[len(flips)], "tok", 1))
+
+    def cross():
+        k = len(mine_rest)
+        mine_rest.append(jnp.stack([steps[k], flips[k]]))
+        other_rest.append(swap(mine_rest[k], "grp", 1))
+
+    advance()
+    grouped = [sort_rows(orders[0], inputs, own_weights, own_bias)]
+    grouped.append(sort_rows(orders[1], near, own_weights, own_bias))
+    (grouped, far, third, steps[1], flips[0]) = together(grouped, far, third, steps[1], flips[0])
+    advance()
+    cross()
+    grouped.append(sort_rows(orders[2], far, own_weights, own_bias))
     unit_inputs = [inputs, near, far, jnp.concatenate(third, axis=0)]
     grouped.append(sort_rows(orders[3], unit_inputs[3], own_weights, own_bias))
-
-    ring = [(i, (i + 2) % n_tok) for i in range(n_tok)]
-    depth = n_tok // 2
-    steps, flips = [rest_rows], []
-    steps.append(lax.ppermute(steps[0], "tok", ring))
-    flips.append(swap(steps[0], "tok", 1))
-    (grouped, steps[1], flips[0]) = together(grouped, steps[1], flips[0])
-    steps.append(lax.ppermute(steps[1], "tok", ring))
-    flips.append(swap(steps[1], "tok", 1))
+    (grouped, steps[2], flips[1], other_rest) = together(grouped, steps[2], flips[1], other_rest)
+    advance()
+    cross()
     sorted_out = attend(is_long, grouped)
-    (sorted_out, steps[2], flips[1]) = together(sorted_out, steps[2], flips[1])
+    (sorted_out, steps[3], flips[2], other_rest) = together(sorted_out, steps[3], flips[2], other_rest)
+    advance()
+    cross()
     mixed = [None] * UNIT
     mixed[3] = mix(orders[3], sorted_out[3])
     mixed[2] = mix(orders[2], sorted_out[2])
     mixed[1] = mix(orders[1], sorted_out[1])
     mixed_parts = exchange_unit(mixed)
-    steps.append(lax.ppermute(steps[2], "tok", ring))
-    flips.append(swap(steps[2], "tok", 1))
-    (steps[3], flips[2], mixed_parts[1:]) = together(steps[3], flips[2], mixed_parts[1:])
-    flips.append(swap(steps[3], "tok", 1))
+    (mixed_parts[1:], flips[-1], other_rest, held_weights) = together(
+        mixed_parts[1:], flips[-1], other_rest, own_weights
+    )
+    cross()
     mixed_parts[0] = mix(orders[0], sorted_out[0])
-    mine_rest = [jnp.stack([steps[k], flips[k]]) for k in range(depth)]
-    shards = mine_rest + [swap(m, "grp", 1) for m in mine_rest]
+    shards = mine_rest + other_rest
     sources = (tok + n_tok - 2 * jnp.arange(depth, dtype=jnp.int32)) & (n_tok - 1)
     sources = (sources[:, None] ^ jnp.arange(2, dtype=jnp.int32)[None, :]).reshape(-1)
     firsts = (sources[None, :] * rows_dev + cores[:, None] * part_rows).reshape(-1)
 
-    held_weights, *shards = lax.optimization_barrier((own_weights, *shards))
     turned_weights = [swap(held_weights, "tok", k) for k in range(1, UNIT)]
     place_bits = jnp.stack([member, core, bit_x, tok & 1, (tok >> 1) & 1, tok >> 2]).astype(jnp.int32)
     table = jnp.concatenate([place_bits, firsts])
@@ -1163,7 +1176,7 @@
 
     more = swap(total, "grp", 1)
     keep = kept_qkv.astype(F32) + swap(sent_qkv, "grp", 1).astype(F32)
-    (keep, more) = together(keep, more)
+    (keep, more, got_now) = together(keep, more, got_now)
     total = total + more
     more = swap(total, "grp", 2)
     unit_got = swap(keep[1].astype(BF16), "tok", UNIT)
@@ -1174,11 +1187,7 @@
     keep = keep[0] + unit_got.astype(F32)
     (keep, more) = together(keep, more)
     total = total + more
-    more = swap(total, "tok", 1)
-    keep = keep + swap(keep.astype(BF16), "grp", 2).astype(F32)
-    (keep, more) = together(keep.astype(BF16), more)
-    total = total + more
-    more = swap(total, "tok", 2)
+    keep = (keep + swap(keep.astype(BF16), "grp", 2).astype(F32)).astype(BF16)
     kept_core = (keep, swap(keep, "grp", 1))
     keep = jnp.concatenate(
         [jnp.where(core == 0, kept_core[0], kept_core[1]), jnp.where(core == 0, kept_core[1], kept_core[0])],
@@ -1190,22 +1199,24 @@
         return lax.all_to_all(value, "tok", split_axis=0, concat_axis=0, tiled=True)
 
     part = to_tok(rotate_in(mine, keep, got, left, n_tok))
-    (part, more, home_grads) = together(part, more, [own_grads[0]] + home_grads[1:])
-    total = total + more
-    more = swap(total, "tok", 4)
+    grad_inputs = grad_first + outer_cols(own_grads[0], own_weights)
+    (part, home_grads, grad_inputs) = together(part, home_grads[1:], grad_inputs)
+    more = swap(total, "tok", 1)
     by_slot_of = lambda value: jnp.transpose(value, (1, 0, 2))
     new_one, new_two, turned = moments(
         place, part, right, by_slot_of(moment_one), by_slot_of(moment_two)
     )
     turned = to_tok(turned)
-    (turned, more) = together(turned, more)
-    vector_total = total + more
+    grad_inputs = grad_inputs + outer_cols(home_grads[0], turned_weights[0])
+    grad_inputs = grad_inputs + outer_cols(home_grads[1], turned_weights[1])
+    (turned, more, grad_inputs, home_grads[2]) = together(turned, more, grad_inputs, home_grads[2])
+    total = total + more
+    total = total + swap(total, "tok", 2)
     change = to_tok(rotate_out(turned, left))
+    vector_total = total + swap(total, "tok", 4)
     new_master = by_slot_of(apply_change(place, change, by_slot_of(master)))
     new_one, new_two = by_slot_of(new_one), by_slot_of(new_two)
-    grad_inputs = grad_first + sum(
-        outer_cols(home_grads[k], own_weights if k == 0 else turned_weights[k - 1]) for k in range(UNIT)
-    )
+    grad_inputs = grad_inputs + outer_cols(home_grads[2], turned_weights[2])
     new_vec_one = BETA_ONE * vector_one + (1.0 - BETA_ONE) * vector_total
     new_vec_two = BETA_TWO * vector_two + (1.0 - BETA_TWO) * vector_total * vector_total
     new_vectors = vectors - RATE_VECTOR * new_vec_one / (jnp.sqrt(new_vec_two) + ADAM_EPS)

time: 612 us -> 562 us (0.918)
  waiting for transfers between devices: 152 us -> 105 us
  starting transfers between devices: 82.6 us -> 89.4 us
  local copies, waits for them, and re-layouts: 54.3 us -> 60.8 us
    ppermute x57, waiting for transfers between devices: 135 us -> 84.4 us  [swap(): return lax.ppermute(value, axis, [(i, i ^ bit) for i in range(size)])]
    unnamed x153 -> x167, local copies, waits for them, and re-layouts: 31.3 us -> 37.9 us
    broadcast_in_dim x1, other arithmetic: 8.27 us -> 2.05 us  [fast(): grad_inputs[None]]
  transfers between devices with their start and end apart: 64 -> 64, of which waited for: 22 -> 18; matrix products, arithmetic and copies ran while one was open for 16% -> 15% of each run, Pallas kernels for 36% -> 40%
where the time goes in v6:
time: 562 us; the launch traced here: 554 us
  Pallas kernels  231 us (41%)
  waiting for transfers between devices  105 us (19%)
  starting transfers between devices  89.4 us (16%)
  local copies, waits for them, and re-layouts  60.8 us (11%)
  other arithmetic  51.1 us (9%)
  matrix products  14.8 us (3%)
    ppermute x57, waiting for transfers between devices, swap(): return lax.ppermute(value, axis, [(i, i ^ bit) for i in range(size)])  84.4 us
    pallas_call x1, Pallas kernels, layer(): pl.pallas_call(functools.partial(layer_body, n_shards), in_specs=[pl.Bloc...  69.8 us
    ppermute x57, starting transfers between devices, swap(): return lax.ppermute(value, axis, [(i, i ^ bit) for i in range(size)])  67.1 us
    unnamed x167, local copies, waits for them, and re-layouts  37.9 us
    pallas_call x4, Pallas kernels, sort_rows(): pl.pallas_call(sort_body, grid=(HEADS_OWN,), in_specs=[pl.BlockSpec((8, c...  27.7 us
    pallas_call x4, Pallas kernels, gather_grads(): pl.pallas_call(gather_grads_body, grid=(HEADS_OWN,), in_specs=[pl.BlockSp...  21 us
    pallas_call x1, Pallas kernels, attend_back(): pl.pallas_call(attend_back_body, grid_spec=pltpu.PrefetchScalarGridSpec(n...  18.9 us
    pallas_call x4, Pallas kernels, mix(): pl.pallas_call(mix_body, grid=(HEADS_OWN,), in_specs=[pl.BlockSpec((8, co...  17.9 us
  transfers between devices with their start and end apart: 64, of which 18 were waited for; matrix products, arithmetic and copies ran while one was open for 15% of the time, Pallas kernels for 40%

profile of v6, /device:TPU:0, one launch (start us, length us, event | category | flops | bytes accessed | tf_op | source)
XLA Modules:
  0.0 554.5 jit_solution(5020741367233345725)
XLA Ops:
  8.8 14.8 %fusion = (bf16[3,768,768]{2,1,0:T(8,128)(2,1)}, bf16[3,768,768]{2,1,0:T(8,128)(2,1)}, bf16[3,768,768]{2,1,0:T(8,128)(2,1)}, bf16[3,768,768]{2,1,0:T(8,128)(2,1)S(1)}) fusion(f32[2,3,768,768]{3,2,1,0:T(8,128)} %param.18), kind=kLoop, calls=%fused_computation.2 | loop fusion | flops 10616832 | bytes 35389440 | tf_op jit(solution)/shard_map/convert_element_type | solution.py:1002
  25.6 6.9 %places.1 = (s32[8,1024]{1,0:T(8,128)}, s32[8,1024]{1,0:T(8,128)}, s32[8,1024]{1,0:T(8,128)}, s32[8,1024]{1,0:T(8,128)}) custom-call(s32[2]{0:T(128)} %get-tuple-element.310.scalars_ref, s32[24,1024]{1,0:T(8,128)} %bitcast.127), custom_call_target="tpu_custom_call" | custom-call | tf_op jit(solution)/shard_map/places/pallas_call | solution.py:96
  63.1 12.9 %collective-permute-done.13 = bf16[4,48,768]{2,1,0:T(8,128)(2,1)S(1)} collective-permute-done((bf16[4,48,768]{2,1,0:T(8,128)(2,1)S(1)}, bf16[4,48,768]{2,1,0:T(8,128)(2,1)S(1)}, u32[]{:S(2)}, u32[]{:S(2)}) %collective-permute-start.13) | collective-permute-done | bytes 294944 | tf_op jit(solution)/shard_map/ppermute | solution.py:947
  79.1 3.9 collective-permute-start.15
  93.3 6.5 %sort_rows.4.refs_0_ = bf16[6,1024,256]{2,1,0:T(8,128)(2,1)S(1)} custom-call(s32[8,1024]{1,0:T(8,128)S(1)} %copy-done.29, bf16[1024,768]{1,0:T(8,128)(2,1)S(1)} %bitcast.111, bf16[768,768]{1,0:T(8,128)(2,1)} %assemble.1.weight_ref, f32[1,768]{1,0:T(1,128)S(1)} %reshape.107.bias_ref), custom_call_target="tpu_custom_call" | custom-call | tf_op jit(solution)/shard_map/sort_rows/pallas_call | solution.py:221
  101.5 7.2 %sort_rows.5.refs_1_ = bf16[6,1024,256]{2,1,0:T(8,128)(2,1)S(1)} custom-call(s32[8,1024]{1,0:T(8,128)} %collective-permute-done.5.place_ref, bf16[1024,768]{1,0:T(8,128)(2,1)} %collective-permute-done.x_ref.refs_5_, bf16[768,768]{1,0:T(8,128)(2,1)} %assemble.1.weight_ref, f32[1,768]{1,0:T(1,128)S(1)} %reshape.107.bias_ref), custom_call_target="tpu_custom_call" | custom-call | tf_op jit(solution)/shard_map/sort_rows/pallas_call | solution.py:221
  113.2 7.1 %sort_rows.6.refs_2_ = bf16[6,1024,256]{2,1,0:T(8,128)(2,1)S(1)} custom-call(s32[8,1024]{1,0:T(8,128)S(1)} %copy-done.33, bf16[1024,768]{1,0:T(8,128)(2,1)} %collective-permute-done.1.x_ref.refs_6_, bf16[768,768]{1,0:T(8,128)(2,1)} %assemble.1.weight_ref, f32[1,768]{1,0:T(1,128)S(1)} %reshape.107.bias_ref), custom_call_target="tpu_custom_call" | custom-call | tf_op jit(solution)/shard_map/sort_rows/pallas_call | solution.py:221
  124.4 6.9 %sort_rows.7.refs_3_ = bf16[6,1024,256]{2,1,0:T(8,128)(2,1)S(1)} custom-call(s32[8,1024]{1,0:T(8,128)S(1)} %copy-done.36, bf16[1024,768]{1,0:T(8,128)(2,1)S(1)} %constant_dynamic-update-slice_fusion.5.x_ref.refs_7_, bf16[768,768]{1,0:T(8,128)(2,1)} %assemble.1.weight_ref, f32[1,768]{1,0:T(1,128)S(1)} %reshape.107.bias_ref), custom_call_target="tpu_custom_call" | custom-call | tf_op jit(solution)/shard_map/sort_rows/pallas_call | solution.py:221
  136.3 16.5 %attend.1 = (bf16[6,1024,128]{2,1,0:T(8,128)(2,1)S(1)}, bf16[6,1024,128]{2,1,0:T(8,128)(2,1)S(1)}, bf16[6,1024,128]{2,1,0:T(8,128)(2,1)S(1)}, bf16[6,1024,128]{2,1,0:T(8,128)(2,1)}) custom-call(s32[1]{0:T(128)} %bitcast.11.long_ref, bf16[6,1024,256]{2,1,0:T(8,128)(2,1)} %copy-done, bf16[6,1024,256]{2,1,0:T(8,128)(2,1)} %copy-done.1, ...), custom_call_target="tpu_custom_call" | custom-call | tf_op jit(solution)/shard_map/attend/pallas_call | solution.py:345
  156.8 5.0 mix.4
  162.7 4.2 mix.5
  167.5 4.4 mix.6
  174.2 15.3 %collective-permute-done.23.refs_9_ = bf16[1536,128]{1,0:T(8,128)(2,1)S(1)} collective-permute-done((bf16[1536,128]{1,0:T(8,128)(2,1)S(1)}, bf16[1536,128]{1,0:T(8,128)(2,1)S(1)}, u32[]{:S(2)}, u32[]{:S(2)}) %collective-permute-start.23) | collective-permute-done | bytes 393248 | tf_op jit(solution)/shard_map/ppermute | solution.py:947
  198.3 4.2 mix.7.refs_8_
  203.3 69.8 %layer.1 = (bf16[1024,768]{1,0:T(8,128)(2,1)}, f32[1024,768]{1,0:T(8,128)}, f32[16,768]{1,0:T(8,128)}, bf16[3,16,3,48,384]{4,3,2,1,0:T(8,128)(2,1)}, bf16[3,16,3...) custom-call(s32[22]{0:T(128)} %concatenate.28.table_ref, ...), custom_call_target="tpu_custom_call" | custom-call | tf_op jit(solution)/shard_map/layer/pallas_call | solution.py:713
  276.8 5.4 collective-permute-done.32
  287.7 6.8 %collective-permute-done.35.rows_ref = bf16[1536,128]{1,0:T(8,128)(2,1)S(1)} collective-permute-done((bf16[1536,128]{1,0:T(8,128)(2,1)}, bf16[1536,128]{1,0:T(8,128)(2,1)S(1)}, u32[]{:S(2)}, u32[]{:S(2)}) %collective-permute-start.35) | collective-permute-done | bytes 393248 | tf_op jit(solution)/shard_map/ppermute | solution.py:947
  297.8 3.8 sort_grads.4.refs_4_
  302.8 4.6 sort_grads.5.refs_5_
  308.6 4.2 sort_grads.6.refs_6_
  313.9 3.8 sort_grads.7.refs_7_
  318.9 18.9 %attend_back.1 = (bf16[6,1024,256]{2,1,0:T(8,128)(2,1)}, bf16[6,1024,256]{2,1,0:T(8,128)(2,1)}, bf16[6,1024,256]{2,1,0:T(8,128)(2,1)}, bf16[6,1024,256]{2,1,0:T(8,128)(2,1)}) custom-call(s32[1]{0:T(128)} %bitcast.11.long_ref, bf16[6,1024,256]{2,1,0:T(8,128)(2,1)} %copy-done, bf16[6,1024,256]{2,1,0:T(8,128)(2,1)} %copy-done.1, ...), custom_call_target="tpu_custom_call" | custom-call | tf_op jit(solution)/shard_map/attend_back/pallas_call | solution.py:389
  348.3 4.8 collective-permute-start.41
  353.1 5.3 gather_grads.4.refs_2_
  358.4 5.1 gather_grads.7.refs_3_
  363.9 6.0 %collective-permute-done.40 = bf16[4,3,48,384]{3,2,1,0:T(8,128)(2,1)} collective-permute-done((bf16[4,3,48,384]{3,2,1,0:T(8,128)(2,1)}, bf16[4,3,48,384]{3,2,1,0:T(8,128)(2,1)}, u32[]{:S(2)}, u32[]{:S(2)}) %collective-permute-start.40) | collective-permute-done | bytes 442400 | tf_op jit(solution)/shard_map/ppermute | solution.py:947
  378.8 4.4 gather_grads.5.refs_0_
  384.3 6.2 %gather_grads.6.refs_1_ = bf16[1024,768]{1,0:T(8,128)(2,1)} custom-call(s32[8,1024]{1,0:T(8,128)} %collective-permute-done.5.place_ref, bf16[6,1024,256]{2,1,0:T(8,128)(2,1)S(1)} %copy-done.12), custom_call_target="tpu_custom_call" | custom-call | tf_op jit(solution)/shard_map/gather_grads/pallas_call | solution.py:482
  390.5 10.8 %qkv_back.1 = (bf16[2,3,96,384]{3,2,1,0:T(8,128)(2,1)}, bf16[2,3,96,384]{3,2,1,0:T(8,128)(2,1)}, f32[8,768]{1,0:T(8,128)}) custom-call(s32[2]{0:T(128)} %get-tuple-element.311.scalars_ref, bf16[1024,768]{1,0:T(8,128)(2,1)} %copy-done.6, bf16[1024,768]{1,0:T(8,128)(2,1)} %gather_grads.6.refs_1_, bf16[1024,768]{1,0:T(8,128)(2,1)} %gather_grads.4.refs_2_, ...), custom_call_target="tpu_custom_call" | custom-call | tf_op jit(solution)/shard_map/qkv_back/pallas_call | solution.py:778
  402.3 8.6 %collective-permute-done.42 = bf16[2,3,48,384]{3,2,1,0:T(8,128)(2,1)} collective-permute-done((bf16[2,3,48,384]{3,2,1,0:T(8,128)(2,1)}, bf16[2,3,48,384]{3,2,1,0:T(8,128)(2,1)}, u32[]{:S(2)}, u32[]{:S(2)}) %collective-permute-start.42) | collective-permute-done | bytes 221216 | tf_op jit(solution)/shard_map/ppermute | solution.py:947
  422.8 3.7 collective-permute-done.48.refs_3_
  429.3 10.5 %collective-permute-done.51 = bf16[3,96,384]{2,1,0:T(8,128)(2,1)S(1)} collective-permute-done((bf16[3,96,384]{2,1,0:T(8,128)(2,1)S(1)}, bf16[3,96,384]{2,1,0:T(8,128)(2,1)S(1)}, u32[]{:S(2)}, u32[]{:S(2)}) %collective-permute-start.51) | collective-permute-done | bytes 221216 | tf_op jit(solution)/shard_map/ppermute | solution.py:947
  453.7 4.1 all-to-all-start
  459.7 6.1 %all-to-all-done.got_ref = bf16[4,3,48,384]{3,2,1,0:T(8,128)(2,1)} async-done(((bf16[4,3,48,384]{3,2,1,0:T(8,128)(2,1)}), bf16[4,3,48,384]{3,2,1,0:T(8,128)(2,1)}, u32[]{:S(2)}, u32[]{:S(2)}) %all-to-all-start) | async-done | bytes 442400 | tf_op jit(solution)/shard_map/all_to_all | solution.py:1186
  466.9 4.4 rotate_in.1
  472.1 5.5 all-to-all-start.1
  477.6 3.3 fusion.19
  486.4 7.0 %all-to-all-done.1.got_ref = bf16[8,3,96,96]{3,2,1,0:T(8,128)(2,1)} async-done(((bf16[8,3,96,96]{3,2,1,0:T(8,128)(2,1)}), bf16[8,3,96,96]{3,2,1,0:T(8,128)(2,1)}, u32[]{:S(2)}, u32[]{:S(2)}) %all-to-all-start.1) | async-done | bytes 442400 | tf_op jit(solution)/shard_map/all_to_all | solution.py:1199
  495.7 8.9 %moments.1 = (f32[3,96,768]{2,1,0:T(8,128)}, f32[3,96,768]{2,1,0:T(8,128)}, bf16[8,3,96,96]{3,2,1,0:T(8,128)(2,1)S(1)}) custom-call(bf16[8,3,96,96]{3,2,1,0:T(8,128)(2,1)} %all-to-all-done.1.got_ref, bf16[3,768,768]{2,1,0:T(8,128)(2,1)} %get-tuple-element.263.high_ref, bf16[3,768,768]{2,1,0:T(8,128)(2,1)} %get-tuple-element.264.low_ref, ...), custom_call_target="tpu_custom_call" | custom-call | tf_op jit(solution)/shard_map/moments/pallas_call | solution.py:882
  505.4 4.2 all-to-all-start.2
  509.6 3.3 fusion.20
  513.0 4.9 add_add_fusion
  517.9 7.4 %all-to-all-done.2.got_ref = bf16[8,3,96,96]{3,2,1,0:T(8,128)(2,1)} async-done(((bf16[8,3,96,96]{3,2,1,0:T(8,128)(2,1)}), bf16[8,3,96,96]{3,2,1,0:T(8,128)(2,1)}, u32[]{:S(2)}, u32[]{:S(2)}) %all-to-all-start.2) | async-done | bytes 442400 | tf_op jit(solution)/shard_map/all_to_all | solution.py:1199
  525.3 4.2 rotate_out.1
  530.3 3.6 all-to-all-start.3
  536.8 3.3 fusion.21
  540.1 4.7 collective-permute-done.58
  544.9 4.6 collective-permute-start.59
  (361 shorter events, 173.3 us)
Async XLA Ops:
  0.6 44.1 %collective-permute-start = (bf16[1024,768]{1,0:T(8,128)(2,1)}, bf16[1024,768]{1,0:T(8,128)(2,1)}, u32[]{:S(2)}, u32[]{:S(2)}) collective-permute-start(bf16[1024,768]{1,0:T(8,128)(2,1)} %bitcast.107), channel_id=1, source_target_pairs={{0,4},{4,0},{8,12},{12,8},{16,20},{20,16},{24,28},{28,24},{1,5},{5... | collective-permute-start | bytes 4718600 | tf_op jit(solution)/shard_map/ppermute | solution.py:947
  3.7 41.1 %collective-permute-start.1 = (bf16[1024,768]{1,0:T(8,128)(2,1)}, bf16[1024,768]{1,0:T(8,128)(2,1)}, u32[]{:S(2)}, u32[]{:S(2)}) collective-permute-start(bf16[1024,768]{1,0:T(8,128)(2,1)} %bitcast.108), channel_id=1, source_target_pairs={{0,8},{4,12},{8,0},{12,4},{16,24},{20,28},{24,16},{28,20},{1,9},{5... | collective-permute-start | bytes 4718600 | tf_op jit(solution)/shard_map/ppermute | solution.py:947
  7.2 28.5 %collective-permute-start.2 = (bf16[3,96,768]{2,1,0:T(8,128)(2,1)}, bf16[3,96,768]{2,1,0:T(8,128)(2,1)}, u32[]{:S(2)}, u32[]{:S(2)}) collective-permute-start(bf16[3,96,768]{2,1,0:T(8,128)(2,1)} %convert_bitcast_fusion.refs_0_), channel_id=1, source_target_pairs={{0,1},{1,0},{2,3},{3,2},{4,5},{5,4},{6,7},{7,6},{8,9},{9,8},{10,11... | collective-permute-start | bytes 1327112 | tf_op jit(solution)/shard_map/ppermute | solution.py:947
  7.2 25.4 %collective-permute-start.3 = (bf16[3,96,768]{2,1,0:T(8,128)(2,1)}, bf16[3,96,768]{2,1,0:T(8,128)(2,1)}, u32[]{:S(2)}, u32[]{:S(2)}) collective-permute-start(bf16[3,96,768]{2,1,0:T(8,128)(2,1)} %convert_bitcast_fusion.refs_0_), channel_id=1, source_target_pairs={{0,2},{1,3},{2,0},{3,1},{4,6},{5,7},{6,4},{7,5},{8,10},{9,11},{10,... | collective-permute-start | bytes 1327112 | tf_op jit(solution)/shard_map/ppermute | solution.py:947
  32.6 12.1 %collective-permute-start.4 = (bf16[3,96,768]{2,1,0:T(8,128)(2,1)}, bf16[3,96,768]{2,1,0:T(8,128)(2,1)}, u32[]{:S(2)}, u32[]{:S(2)}) collective-permute-start(bf16[3,96,768]{2,1,0:T(8,128)(2,1)} %collective-permute-done.3.refs_2_), channel_id=1, source_target_pairs={{0,1},{1,0},{2,3},{3,2},{4,5},{5,4},{6,7},{7,6},{8,9},{9,8},{10,11... | collective-permute-start | bytes 1327112 | tf_op jit(solution)/shard_map/ppermute | solution.py:947
  46.8 11.6 %collective-permute-start.10 = (bf16[48,768]{1,0:T(8,128)(2,1)S(1)}, bf16[48,768]{1,0:T(8,128)(2,1)S(1)}, u32[]{:S(2)}, u32[]{:S(2)}) collective-permute-start(bf16[48,768]{1,0:T(8,128)(2,1)S(1)} %get-tuple-element.161), channel_id=1, source_target_pairs={{0,4},{4,0},{8,12},{12,8},{16,20},{20,16},{24,28},{28,24},{1,5},{5... | collective-permute-start | bytes 221192 | tf_op jit(solution)/shard_map/ppermute | solution.py:947
  53.1 24.2 %collective-permute-start.8 = (bf16[512,768]{1,0:T(8,128)(2,1)}, bf16[512,768]{1,0:T(8,128)(2,1)}, u32[]{:S(2)}, u32[]{:S(2)}) collective-permute-start(bf16[512,768]{1,0:T(8,128)(2,1)} %slice.189), channel_id=1, source_target_pairs={{0,8},{4,12},{8,0},{12,4},{16,24},{20,28},{24,16},{28,20},{1,9},{5... | collective-permute-start | bytes 2359304 | tf_op jit(solution)/shard_map/ppermute | solution.py:947
  56.9 20.3 %collective-permute-start.9 = (bf16[512,768]{1,0:T(8,128)(2,1)}, bf16[512,768]{1,0:T(8,128)(2,1)}, u32[]{:S(2)}, u32[]{:S(2)}) collective-permute-start(bf16[512,768]{1,0:T(8,128)(2,1)} %slice.190), channel_id=1, source_target_pairs={{0,4},{4,0},{8,12},{12,8},{16,20},{20,16},{24,28},{28,24},{1,5},{5... | collective-permute-start | bytes 2359304 | tf_op jit(solution)/shard_map/ppermute | solution.py:947
  58.5 17.5 %collective-permute-start.13 = (bf16[4,48,768]{2,1,0:T(8,128)(2,1)S(1)}, bf16[4,48,768]{2,1,0:T(8,128)(2,1)S(1)}, u32[]{:S(2)}, u32[]{:S(2)}) collective-permute-start(bf16[4,48,768]{2,1,0:T(8,128)(2,1)S(1)} %pad_maximum_fusion.5), channel_id=1, source_target_pairs={{0,16},{4,20},{8,24},{12,28},{16,0},{20,4},{24,8},{28,12},{1,17},{... | collective-permute-start | bytes 884744 | tf_op jit(solution)/shard_map/ppermute | solution.py:947
  79.1 31.3 %collective-permute-start.15 = (bf16[9,48,768]{2,1,0:T(8,128)(2,1)}, bf16[9,48,768]{2,1,0:T(8,128)(2,1)}, u32[]{:S(2)}, u32[]{:S(2)}) collective-permute-start(bf16[9,48,768]{2,1,0:T(8,128)(2,1)} %copy-done.26), channel_id=1, source_target_pairs={{0,8},{4,12},{8,16},{12,20},{16,24},{20,28},{24,0},{28,4},{1,9},{5... | collective-permute-start | bytes 1990664 | tf_op jit(solution)/shard_map/ppermute | solution.py:1089
  83.0 27.4 %collective-permute-start.16 = (bf16[9,48,768]{2,1,0:T(8,128)(2,1)}, bf16[9,48,768]{2,1,0:T(8,128)(2,1)}, u32[]{:S(2)}, u32[]{:S(2)}) collective-permute-start(bf16[9,48,768]{2,1,0:T(8,128)(2,1)} %copy-done.26), channel_id=1, source_target_pairs={{0,4},{4,0},{8,12},{12,8},{16,20},{20,16},{24,28},{28,24},{1,5},{5... | collective-permute-start | bytes 1990664 | tf_op jit(solution)/shard_map/ppermute | solution.py:947
  111.6 21.2 %collective-permute-start.19 = (bf16[2,9,48,768]{3,2,1,0:T(8,128)(2,1)S(1)}, bf16[2,9,48,768]{3,2,1,0:T(8,128)(2,1)S(1)}, u32[]{:S(2)}, u32[]{:S(2)}) collective-permute-start(bf16[2,9,48,768]{3,2,1,0:T(8,128)(2,1)S(1)} %pad_maximum_fusion.refs_0_), channel_id=1, source_target_pairs={{0,1},{1,0},{2,3},{3,2},{4,5},{5,4},{6,7},{7,6},{8,9},{9,8},{10,11... | collective-permute-start | bytes 3981320 | tf_op jit(solution)/shard_map/ppermute | solution.py:947
  111.7 21.2 %collective-permute-start.17 = (bf16[9,48,768]{2,1,0:T(8,128)(2,1)}, bf16[9,48,768]{2,1,0:T(8,128)(2,1)S(1)}, u32[]{:S(2)}, u32[]{:S(2)}) collective-permute-start(bf16[9,48,768]{2,1,0:T(8,128)(2,1)} %collective-permute-done.15), channel_id=1, source_target_pairs={{0,8},{4,12},{8,16},{12,20},{16,24},{20,28},{24,0},{28,4},{1,9},{5... | collective-permute-start | bytes 1990664 | tf_op jit(solution)/shard_map/ppermute | solution.py:1089
  112.4 20.5 %collective-permute-start.18 = (bf16[9,48,768]{2,1,0:T(8,128)(2,1)}, bf16[9,48,768]{2,1,0:T(8,128)(2,1)S(1)}, u32[]{:S(2)}, u32[]{:S(2)}) collective-permute-start(bf16[9,48,768]{2,1,0:T(8,128)(2,1)} %collective-permute-done.15), channel_id=1, source_target_pairs={{0,4},{4,0},{8,12},{12,8},{16,20},{20,16},{24,28},{28,24},{1,5},{5... | collective-permute-start | bytes 1990664 | tf_op jit(solution)/shard_map/ppermute | solution.py:947
  134.6 19.4 %collective-permute-start.22 = (bf16[2,9,48,768]{3,2,1,0:T(8,128)(2,1)S(1)}, bf16[2,9,48,768]{3,2,1,0:T(8,128)(2,1)S(1)}, u32[]{:S(2)}, u32[]{:S(2)}) collective-permute-start(bf16[2,9,48,768]{3,2,1,0:T(8,128)(2,1)S(1)} %pad_maximum_fusion.1.refs_1_), channel_id=1, source_target_pairs={{0,1},{1,0},{2,3},{3,2},{4,5},{5,4},{6,7},{7,6},{8,9},{9,8},{10,11... | collective-permute-start | bytes 3981320 | tf_op jit(solution)/shard_map/ppermute | solution.py:947
  134.7 19.3 %collective-permute-start.20 = (bf16[9,48,768]{2,1,0:T(8,128)(2,1)S(1)}, bf16[9,48,768]{2,1,0:T(8,128)(2,1)S(1)}, u32[]{:S(2)}, u32[]{:S(2)}) collective-permute-start(bf16[9,48,768]{2,1,0:T(8,128)(2,1)S(1)} %collective-permute-done.17), channel_id=1, source_target_pairs={{0,8},{4,12},{8,16},{12,20},{16,24},{20,28},{24,0},{28,4},{1,9},{5... | collective-permute-start | bytes 1990664 | tf_op jit(solution)/shard_map/ppermute | solution.py:1089
  135.1 18.9 %collective-permute-start.21 = (bf16[9,48,768]{2,1,0:T(8,128)(2,1)S(1)}, bf16[9,48,768]{2,1,0:T(8,128)(2,1)S(1)}, u32[]{:S(2)}, u32[]{:S(2)}) collective-permute-start(bf16[9,48,768]{2,1,0:T(8,128)(2,1)S(1)} %collective-permute-done.17), channel_id=1, source_target_pairs={{0,4},{4,0},{8,12},{12,8},{16,20},{20,16},{24,28},{28,24},{1,5},{5... | collective-permute-start | bytes 1990664 | tf_op jit(solution)/shard_map/ppermute | solution.py:947
  155.2 34.3 %collective-permute-start.27 = (bf16[2,9,48,768]{3,2,1,0:T(8,128)(2,1)S(1)}, bf16[2,9,48,768]{3,2,1,0:T(8,128)(2,1)S(1)}, u32[]{:S(2)}, u32[]{:S(2)}) collective-permute-start(bf16[2,9,48,768]{3,2,1,0:T(8,128)(2,1)S(1)} %pad_maximum_fusion.2.refs_2_), channel_id=1, source_target_pairs={{0,1},{1,0},{2,3},{3,2},{4,5},{5,4},{6,7},{7,6},{8,9},{9,8},{10,11... | collective-permute-start | bytes 3981320 | tf_op jit(solution)/shard_map/ppermute | solution.py:947
  155.4 34.1 %collective-permute-start.26 = (bf16[9,48,768]{2,1,0:T(8,128)(2,1)S(1)}, bf16[9,48,768]{2,1,0:T(8,128)(2,1)S(1)}, u32[]{:S(2)}, u32[]{:S(2)}) collective-permute-start(bf16[9,48,768]{2,1,0:T(8,128)(2,1)S(1)} %collective-permute-done.20), channel_id=1, source_target_pairs={{0,4},{4,0},{8,12},{12,8},{16,20},{20,16},{24,28},{28,24},{1,5},{5... | collective-permute-start | bytes 1990664 | tf_op jit(solution)/shard_map/ppermute | solution.py:947
  161.8 27.7 %collective-permute-start.23 = (bf16[1536,128]{1,0:T(8,128)(2,1)S(1)}, bf16[1536,128]{1,0:T(8,128)(2,1)S(1)}, u32[]{:S(2)}, u32[]{:S(2)}) collective-permute-start(bf16[1536,128]{1,0:T(8,128)(2,1)S(1)} %mix.4), channel_id=1, source_target_pairs={{0,4},{4,0},{8,12},{12,8},{16,20},{20,16},{24,28},{28,24},{1,5},{5... | collective-permute-start | bytes 1179656 | tf_op jit(solution)/shard_map/ppermute | solution.py:947
  166.9 22.6 %collective-permute-start.24 = (bf16[1536,128]{1,0:T(8,128)(2,1)S(1)}, bf16[1536,128]{1,0:T(8,128)(2,1)S(1)}, u32[]{:S(2)}, u32[]{:S(2)}) collective-permute-start(bf16[1536,128]{1,0:T(8,128)(2,1)S(1)} %mix.5), channel_id=1, source_target_pairs={{0,8},{4,12},{8,0},{12,4},{16,24},{20,28},{24,16},{28,20},{1,9},{5... | collective-permute-start | bytes 1179656 | tf_op jit(solution)/shard_map/ppermute | solution.py:947
  172.0 17.5 %collective-permute-start.25 = (bf16[1536,128]{1,0:T(8,128)(2,1)S(1)}, bf16[1536,128]{1,0:T(8,128)(2,1)S(1)}, u32[]{:S(2)}, u32[]{:S(2)}) collective-permute-start(bf16[1536,128]{1,0:T(8,128)(2,1)S(1)} %mix.6), channel_id=1, source_target_pairs={{0,12},{4,8},{8,4},{12,0},{16,28},{20,24},{24,20},{28,16},{1,13},{... | collective-permute-start | bytes 1179656 | tf_op jit(solution)/shard_map/ppermute | solution.py:947
  191.9 11.4 %collective-permute-start.28 = (bf16[2,9,48,768]{3,2,1,0:T(8,128)(2,1)}, bf16[2,9,48,768]{3,2,1,0:T(8,128)(2,1)}, u32[]{:S(2)}, u32[]{:S(2)}) collective-permute-start(bf16[2,9,48,768]{3,2,1,0:T(8,128)(2,1)} %pad_maximum_fusion.3.refs_3_), channel_id=1, source_target_pairs={{0,1},{1,0},{2,3},{3,2},{4,5},{5,4},{6,7},{7,6},{8,9},{9,8},{10,11... | collective-permute-start | bytes 3981320 | tf_op jit(solution)/shard_map/ppermute | solution.py:947
  191.9 81.2 %collective-permute-start.29 = (bf16[768,768]{1,0:T(8,128)(2,1)}, bf16[768,768]{1,0:T(8,128)(2,1)}, u32[]{:S(2)}, u32[]{:S(2)}) collective-permute-start(bf16[768,768]{1,0:T(8,128)(2,1)} %assemble.1.weight_ref), channel_id=1, source_target_pairs={{0,4},{4,0},{8,12},{12,8},{16,20},{20,16},{24,28},{28,24},{1,5},{5... | collective-permute-start | bytes 3538952 | tf_op jit(solution)/shard_map/ppermute | solution.py:947
  193.4 79.7 %collective-permute-start.30 = (bf16[768,768]{1,0:T(8,128)(2,1)}, bf16[768,768]{1,0:T(8,128)(2,1)}, u32[]{:S(2)}, u32[]{:S(2)}) collective-permute-start(bf16[768,768]{1,0:T(8,128)(2,1)} %assemble.1.weight_ref), channel_id=1, source_target_pairs={{0,8},{4,12},{8,0},{12,4},{16,24},{20,28},{24,16},{28,20},{1,9},{5... | collective-permute-start | bytes 3538952 | tf_op jit(solution)/shard_map/ppermute | solution.py:947
  193.6 79.5 %collective-permute-start.31 = (bf16[768,768]{1,0:T(8,128)(2,1)}, bf16[768,768]{1,0:T(8,128)(2,1)}, u32[]{:S(2)}, u32[]{:S(2)}) collective-permute-start(bf16[768,768]{1,0:T(8,128)(2,1)} %assemble.1.weight_ref), channel_id=1, source_target_pairs={{0,12},{4,8},{8,4},{12,0},{16,28},{20,24},{24,20},{28,16},{1,13},{... | collective-permute-start | bytes 3538952 | tf_op jit(solution)/shard_map/ppermute | solution.py:947
  273.2 14.5 %collective-permute-start.33 = (bf16[1536,128]{1,0:T(8,128)(2,1)}, bf16[1536,128]{1,0:T(8,128)(2,1)S(1)}, u32[]{:S(2)}, u32[]{:S(2)}) collective-permute-start(bf16[1536,128]{1,0:T(8,128)(2,1)} %get-tuple-element.217), channel_id=1, source_target_pairs={{0,4},{4,0},{8,12},{12,8},{16,20},{20,16},{24,28},{28,24},{1,5},{5... | collective-permute-start | bytes 1179656 | tf_op jit(solution)/shard_map/ppermute | solution.py:947
  274.7 13.0 %collective-permute-start.34 = (bf16[1536,128]{1,0:T(8,128)(2,1)}, bf16[1536,128]{1,0:T(8,128)(2,1)S(1)}, u32[]{:S(2)}, u32[]{:S(2)}) collective-permute-start(bf16[1536,128]{1,0:T(8,128)(2,1)} %get-tuple-element.218), channel_id=1, source_target_pairs={{0,8},{4,12},{8,0},{12,4},{16,24},{20,28},{24,16},{28,20},{1,9},{5... | collective-permute-start | bytes 1179656 | tf_op jit(solution)/shard_map/ppermute | solution.py:947
  274.9 19.7 %collective-permute-start.35 = (bf16[1536,128]{1,0:T(8,128)(2,1)}, bf16[1536,128]{1,0:T(8,128)(2,1)S(1)}, u32[]{:S(2)}, u32[]{:S(2)}) collective-permute-start(bf16[1536,128]{1,0:T(8,128)(2,1)} %get-tuple-element.219), channel_id=1, source_target_pairs={{0,12},{4,8},{8,4},{12,0},{16,28},{20,24},{24,20},{28,16},{1,13},{... | collective-permute-start | bytes 1179656 | tf_op jit(solution)/shard_map/ppermute | solution.py:947
  294.6 43.3 %collective-permute-start.36 = (bf16[8,3,48,384]{3,2,1,0:T(8,128)(2,1)}, bf16[8,3,48,384]{3,2,1,0:T(8,128)(2,1)}, u32[]{:S(2)}, u32[]{:S(2)}) collective-permute-start(bf16[8,3,48,384]{3,2,1,0:T(8,128)(2,1)} %fusion.5), channel_id=1, source_target_pairs={{0,2},{1,3},{2,0},{3,1},{4,6},{5,7},{6,4},{7,5},{8,10},{9,11},{10,... | collective-permute-start | bytes 2654216 | tf_op jit(solution)/shard_map/ppermute | solution.py:947
  296.1 44.7 %collective-permute-start.37 = (bf16[8,3,48,384]{3,2,1,0:T(8,128)(2,1)}, bf16[8,3,48,384]{3,2,1,0:T(8,128)(2,1)}, u32[]{:S(2)}, u32[]{:S(2)}) collective-permute-start(bf16[8,3,48,384]{3,2,1,0:T(8,128)(2,1)} %fusion.6), channel_id=1, source_target_pairs={{0,4},{4,0},{8,12},{12,8},{16,20},{20,16},{24,28},{28,24},{1,5},{5... | collective-permute-start | bytes 2654216 | tf_op jit(solution)/shard_map/ppermute | solution.py:947
  297.5 45.6 %collective-permute-start.38 = (bf16[8,3,48,384]{3,2,1,0:T(8,128)(2,1)S(1)}, bf16[8,3,48,384]{3,2,1,0:T(8,128)(2,1)}, u32[]{:S(2)}, u32[]{:S(2)}) collective-permute-start(bf16[8,3,48,384]{3,2,1,0:T(8,128)(2,1)S(1)} %fusion.7), channel_id=1, source_target_pairs={{0,8},{4,12},{8,0},{12,4},{16,24},{20,28},{24,16},{28,20},{1,9},{5... | collective-permute-start | bytes 2654216 | tf_op jit(solution)/shard_map/ppermute | solution.py:947
  346.0 17.8 %collective-permute-start.39 = (bf16[4,3,48,384]{3,2,1,0:T(8,128)(2,1)}, bf16[4,3,48,384]{3,2,1,0:T(8,128)(2,1)S(1)}, u32[]{:S(2)}, u32[]{:S(2)}) collective-permute-start(bf16[4,3,48,384]{3,2,1,0:T(8,128)(2,1)} %slice.333), channel_id=1, source_target_pairs={{0,4},{4,0},{8,12},{12,8},{16,20},{20,16},{24,28},{28,24},{1,5},{5... | collective-permute-start | bytes 1327112 | tf_op jit(solution)/shard_map/ppermute | solution.py:947
  347.0 22.9 %collective-permute-start.40 = (bf16[4,3,48,384]{3,2,1,0:T(8,128)(2,1)}, bf16[4,3,48,384]{3,2,1,0:T(8,128)(2,1)}, u32[]{:S(2)}, u32[]{:S(2)}) collective-permute-start(bf16[4,3,48,384]{3,2,1,0:T(8,128)(2,1)} %slice.332), channel_id=1, source_target_pairs={{0,8},{4,12},{8,0},{12,4},{16,24},{20,28},{24,16},{28,20},{1,9},{5... | collective-permute-start | bytes 1327112 | tf_op jit(solution)/shard_map/ppermute | solution.py:947
  348.3 24.1 %collective-permute-start.41 = (bf16[4,3,48,384]{3,2,1,0:T(8,128)(2,1)}, bf16[4,3,48,384]{3,2,1,0:T(8,128)(2,1)}, u32[]{:S(2)}, u32[]{:S(2)}) collective-permute-start(bf16[4,3,48,384]{3,2,1,0:T(8,128)(2,1)} %slice.331), channel_id=1, source_target_pairs={{0,16},{4,20},{8,24},{12,28},{16,0},{20,4},{24,8},{28,12},{1,17},{... | collective-permute-start | bytes 1327112 | tf_op jit(solution)/shard_map/ppermute | solution.py:947
  363.5 52.7 %collective-permute-start.45 = (bf16[1024,768]{1,0:T(8,128)(2,1)}, bf16[1024,768]{1,0:T(8,128)(2,1)}, u32[]{:S(2)}, u32[]{:S(2)}) collective-permute-start(bf16[1024,768]{1,0:T(8,128)(2,1)} %gather_grads.7.refs_3_), channel_id=1, source_target_pairs={{0,12},{4,8},{8,4},{12,0},{16,28},{20,24},{24,20},{28,16},{1,13},{... | collective-permute-start | bytes 4718600 | tf_op jit(solution)/shard_map/ppermute | solution.py:947
  374.3 36.5 %collective-permute-start.42 = (bf16[2,3,48,384]{3,2,1,0:T(8,128)(2,1)}, bf16[2,3,48,384]{3,2,1,0:T(8,128)(2,1)}, u32[]{:S(2)}, u32[]{:S(2)}) collective-permute-start(bf16[2,3,48,384]{3,2,1,0:T(8,128)(2,1)} %slice.336), channel_id=1, source_target_pairs={{0,8},{4,12},{8,0},{12,4},{16,24},{20,28},{24,16},{28,20},{1,9},{5... | collective-permute-start | bytes 663560 | tf_op jit(solution)/shard_map/ppermute | solution.py:947
  376.2 36.5 %collective-permute-start.43 = (bf16[2,3,48,384]{3,2,1,0:T(8,128)(2,1)}, bf16[2,3,48,384]{3,2,1,0:T(8,128)(2,1)}, u32[]{:S(2)}, u32[]{:S(2)}) collective-permute-start(bf16[2,3,48,384]{3,2,1,0:T(8,128)(2,1)} %slice.335), channel_id=1, source_target_pairs={{0,16},{4,20},{8,24},{12,28},{16,0},{20,4},{24,8},{28,12},{1,17},{... | collective-permute-start | bytes 663560 | tf_op jit(solution)/shard_map/ppermute | solution.py:947
  378.2 36.3 %collective-permute-start.44 = (bf16[2,3,48,384]{3,2,1,0:T(8,128)(2,1)}, bf16[2,3,48,384]{3,2,1,0:T(8,128)(2,1)}, u32[]{:S(2)}, u32[]{:S(2)}) collective-permute-start(bf16[2,3,48,384]{3,2,1,0:T(8,128)(2,1)} %slice.334), channel_id=1, source_target_pairs={{0,2},{1,3},{2,0},{3,1},{4,6},{5,7},{6,4},{7,5},{8,10},{9,11},{10,... | collective-permute-start | bytes 663560 | tf_op jit(solution)/shard_map/ppermute | solution.py:947
  428.5 11.3 %collective-permute-start.51 = (bf16[3,96,384]{2,1,0:T(8,128)(2,1)S(1)}, bf16[3,96,384]{2,1,0:T(8,128)(2,1)S(1)}, u32[]{:S(2)}, u32[]{:S(2)}) collective-permute-start(bf16[3,96,384]{2,1,0:T(8,128)(2,1)S(1)} %fusion.8), channel_id=1, source_target_pairs={{0,16},{4,20},{8,24},{12,28},{16,0},{20,4},{24,8},{28,12},{1,17},{... | collective-permute-start | bytes 663560 | tf_op jit(solution)/shard_map/ppermute | solution.py:947
  428.7 11.2 %collective-permute-start.52 = (f32[12,768]{1,0:T(8,128)S(1)}, f32[12,768]{1,0:T(8,128)}, u32[]{:S(2)}, u32[]{:S(2)}) collective-permute-start(f32[12,768]{1,0:T(8,128)S(1)} %add.164), channel_id=1, source_target_pairs={{0,2},{1,3},{2,0},{3,1},{4,6},{5,7},{6,4},{7,5},{8,10},{9,11},{10,... | collective-permute-start | bytes 110600 | tf_op jit(solution)/shard_map/ppermute | solution.py:947
  440.5 45.9 %collective-permute-start.55 = (bf16[1024,768]{1,0:T(8,128)(2,1)}, bf16[1024,768]{1,0:T(8,128)(2,1)}, u32[]{:S(2)}, u32[]{:S(2)}) collective-permute-start(bf16[1024,768]{1,0:T(8,128)(2,1)} %gather_grads.6.refs_1_), channel_id=1, source_target_pairs={{0,4},{4,0},{8,12},{12,8},{16,20},{20,16},{24,28},{28,24},{1,5},{5... | collective-permute-start | bytes 4718600 | tf_op jit(solution)/shard_map/ppermute | solution.py:947
  442.7 43.7 %collective-permute-start.56 = (bf16[1024,768]{1,0:T(8,128)(2,1)}, bf16[1024,768]{1,0:T(8,128)(2,1)}, u32[]{:S(2)}, u32[]{:S(2)}) collective-permute-start(bf16[1024,768]{1,0:T(8,128)(2,1)} %gather_grads.4.refs_2_), channel_id=1, source_target_pairs={{0,8},{4,12},{8,0},{12,4},{16,24},{20,28},{24,16},{28,20},{1,9},{5... | collective-permute-start | bytes 4718600 | tf_op jit(solution)/shard_map/ppermute | solution.py:947
  453.7 12.2 %all-to-all-start = ((bf16[4,3,48,384]{3,2,1,0:T(8,128)(2,1)}), bf16[4,3,48,384]{3,2,1,0:T(8,128)(2,1)}, u32[]{:S(2)}, u32[]{:S(2)}) async-start(bf16[4,3,48,384]{3,2,1,0:T(8,128)(2,1)} %copy-done.18), calls=%async_computation | async-start | bytes 884736 | tf_op jit(solution)/shard_map/all_to_all | solution.py:1186
  472.1 21.3 %all-to-all-start.1 = ((bf16[8,3,96,96]{3,2,1,0:T(8,128)(2,1)}), bf16[8,3,96,96]{3,2,1,0:T(8,128)(2,1)}, u32[]{:S(2)}, u32[]{:S(2)}) async-start(bf16[8,3,96,96]{3,2,1,0:T(8,128)(2,1)} %copy-done.17), calls=%async_computation.1 | async-start | bytes 1179648 | tf_op jit(solution)/shard_map/all_to_all | solution.py:1199
  484.4 33.5 %collective-permute-start.57 = (f32[12,768]{1,0:T(8,128)}, f32[12,768]{1,0:T(8,128)}, u32[]{:S(2)}, u32[]{:S(2)}) collective-permute-start(f32[12,768]{1,0:T(8,128)} %add.167), channel_id=1, source_target_pairs={{0,4},{4,0},{8,12},{12,8},{16,20},{20,16},{24,28},{28,24},{1,5},{5... | collective-permute-start | bytes 110600 | tf_op jit(solution)/shard_map/ppermute | solution.py:947
  505.4 19.8 %all-to-all-start.2 = ((bf16[8,3,96,96]{3,2,1,0:T(8,128)(2,1)}), bf16[8,3,96,96]{3,2,1,0:T(8,128)(2,1)}, u32[]{:S(2)}, u32[]{:S(2)}) async-start(bf16[8,3,96,96]{3,2,1,0:T(8,128)(2,1)} %copy-done.28), calls=%async_computation.2 | async-start | bytes 1179648 | tf_op jit(solution)/shard_map/all_to_all | solution.py:1199
  530.3 22.5 %all-to-all-start.3 = ((bf16[8,3,96,96]{3,2,1,0:T(8,128)(2,1)}), bf16[8,3,96,96]{3,2,1,0:T(8,128)(2,1)S(1)}, u32[]{:S(2)}, u32[]{:S(2)}) async-start(bf16[8,3,96,96]{3,2,1,0:T(8,128)(2,1)} %copy-done.16), calls=%async_computation.3 | async-start | bytes 1179648 | tf_op jit(solution)/shard_map/all_to_all | solution.py:1199
  (97 other events, 551.1 us)

commit v7 on v6

--- a/solution.py
+++ b/solution.py
@@ -1056,7 +1056,7 @@
     across = swap(over, "grp", 1)
 
     orders = exchange_unit(placed)
-    (near, far, beside, over, across, orders) = together(near, far, beside, over, across, orders)
+    (near, far, beside, over, across) = together(near, far, beside, over, across)
     part_rows = rows_dev // 2
 
     scalars = jnp.concatenate([block_slot, jnp.stack([grp, core, member])]).astype(jnp.int32)
@@ -1064,6 +1064,7 @@
     theirs = exchange_unit(by_owner)
     half = tok_count // 2
     third = (swap(near[:half], "tok", 2), swap(far[half:], "tok", 1))
+    (theirs, orders) = together(theirs, orders)
     theirs = jnp.stack(theirs)
     theirs_far = swap(theirs, "tok", UNIT)
     mine_all = jnp.concatenate([theirs, theirs_far], axis=0)
@@ -1147,25 +1148,28 @@
         return [k + g.astype(F32) for k, g in zip(kept_now, got_now)]
 
     kept_now, sent_now = halves(sums_of)
-    (sent_now, grad_parts) = together(sent_now, grad_parts)
+    sorted_grads = [sort_grads(orders[0], grad_parts[0])]
+    (sent_now, grad_parts, sorted_grads) = together(sent_now, grad_parts, sorted_grads)
     got_now = exchanged(sent_now, 0)
-    sorted_grads = [sort_grads(orders[k], grad_parts[k]) for k in range(UNIT)]
+    sorted_grads += [sort_grads(orders[k], grad_parts[k]) for k in range(1, UNIT)]
     sorted_back = attend_back(is_long, grouped, sorted_grads)
     kept_now, sent_now = halves(joined(kept_now, got_now))
     (sent_now, sorted_back) = together(sent_now, sorted_back)
     got_now = exchanged(sent_now, 1)
     own_grads = [None] * UNIT
     own_grads[3] = gather_grads(orders[3], sorted_back[3])
-    home_grads = [None, None, None, swap(own_grads[3], "tok", 3)]
     own_grads[2] = gather_grads(orders[2], sorted_back[2])
     kept_now, sent_now = halves(joined(kept_now, got_now))
-    (sent_now, own_grads[2], sorted_back) = together(sent_now, own_grads[2], sorted_back)
+    (sent_now, own_grads[2], own_grads[3], sorted_back) = together(
+        sent_now, own_grads[2], own_grads[3], sorted_back
+    )
     got_now = exchanged(sent_now, 2)
+    home_grads = [None, None, None, swap(own_grads[3], "tok", 3)]
     for k in (1, 0):
         own_grads[k] = gather_grads(orders[k], sorted_back[k])
     kept_qkv, sent_qkv, bias_qkv = qkv_back(jnp.stack([core, unit]).astype(jnp.int32), own_grads, unit_inputs)
+    (got_now, kept_qkv, sent_qkv) = together(got_now, kept_qkv, sent_qkv)
     kept_now, sent_now = halves(joined(kept_now, got_now))
-    (sent_now, sent_qkv, home_grads[3]) = together(sent_now, sent_qkv, home_grads[3])
     got_now = exchanged(sent_now, 3)
 
     bias_query, _, bias_value = join_heads(bias_qkv[0])
@@ -1176,17 +1180,18 @@
 
     more = swap(total, "grp", 1)
     keep = kept_qkv.astype(F32) + swap(sent_qkv, "grp", 1).astype(F32)
-    (keep, more, got_now) = together(keep, more, got_now)
+    (keep, more) = together(keep, more)
     total = total + more
     more = swap(total, "grp", 2)
     unit_got = swap(keep[1].astype(BF16), "tok", UNIT)
+    keep = keep[0] + unit_got.astype(F32)
+    (keep, more, got_now, home_grads[3]) = together(keep, more, got_now, home_grads[3])
+    total = total + more
+    more = swap(total, "tok", 1)
     home_grads[1] = swap(own_grads[1], "tok", 1)
     home_grads[2] = swap(own_grads[2], "tok", 2)
     sent = pack(slot_block, kept_now, got_now, n_grp, slots)
     got = lax.all_to_all(sent, "grp", split_axis=0, concat_axis=0, tiled=True)
-    keep = keep[0] + unit_got.astype(F32)
-    (keep, more) = together(keep, more)
-    total = total + more
     keep = (keep + swap(keep.astype(BF16), "grp", 2).astype(F32)).astype(BF16)
     kept_core = (keep, swap(keep, "grp", 1))
     keep = jnp.concatenate(
@@ -1200,8 +1205,9 @@
 
     part = to_tok(rotate_in(mine, keep, got, left, n_tok))
     grad_inputs = grad_first + outer_cols(own_grads[0], own_weights)
-    (part, home_grads, grad_inputs) = together(part, home_grads[1:], grad_inputs)
-    more = swap(total, "tok", 1)
+    (part, home_grads, grad_inputs, more) = together(part, home_grads[1:], grad_inputs, more)
+    total = total + more
+    more = swap(total, "tok", 2)
     by_slot_of = lambda value: jnp.transpose(value, (1, 0, 2))
     new_one, new_two, turned = moments(
         place, part, right, by_slot_of(moment_one), by_slot_of(moment_two)
@@ -1211,7 +1217,6 @@
     grad_inputs = grad_inputs + outer_cols(home_grads[1], turned_weights[1])
     (turned, more, grad_inputs, home_grads[2]) = together(turned, more, grad_inputs, home_grads[2])
     total = total + more
-    total = total + swap(total, "tok", 2)
     change = to_tok(rotate_out(turned, left))
     vector_total = total + swap(total, "tok", 4)
     new_master = by_slot_of(apply_change(place, change, by_slot_of(master)))

time: 562 us -> 548 us (0.975)
  waiting for transfers between devices: 105 us -> 92.2 us
    ppermute x57, waiting for transfers between devices: 84.4 us -> 73.6 us  [swap(): return lax.ppermute(value, axis, [(i, i ^ bit) for i in range(size)])]
    unnamed x167 -> x189, local copies, waits for them, and re-layouts: 37.9 us -> 39.9 us
  transfers between devices with their start and end apart: 64 -> 64, of which waited for: 18 -> 19; matrix products, arithmetic and copies ran while one was open for 15% -> 15% of each run, Pallas kernels for 40% -> 39%
where the time goes in v7:
time: 548 us; the launch traced here: 540 us
  Pallas kernels  229 us (42%)
  waiting for transfers between devices  92.2 us (17%)
  starting transfers between devices  90.2 us (16%)
  local copies, waits for them, and re-layouts  60.5 us (11%)
  other arithmetic  51.1 us (9%)
  matrix products  14.7 us (3%)
    ppermute x57, waiting for transfers between devices, swap(): return lax.ppermute(value, axis, [(i, i ^ bit) for i in range(size)])  73.6 us
    pallas_call x1, Pallas kernels, layer(): pl.pallas_call(functools.partial(layer_body, n_shards), in_specs=[pl.Bloc...  69.8 us
    ppermute x57, starting transfers between devices, swap(): return lax.ppermute(value, axis, [(i, i ^ bit) for i in range(size)])  66.8 us
    unnamed x189, local copies, waits for them, and re-layouts  39.9 us
    pallas_call x4, Pallas kernels, sort_rows(): pl.pallas_call(sort_body, grid=(HEADS_OWN,), in_specs=[pl.BlockSpec((8, c...  27.7 us
    pallas_call x4, Pallas kernels, gather_grads(): pl.pallas_call(gather_grads_body, grid=(HEADS_OWN,), in_specs=[pl.BlockSp...  20.2 us
    pallas_call x1, Pallas kernels, attend_back(): pl.pallas_call(attend_back_body, grid_spec=pltpu.PrefetchScalarGridSpec(n...  19.1 us
    pallas_call x4, Pallas kernels, mix(): pl.pallas_call(mix_body, grid=(HEADS_OWN,), in_specs=[pl.BlockSpec((8, co...  17.2 us
  transfers between devices with their start and end apart: 64, of which 19 were waited for; matrix products, arithmetic and copies ran while one was open for 15% of the time, Pallas kernels for 39%

profile of v7, /device:TPU:0, one launch (start us, length us, event | category | flops | bytes accessed | tf_op | source)
XLA Modules:
  0.0 540.0 jit_solution(9295863288933738565)
XLA Ops:
  0.6 3.0 collective-permute-start
  11.4 6.9 %places.1 = (s32[8,1024]{1,0:T(8,128)}, s32[8,1024]{1,0:T(8,128)}, s32[8,1024]{1,0:T(8,128)}, s32[8,1024]{1,0:T(8,128)}) custom-call(s32[2]{0:T(128)} %get-tuple-element.324.scalars_ref, s32[24,1024]{1,0:T(8,128)} %bitcast.127), custom_call_target="tpu_custom_call" | custom-call | tf_op jit(solution)/shard_map/places/pallas_call | solution.py:96
  18.3 14.8 %fusion = (bf16[3,768,768]{2,1,0:T(8,128)(2,1)}, bf16[3,768,768]{2,1,0:T(8,128)(2,1)}, bf16[3,768,768]{2,1,0:T(8,128)(2,1)}, bf16[3,768,768]{2,1,0:T(8,128)(2,1)S(1)}) fusion(f32[2,3,768,768]{3,2,1,0:T(8,128)} %param.18), kind=kLoop, calls=%fused_computation.2 | loop fusion | flops 10616832 | bytes 35389440 | tf_op jit(solution)/shard_map/convert_element_type | solution.py:1002
  63.2 13.8 %collective-permute-done.13 = bf16[4,48,768]{2,1,0:T(8,128)(2,1)S(1)} collective-permute-done((bf16[4,48,768]{2,1,0:T(8,128)(2,1)S(1)}, bf16[4,48,768]{2,1,0:T(8,128)(2,1)S(1)}, u32[]{:S(2)}, u32[]{:S(2)}) %collective-permute-start.13) | collective-permute-done | bytes 294944 | tf_op jit(solution)/shard_map/ppermute | solution.py:947
  80.0 5.1 collective-permute-start.15
  89.7 3.2 assemble.1.weight_ref
  95.1 6.5 %sort_rows.4.refs_0_ = bf16[6,1024,256]{2,1,0:T(8,128)(2,1)S(1)} custom-call(s32[8,1024]{1,0:T(8,128)S(1)} %copy-done.29, bf16[1024,768]{1,0:T(8,128)(2,1)S(1)} %bitcast.111, bf16[768,768]{1,0:T(8,128)(2,1)} %assemble.1.weight_ref, f32[1,768]{1,0:T(1,128)S(1)} %reshape.107.bias_ref), custom_call_target="tpu_custom_call" | custom-call | tf_op jit(solution)/shard_map/sort_rows/pallas_call | solution.py:221
  103.3 7.2 %sort_rows.5.refs_1_ = bf16[6,1024,256]{2,1,0:T(8,128)(2,1)S(1)} custom-call(s32[8,1024]{1,0:T(8,128)S(1)} %copy-done.33, bf16[1024,768]{1,0:T(8,128)(2,1)} %collective-permute-done.x_ref.refs_5_, bf16[768,768]{1,0:T(8,128)(2,1)} %assemble.1.weight_ref, f32[1,768]{1,0:T(1,128)S(1)} %reshape.107.bias_ref), custom_call_target="tpu_custom_call" | custom-call | tf_op jit(solution)/shard_map/sort_rows/pallas_call | solution.py:221
  114.9 7.1 %sort_rows.6.refs_2_ = bf16[6,1024,256]{2,1,0:T(8,128)(2,1)S(1)} custom-call(s32[8,1024]{1,0:T(8,128)S(1)} %copy-done.36, bf16[1024,768]{1,0:T(8,128)(2,1)} %collective-permute-done.1.x_ref.refs_6_, bf16[768,768]{1,0:T(8,128)(2,1)} %assemble.1.weight_ref, f32[1,768]{1,0:T(1,128)S(1)} %reshape.107.bias_ref), custom_call_target="tpu_custom_call" | custom-call | tf_op jit(solution)/shard_map/sort_rows/pallas_call | solution.py:221
  126.1 6.9 %sort_rows.7.refs_3_ = bf16[6,1024,256]{2,1,0:T(8,128)(2,1)S(1)} custom-call(s32[8,1024]{1,0:T(8,128)S(1)} %copy-done.39, bf16[1024,768]{1,0:T(8,128)(2,1)S(1)} %constant_dynamic-update-slice_fusion.5.x_ref.refs_7_, bf16[768,768]{1,0:T(8,128)(2,1)} %assemble.1.weight_ref, f32[1,768]{1,0:T(1,128)S(1)} %reshape.107.bias_ref), custom_call_target="tpu_custom_call" | custom-call | tf_op jit(solution)/shard_map/sort_rows/pallas_call | solution.py:221
  138.0 16.5 %attend.1 = (bf16[6,1024,128]{2,1,0:T(8,128)(2,1)S(1)}, bf16[6,1024,128]{2,1,0:T(8,128)(2,1)S(1)}, bf16[6,1024,128]{2,1,0:T(8,128)(2,1)S(1)}, bf16[6,1024,128]{2,1,0:T(8,128)(2,1)}) custom-call(s32[1]{0:T(128)} %bitcast.11.long_ref, bf16[6,1024,256]{2,1,0:T(8,128)(2,1)} %copy-done, bf16[6,1024,256]{2,1,0:T(8,128)(2,1)} %copy-done.1, ...), custom_call_target="tpu_custom_call" | custom-call | tf_op jit(solution)/shard_map/attend/pallas_call | solution.py:345
  158.5 4.2 mix.4
  163.6 4.2 mix.5
  168.5 4.4 mix.6
  175.1 16.3 %collective-permute-done.23.refs_9_ = bf16[1536,128]{1,0:T(8,128)(2,1)S(1)} collective-permute-done((bf16[1536,128]{1,0:T(8,128)(2,1)S(1)}, bf16[1536,128]{1,0:T(8,128)(2,1)S(1)}, u32[]{:S(2)}, u32[]{:S(2)}) %collective-permute-start.23) | collective-permute-done | bytes 393248 | tf_op jit(solution)/shard_map/ppermute | solution.py:947
  200.3 4.2 mix.7.refs_8_
  205.3 69.8 %layer.1 = (bf16[1024,768]{1,0:T(8,128)(2,1)}, f32[1024,768]{1,0:T(8,128)}, f32[16,768]{1,0:T(8,128)}, bf16[3,16,3,48,384]{4,3,2,1,0:T(8,128)(2,1)}, bf16[3,16,3...) custom-call(s32[22]{0:T(128)} %concatenate.28.table_ref, ...), custom_call_target="tpu_custom_call" | custom-call | tf_op jit(solution)/shard_map/layer/pallas_call | solution.py:713
  279.7 3.8 sort_grads.4.refs_4_
  284.2 4.6 convert_add_fusion
  293.4 3.1 collective-permute-done.35.rows_ref
  299.4 3.8 sort_grads.5.refs_5_
  304.5 4.2 sort_grads.6.refs_6_
  309.9 3.8 sort_grads.7.refs_7_
  314.9 19.1 %attend_back.1 = (bf16[6,1024,256]{2,1,0:T(8,128)(2,1)}, bf16[6,1024,256]{2,1,0:T(8,128)(2,1)}, bf16[6,1024,256]{2,1,0:T(8,128)(2,1)}, bf16[6,1024,256]{2,1,0:T(8,128)(2,1)}) custom-call(s32[1]{0:T(128)} %bitcast.11.long_ref, bf16[6,1024,256]{2,1,0:T(8,128)(2,1)} %copy-done, bf16[6,1024,256]{2,1,0:T(8,128)(2,1)} %copy-done.1, ...), custom_call_target="tpu_custom_call" | custom-call | tf_op jit(solution)/shard_map/attend_back/pallas_call | solution.py:389
  344.4 4.6 collective-permute-start.41
  349.0 5.3 gather_grads.4.refs_2_
  354.3 5.1 gather_grads.5.refs_3_
  360.2 2.9 collective-permute-done.40
  371.3 4.4 gather_grads.6.refs_0_
  376.8 5.5 %gather_grads.7.refs_1_ = bf16[1024,768]{1,0:T(8,128)(2,1)} custom-call(s32[8,1024]{1,0:T(8,128)S(1)} %copy-done.34, bf16[6,1024,256]{2,1,0:T(8,128)(2,1)S(1)} %copy-done.12), custom_call_target="tpu_custom_call" | custom-call | tf_op jit(solution)/shard_map/gather_grads/pallas_call | solution.py:482
  382.5 10.8 %qkv_back.1 = (bf16[2,3,96,384]{3,2,1,0:T(8,128)(2,1)}, bf16[2,3,96,384]{3,2,1,0:T(8,128)(2,1)}, f32[8,768]{1,0:T(8,128)}) custom-call(s32[2]{0:T(128)} %get-tuple-element.325.scalars_ref, bf16[1024,768]{1,0:T(8,128)(2,1)} %copy-done.6, bf16[1024,768]{1,0:T(8,128)(2,1)} %gather_grads.7.refs_1_, bf16[1024,768]{1,0:T(8,128)(2,1)} %gather_grads.4.refs_2_, ...), custom_call_target="tpu_custom_call" | custom-call | tf_op jit(solution)/shard_map/qkv_back/pallas_call | solution.py:778
  405.6 14.5 %collective-permute-done.47 = bf16[3,96,384]{2,1,0:T(8,128)(2,1)S(1)} collective-permute-done((bf16[3,96,384]{2,1,0:T(8,128)(2,1)S(1)}, bf16[3,96,384]{2,1,0:T(8,128)(2,1)S(1)}, u32[]{:S(2)}, u32[]{:S(2)}) %collective-permute-start.47) | collective-permute-done | bytes 221216 | tf_op jit(solution)/shard_map/ppermute | solution.py:947
  439.3 4.1 all-to-all-start
  445.3 6.1 %all-to-all-done.got_ref = bf16[4,3,48,384]{3,2,1,0:T(8,128)(2,1)} async-done(((bf16[4,3,48,384]{3,2,1,0:T(8,128)(2,1)}), bf16[4,3,48,384]{3,2,1,0:T(8,128)(2,1)}, u32[]{:S(2)}, u32[]{:S(2)}) %all-to-all-start) | async-done | bytes 442400 | tf_op jit(solution)/shard_map/all_to_all | solution.py:1194
  452.5 4.4 rotate_in.1
  457.7 5.5 %all-to-all-start.1 = ((bf16[8,3,96,96]{3,2,1,0:T(8,128)(2,1)}), bf16[8,3,96,96]{3,2,1,0:T(8,128)(2,1)}, u32[]{:S(2)}, u32[]{:S(2)}) async-start(bf16[8,3,96,96]{3,2,1,0:T(8,128)(2,1)} %copy-done.16), calls=%async_computation.1 | async-start | bytes 1179648 | tf_op jit(solution)/shard_map/all_to_all | solution.py:1204
  466.1 3.3 fusion.19
  471.5 7.5 %all-to-all-done.1.got_ref = bf16[8,3,96,96]{3,2,1,0:T(8,128)(2,1)} async-done(((bf16[8,3,96,96]{3,2,1,0:T(8,128)(2,1)}), bf16[8,3,96,96]{3,2,1,0:T(8,128)(2,1)}, u32[]{:S(2)}, u32[]{:S(2)}) %all-to-all-start.1) | async-done | bytes 442400 | tf_op jit(solution)/shard_map/all_to_all | solution.py:1204
  481.3 8.9 %moments.1 = (f32[3,96,768]{2,1,0:T(8,128)}, f32[3,96,768]{2,1,0:T(8,128)}, bf16[8,3,96,96]{3,2,1,0:T(8,128)(2,1)S(1)}) custom-call(bf16[8,3,96,96]{3,2,1,0:T(8,128)(2,1)} %all-to-all-done.1.got_ref, bf16[3,768,768]{2,1,0:T(8,128)(2,1)} %get-tuple-element.277.high_ref, bf16[3,768,768]{2,1,0:T(8,128)(2,1)} %get-tuple-element.278.low_ref, ...), custom_call_target="tpu_custom_call" | custom-call | tf_op jit(solution)/shard_map/moments/pallas_call | solution.py:882
  491.0 4.2 all-to-all-start.2
  498.1 3.2 fusion.20
  501.2 4.9 add_add_fusion
  506.1 4.7 all-to-all-done.2.got_ref
  510.9 4.2 rotate_out.1
  515.9 3.6 all-to-all-start.3
  520.4 2.9 collective-permute-start.59
  523.3 3.3 fusion.21
  528.7 9.0 %collective-permute-done.59 = f32[12,768]{1,0:T(8,128)S(1)} collective-permute-done((f32[12,768]{1,0:T(8,128)S(1)}, f32[12,768]{1,0:T(8,128)S(1)}, u32[]{:S(2)}, u32[]{:S(2)}) %collective-permute-start.59) | collective-permute-done | bytes 36896 | tf_op jit(solution)/shard_map/ppermute | solution.py:947
  (383 shorter events, 167.5 us)
Async XLA Ops:
  0.6 37.7 %collective-permute-start = (bf16[1024,768]{1,0:T(8,128)(2,1)}, bf16[1024,768]{1,0:T(8,128)(2,1)}, u32[]{:S(2)}, u32[]{:S(2)}) collective-permute-start(bf16[1024,768]{1,0:T(8,128)(2,1)} %bitcast.107), channel_id=1, source_target_pairs={{0,4},{4,0},{8,12},{12,8},{16,20},{20,16},{24,28},{28,24},{1,5},{5... | collective-permute-start | bytes 4718600 | tf_op jit(solution)/shard_map/ppermute | solution.py:947
  3.7 36.2 %collective-permute-start.1 = (bf16[1024,768]{1,0:T(8,128)(2,1)}, bf16[1024,768]{1,0:T(8,128)(2,1)}, u32[]{:S(2)}, u32[]{:S(2)}) collective-permute-start(bf16[1024,768]{1,0:T(8,128)(2,1)} %bitcast.108), channel_id=1, source_target_pairs={{0,8},{4,12},{8,0},{12,4},{16,24},{20,28},{24,16},{28,20},{1,9},{5... | collective-permute-start | bytes 4718600 | tf_op jit(solution)/shard_map/ppermute | solution.py:947
  7.2 28.8 %collective-permute-start.2 = (bf16[3,96,768]{2,1,0:T(8,128)(2,1)}, bf16[3,96,768]{2,1,0:T(8,128)(2,1)}, u32[]{:S(2)}, u32[]{:S(2)}) collective-permute-start(bf16[3,96,768]{2,1,0:T(8,128)(2,1)} %convert_bitcast_fusion.refs_0_), channel_id=1, source_target_pairs={{0,1},{1,0},{2,3},{3,2},{4,5},{5,4},{6,7},{7,6},{8,9},{9,8},{10,11... | collective-permute-start | bytes 1327112 | tf_op jit(solution)/shard_map/ppermute | solution.py:947
  7.2 25.9 %collective-permute-start.3 = (bf16[3,96,768]{2,1,0:T(8,128)(2,1)}, bf16[3,96,768]{2,1,0:T(8,128)(2,1)}, u32[]{:S(2)}, u32[]{:S(2)}) collective-permute-start(bf16[3,96,768]{2,1,0:T(8,128)(2,1)} %convert_bitcast_fusion.refs_0_), channel_id=1, source_target_pairs={{0,2},{1,3},{2,0},{3,1},{4,6},{5,7},{6,4},{7,5},{8,10},{9,11},{10,... | collective-permute-start | bytes 1327112 | tf_op jit(solution)/shard_map/ppermute | solution.py:947
  41.9 16.0 %collective-permute-start.7 = (bf16[48,768]{1,0:T(8,128)(2,1)S(1)}, bf16[48,768]{1,0:T(8,128)(2,1)S(1)}, u32[]{:S(2)}, u32[]{:S(2)}) collective-permute-start(bf16[48,768]{1,0:T(8,128)(2,1)S(1)} %get-tuple-element.164), channel_id=1, source_target_pairs={{0,4},{4,0},{8,12},{12,8},{16,20},{20,16},{24,28},{28,24},{1,5},{5... | collective-permute-start | bytes 221192 | tf_op jit(solution)/shard_map/ppermute | solution.py:947
  42.4 15.6 %collective-permute-start.8 = (bf16[48,768]{1,0:T(8,128)(2,1)S(1)}, bf16[48,768]{1,0:T(8,128)(2,1)S(1)}, u32[]{:S(2)}, u32[]{:S(2)}) collective-permute-start(bf16[48,768]{1,0:T(8,128)(2,1)S(1)} %get-tuple-element.165), channel_id=1, source_target_pairs={{0,8},{4,12},{8,0},{12,4},{16,24},{20,28},{24,16},{28,20},{1,9},{5... | collective-permute-start | bytes 221192 | tf_op jit(solution)/shard_map/ppermute | solution.py:947
  55.8 23.4 %collective-permute-start.5 = (bf16[512,768]{1,0:T(8,128)(2,1)}, bf16[512,768]{1,0:T(8,128)(2,1)}, u32[]{:S(2)}, u32[]{:S(2)}) collective-permute-start(bf16[512,768]{1,0:T(8,128)(2,1)} %slice.189), channel_id=1, source_target_pairs={{0,8},{4,12},{8,0},{12,4},{16,24},{20,28},{24,16},{28,20},{1,9},{5... | collective-permute-start | bytes 2359304 | tf_op jit(solution)/shard_map/ppermute | solution.py:947
  56.0 23.3 %collective-permute-start.6 = (bf16[512,768]{1,0:T(8,128)(2,1)}, bf16[512,768]{1,0:T(8,128)(2,1)}, u32[]{:S(2)}, u32[]{:S(2)}) collective-permute-start(bf16[512,768]{1,0:T(8,128)(2,1)} %slice.190), channel_id=1, source_target_pairs={{0,4},{4,0},{8,12},{12,8},{16,20},{20,16},{24,28},{28,24},{1,5},{5... | collective-permute-start | bytes 2359304 | tf_op jit(solution)/shard_map/ppermute | solution.py:947
  59.3 17.7 %collective-permute-start.13 = (bf16[4,48,768]{2,1,0:T(8,128)(2,1)S(1)}, bf16[4,48,768]{2,1,0:T(8,128)(2,1)S(1)}, u32[]{:S(2)}, u32[]{:S(2)}) collective-permute-start(bf16[4,48,768]{2,1,0:T(8,128)(2,1)S(1)} %pad_maximum_fusion.5), channel_id=1, source_target_pairs={{0,16},{4,20},{8,24},{12,28},{16,0},{20,4},{24,8},{28,12},{1,17},{... | collective-permute-start | bytes 884744 | tf_op jit(solution)/shard_map/ppermute | solution.py:947
  80.0 32.1 %collective-permute-start.15 = (bf16[9,48,768]{2,1,0:T(8,128)(2,1)}, bf16[9,48,768]{2,1,0:T(8,128)(2,1)}, u32[]{:S(2)}, u32[]{:S(2)}) collective-permute-start(bf16[9,48,768]{2,1,0:T(8,128)(2,1)} %copy-done.26), channel_id=1, source_target_pairs={{0,8},{4,12},{8,16},{12,20},{16,24},{20,28},{24,0},{28,4},{1,9},{5... | collective-permute-start | bytes 1990664 | tf_op jit(solution)/shard_map/ppermute | solution.py:1090
  85.1 27.0 %collective-permute-start.16 = (bf16[9,48,768]{2,1,0:T(8,128)(2,1)}, bf16[9,48,768]{2,1,0:T(8,128)(2,1)}, u32[]{:S(2)}, u32[]{:S(2)}) collective-permute-start(bf16[9,48,768]{2,1,0:T(8,128)(2,1)} %copy-done.26), channel_id=1, source_target_pairs={{0,4},{4,0},{8,12},{12,8},{16,20},{20,16},{24,28},{28,24},{1,5},{5... | collective-permute-start | bytes 1990664 | tf_op jit(solution)/shard_map/ppermute | solution.py:947
  113.3 21.3 %collective-permute-start.19 = (bf16[2,9,48,768]{3,2,1,0:T(8,128)(2,1)S(1)}, bf16[2,9,48,768]{3,2,1,0:T(8,128)(2,1)S(1)}, u32[]{:S(2)}, u32[]{:S(2)}) collective-permute-start(bf16[2,9,48,768]{3,2,1,0:T(8,128)(2,1)S(1)} %pad_maximum_fusion.refs_0_), channel_id=1, source_target_pairs={{0,1},{1,0},{2,3},{3,2},{4,5},{5,4},{6,7},{7,6},{8,9},{9,8},{10,11... | collective-permute-start | bytes 3981320 | tf_op jit(solution)/shard_map/ppermute | solution.py:947
  113.4 21.2 %collective-permute-start.17 = (bf16[9,48,768]{2,1,0:T(8,128)(2,1)}, bf16[9,48,768]{2,1,0:T(8,128)(2,1)S(1)}, u32[]{:S(2)}, u32[]{:S(2)}) collective-permute-start(bf16[9,48,768]{2,1,0:T(8,128)(2,1)} %collective-permute-done.15), channel_id=1, source_target_pairs={{0,8},{4,12},{8,16},{12,20},{16,24},{20,28},{24,0},{28,4},{1,9},{5... | collective-permute-start | bytes 1990664 | tf_op jit(solution)/shard_map/ppermute | solution.py:1090
  114.1 20.6 %collective-permute-start.18 = (bf16[9,48,768]{2,1,0:T(8,128)(2,1)}, bf16[9,48,768]{2,1,0:T(8,128)(2,1)S(1)}, u32[]{:S(2)}, u32[]{:S(2)}) collective-permute-start(bf16[9,48,768]{2,1,0:T(8,128)(2,1)} %collective-permute-done.15), channel_id=1, source_target_pairs={{0,4},{4,0},{8,12},{12,8},{16,20},{20,16},{24,28},{28,24},{1,5},{5... | collective-permute-start | bytes 1990664 | tf_op jit(solution)/shard_map/ppermute | solution.py:947
  136.4 19.6 %collective-permute-start.22 = (bf16[2,9,48,768]{3,2,1,0:T(8,128)(2,1)S(1)}, bf16[2,9,48,768]{3,2,1,0:T(8,128)(2,1)S(1)}, u32[]{:S(2)}, u32[]{:S(2)}) collective-permute-start(bf16[2,9,48,768]{3,2,1,0:T(8,128)(2,1)S(1)} %pad_maximum_fusion.1.refs_1_), channel_id=1, source_target_pairs={{0,1},{1,0},{2,3},{3,2},{4,5},{5,4},{6,7},{7,6},{8,9},{9,8},{10,11... | collective-permute-start | bytes 3981320 | tf_op jit(solution)/shard_map/ppermute | solution.py:947
  136.6 19.3 %collective-permute-start.20 = (bf16[9,48,768]{2,1,0:T(8,128)(2,1)S(1)}, bf16[9,48,768]{2,1,0:T(8,128)(2,1)S(1)}, u32[]{:S(2)}, u32[]{:S(2)}) collective-permute-start(bf16[9,48,768]{2,1,0:T(8,128)(2,1)S(1)} %collective-permute-done.17), channel_id=1, source_target_pairs={{0,8},{4,12},{8,16},{12,20},{16,24},{20,28},{24,0},{28,4},{1,9},{5... | collective-permute-start | bytes 1990664 | tf_op jit(solution)/shard_map/ppermute | solution.py:1090
  136.8 19.1 %collective-permute-start.21 = (bf16[9,48,768]{2,1,0:T(8,128)(2,1)S(1)}, bf16[9,48,768]{2,1,0:T(8,128)(2,1)S(1)}, u32[]{:S(2)}, u32[]{:S(2)}) collective-permute-start(bf16[9,48,768]{2,1,0:T(8,128)(2,1)S(1)} %collective-permute-done.17), channel_id=1, source_target_pairs={{0,4},{4,0},{8,12},{12,8},{16,20},{20,16},{24,28},{28,24},{1,5},{5... | collective-permute-start | bytes 1990664 | tf_op jit(solution)/shard_map/ppermute | solution.py:947
  157.2 34.3 %collective-permute-start.27 = (bf16[2,9,48,768]{3,2,1,0:T(8,128)(2,1)S(1)}, bf16[2,9,48,768]{3,2,1,0:T(8,128)(2,1)S(1)}, u32[]{:S(2)}, u32[]{:S(2)}) collective-permute-start(bf16[2,9,48,768]{3,2,1,0:T(8,128)(2,1)S(1)} %pad_maximum_fusion.2.refs_2_), channel_id=1, source_target_pairs={{0,1},{1,0},{2,3},{3,2},{4,5},{5,4},{6,7},{7,6},{8,9},{9,8},{10,11... | collective-permute-start | bytes 3981320 | tf_op jit(solution)/shard_map/ppermute | solution.py:947
  157.2 34.2 %collective-permute-start.26 = (bf16[9,48,768]{2,1,0:T(8,128)(2,1)S(1)}, bf16[9,48,768]{2,1,0:T(8,128)(2,1)S(1)}, u32[]{:S(2)}, u32[]{:S(2)}) collective-permute-start(bf16[9,48,768]{2,1,0:T(8,128)(2,1)S(1)} %collective-permute-done.20), channel_id=1, source_target_pairs={{0,4},{4,0},{8,12},{12,8},{16,20},{20,16},{24,28},{28,24},{1,5},{5... | collective-permute-start | bytes 1990664 | tf_op jit(solution)/shard_map/ppermute | solution.py:947
  162.7 28.7 %collective-permute-start.23 = (bf16[1536,128]{1,0:T(8,128)(2,1)S(1)}, bf16[1536,128]{1,0:T(8,128)(2,1)S(1)}, u32[]{:S(2)}, u32[]{:S(2)}) collective-permute-start(bf16[1536,128]{1,0:T(8,128)(2,1)S(1)} %mix.4), channel_id=1, source_target_pairs={{0,4},{4,0},{8,12},{12,8},{16,20},{20,16},{24,28},{28,24},{1,5},{5... | collective-permute-start | bytes 1179656 | tf_op jit(solution)/shard_map/ppermute | solution.py:947
  167.9 23.5 %collective-permute-start.24 = (bf16[1536,128]{1,0:T(8,128)(2,1)S(1)}, bf16[1536,128]{1,0:T(8,128)(2,1)S(1)}, u32[]{:S(2)}, u32[]{:S(2)}) collective-permute-start(bf16[1536,128]{1,0:T(8,128)(2,1)S(1)} %mix.5), channel_id=1, source_target_pairs={{0,8},{4,12},{8,0},{12,4},{16,24},{20,28},{24,16},{28,20},{1,9},{5... | collective-permute-start | bytes 1179656 | tf_op jit(solution)/shard_map/ppermute | solution.py:947
  172.9 18.5 %collective-permute-start.25 = (bf16[1536,128]{1,0:T(8,128)(2,1)S(1)}, bf16[1536,128]{1,0:T(8,128)(2,1)S(1)}, u32[]{:S(2)}, u32[]{:S(2)}) collective-permute-start(bf16[1536,128]{1,0:T(8,128)(2,1)S(1)} %mix.6), channel_id=1, source_target_pairs={{0,12},{4,8},{8,4},{12,0},{16,28},{20,24},{24,20},{28,16},{1,13},{... | collective-permute-start | bytes 1179656 | tf_op jit(solution)/shard_map/ppermute | solution.py:947
  193.8 81.2 %collective-permute-start.29 = (bf16[768,768]{1,0:T(8,128)(2,1)}, bf16[768,768]{1,0:T(8,128)(2,1)}, u32[]{:S(2)}, u32[]{:S(2)}) collective-permute-start(bf16[768,768]{1,0:T(8,128)(2,1)} %assemble.1.weight_ref), channel_id=1, source_target_pairs={{0,4},{4,0},{8,12},{12,8},{16,20},{20,16},{24,28},{28,24},{1,5},{5... | collective-permute-start | bytes 3538952 | tf_op jit(solution)/shard_map/ppermute | solution.py:947
  195.1 80.0 %collective-permute-start.30 = (bf16[768,768]{1,0:T(8,128)(2,1)}, bf16[768,768]{1,0:T(8,128)(2,1)}, u32[]{:S(2)}, u32[]{:S(2)}) collective-permute-start(bf16[768,768]{1,0:T(8,128)(2,1)} %assemble.1.weight_ref), channel_id=1, source_target_pairs={{0,8},{4,12},{8,0},{12,4},{16,24},{20,28},{24,16},{28,20},{1,9},{5... | collective-permute-start | bytes 3538952 | tf_op jit(solution)/shard_map/ppermute | solution.py:947
  195.1 80.0 %collective-permute-start.31 = (bf16[768,768]{1,0:T(8,128)(2,1)}, bf16[768,768]{1,0:T(8,128)(2,1)}, u32[]{:S(2)}, u32[]{:S(2)}) collective-permute-start(bf16[768,768]{1,0:T(8,128)(2,1)} %assemble.1.weight_ref), channel_id=1, source_target_pairs={{0,12},{4,8},{8,4},{12,0},{16,28},{20,24},{24,20},{28,16},{1,13},{... | collective-permute-start | bytes 3538952 | tf_op jit(solution)/shard_map/ppermute | solution.py:947
  275.1 18.2 %collective-permute-start.33 = (bf16[1536,128]{1,0:T(8,128)(2,1)}, bf16[1536,128]{1,0:T(8,128)(2,1)S(1)}, u32[]{:S(2)}, u32[]{:S(2)}) collective-permute-start(bf16[1536,128]{1,0:T(8,128)(2,1)} %get-tuple-element.228), channel_id=1, source_target_pairs={{0,4},{4,0},{8,12},{12,8},{16,20},{20,16},{24,28},{28,24},{1,5},{5... | collective-permute-start | bytes 1179656 | tf_op jit(solution)/shard_map/ppermute | solution.py:947
  276.4 17.0 %collective-permute-start.34 = (bf16[1536,128]{1,0:T(8,128)(2,1)}, bf16[1536,128]{1,0:T(8,128)(2,1)S(1)}, u32[]{:S(2)}, u32[]{:S(2)}) collective-permute-start(bf16[1536,128]{1,0:T(8,128)(2,1)} %get-tuple-element.229), channel_id=1, source_target_pairs={{0,8},{4,12},{8,0},{12,4},{16,24},{20,28},{24,16},{28,20},{1,9},{5... | collective-permute-start | bytes 1179656 | tf_op jit(solution)/shard_map/ppermute | solution.py:947
  276.4 20.1 %collective-permute-start.35 = (bf16[1536,128]{1,0:T(8,128)(2,1)}, bf16[1536,128]{1,0:T(8,128)(2,1)S(1)}, u32[]{:S(2)}, u32[]{:S(2)}) collective-permute-start(bf16[1536,128]{1,0:T(8,128)(2,1)} %get-tuple-element.230), channel_id=1, source_target_pairs={{0,12},{4,8},{8,4},{12,0},{16,28},{20,24},{24,20},{28,16},{1,13},{... | collective-permute-start | bytes 1179656 | tf_op jit(solution)/shard_map/ppermute | solution.py:947
  296.5 37.5 %collective-permute-start.36 = (bf16[8,3,48,384]{3,2,1,0:T(8,128)(2,1)}, bf16[8,3,48,384]{3,2,1,0:T(8,128)(2,1)}, u32[]{:S(2)}, u32[]{:S(2)}) collective-permute-start(bf16[8,3,48,384]{3,2,1,0:T(8,128)(2,1)} %fusion.5), channel_id=1, source_target_pairs={{0,2},{1,3},{2,0},{3,1},{4,6},{5,7},{6,4},{7,5},{8,10},{9,11},{10,... | collective-permute-start | bytes 2654216 | tf_op jit(solution)/shard_map/ppermute | solution.py:947
  298.0 37.6 %collective-permute-start.37 = (bf16[8,3,48,384]{3,2,1,0:T(8,128)(2,1)}, bf16[8,3,48,384]{3,2,1,0:T(8,128)(2,1)}, u32[]{:S(2)}, u32[]{:S(2)}) collective-permute-start(bf16[8,3,48,384]{3,2,1,0:T(8,128)(2,1)} %fusion.6), channel_id=1, source_target_pairs={{0,4},{4,0},{8,12},{12,8},{16,20},{20,16},{24,28},{28,24},{1,5},{5... | collective-permute-start | bytes 2654216 | tf_op jit(solution)/shard_map/ppermute | solution.py:947
  299.2 39.4 %collective-permute-start.38 = (bf16[8,3,48,384]{3,2,1,0:T(8,128)(2,1)}, bf16[8,3,48,384]{3,2,1,0:T(8,128)(2,1)}, u32[]{:S(2)}, u32[]{:S(2)}) collective-permute-start(bf16[8,3,48,384]{3,2,1,0:T(8,128)(2,1)} %fusion.7), channel_id=1, source_target_pairs={{0,8},{4,12},{8,0},{12,4},{16,24},{20,28},{24,16},{28,20},{1,9},{5... | collective-permute-start | bytes 2654216 | tf_op jit(solution)/shard_map/ppermute | solution.py:947
  341.8 17.6 %collective-permute-start.39 = (bf16[4,3,48,384]{3,2,1,0:T(8,128)(2,1)S(1)}, bf16[4,3,48,384]{3,2,1,0:T(8,128)(2,1)S(1)}, u32[]{:S(2)}, u32[]{:S(2)}) collective-permute-start(bf16[4,3,48,384]{3,2,1,0:T(8,128)(2,1)S(1)} %slice.333), channel_id=1, source_target_pairs={{0,4},{4,0},{8,12},{12,8},{16,20},{20,16},{24,28},{28,24},{1,5},{5... | collective-permute-start | bytes 1327112 | tf_op jit(solution)/shard_map/ppermute | solution.py:947
  342.8 20.4 %collective-permute-start.40 = (bf16[4,3,48,384]{3,2,1,0:T(8,128)(2,1)S(1)}, bf16[4,3,48,384]{3,2,1,0:T(8,128)(2,1)S(1)}, u32[]{:S(2)}, u32[]{:S(2)}) collective-permute-start(bf16[4,3,48,384]{3,2,1,0:T(8,128)(2,1)S(1)} %slice.332), channel_id=1, source_target_pairs={{0,8},{4,12},{8,0},{12,4},{16,24},{20,28},{24,16},{28,20},{1,9},{5... | collective-permute-start | bytes 1327112 | tf_op jit(solution)/shard_map/ppermute | solution.py:947
  344.4 21.8 %collective-permute-start.41 = (bf16[4,3,48,384]{3,2,1,0:T(8,128)(2,1)S(1)}, bf16[4,3,48,384]{3,2,1,0:T(8,128)(2,1)S(1)}, u32[]{:S(2)}, u32[]{:S(2)}) collective-permute-start(bf16[4,3,48,384]{3,2,1,0:T(8,128)(2,1)S(1)} %slice.331), channel_id=1, source_target_pairs={{0,16},{4,20},{8,24},{12,28},{16,0},{20,4},{24,8},{28,12},{1,17},{... | collective-permute-start | bytes 1327112 | tf_op jit(solution)/shard_map/ppermute | solution.py:947
  367.1 28.4 %collective-permute-start.42 = (bf16[2,3,48,384]{3,2,1,0:T(8,128)(2,1)}, bf16[2,3,48,384]{3,2,1,0:T(8,128)(2,1)}, u32[]{:S(2)}, u32[]{:S(2)}) collective-permute-start(bf16[2,3,48,384]{3,2,1,0:T(8,128)(2,1)} %slice.336), channel_id=1, source_target_pairs={{0,8},{4,12},{8,0},{12,4},{16,24},{20,28},{24,16},{28,20},{1,9},{5... | collective-permute-start | bytes 663560 | tf_op jit(solution)/shard_map/ppermute | solution.py:947
  367.5 28.0 %collective-permute-start.43 = (bf16[2,3,48,384]{3,2,1,0:T(8,128)(2,1)}, bf16[2,3,48,384]{3,2,1,0:T(8,128)(2,1)}, u32[]{:S(2)}, u32[]{:S(2)}) collective-permute-start(bf16[2,3,48,384]{3,2,1,0:T(8,128)(2,1)} %slice.335), channel_id=1, source_target_pairs={{0,16},{4,20},{8,24},{12,28},{16,0},{20,4},{24,8},{28,12},{1,17},{... | collective-permute-start | bytes 663560 | tf_op jit(solution)/shard_map/ppermute | solution.py:947
  370.1 25.5 %collective-permute-start.44 = (bf16[2,3,48,384]{3,2,1,0:T(8,128)(2,1)}, bf16[2,3,48,384]{3,2,1,0:T(8,128)(2,1)}, u32[]{:S(2)}, u32[]{:S(2)}) collective-permute-start(bf16[2,3,48,384]{3,2,1,0:T(8,128)(2,1)} %slice.334), channel_id=1, source_target_pairs={{0,2},{1,3},{2,0},{3,1},{4,6},{5,7},{6,4},{7,5},{8,10},{9,11},{10,... | collective-permute-start | bytes 663560 | tf_op jit(solution)/shard_map/ppermute | solution.py:947
  382.3 42.6 %collective-permute-start.52 = (bf16[1024,768]{1,0:T(8,128)(2,1)}, bf16[1024,768]{1,0:T(8,128)(2,1)}, u32[]{:S(2)}, u32[]{:S(2)}) collective-permute-start(bf16[1024,768]{1,0:T(8,128)(2,1)} %gather_grads.5.refs_3_), channel_id=1, source_target_pairs={{0,12},{4,8},{8,4},{12,0},{16,28},{20,24},{24,20},{28,16},{1,13},{... | collective-permute-start | bytes 4718600 | tf_op jit(solution)/shard_map/ppermute | solution.py:947
  397.2 24.0 %collective-permute-start.49 = (bf16[1,3,48,384]{3,2,1,0:T(8,128)(2,1)S(1)}, bf16[1,3,48,384]{3,2,1,0:T(8,128)(2,1)S(1)}, u32[]{:S(2)}, u32[]{:S(2)}) collective-permute-start(bf16[1,3,48,384]{3,2,1,0:T(8,128)(2,1)S(1)} %slice.339), channel_id=1, source_target_pairs={{0,16},{4,20},{8,24},{12,28},{16,0},{20,4},{24,8},{28,12},{1,17},{... | collective-permute-start | bytes 331784 | tf_op jit(solution)/shard_map/ppermute | solution.py:947
  400.4 21.4 %collective-permute-start.50 = (bf16[1,3,48,384]{3,2,1,0:T(8,128)(2,1)S(1)}, bf16[1,3,48,384]{3,2,1,0:T(8,128)(2,1)S(1)}, u32[]{:S(2)}, u32[]{:S(2)}) collective-permute-start(bf16[1,3,48,384]{3,2,1,0:T(8,128)(2,1)S(1)} %slice.338), channel_id=1, source_target_pairs={{0,2},{1,3},{2,0},{3,1},{4,6},{5,7},{6,4},{7,5},{8,10},{9,11},{10,... | collective-permute-start | bytes 331784 | tf_op jit(solution)/shard_map/ppermute | solution.py:947
  401.3 18.8 %collective-permute-start.47 = (bf16[3,96,384]{2,1,0:T(8,128)(2,1)S(1)}, bf16[3,96,384]{2,1,0:T(8,128)(2,1)S(1)}, u32[]{:S(2)}, u32[]{:S(2)}) collective-permute-start(bf16[3,96,384]{2,1,0:T(8,128)(2,1)S(1)} %fusion.8), channel_id=1, source_target_pairs={{0,16},{4,20},{8,24},{12,28},{16,0},{20,4},{24,8},{28,12},{1,17},{... | collective-permute-start | bytes 663560 | tf_op jit(solution)/shard_map/ppermute | solution.py:947
  404.3 18.2 %collective-permute-start.51 = (bf16[1,3,48,384]{3,2,1,0:T(8,128)(2,1)S(1)}, bf16[1,3,48,384]{3,2,1,0:T(8,128)(2,1)S(1)}, u32[]{:S(2)}, u32[]{:S(2)}) collective-permute-start(bf16[1,3,48,384]{3,2,1,0:T(8,128)(2,1)S(1)} %slice.337), channel_id=1, source_target_pairs={{0,4},{4,0},{8,12},{12,8},{16,20},{20,16},{24,28},{28,24},{1,5},{5... | collective-permute-start | bytes 331784 | tf_op jit(solution)/shard_map/ppermute | solution.py:947
  426.5 45.0 %collective-permute-start.55 = (bf16[1024,768]{1,0:T(8,128)(2,1)}, bf16[1024,768]{1,0:T(8,128)(2,1)}, u32[]{:S(2)}, u32[]{:S(2)}) collective-permute-start(bf16[1024,768]{1,0:T(8,128)(2,1)} %gather_grads.7.refs_1_), channel_id=1, source_target_pairs={{0,4},{4,0},{8,12},{12,8},{16,20},{20,16},{24,28},{28,24},{1,5},{5... | collective-permute-start | bytes 4718600 | tf_op jit(solution)/shard_map/ppermute | solution.py:947
  427.5 44.0 %collective-permute-start.56 = (bf16[1024,768]{1,0:T(8,128)(2,1)}, bf16[1024,768]{1,0:T(8,128)(2,1)}, u32[]{:S(2)}, u32[]{:S(2)}) collective-permute-start(bf16[1024,768]{1,0:T(8,128)(2,1)} %gather_grads.4.refs_2_), channel_id=1, source_target_pairs={{0,8},{4,12},{8,0},{12,4},{16,24},{20,28},{24,16},{28,20},{1,9},{5... | collective-permute-start | bytes 4718600 | tf_op jit(solution)/shard_map/ppermute | solution.py:947
  457.7 21.3 %all-to-all-start.1 = ((bf16[8,3,96,96]{3,2,1,0:T(8,128)(2,1)}), bf16[8,3,96,96]{3,2,1,0:T(8,128)(2,1)}, u32[]{:S(2)}, u32[]{:S(2)}) async-start(bf16[8,3,96,96]{3,2,1,0:T(8,128)(2,1)} %copy-done.16), calls=%async_computation.1 | async-start | bytes 1179648 | tf_op jit(solution)/shard_map/all_to_all | solution.py:1204
  491.0 19.8 %all-to-all-start.2 = ((bf16[8,3,96,96]{3,2,1,0:T(8,128)(2,1)}), bf16[8,3,96,96]{3,2,1,0:T(8,128)(2,1)}, u32[]{:S(2)}, u32[]{:S(2)}) async-start(bf16[8,3,96,96]{3,2,1,0:T(8,128)(2,1)} %copy-done.28), calls=%async_computation.2 | async-start | bytes 1179648 | tf_op jit(solution)/shard_map/all_to_all | solution.py:1204
  515.9 22.5 %all-to-all-start.3 = ((bf16[8,3,96,96]{3,2,1,0:T(8,128)(2,1)}), bf16[8,3,96,96]{3,2,1,0:T(8,128)(2,1)S(1)}, u32[]{:S(2)}, u32[]{:S(2)}) async-start(bf16[8,3,96,96]{3,2,1,0:T(8,128)(2,1)} %copy-done.17), calls=%async_computation.3 | async-start | bytes 1179648 | tf_op jit(solution)/shard_map/all_to_all | solution.py:1204
  520.4 17.3 %collective-permute-start.59 = (f32[12,768]{1,0:T(8,128)S(1)}, f32[12,768]{1,0:T(8,128)S(1)}, u32[]{:S(2)}, u32[]{:S(2)}) collective-permute-start(f32[12,768]{1,0:T(8,128)S(1)} %add.172), channel_id=1, source_target_pairs={{0,16},{4,20},{8,24},{12,28},{16,0},{20,4},{24,8},{28,12},{1,17},{... | collective-permute-start | bytes 110600 | tf_op jit(solution)/shard_map/ppermute | solution.py:947
  (108 other events, 691.5 us)

commit v8 on v7

--- a/solution.py
+++ b/solution.py
@@ -1115,12 +1115,13 @@
     mixed[3] = mix(orders[3], sorted_out[3])
     mixed[2] = mix(orders[2], sorted_out[2])
     mixed[1] = mix(orders[1], sorted_out[1])
+    (mixed[3], last) = together(mixed[3], sorted_out[0])
+    mixed[0] = mix(orders[0], last)
     mixed_parts = exchange_unit(mixed)
-    (mixed_parts[1:], flips[-1], other_rest, held_weights) = together(
-        mixed_parts[1:], flips[-1], other_rest, own_weights
+    (mixed_parts, flips[-1], other_rest, held_weights) = together(
+        mixed_parts, flips[-1], other_rest, own_weights
     )
     cross()
-    mixed_parts[0] = mix(orders[0], sorted_out[0])
     shards = mine_rest + other_rest
     sources = (tok + n_tok - 2 * jnp.arange(depth, dtype=jnp.int32)) & (n_tok - 1)
     sources = (sources[:, None] ^ jnp.arange(2, dtype=jnp.int32)[None, :]).reshape(-1)
@@ -1182,12 +1183,12 @@
     keep = kept_qkv.astype(F32) + swap(sent_qkv, "grp", 1).astype(F32)
     (keep, more) = together(keep, more)
     total = total + more
-    more = swap(total, "grp", 2)
+    more = swap(total, "tok", 1)
     unit_got = swap(keep[1].astype(BF16), "tok", UNIT)
     keep = keep[0] + unit_got.astype(F32)
     (keep, more, got_now, home_grads[3]) = together(keep, more, got_now, home_grads[3])
     total = total + more
-    more = swap(total, "tok", 1)
+    more = swap(total, "tok", 2)
     home_grads[1] = swap(own_grads[1], "tok", 1)
     home_grads[2] = swap(own_grads[2], "tok", 2)
     sent = pack(slot_block, kept_now, got_now, n_grp, slots)
@@ -1207,7 +1208,7 @@
     grad_inputs = grad_first + outer_cols(own_grads[0], own_weights)
     (part, home_grads, grad_inputs, more) = together(part, home_grads[1:], grad_inputs, more)
     total = total + more
-    more = swap(total, "tok", 2)
+    more = swap(total, "tok", 4)
     by_slot_of = lambda value: jnp.transpose(value, (1, 0, 2))
     new_one, new_two, turned = moments(
         place, part, right, by_slot_of(moment_one), by_slot_of(moment_two)
@@ -1218,7 +1219,7 @@
     (turned, more, grad_inputs, home_grads[2]) = together(turned, more, grad_inputs, home_grads[2])
     total = total + more
     change = to_tok(rotate_out(turned, left))
-    vector_total = total + swap(total, "tok", 4)
+    vector_total = total + swap(total, "grp", 2)
     new_master = by_slot_of(apply_change(place, change, by_slot_of(master)))
     new_one, new_two = by_slot_of(new_one), by_slot_of(new_two)
     grad_inputs = grad_inputs + outer_cols(home_grads[2], turned_weights[2])

time: 548 us -> 540 us (0.985)
    unnamed x189 -> x185, local copies, waits for them, and re-layouts: 39.9 us -> 36.6 us
  transfers between devices with their start and end apart: 64 -> 64, of which waited for: 19 -> 22; matrix products, arithmetic and copies ran while one was open for 15% -> 16% of each run, Pallas kernels for 39% -> 40%
where the time goes in v8:
time: 540 us; the launch traced here: 532 us
  Pallas kernels  228 us (42%)
  waiting for transfers between devices  90.6 us (17%)
  starting transfers between devices  87.5 us (16%)
  local copies, waits for them, and re-layouts  57.1 us (11%)
  other arithmetic  51.1 us (9%)
  matrix products  14.7 us (3%)
    pallas_call x1, Pallas kernels, layer(): pl.pallas_call(functools.partial(layer_body, n_shards), in_specs=[pl.Bloc...  69.8 us
    ppermute x57, waiting for transfers between devices, swap(): return lax.ppermute(value, axis, [(i, i ^ bit) for i in range(size)])  68.6 us
    ppermute x57, starting transfers between devices, swap(): return lax.ppermute(value, axis, [(i, i ^ bit) for i in range(size)])  64.4 us
    unnamed x185, local copies, waits for them, and re-layouts  36.6 us
    pallas_call x4, Pallas kernels, sort_rows(): pl.pallas_call(sort_body, grid=(HEADS_OWN,), in_specs=[pl.BlockSpec((8, c...  27.7 us
    pallas_call x4, Pallas kernels, gather_grads(): pl.pallas_call(gather_grads_body, grid=(HEADS_OWN,), in_specs=[pl.BlockSp...  20 us
    pallas_call x1, Pallas kernels, attend_back(): pl.pallas_call(attend_back_body, grid_spec=pltpu.PrefetchScalarGridSpec(n...  19.1 us
    pallas_call x4, Pallas kernels, mix(): pl.pallas_call(mix_body, grid=(HEADS_OWN,), in_specs=[pl.BlockSpec((8, co...  17.2 us
  transfers between devices with their start and end apart: 64, of which 22 were waited for; matrix products, arithmetic and copies ran while one was open for 16% of the time, Pallas kernels for 40%

profile of v8, /device:TPU:0, one launch (start us, length us, event | category | flops | bytes accessed | tf_op | source)
XLA Modules:
  0.0 532.0 jit_solution(9444333934594501442)
XLA Ops:
  0.6 3.0 collective-permute-start
  11.4 6.9 %places.1 = (s32[8,1024]{1,0:T(8,128)}, s32[8,1024]{1,0:T(8,128)}, s32[8,1024]{1,0:T(8,128)}, s32[8,1024]{1,0:T(8,128)}) custom-call(s32[2]{0:T(128)} %get-tuple-element.330.scalars_ref, s32[24,1024]{1,0:T(8,128)} %bitcast.127), custom_call_target="tpu_custom_call" | custom-call | tf_op jit(solution)/shard_map/places/pallas_call | solution.py:96
  18.3 14.8 %fusion = (bf16[3,768,768]{2,1,0:T(8,128)(2,1)}, bf16[3,768,768]{2,1,0:T(8,128)(2,1)}, bf16[3,768,768]{2,1,0:T(8,128)(2,1)}, bf16[3,768,768]{2,1,0:T(8,128)(2,1)S(1)}) fusion(f32[2,3,768,768]{3,2,1,0:T(8,128)} %param.18), kind=kLoop, calls=%fused_computation.2 | loop fusion | flops 10616832 | bytes 35389440 | tf_op jit(solution)/shard_map/convert_element_type | solution.py:1002
  63.2 13.8 %collective-permute-done.13 = bf16[4,48,768]{2,1,0:T(8,128)(2,1)S(1)} collective-permute-done((bf16[4,48,768]{2,1,0:T(8,128)(2,1)S(1)}, bf16[4,48,768]{2,1,0:T(8,128)(2,1)S(1)}, u32[]{:S(2)}, u32[]{:S(2)}) %collective-permute-start.13) | collective-permute-done | bytes 294944 | tf_op jit(solution)/shard_map/ppermute | solution.py:947
  80.0 5.1 collective-permute-start.15
  89.8 3.2 assemble.1.weight_ref
  95.1 6.6 %sort_rows.4.refs_0_ = bf16[6,1024,256]{2,1,0:T(8,128)(2,1)S(1)} custom-call(s32[8,1024]{1,0:T(8,128)S(1)} %copy-done.27, bf16[1024,768]{1,0:T(8,128)(2,1)S(1)} %bitcast.111, bf16[768,768]{1,0:T(8,128)(2,1)} %assemble.1.weight_ref, f32[1,768]{1,0:T(1,128)S(1)} %reshape.107.bias_ref), custom_call_target="tpu_custom_call" | custom-call | tf_op jit(solution)/shard_map/sort_rows/pallas_call | solution.py:221
  103.3 7.2 %sort_rows.5.refs_1_ = bf16[6,1024,256]{2,1,0:T(8,128)(2,1)S(1)} custom-call(s32[8,1024]{1,0:T(8,128)S(1)} %copy-done.31, bf16[1024,768]{1,0:T(8,128)(2,1)} %collective-permute-done.x_ref.refs_5_, bf16[768,768]{1,0:T(8,128)(2,1)} %assemble.1.weight_ref, f32[1,768]{1,0:T(1,128)S(1)} %reshape.107.bias_ref), custom_call_target="tpu_custom_call" | custom-call | tf_op jit(solution)/shard_map/sort_rows/pallas_call | solution.py:221
  115.0 7.1 %sort_rows.6.refs_2_ = bf16[6,1024,256]{2,1,0:T(8,128)(2,1)S(1)} custom-call(s32[8,1024]{1,0:T(8,128)S(1)} %copy-done.34, bf16[1024,768]{1,0:T(8,128)(2,1)} %collective-permute-done.1.x_ref.refs_6_, bf16[768,768]{1,0:T(8,128)(2,1)} %assemble.1.weight_ref, f32[1,768]{1,0:T(1,128)S(1)} %reshape.107.bias_ref), custom_call_target="tpu_custom_call" | custom-call | tf_op jit(solution)/shard_map/sort_rows/pallas_call | solution.py:221
  126.2 6.9 %sort_rows.7.refs_3_ = bf16[6,1024,256]{2,1,0:T(8,128)(2,1)S(1)} custom-call(s32[8,1024]{1,0:T(8,128)S(1)} %copy-done.37, bf16[1024,768]{1,0:T(8,128)(2,1)S(1)} %constant_dynamic-update-slice_fusion.5.x_ref.refs_7_, bf16[768,768]{1,0:T(8,128)(2,1)} %assemble.1.weight_ref, f32[1,768]{1,0:T(1,128)S(1)} %reshape.107.bias_ref), custom_call_target="tpu_custom_call" | custom-call | tf_op jit(solution)/shard_map/sort_rows/pallas_call | solution.py:221
  138.0 16.5 %attend.1 = (bf16[6,1024,128]{2,1,0:T(8,128)(2,1)S(1)}, bf16[6,1024,128]{2,1,0:T(8,128)(2,1)S(1)}, bf16[6,1024,128]{2,1,0:T(8,128)(2,1)S(1)}, bf16[6,1024,128]{2,1,0:T(8,128)(2,1)}) custom-call(s32[1]{0:T(128)} %bitcast.11.long_ref, bf16[6,1024,256]{2,1,0:T(8,128)(2,1)} %copy-done, bf16[6,1024,256]{2,1,0:T(8,128)(2,1)} %copy-done.1, ...), custom_call_target="tpu_custom_call" | custom-call | tf_op jit(solution)/shard_map/attend/pallas_call | solution.py:345
  158.5 4.2 mix.4
  162.8 4.3 mix.6
  168.0 4.4 mix.7
  175.1 4.2 mix.5.refs_8_
  184.5 7.9 %collective-permute-done.25.refs_11_ = bf16[1536,128]{1,0:T(8,128)(2,1)S(1)} collective-permute-done((bf16[1536,128]{1,0:T(8,128)(2,1)S(1)}, bf16[1536,128]{1,0:T(8,128)(2,1)S(1)}, u32[]{:S(2)}, u32[]{:S(2)}) %collective-permute-start.25) | collective-permute-done | bytes 393248 | tf_op jit(solution)/shard_map/ppermute | solution.py:947
  199.0 69.8 %layer.1 = (bf16[1024,768]{1,0:T(8,128)(2,1)}, f32[1024,768]{1,0:T(8,128)}, f32[16,768]{1,0:T(8,128)}, bf16[3,16,3,48,384]{4,3,2,1,0:T(8,128)(2,1)}, bf16[3,16,3...) custom-call(s32[22]{0:T(128)} %concatenate.28.table_ref, ...), custom_call_target="tpu_custom_call" | custom-call | tf_op jit(solution)/shard_map/layer/pallas_call | solution.py:713
  273.4 3.8 sort_grads.4.refs_4_
  277.9 4.6 convert_add_fusion
  287.1 3.1 collective-permute-done.35.rows_ref
  292.9 3.8 sort_grads.5.refs_5_
  297.9 4.2 sort_grads.6.refs_6_
  303.3 3.8 sort_grads.7.refs_7_
  308.3 19.1 %attend_back.1 = (bf16[6,1024,256]{2,1,0:T(8,128)(2,1)}, bf16[6,1024,256]{2,1,0:T(8,128)(2,1)}, bf16[6,1024,256]{2,1,0:T(8,128)(2,1)}, bf16[6,1024,256]{2,1,0:T(8,128)(2,1)}) custom-call(s32[1]{0:T(128)} %bitcast.11.long_ref, bf16[6,1024,256]{2,1,0:T(8,128)(2,1)} %copy-done, bf16[6,1024,256]{2,1,0:T(8,128)(2,1)} %copy-done.1, ...), custom_call_target="tpu_custom_call" | custom-call | tf_op jit(solution)/shard_map/attend_back/pallas_call | solution.py:389
  338.1 3.2 collective-permute-start.41
  341.2 5.3 gather_grads.4.refs_2_
  346.5 5.1 gather_grads.5.refs_3_
  352.4 3.3 collective-permute-done.40
  363.4 4.4 gather_grads.6.refs_0_
  368.9 5.3 gather_grads.7.refs_1_
  374.8 10.8 %qkv_back.1 = (bf16[2,3,96,384]{3,2,1,0:T(8,128)(2,1)}, bf16[2,3,96,384]{3,2,1,0:T(8,128)(2,1)}, f32[8,768]{1,0:T(8,128)}) custom-call(s32[2]{0:T(128)} %get-tuple-element.331.scalars_ref, bf16[1024,768]{1,0:T(8,128)(2,1)} %copy-done.6, bf16[1024,768]{1,0:T(8,128)(2,1)} %gather_grads.7.refs_1_, bf16[1024,768]{1,0:T(8,128)(2,1)} %gather_grads.4.refs_2_, ...), custom_call_target="tpu_custom_call" | custom-call | tf_op jit(solution)/shard_map/qkv_back/pallas_call | solution.py:778
  397.9 15.1 %collective-permute-done.47 = bf16[3,96,384]{2,1,0:T(8,128)(2,1)S(1)} collective-permute-done((bf16[3,96,384]{2,1,0:T(8,128)(2,1)S(1)}, bf16[3,96,384]{2,1,0:T(8,128)(2,1)S(1)}, u32[]{:S(2)}, u32[]{:S(2)}) %collective-permute-start.47) | collective-permute-done | bytes 221216 | tf_op jit(solution)/shard_map/ppermute | solution.py:947
  420.7 3.0 collective-permute-start.56
  432.0 4.1 all-to-all-start
  438.0 6.2 %all-to-all-done.got_ref = bf16[4,3,48,384]{3,2,1,0:T(8,128)(2,1)} async-done(((bf16[4,3,48,384]{3,2,1,0:T(8,128)(2,1)}), bf16[4,3,48,384]{3,2,1,0:T(8,128)(2,1)}, u32[]{:S(2)}, u32[]{:S(2)}) %all-to-all-start) | async-done | bytes 442400 | tf_op jit(solution)/shard_map/all_to_all | solution.py:1195
  445.2 4.4 rotate_in.1
  450.4 5.2 all-to-all-start.1
  458.5 3.3 fusion.19
  466.3 5.3 all-to-all-done.1.got_ref
  474.0 8.9 %moments.1 = (f32[3,96,768]{2,1,0:T(8,128)}, f32[3,96,768]{2,1,0:T(8,128)}, bf16[8,3,96,96]{3,2,1,0:T(8,128)(2,1)S(1)}) custom-call(bf16[8,3,96,96]{3,2,1,0:T(8,128)(2,1)} %all-to-all-done.1.got_ref, bf16[3,768,768]{2,1,0:T(8,128)(2,1)} %get-tuple-element.283.high_ref, bf16[3,768,768]{2,1,0:T(8,128)(2,1)} %get-tuple-element.284.low_ref, ...), custom_call_target="tpu_custom_call" | custom-call | tf_op jit(solution)/shard_map/moments/pallas_call | solution.py:882
  483.7 4.2 all-to-all-start.2
  491.6 3.2 fusion.20
  494.8 4.9 add_add_fusion
  499.7 5.9 %collective-permute-done.58 = f32[12,768]{1,0:T(8,128)} collective-permute-done((f32[12,768]{1,0:T(8,128)S(1)}, f32[12,768]{1,0:T(8,128)}, u32[]{:S(2)}, u32[]{:S(2)}) %collective-permute-start.58) | collective-permute-done | bytes 36896 | tf_op jit(solution)/shard_map/ppermute | solution.py:947
  505.7 4.2 rotate_out.1
  510.7 3.6 all-to-all-start.3
  515.2 3.3 fusion.21
  521.3 9.1 %all-to-all-done.3.got_ref = bf16[8,3,96,96]{3,2,1,0:T(8,128)(2,1)S(1)} async-done(((bf16[8,3,96,96]{3,2,1,0:T(8,128)(2,1)}), bf16[8,3,96,96]{3,2,1,0:T(8,128)(2,1)S(1)}, u32[]{:S(2)}, u32[]{:S(2)}) %all-to-all-start.3) | async-done | bytes 442400 | tf_op jit(solution)/shard_map/all_to_all | solution.py:1205
  (379 shorter events, 169.7 us)
Async XLA Ops:
  0.6 37.7 %collective-permute-start = (bf16[1024,768]{1,0:T(8,128)(2,1)}, bf16[1024,768]{1,0:T(8,128)(2,1)}, u32[]{:S(2)}, u32[]{:S(2)}) collective-permute-start(bf16[1024,768]{1,0:T(8,128)(2,1)} %bitcast.107), channel_id=1, source_target_pairs={{0,4},{4,0},{8,12},{12,8},{16,20},{20,16},{24,28},{28,24},{1,5},{5... | collective-permute-start | bytes 4718600 | tf_op jit(solution)/shard_map/ppermute | solution.py:947
  3.7 36.2 %collective-permute-start.1 = (bf16[1024,768]{1,0:T(8,128)(2,1)}, bf16[1024,768]{1,0:T(8,128)(2,1)}, u32[]{:S(2)}, u32[]{:S(2)}) collective-permute-start(bf16[1024,768]{1,0:T(8,128)(2,1)} %bitcast.108), channel_id=1, source_target_pairs={{0,8},{4,12},{8,0},{12,4},{16,24},{20,28},{24,16},{28,20},{1,9},{5... | collective-permute-start | bytes 4718600 | tf_op jit(solution)/shard_map/ppermute | solution.py:947
  7.2 28.8 %collective-permute-start.2 = (bf16[3,96,768]{2,1,0:T(8,128)(2,1)}, bf16[3,96,768]{2,1,0:T(8,128)(2,1)}, u32[]{:S(2)}, u32[]{:S(2)}) collective-permute-start(bf16[3,96,768]{2,1,0:T(8,128)(2,1)} %convert_bitcast_fusion.refs_0_), channel_id=1, source_target_pairs={{0,1},{1,0},{2,3},{3,2},{4,5},{5,4},{6,7},{7,6},{8,9},{9,8},{10,11... | collective-permute-start | bytes 1327112 | tf_op jit(solution)/shard_map/ppermute | solution.py:947
  7.2 25.9 %collective-permute-start.3 = (bf16[3,96,768]{2,1,0:T(8,128)(2,1)}, bf16[3,96,768]{2,1,0:T(8,128)(2,1)}, u32[]{:S(2)}, u32[]{:S(2)}) collective-permute-start(bf16[3,96,768]{2,1,0:T(8,128)(2,1)} %convert_bitcast_fusion.refs_0_), channel_id=1, source_target_pairs={{0,2},{1,3},{2,0},{3,1},{4,6},{5,7},{6,4},{7,5},{8,10},{9,11},{10,... | collective-permute-start | bytes 1327112 | tf_op jit(solution)/shard_map/ppermute | solution.py:947
  41.9 16.0 %collective-permute-start.7 = (bf16[48,768]{1,0:T(8,128)(2,1)S(1)}, bf16[48,768]{1,0:T(8,128)(2,1)S(1)}, u32[]{:S(2)}, u32[]{:S(2)}) collective-permute-start(bf16[48,768]{1,0:T(8,128)(2,1)S(1)} %get-tuple-element.167), channel_id=1, source_target_pairs={{0,4},{4,0},{8,12},{12,8},{16,20},{20,16},{24,28},{28,24},{1,5},{5... | collective-permute-start | bytes 221192 | tf_op jit(solution)/shard_map/ppermute | solution.py:947
  42.4 15.6 %collective-permute-start.8 = (bf16[48,768]{1,0:T(8,128)(2,1)S(1)}, bf16[48,768]{1,0:T(8,128)(2,1)S(1)}, u32[]{:S(2)}, u32[]{:S(2)}) collective-permute-start(bf16[48,768]{1,0:T(8,128)(2,1)S(1)} %get-tuple-element.168), channel_id=1, source_target_pairs={{0,8},{4,12},{8,0},{12,4},{16,24},{20,28},{24,16},{28,20},{1,9},{5... | collective-permute-start | bytes 221192 | tf_op jit(solution)/shard_map/ppermute | solution.py:947
  44.1 13.9 %collective-permute-start.9 = (bf16[48,768]{1,0:T(8,128)(2,1)S(1)}, bf16[48,768]{1,0:T(8,128)(2,1)S(1)}, u32[]{:S(2)}, u32[]{:S(2)}) collective-permute-start(bf16[48,768]{1,0:T(8,128)(2,1)S(1)} %get-tuple-element.169), channel_id=1, source_target_pairs={{0,12},{4,8},{8,4},{12,0},{16,28},{20,24},{24,20},{28,16},{1,13},{... | collective-permute-start | bytes 221192 | tf_op jit(solution)/shard_map/ppermute | solution.py:947
  55.8 23.4 %collective-permute-start.5 = (bf16[512,768]{1,0:T(8,128)(2,1)}, bf16[512,768]{1,0:T(8,128)(2,1)}, u32[]{:S(2)}, u32[]{:S(2)}) collective-permute-start(bf16[512,768]{1,0:T(8,128)(2,1)} %slice.189), channel_id=1, source_target_pairs={{0,8},{4,12},{8,0},{12,4},{16,24},{20,28},{24,16},{28,20},{1,9},{5... | collective-permute-start | bytes 2359304 | tf_op jit(solution)/shard_map/ppermute | solution.py:947
  56.0 23.3 %collective-permute-start.6 = (bf16[512,768]{1,0:T(8,128)(2,1)}, bf16[512,768]{1,0:T(8,128)(2,1)}, u32[]{:S(2)}, u32[]{:S(2)}) collective-permute-start(bf16[512,768]{1,0:T(8,128)(2,1)} %slice.190), channel_id=1, source_target_pairs={{0,4},{4,0},{8,12},{12,8},{16,20},{20,16},{24,28},{28,24},{1,5},{5... | collective-permute-start | bytes 2359304 | tf_op jit(solution)/shard_map/ppermute | solution.py:947
  59.3 17.7 %collective-permute-start.13 = (bf16[4,48,768]{2,1,0:T(8,128)(2,1)S(1)}, bf16[4,48,768]{2,1,0:T(8,128)(2,1)S(1)}, u32[]{:S(2)}, u32[]{:S(2)}) collective-permute-start(bf16[4,48,768]{2,1,0:T(8,128)(2,1)S(1)} %pad_maximum_fusion.5), channel_id=1, source_target_pairs={{0,16},{4,20},{8,24},{12,28},{16,0},{20,4},{24,8},{28,12},{1,17},{... | collective-permute-start | bytes 884744 | tf_op jit(solution)/shard_map/ppermute | solution.py:947
  80.0 32.1 %collective-permute-start.15 = (bf16[9,48,768]{2,1,0:T(8,128)(2,1)}, bf16[9,48,768]{2,1,0:T(8,128)(2,1)}, u32[]{:S(2)}, u32[]{:S(2)}) collective-permute-start(bf16[9,48,768]{2,1,0:T(8,128)(2,1)} %copy-done.24), channel_id=1, source_target_pairs={{0,8},{4,12},{8,16},{12,20},{16,24},{20,28},{24,0},{28,4},{1,9},{5... | collective-permute-start | bytes 1990664 | tf_op jit(solution)/shard_map/ppermute | solution.py:1090
  85.1 27.1 %collective-permute-start.16 = (bf16[9,48,768]{2,1,0:T(8,128)(2,1)}, bf16[9,48,768]{2,1,0:T(8,128)(2,1)}, u32[]{:S(2)}, u32[]{:S(2)}) collective-permute-start(bf16[9,48,768]{2,1,0:T(8,128)(2,1)} %copy-done.24), channel_id=1, source_target_pairs={{0,4},{4,0},{8,12},{12,8},{16,20},{20,16},{24,28},{28,24},{1,5},{5... | collective-permute-start | bytes 1990664 | tf_op jit(solution)/shard_map/ppermute | solution.py:947
  113.4 21.3 %collective-permute-start.19 = (bf16[2,9,48,768]{3,2,1,0:T(8,128)(2,1)S(1)}, bf16[2,9,48,768]{3,2,1,0:T(8,128)(2,1)S(1)}, u32[]{:S(2)}, u32[]{:S(2)}) collective-permute-start(bf16[2,9,48,768]{3,2,1,0:T(8,128)(2,1)S(1)} %pad_maximum_fusion.refs_0_), channel_id=1, source_target_pairs={{0,1},{1,0},{2,3},{3,2},{4,5},{5,4},{6,7},{7,6},{8,9},{9,8},{10,11... | collective-permute-start | bytes 3981320 | tf_op jit(solution)/shard_map/ppermute | solution.py:947
  113.5 21.2 %collective-permute-start.17 = (bf16[9,48,768]{2,1,0:T(8,128)(2,1)}, bf16[9,48,768]{2,1,0:T(8,128)(2,1)S(1)}, u32[]{:S(2)}, u32[]{:S(2)}) collective-permute-start(bf16[9,48,768]{2,1,0:T(8,128)(2,1)} %collective-permute-done.15), channel_id=1, source_target_pairs={{0,8},{4,12},{8,16},{12,20},{16,24},{20,28},{24,0},{28,4},{1,9},{5... | collective-permute-start | bytes 1990664 | tf_op jit(solution)/shard_map/ppermute | solution.py:1090
  114.1 20.6 %collective-permute-start.18 = (bf16[9,48,768]{2,1,0:T(8,128)(2,1)}, bf16[9,48,768]{2,1,0:T(8,128)(2,1)S(1)}, u32[]{:S(2)}, u32[]{:S(2)}) collective-permute-start(bf16[9,48,768]{2,1,0:T(8,128)(2,1)} %collective-permute-done.15), channel_id=1, source_target_pairs={{0,4},{4,0},{8,12},{12,8},{16,20},{20,16},{24,28},{28,24},{1,5},{5... | collective-permute-start | bytes 1990664 | tf_op jit(solution)/shard_map/ppermute | solution.py:947
  136.4 19.6 %collective-permute-start.22 = (bf16[2,9,48,768]{3,2,1,0:T(8,128)(2,1)S(1)}, bf16[2,9,48,768]{3,2,1,0:T(8,128)(2,1)S(1)}, u32[]{:S(2)}, u32[]{:S(2)}) collective-permute-start(bf16[2,9,48,768]{3,2,1,0:T(8,128)(2,1)S(1)} %pad_maximum_fusion.1.refs_1_), channel_id=1, source_target_pairs={{0,1},{1,0},{2,3},{3,2},{4,5},{5,4},{6,7},{7,6},{8,9},{9,8},{10,11... | collective-permute-start | bytes 3981320 | tf_op jit(solution)/shard_map/ppermute | solution.py:947
  136.6 19.3 %collective-permute-start.20 = (bf16[9,48,768]{2,1,0:T(8,128)(2,1)S(1)}, bf16[9,48,768]{2,1,0:T(8,128)(2,1)S(1)}, u32[]{:S(2)}, u32[]{:S(2)}) collective-permute-start(bf16[9,48,768]{2,1,0:T(8,128)(2,1)S(1)} %collective-permute-done.17), channel_id=1, source_target_pairs={{0,8},{4,12},{8,16},{12,20},{16,24},{20,28},{24,0},{28,4},{1,9},{5... | collective-permute-start | bytes 1990664 | tf_op jit(solution)/shard_map/ppermute | solution.py:1090
  136.9 19.1 %collective-permute-start.21 = (bf16[9,48,768]{2,1,0:T(8,128)(2,1)S(1)}, bf16[9,48,768]{2,1,0:T(8,128)(2,1)S(1)}, u32[]{:S(2)}, u32[]{:S(2)}) collective-permute-start(bf16[9,48,768]{2,1,0:T(8,128)(2,1)S(1)} %collective-permute-done.17), channel_id=1, source_target_pairs={{0,4},{4,0},{8,12},{12,8},{16,20},{20,16},{24,28},{28,24},{1,5},{5... | collective-permute-start | bytes 1990664 | tf_op jit(solution)/shard_map/ppermute | solution.py:947
  157.2 35.2 %collective-permute-start.27 = (bf16[2,9,48,768]{3,2,1,0:T(8,128)(2,1)S(1)}, bf16[2,9,48,768]{3,2,1,0:T(8,128)(2,1)S(1)}, u32[]{:S(2)}, u32[]{:S(2)}) collective-permute-start(bf16[2,9,48,768]{3,2,1,0:T(8,128)(2,1)S(1)} %pad_maximum_fusion.2.refs_2_), channel_id=1, source_target_pairs={{0,1},{1,0},{2,3},{3,2},{4,5},{5,4},{6,7},{7,6},{8,9},{9,8},{10,11... | collective-permute-start | bytes 3981320 | tf_op jit(solution)/shard_map/ppermute | solution.py:947
  157.3 35.2 %collective-permute-start.26 = (bf16[9,48,768]{2,1,0:T(8,128)(2,1)S(1)}, bf16[9,48,768]{2,1,0:T(8,128)(2,1)S(1)}, u32[]{:S(2)}, u32[]{:S(2)}) collective-permute-start(bf16[9,48,768]{2,1,0:T(8,128)(2,1)S(1)} %collective-permute-done.20), channel_id=1, source_target_pairs={{0,4},{4,0},{8,12},{12,8},{16,20},{20,16},{24,28},{28,24},{1,5},{5... | collective-permute-start | bytes 1990664 | tf_op jit(solution)/shard_map/ppermute | solution.py:947
  167.0 16.1 %collective-permute-start.23 = (bf16[1536,128]{1,0:T(8,128)(2,1)S(1)}, bf16[1536,128]{1,0:T(8,128)(2,1)S(1)}, u32[]{:S(2)}, u32[]{:S(2)}) collective-permute-start(bf16[1536,128]{1,0:T(8,128)(2,1)S(1)} %mix.6), channel_id=1, source_target_pairs={{0,4},{4,0},{8,12},{12,8},{16,20},{20,16},{24,28},{28,24},{1,5},{5... | collective-permute-start | bytes 1179656 | tf_op jit(solution)/shard_map/ppermute | solution.py:947
  172.5 19.9 %collective-permute-start.25 = (bf16[1536,128]{1,0:T(8,128)(2,1)S(1)}, bf16[1536,128]{1,0:T(8,128)(2,1)S(1)}, u32[]{:S(2)}, u32[]{:S(2)}) collective-permute-start(bf16[1536,128]{1,0:T(8,128)(2,1)S(1)} %mix.4), channel_id=1, source_target_pairs={{0,12},{4,8},{8,4},{12,0},{16,28},{20,24},{24,20},{28,16},{1,13},{... | collective-permute-start | bytes 1179656 | tf_op jit(solution)/shard_map/ppermute | solution.py:947
  194.8 74.0 %collective-permute-start.29 = (bf16[768,768]{1,0:T(8,128)(2,1)}, bf16[768,768]{1,0:T(8,128)(2,1)}, u32[]{:S(2)}, u32[]{:S(2)}) collective-permute-start(bf16[768,768]{1,0:T(8,128)(2,1)} %assemble.1.weight_ref), channel_id=1, source_target_pairs={{0,4},{4,0},{8,12},{12,8},{16,20},{20,16},{24,28},{28,24},{1,5},{5... | collective-permute-start | bytes 3538952 | tf_op jit(solution)/shard_map/ppermute | solution.py:947
  195.7 73.1 %collective-permute-start.30 = (bf16[768,768]{1,0:T(8,128)(2,1)}, bf16[768,768]{1,0:T(8,128)(2,1)}, u32[]{:S(2)}, u32[]{:S(2)}) collective-permute-start(bf16[768,768]{1,0:T(8,128)(2,1)} %assemble.1.weight_ref), channel_id=1, source_target_pairs={{0,8},{4,12},{8,0},{12,4},{16,24},{20,28},{24,16},{28,20},{1,9},{5... | collective-permute-start | bytes 3538952 | tf_op jit(solution)/shard_map/ppermute | solution.py:947
  196.0 72.8 %collective-permute-start.31 = (bf16[768,768]{1,0:T(8,128)(2,1)}, bf16[768,768]{1,0:T(8,128)(2,1)}, u32[]{:S(2)}, u32[]{:S(2)}) collective-permute-start(bf16[768,768]{1,0:T(8,128)(2,1)} %assemble.1.weight_ref), channel_id=1, source_target_pairs={{0,12},{4,8},{8,4},{12,0},{16,28},{20,24},{24,20},{28,16},{1,13},{... | collective-permute-start | bytes 3538952 | tf_op jit(solution)/shard_map/ppermute | solution.py:947
  268.9 18.2 %collective-permute-start.33 = (bf16[1536,128]{1,0:T(8,128)(2,1)}, bf16[1536,128]{1,0:T(8,128)(2,1)S(1)}, u32[]{:S(2)}, u32[]{:S(2)}) collective-permute-start(bf16[1536,128]{1,0:T(8,128)(2,1)} %get-tuple-element.234), channel_id=1, source_target_pairs={{0,4},{4,0},{8,12},{12,8},{16,20},{20,16},{24,28},{28,24},{1,5},{5... | collective-permute-start | bytes 1179656 | tf_op jit(solution)/shard_map/ppermute | solution.py:947
  269.8 17.3 %collective-permute-start.34 = (bf16[1536,128]{1,0:T(8,128)(2,1)}, bf16[1536,128]{1,0:T(8,128)(2,1)S(1)}, u32[]{:S(2)}, u32[]{:S(2)}) collective-permute-start(bf16[1536,128]{1,0:T(8,128)(2,1)} %get-tuple-element.235), channel_id=1, source_target_pairs={{0,8},{4,12},{8,0},{12,4},{16,24},{20,28},{24,16},{28,20},{1,9},{5... | collective-permute-start | bytes 1179656 | tf_op jit(solution)/shard_map/ppermute | solution.py:947
  270.1 20.2 %collective-permute-start.35 = (bf16[1536,128]{1,0:T(8,128)(2,1)}, bf16[1536,128]{1,0:T(8,128)(2,1)S(1)}, u32[]{:S(2)}, u32[]{:S(2)}) collective-permute-start(bf16[1536,128]{1,0:T(8,128)(2,1)} %get-tuple-element.236), channel_id=1, source_target_pairs={{0,12},{4,8},{8,4},{12,0},{16,28},{20,24},{24,20},{28,16},{1,13},{... | collective-permute-start | bytes 1179656 | tf_op jit(solution)/shard_map/ppermute | solution.py:947
  290.2 37.1 %collective-permute-start.36 = (bf16[8,3,48,384]{3,2,1,0:T(8,128)(2,1)}, bf16[8,3,48,384]{3,2,1,0:T(8,128)(2,1)}, u32[]{:S(2)}, u32[]{:S(2)}) collective-permute-start(bf16[8,3,48,384]{3,2,1,0:T(8,128)(2,1)} %fusion.5), channel_id=1, source_target_pairs={{0,2},{1,3},{2,0},{3,1},{4,6},{5,7},{6,4},{7,5},{8,10},{9,11},{10,... | collective-permute-start | bytes 2654216 | tf_op jit(solution)/shard_map/ppermute | solution.py:947
  291.7 37.2 %collective-permute-start.37 = (bf16[8,3,48,384]{3,2,1,0:T(8,128)(2,1)}, bf16[8,3,48,384]{3,2,1,0:T(8,128)(2,1)}, u32[]{:S(2)}, u32[]{:S(2)}) collective-permute-start(bf16[8,3,48,384]{3,2,1,0:T(8,128)(2,1)} %fusion.6), channel_id=1, source_target_pairs={{0,4},{4,0},{8,12},{12,8},{16,20},{20,16},{24,28},{28,24},{1,5},{5... | collective-permute-start | bytes 2654216 | tf_op jit(solution)/shard_map/ppermute | solution.py:947
  292.6 39.4 %collective-permute-start.38 = (bf16[8,3,48,384]{3,2,1,0:T(8,128)(2,1)}, bf16[8,3,48,384]{3,2,1,0:T(8,128)(2,1)}, u32[]{:S(2)}, u32[]{:S(2)}) collective-permute-start(bf16[8,3,48,384]{3,2,1,0:T(8,128)(2,1)} %fusion.7), channel_id=1, source_target_pairs={{0,8},{4,12},{8,0},{12,4},{16,24},{20,28},{24,16},{28,20},{1,9},{5... | collective-permute-start | bytes 2654216 | tf_op jit(solution)/shard_map/ppermute | solution.py:947
  335.1 16.4 %collective-permute-start.39 = (bf16[4,3,48,384]{3,2,1,0:T(8,128)(2,1)S(1)}, bf16[4,3,48,384]{3,2,1,0:T(8,128)(2,1)S(1)}, u32[]{:S(2)}, u32[]{:S(2)}) collective-permute-start(bf16[4,3,48,384]{3,2,1,0:T(8,128)(2,1)S(1)} %slice.333), channel_id=1, source_target_pairs={{0,4},{4,0},{8,12},{12,8},{16,20},{20,16},{24,28},{28,24},{1,5},{5... | collective-permute-start | bytes 1327112 | tf_op jit(solution)/shard_map/ppermute | solution.py:947
  336.3 19.4 %collective-permute-start.40 = (bf16[4,3,48,384]{3,2,1,0:T(8,128)(2,1)S(1)}, bf16[4,3,48,384]{3,2,1,0:T(8,128)(2,1)S(1)}, u32[]{:S(2)}, u32[]{:S(2)}) collective-permute-start(bf16[4,3,48,384]{3,2,1,0:T(8,128)(2,1)S(1)} %slice.332), channel_id=1, source_target_pairs={{0,8},{4,12},{8,0},{12,4},{16,24},{20,28},{24,16},{28,20},{1,9},{5... | collective-permute-start | bytes 1327112 | tf_op jit(solution)/shard_map/ppermute | solution.py:947
  338.1 21.2 %collective-permute-start.41 = (bf16[4,3,48,384]{3,2,1,0:T(8,128)(2,1)S(1)}, bf16[4,3,48,384]{3,2,1,0:T(8,128)(2,1)S(1)}, u32[]{:S(2)}, u32[]{:S(2)}) collective-permute-start(bf16[4,3,48,384]{3,2,1,0:T(8,128)(2,1)S(1)} %slice.331), channel_id=1, source_target_pairs={{0,16},{4,20},{8,24},{12,28},{16,0},{20,4},{24,8},{28,12},{1,17},{... | collective-permute-start | bytes 1327112 | tf_op jit(solution)/shard_map/ppermute | solution.py:947
  360.2 27.6 %collective-permute-start.42 = (bf16[2,3,48,384]{3,2,1,0:T(8,128)(2,1)}, bf16[2,3,48,384]{3,2,1,0:T(8,128)(2,1)}, u32[]{:S(2)}, u32[]{:S(2)}) collective-permute-start(bf16[2,3,48,384]{3,2,1,0:T(8,128)(2,1)} %slice.336), channel_id=1, source_target_pairs={{0,8},{4,12},{8,0},{12,4},{16,24},{20,28},{24,16},{28,20},{1,9},{5... | collective-permute-start | bytes 663560 | tf_op jit(solution)/shard_map/ppermute | solution.py:947
  360.2 27.6 %collective-permute-start.43 = (bf16[2,3,48,384]{3,2,1,0:T(8,128)(2,1)}, bf16[2,3,48,384]{3,2,1,0:T(8,128)(2,1)}, u32[]{:S(2)}, u32[]{:S(2)}) collective-permute-start(bf16[2,3,48,384]{3,2,1,0:T(8,128)(2,1)} %slice.335), channel_id=1, source_target_pairs={{0,16},{4,20},{8,24},{12,28},{16,0},{20,4},{24,8},{28,12},{1,17},{... | collective-permute-start | bytes 663560 | tf_op jit(solution)/shard_map/ppermute | solution.py:947
  362.1 25.7 %collective-permute-start.44 = (bf16[2,3,48,384]{3,2,1,0:T(8,128)(2,1)}, bf16[2,3,48,384]{3,2,1,0:T(8,128)(2,1)}, u32[]{:S(2)}, u32[]{:S(2)}) collective-permute-start(bf16[2,3,48,384]{3,2,1,0:T(8,128)(2,1)} %slice.334), channel_id=1, source_target_pairs={{0,2},{1,3},{2,0},{3,1},{4,6},{5,7},{6,4},{7,5},{8,10},{9,11},{10,... | collective-permute-start | bytes 663560 | tf_op jit(solution)/shard_map/ppermute | solution.py:947
  374.2 42.9 %collective-permute-start.52 = (bf16[1024,768]{1,0:T(8,128)(2,1)}, bf16[1024,768]{1,0:T(8,128)(2,1)}, u32[]{:S(2)}, u32[]{:S(2)}) collective-permute-start(bf16[1024,768]{1,0:T(8,128)(2,1)} %gather_grads.5.refs_3_), channel_id=1, source_target_pairs={{0,12},{4,8},{8,4},{12,0},{16,28},{20,24},{24,20},{28,16},{1,13},{... | collective-permute-start | bytes 4718600 | tf_op jit(solution)/shard_map/ppermute | solution.py:947
  389.5 24.7 %collective-permute-start.49 = (bf16[1,3,48,384]{3,2,1,0:T(8,128)(2,1)S(1)}, bf16[1,3,48,384]{3,2,1,0:T(8,128)(2,1)S(1)}, u32[]{:S(2)}, u32[]{:S(2)}) collective-permute-start(bf16[1,3,48,384]{3,2,1,0:T(8,128)(2,1)S(1)} %slice.339), channel_id=1, source_target_pairs={{0,16},{4,20},{8,24},{12,28},{16,0},{20,4},{24,8},{28,12},{1,17},{... | collective-permute-start | bytes 331784 | tf_op jit(solution)/shard_map/ppermute | solution.py:947
  392.7 22.2 %collective-permute-start.50 = (bf16[1,3,48,384]{3,2,1,0:T(8,128)(2,1)S(1)}, bf16[1,3,48,384]{3,2,1,0:T(8,128)(2,1)S(1)}, u32[]{:S(2)}, u32[]{:S(2)}) collective-permute-start(bf16[1,3,48,384]{3,2,1,0:T(8,128)(2,1)S(1)} %slice.338), channel_id=1, source_target_pairs={{0,2},{1,3},{2,0},{3,1},{4,6},{5,7},{6,4},{7,5},{8,10},{9,11},{10,... | collective-permute-start | bytes 331784 | tf_op jit(solution)/shard_map/ppermute | solution.py:947
  394.3 18.6 %collective-permute-start.47 = (bf16[3,96,384]{2,1,0:T(8,128)(2,1)S(1)}, bf16[3,96,384]{2,1,0:T(8,128)(2,1)S(1)}, u32[]{:S(2)}, u32[]{:S(2)}) collective-permute-start(bf16[3,96,384]{2,1,0:T(8,128)(2,1)S(1)} %fusion.8), channel_id=1, source_target_pairs={{0,16},{4,20},{8,24},{12,28},{16,0},{20,4},{24,8},{28,12},{1,17},{... | collective-permute-start | bytes 663560 | tf_op jit(solution)/shard_map/ppermute | solution.py:947
  396.5 19.0 %collective-permute-start.51 = (bf16[1,3,48,384]{3,2,1,0:T(8,128)(2,1)S(1)}, bf16[1,3,48,384]{3,2,1,0:T(8,128)(2,1)S(1)}, u32[]{:S(2)}, u32[]{:S(2)}) collective-permute-start(bf16[1,3,48,384]{3,2,1,0:T(8,128)(2,1)S(1)} %slice.337), channel_id=1, source_target_pairs={{0,4},{4,0},{8,12},{12,8},{16,20},{20,16},{24,28},{28,24},{1,5},{5... | collective-permute-start | bytes 331784 | tf_op jit(solution)/shard_map/ppermute | solution.py:947
  419.5 44.4 %collective-permute-start.55 = (bf16[1024,768]{1,0:T(8,128)(2,1)}, bf16[1024,768]{1,0:T(8,128)(2,1)}, u32[]{:S(2)}, u32[]{:S(2)}) collective-permute-start(bf16[1024,768]{1,0:T(8,128)(2,1)} %gather_grads.7.refs_1_), channel_id=1, source_target_pairs={{0,4},{4,0},{8,12},{12,8},{16,20},{20,16},{24,28},{28,24},{1,5},{5... | collective-permute-start | bytes 4718600 | tf_op jit(solution)/shard_map/ppermute | solution.py:947
  420.7 43.2 %collective-permute-start.56 = (bf16[1024,768]{1,0:T(8,128)(2,1)}, bf16[1024,768]{1,0:T(8,128)(2,1)}, u32[]{:S(2)}, u32[]{:S(2)}) collective-permute-start(bf16[1024,768]{1,0:T(8,128)(2,1)} %gather_grads.4.refs_2_), channel_id=1, source_target_pairs={{0,8},{4,12},{8,0},{12,4},{16,24},{20,28},{24,16},{28,20},{1,9},{5... | collective-permute-start | bytes 4718600 | tf_op jit(solution)/shard_map/ppermute | solution.py:947
  450.4 21.3 %all-to-all-start.1 = ((bf16[8,3,96,96]{3,2,1,0:T(8,128)(2,1)}), bf16[8,3,96,96]{3,2,1,0:T(8,128)(2,1)}, u32[]{:S(2)}, u32[]{:S(2)}) async-start(bf16[8,3,96,96]{3,2,1,0:T(8,128)(2,1)} %copy-done.16), calls=%async_computation.1 | async-start | bytes 1179648 | tf_op jit(solution)/shard_map/all_to_all | solution.py:1205
  483.7 21.9 %all-to-all-start.2 = ((bf16[8,3,96,96]{3,2,1,0:T(8,128)(2,1)}), bf16[8,3,96,96]{3,2,1,0:T(8,128)(2,1)}, u32[]{:S(2)}, u32[]{:S(2)}) async-start(bf16[8,3,96,96]{3,2,1,0:T(8,128)(2,1)} %copy-done.26), calls=%async_computation.2 | async-start | bytes 1179648 | tf_op jit(solution)/shard_map/all_to_all | solution.py:1205
  488.8 16.9 %collective-permute-start.58 = (f32[12,768]{1,0:T(8,128)S(1)}, f32[12,768]{1,0:T(8,128)}, u32[]{:S(2)}, u32[]{:S(2)}) collective-permute-start(f32[12,768]{1,0:T(8,128)S(1)} %add.168), channel_id=1, source_target_pairs={{0,16},{4,20},{8,24},{12,28},{16,0},{20,4},{24,8},{28,12},{1,17},{... | collective-permute-start | bytes 110600 | tf_op jit(solution)/shard_map/ppermute | solution.py:947
  510.7 19.7 %all-to-all-start.3 = ((bf16[8,3,96,96]{3,2,1,0:T(8,128)(2,1)}), bf16[8,3,96,96]{3,2,1,0:T(8,128)(2,1)S(1)}, u32[]{:S(2)}, u32[]{:S(2)}) async-start(bf16[8,3,96,96]{3,2,1,0:T(8,128)(2,1)} %copy-done.17), calls=%async_computation.3 | async-start | bytes 1179648 | tf_op jit(solution)/shard_map/all_to_all | solution.py:1205
  (106 other events, 665.9 us)

commit v9 on v8

--- a/solution.py
+++ b/solution.py
@@ -337,7 +337,7 @@
         mixed = products("uce,ued->ucd", jnp.swapaxes(probs, 1, 2), first).astype(BF16)
         spread(results, runs, where, share, slice(0, TILE), mixed)
 
-    for_each_batch(long_ref[0], grouped[0].shape[1], 8, work)
+    for_each_batch(long_ref[0], grouped[0].shape[1], 16, work)
 
 
 def attend(is_long, grouped):
@@ -1170,7 +1170,8 @@
         own_grads[k] = gather_grads(orders[k], sorted_back[k])
     kept_qkv, sent_qkv, bias_qkv = qkv_back(jnp.stack([core, unit]).astype(jnp.int32), own_grads, unit_inputs)
     (got_now, kept_qkv, sent_qkv) = together(got_now, kept_qkv, sent_qkv)
-    kept_now, sent_now = halves(joined(kept_now, got_now))
+    kept_now = joined(kept_now, got_now)
+    sent_now = halves(kept_now)[1]
     got_now = exchanged(sent_now, 3)
 
     bias_query, _, bias_value = join_heads(bias_qkv[0])

time: 540 us -> 540 us (level)
    unnamed x185 -> x191, local copies, waits for them, and re-layouts: 36.6 us -> 41.1 us
  transfers between devices with their start and end apart: 64 -> 64, of which waited for: 22 -> 22; matrix products, arithmetic and copies ran while one was open for 16% -> 15% of each run, Pallas kernels for 40% -> 39%
where the time goes in v9:
time: 540 us; the launch traced here: 532 us
  Pallas kernels  223 us (41%)
  waiting for transfers between devices  94.4 us (17%)
  starting transfers between devices  86.6 us (16%)
  local copies, waits for them, and re-layouts  58.7 us (11%)
  other arithmetic  51.1 us (9%)
  matrix products  14.7 us (3%)
    pallas_call x1, Pallas kernels, layer(): pl.pallas_call(functools.partial(layer_body, n_shards), in_specs=[pl.Bloc...  69.8 us
    ppermute x57, waiting for transfers between devices, swap(): return lax.ppermute(value, axis, [(i, i ^ bit) for i in range(size)])  68 us
    ppermute x57, starting transfers between devices, swap(): return lax.ppermute(value, axis, [(i, i ^ bit) for i in range(size)])  63.9 us
    unnamed x191, local copies, waits for them, and re-layouts  41.1 us
    pallas_call x4, Pallas kernels, sort_rows(): pl.pallas_call(sort_body, grid=(HEADS_OWN,), in_specs=[pl.BlockSpec((8, c...  27.7 us
    pallas_call x4, Pallas kernels, gather_grads(): pl.pallas_call(gather_grads_body, grid=(HEADS_OWN,), in_specs=[pl.BlockSp...  20 us
    pallas_call x1, Pallas kernels, attend_back(): pl.pallas_call(attend_back_body, grid_spec=pltpu.PrefetchScalarGridSpec(n...  19.1 us
    pallas_call x4, Pallas kernels, mix(): pl.pallas_call(mix_body, grid=(HEADS_OWN,), in_specs=[pl.BlockSpec((8, co...  17.2 us
  transfers between devices with their start and end apart: 64, of which 22 were waited for; matrix products, arithmetic and copies ran while one was open for 15% of the time, Pallas kernels for 39%

profile of v9, /device:TPU:0, one launch (start us, length us, event | category | flops | bytes accessed | tf_op | source)
XLA Modules:
  0.0 531.7 jit_solution(16742607934927823923)
XLA Ops:
  0.6 3.0 collective-permute-start
  11.4 6.9 %places.1 = (s32[8,1024]{1,0:T(8,128)}, s32[8,1024]{1,0:T(8,128)}, s32[8,1024]{1,0:T(8,128)}, s32[8,1024]{1,0:T(8,128)}) custom-call(s32[2]{0:T(128)} %get-tuple-element.330.scalars_ref, s32[24,1024]{1,0:T(8,128)} %bitcast.127), custom_call_target="tpu_custom_call" | custom-call | tf_op jit(solution)/shard_map/places/pallas_call | solution.py:96
  18.3 14.9 %fusion = (bf16[3,768,768]{2,1,0:T(8,128)(2,1)}, bf16[3,768,768]{2,1,0:T(8,128)(2,1)}, bf16[3,768,768]{2,1,0:T(8,128)(2,1)}, bf16[3,768,768]{2,1,0:T(8,128)(2,1)S(1)}) fusion(f32[2,3,768,768]{3,2,1,0:T(8,128)} %param.18), kind=kLoop, calls=%fused_computation.2 | loop fusion | flops 10616832 | bytes 35389440 | tf_op jit(solution)/shard_map/convert_element_type | solution.py:1002
  63.2 13.8 %collective-permute-done.13 = bf16[4,48,768]{2,1,0:T(8,128)(2,1)S(1)} collective-permute-done((bf16[4,48,768]{2,1,0:T(8,128)(2,1)S(1)}, bf16[4,48,768]{2,1,0:T(8,128)(2,1)S(1)}, u32[]{:S(2)}, u32[]{:S(2)}) %collective-permute-start.13) | collective-permute-done | bytes 294944 | tf_op jit(solution)/shard_map/ppermute | solution.py:947
  80.0 5.1 collective-permute-start.15
  89.7 3.2 assemble.1.weight_ref
  95.0 6.6 %sort_rows.4.refs_0_ = bf16[6,1024,256]{2,1,0:T(8,128)(2,1)S(1)} custom-call(s32[8,1024]{1,0:T(8,128)S(1)} %copy-done.33, bf16[1024,768]{1,0:T(8,128)(2,1)S(1)} %bitcast.111, bf16[768,768]{1,0:T(8,128)(2,1)} %assemble.1.weight_ref, f32[1,768]{1,0:T(1,128)S(1)} %reshape.107.bias_ref), custom_call_target="tpu_custom_call" | custom-call | tf_op jit(solution)/shard_map/sort_rows/pallas_call | solution.py:221
  103.3 7.2 %sort_rows.5.refs_1_ = bf16[6,1024,256]{2,1,0:T(8,128)(2,1)S(1)} custom-call(s32[8,1024]{1,0:T(8,128)S(1)} %copy-done.37, bf16[1024,768]{1,0:T(8,128)(2,1)} %collective-permute-done.x_ref.refs_5_, bf16[768,768]{1,0:T(8,128)(2,1)} %assemble.1.weight_ref, f32[1,768]{1,0:T(1,128)S(1)} %reshape.107.bias_ref), custom_call_target="tpu_custom_call" | custom-call | tf_op jit(solution)/shard_map/sort_rows/pallas_call | solution.py:221
  114.9 7.1 %sort_rows.6.refs_2_ = bf16[6,1024,256]{2,1,0:T(8,128)(2,1)S(1)} custom-call(s32[8,1024]{1,0:T(8,128)S(1)} %copy-done.40, bf16[1024,768]{1,0:T(8,128)(2,1)} %collective-permute-done.1.x_ref.refs_6_, bf16[768,768]{1,0:T(8,128)(2,1)} %assemble.1.weight_ref, f32[1,768]{1,0:T(1,128)S(1)} %reshape.107.bias_ref), custom_call_target="tpu_custom_call" | custom-call | tf_op jit(solution)/shard_map/sort_rows/pallas_call | solution.py:221
  126.1 6.9 %sort_rows.7.refs_3_ = bf16[6,1024,256]{2,1,0:T(8,128)(2,1)S(1)} custom-call(s32[8,1024]{1,0:T(8,128)S(1)} %copy-done.43, bf16[1024,768]{1,0:T(8,128)(2,1)S(1)} %constant_dynamic-update-slice_fusion.5.x_ref.refs_7_, bf16[768,768]{1,0:T(8,128)(2,1)} %assemble.1.weight_ref, f32[1,768]{1,0:T(1,128)S(1)} %reshape.107.bias_ref), custom_call_target="tpu_custom_call" | custom-call | tf_op jit(solution)/shard_map/sort_rows/pallas_call | solution.py:221
  138.0 11.4 %attend.1 = (bf16[6,1024,128]{2,1,0:T(8,128)(2,1)S(1)}, bf16[6,1024,128]{2,1,0:T(8,128)(2,1)S(1)}, bf16[6,1024,128]{2,1,0:T(8,128)(2,1)S(1)}, bf16[6,1024,128]{2,1,0:T(8,128)(2,1)}) custom-call(s32[1]{0:T(128)} %bitcast.11.long_ref, bf16[6,1024,256]{2,1,0:T(8,128)(2,1)} %copy-done, bf16[6,1024,256]{2,1,0:T(8,128)(2,1)} %copy-done.1, ...), custom_call_target="tpu_custom_call" | custom-call | tf_op jit(solution)/shard_map/attend/pallas_call | solution.py:345
  149.4 6.5 %collective-permute-done.20 = bf16[9,48,768]{2,1,0:T(8,128)(2,1)S(1)} collective-permute-done((bf16[9,48,768]{2,1,0:T(8,128)(2,1)S(1)}, bf16[9,48,768]{2,1,0:T(8,128)(2,1)S(1)}, u32[]{:S(2)}, u32[]{:S(2)}) %collective-permute-start.20) | collective-permute-done | bytes 663584 | tf_op jit(solution)/shard_map/ppermute | solution.py:1090
  158.4 4.2 mix.4
  162.7 4.3 mix.6
  167.9 4.4 mix.7
  175.0 4.2 mix.5.refs_8_
  180.0 3.0 collective-permute-done.23.refs_9_
  184.4 7.9 %collective-permute-done.25.refs_11_ = bf16[1536,128]{1,0:T(8,128)(2,1)S(1)} collective-permute-done((bf16[1536,128]{1,0:T(8,128)(2,1)S(1)}, bf16[1536,128]{1,0:T(8,128)(2,1)S(1)}, u32[]{:S(2)}, u32[]{:S(2)}) %collective-permute-start.25) | collective-permute-done | bytes 393248 | tf_op jit(solution)/shard_map/ppermute | solution.py:947
  198.9 69.8 %layer.1 = (bf16[1024,768]{1,0:T(8,128)(2,1)}, f32[1024,768]{1,0:T(8,128)}, f32[16,768]{1,0:T(8,128)}, bf16[3,16,3,48,384]{4,3,2,1,0:T(8,128)(2,1)}, bf16[3,16,3...) custom-call(s32[22]{0:T(128)} %concatenate.28.table_ref, ...), custom_call_target="tpu_custom_call" | custom-call | tf_op jit(solution)/shard_map/layer/pallas_call | solution.py:713
  273.4 3.8 sort_grads.4.refs_4_
  277.9 4.6 convert_add_fusion
  287.1 3.1 collective-permute-done.35.rows_ref
  292.8 3.8 sort_grads.5.refs_5_
  297.9 4.2 sort_grads.6.refs_6_
  303.2 3.8 sort_grads.7.refs_7_
  308.2 19.1 %attend_back.1 = (bf16[6,1024,256]{2,1,0:T(8,128)(2,1)}, bf16[6,1024,256]{2,1,0:T(8,128)(2,1)}, bf16[6,1024,256]{2,1,0:T(8,128)(2,1)}, bf16[6,1024,256]{2,1,0:T(8,128)(2,1)}) custom-call(s32[1]{0:T(128)} %bitcast.11.long_ref, bf16[6,1024,256]{2,1,0:T(8,128)(2,1)} %copy-done, bf16[6,1024,256]{2,1,0:T(8,128)(2,1)} %copy-done.1, ...), custom_call_target="tpu_custom_call" | custom-call | tf_op jit(solution)/shard_map/attend_back/pallas_call | solution.py:389
  340.8 5.3 gather_grads.4.refs_2_
  346.0 5.1 gather_grads.5.refs_3_
  352.0 3.3 collective-permute-done.40
  362.3 4.4 gather_grads.6.refs_0_
  367.8 5.3 gather_grads.7.refs_1_
  374.0 10.8 %qkv_back.1 = (bf16[2,3,96,384]{3,2,1,0:T(8,128)(2,1)}, bf16[2,3,96,384]{3,2,1,0:T(8,128)(2,1)}, f32[8,768]{1,0:T(8,128)}) custom-call(s32[2]{0:T(128)} %get-tuple-element.331.scalars_ref, bf16[1024,768]{1,0:T(8,128)(2,1)} %copy-done.6, bf16[1024,768]{1,0:T(8,128)(2,1)} %gather_grads.7.refs_1_, bf16[1024,768]{1,0:T(8,128)(2,1)} %gather_grads.4.refs_2_, ...), custom_call_target="tpu_custom_call" | custom-call | tf_op jit(solution)/shard_map/qkv_back/pallas_call | solution.py:778
  399.1 14.0 %collective-permute-done.47 = bf16[3,96,384]{2,1,0:T(8,128)(2,1)S(1)} collective-permute-done((bf16[3,96,384]{2,1,0:T(8,128)(2,1)S(1)}, bf16[3,96,384]{2,1,0:T(8,128)(2,1)S(1)}, u32[]{:S(2)}, u32[]{:S(2)}) %collective-permute-start.47) | collective-permute-done | bytes 221216 | tf_op jit(solution)/shard_map/ppermute | solution.py:947
  432.2 4.1 all-to-all-start
  438.2 6.1 %all-to-all-done.got_ref = bf16[4,3,48,384]{3,2,1,0:T(8,128)(2,1)} async-done(((bf16[4,3,48,384]{3,2,1,0:T(8,128)(2,1)}), bf16[4,3,48,384]{3,2,1,0:T(8,128)(2,1)}, u32[]{:S(2)}, u32[]{:S(2)}) %all-to-all-start) | async-done | bytes 442400 | tf_op jit(solution)/shard_map/all_to_all | solution.py:1196
  445.4 4.4 rotate_in.1
  450.6 4.9 all-to-all-start.1
  458.4 3.3 fusion.19
  466.1 5.2 all-to-all-done.1.got_ref
  473.6 8.9 %moments.1 = (f32[3,96,768]{2,1,0:T(8,128)}, f32[3,96,768]{2,1,0:T(8,128)}, bf16[8,3,96,96]{3,2,1,0:T(8,128)(2,1)S(1)}) custom-call(bf16[8,3,96,96]{3,2,1,0:T(8,128)(2,1)} %all-to-all-done.1.got_ref, bf16[3,768,768]{2,1,0:T(8,128)(2,1)} %get-tuple-element.283.high_ref, bf16[3,768,768]{2,1,0:T(8,128)(2,1)} %get-tuple-element.284.low_ref, ...), custom_call_target="tpu_custom_call" | custom-call | tf_op jit(solution)/shard_map/moments/pallas_call | solution.py:882
  483.4 4.2 all-to-all-start.2
  491.3 3.2 fusion.20
  494.5 4.9 add_add_fusion
  499.4 5.9 %collective-permute-done.58 = f32[12,768]{1,0:T(8,128)} collective-permute-done((f32[12,768]{1,0:T(8,128)S(1)}, f32[12,768]{1,0:T(8,128)}, u32[]{:S(2)}, u32[]{:S(2)}) %collective-permute-start.58) | collective-permute-done | bytes 36896 | tf_op jit(solution)/shard_map/ppermute | solution.py:947
  505.3 4.2 rotate_out.1
  510.4 3.6 all-to-all-start.3
  515.3 3.3 fusion.21
  521.5 8.6 %all-to-all-done.3.got_ref = bf16[8,3,96,96]{3,2,1,0:T(8,128)(2,1)S(1)} async-done(((bf16[8,3,96,96]{3,2,1,0:T(8,128)(2,1)}), bf16[8,3,96,96]{3,2,1,0:T(8,128)(2,1)S(1)}, u32[]{:S(2)}, u32[]{:S(2)}) %all-to-all-start.3) | async-done | bytes 442400 | tf_op jit(solution)/shard_map/all_to_all | solution.py:1206
  (382 shorter events, 173.0 us)
Async XLA Ops:
  0.6 37.7 %collective-permute-start = (bf16[1024,768]{1,0:T(8,128)(2,1)}, bf16[1024,768]{1,0:T(8,128)(2,1)}, u32[]{:S(2)}, u32[]{:S(2)}) collective-permute-start(bf16[1024,768]{1,0:T(8,128)(2,1)} %bitcast.107), channel_id=1, source_target_pairs={{0,4},{4,0},{8,12},{12,8},{16,20},{20,16},{24,28},{28,24},{1,5},{5... | collective-permute-start | bytes 4718600 | tf_op jit(solution)/shard_map/ppermute | solution.py:947
  3.7 36.2 %collective-permute-start.1 = (bf16[1024,768]{1,0:T(8,128)(2,1)}, bf16[1024,768]{1,0:T(8,128)(2,1)}, u32[]{:S(2)}, u32[]{:S(2)}) collective-permute-start(bf16[1024,768]{1,0:T(8,128)(2,1)} %bitcast.108), channel_id=1, source_target_pairs={{0,8},{4,12},{8,0},{12,4},{16,24},{20,28},{24,16},{28,20},{1,9},{5... | collective-permute-start | bytes 4718600 | tf_op jit(solution)/shard_map/ppermute | solution.py:947
  7.2 28.8 %collective-permute-start.2 = (bf16[3,96,768]{2,1,0:T(8,128)(2,1)}, bf16[3,96,768]{2,1,0:T(8,128)(2,1)}, u32[]{:S(2)}, u32[]{:S(2)}) collective-permute-start(bf16[3,96,768]{2,1,0:T(8,128)(2,1)} %convert_bitcast_fusion.refs_0_), channel_id=1, source_target_pairs={{0,1},{1,0},{2,3},{3,2},{4,5},{5,4},{6,7},{7,6},{8,9},{9,8},{10,11... | collective-permute-start | bytes 1327112 | tf_op jit(solution)/shard_map/ppermute | solution.py:947
  7.2 26.0 %collective-permute-start.3 = (bf16[3,96,768]{2,1,0:T(8,128)(2,1)}, bf16[3,96,768]{2,1,0:T(8,128)(2,1)}, u32[]{:S(2)}, u32[]{:S(2)}) collective-permute-start(bf16[3,96,768]{2,1,0:T(8,128)(2,1)} %convert_bitcast_fusion.refs_0_), channel_id=1, source_target_pairs={{0,2},{1,3},{2,0},{3,1},{4,6},{5,7},{6,4},{7,5},{8,10},{9,11},{10,... | collective-permute-start | bytes 1327112 | tf_op jit(solution)/shard_map/ppermute | solution.py:947
  41.9 16.0 %collective-permute-start.7 = (bf16[48,768]{1,0:T(8,128)(2,1)S(1)}, bf16[48,768]{1,0:T(8,128)(2,1)S(1)}, u32[]{:S(2)}, u32[]{:S(2)}) collective-permute-start(bf16[48,768]{1,0:T(8,128)(2,1)S(1)} %get-tuple-element.167), channel_id=1, source_target_pairs={{0,4},{4,0},{8,12},{12,8},{16,20},{20,16},{24,28},{28,24},{1,5},{5... | collective-permute-start | bytes 221192 | tf_op jit(solution)/shard_map/ppermute | solution.py:947
  42.4 15.6 %collective-permute-start.8 = (bf16[48,768]{1,0:T(8,128)(2,1)S(1)}, bf16[48,768]{1,0:T(8,128)(2,1)S(1)}, u32[]{:S(2)}, u32[]{:S(2)}) collective-permute-start(bf16[48,768]{1,0:T(8,128)(2,1)S(1)} %get-tuple-element.168), channel_id=1, source_target_pairs={{0,8},{4,12},{8,0},{12,4},{16,24},{20,28},{24,16},{28,20},{1,9},{5... | collective-permute-start | bytes 221192 | tf_op jit(solution)/shard_map/ppermute | solution.py:947
  44.1 13.9 %collective-permute-start.9 = (bf16[48,768]{1,0:T(8,128)(2,1)S(1)}, bf16[48,768]{1,0:T(8,128)(2,1)S(1)}, u32[]{:S(2)}, u32[]{:S(2)}) collective-permute-start(bf16[48,768]{1,0:T(8,128)(2,1)S(1)} %get-tuple-element.169), channel_id=1, source_target_pairs={{0,12},{4,8},{8,4},{12,0},{16,28},{20,24},{24,20},{28,16},{1,13},{... | collective-permute-start | bytes 221192 | tf_op jit(solution)/shard_map/ppermute | solution.py:947
  55.8 23.4 %collective-permute-start.5 = (bf16[512,768]{1,0:T(8,128)(2,1)}, bf16[512,768]{1,0:T(8,128)(2,1)}, u32[]{:S(2)}, u32[]{:S(2)}) collective-permute-start(bf16[512,768]{1,0:T(8,128)(2,1)} %slice.180), channel_id=1, source_target_pairs={{0,8},{4,12},{8,0},{12,4},{16,24},{20,28},{24,16},{28,20},{1,9},{5... | collective-permute-start | bytes 2359304 | tf_op jit(solution)/shard_map/ppermute | solution.py:947
  56.0 23.3 %collective-permute-start.6 = (bf16[512,768]{1,0:T(8,128)(2,1)}, bf16[512,768]{1,0:T(8,128)(2,1)}, u32[]{:S(2)}, u32[]{:S(2)}) collective-permute-start(bf16[512,768]{1,0:T(8,128)(2,1)} %slice.181), channel_id=1, source_target_pairs={{0,4},{4,0},{8,12},{12,8},{16,20},{20,16},{24,28},{28,24},{1,5},{5... | collective-permute-start | bytes 2359304 | tf_op jit(solution)/shard_map/ppermute | solution.py:947
  59.3 17.7 %collective-permute-start.13 = (bf16[4,48,768]{2,1,0:T(8,128)(2,1)S(1)}, bf16[4,48,768]{2,1,0:T(8,128)(2,1)S(1)}, u32[]{:S(2)}, u32[]{:S(2)}) collective-permute-start(bf16[4,48,768]{2,1,0:T(8,128)(2,1)S(1)} %pad_maximum_fusion.5), channel_id=1, source_target_pairs={{0,16},{4,20},{8,24},{12,28},{16,0},{20,4},{24,8},{28,12},{1,17},{... | collective-permute-start | bytes 884744 | tf_op jit(solution)/shard_map/ppermute | solution.py:947
  80.0 32.0 %collective-permute-start.15 = (bf16[9,48,768]{2,1,0:T(8,128)(2,1)}, bf16[9,48,768]{2,1,0:T(8,128)(2,1)}, u32[]{:S(2)}, u32[]{:S(2)}) collective-permute-start(bf16[9,48,768]{2,1,0:T(8,128)(2,1)} %copy-done.30), channel_id=1, source_target_pairs={{0,8},{4,12},{8,16},{12,20},{16,24},{20,28},{24,0},{28,4},{1,9},{5... | collective-permute-start | bytes 1990664 | tf_op jit(solution)/shard_map/ppermute | solution.py:1090
  85.1 27.0 %collective-permute-start.16 = (bf16[9,48,768]{2,1,0:T(8,128)(2,1)}, bf16[9,48,768]{2,1,0:T(8,128)(2,1)}, u32[]{:S(2)}, u32[]{:S(2)}) collective-permute-start(bf16[9,48,768]{2,1,0:T(8,128)(2,1)} %copy-done.30), channel_id=1, source_target_pairs={{0,4},{4,0},{8,12},{12,8},{16,20},{20,16},{24,28},{28,24},{1,5},{5... | collective-permute-start | bytes 1990664 | tf_op jit(solution)/shard_map/ppermute | solution.py:947
  113.3 21.3 %collective-permute-start.19 = (bf16[2,9,48,768]{3,2,1,0:T(8,128)(2,1)S(1)}, bf16[2,9,48,768]{3,2,1,0:T(8,128)(2,1)S(1)}, u32[]{:S(2)}, u32[]{:S(2)}) collective-permute-start(bf16[2,9,48,768]{3,2,1,0:T(8,128)(2,1)S(1)} %pad_maximum_fusion.refs_0_), channel_id=1, source_target_pairs={{0,1},{1,0},{2,3},{3,2},{4,5},{5,4},{6,7},{7,6},{8,9},{9,8},{10,11... | collective-permute-start | bytes 3981320 | tf_op jit(solution)/shard_map/ppermute | solution.py:947
  113.4 21.2 %collective-permute-start.17 = (bf16[9,48,768]{2,1,0:T(8,128)(2,1)}, bf16[9,48,768]{2,1,0:T(8,128)(2,1)S(1)}, u32[]{:S(2)}, u32[]{:S(2)}) collective-permute-start(bf16[9,48,768]{2,1,0:T(8,128)(2,1)} %collective-permute-done.15), channel_id=1, source_target_pairs={{0,8},{4,12},{8,16},{12,20},{16,24},{20,28},{24,0},{28,4},{1,9},{5... | collective-permute-start | bytes 1990664 | tf_op jit(solution)/shard_map/ppermute | solution.py:1090
  114.0 20.6 %collective-permute-start.18 = (bf16[9,48,768]{2,1,0:T(8,128)(2,1)}, bf16[9,48,768]{2,1,0:T(8,128)(2,1)S(1)}, u32[]{:S(2)}, u32[]{:S(2)}) collective-permute-start(bf16[9,48,768]{2,1,0:T(8,128)(2,1)} %collective-permute-done.15), channel_id=1, source_target_pairs={{0,4},{4,0},{8,12},{12,8},{16,20},{20,16},{24,28},{28,24},{1,5},{5... | collective-permute-start | bytes 1990664 | tf_op jit(solution)/shard_map/ppermute | solution.py:947
  136.3 19.5 %collective-permute-start.22 = (bf16[2,9,48,768]{3,2,1,0:T(8,128)(2,1)S(1)}, bf16[2,9,48,768]{3,2,1,0:T(8,128)(2,1)S(1)}, u32[]{:S(2)}, u32[]{:S(2)}) collective-permute-start(bf16[2,9,48,768]{3,2,1,0:T(8,128)(2,1)S(1)} %pad_maximum_fusion.1.refs_1_), channel_id=1, source_target_pairs={{0,1},{1,0},{2,3},{3,2},{4,5},{5,4},{6,7},{7,6},{8,9},{9,8},{10,11... | collective-permute-start | bytes 3981320 | tf_op jit(solution)/shard_map/ppermute | solution.py:947
  136.5 19.3 %collective-permute-start.20 = (bf16[9,48,768]{2,1,0:T(8,128)(2,1)S(1)}, bf16[9,48,768]{2,1,0:T(8,128)(2,1)S(1)}, u32[]{:S(2)}, u32[]{:S(2)}) collective-permute-start(bf16[9,48,768]{2,1,0:T(8,128)(2,1)S(1)} %collective-permute-done.17), channel_id=1, source_target_pairs={{0,8},{4,12},{8,16},{12,20},{16,24},{20,28},{24,0},{28,4},{1,9},{5... | collective-permute-start | bytes 1990664 | tf_op jit(solution)/shard_map/ppermute | solution.py:1090
  136.8 19.1 %collective-permute-start.21 = (bf16[9,48,768]{2,1,0:T(8,128)(2,1)S(1)}, bf16[9,48,768]{2,1,0:T(8,128)(2,1)S(1)}, u32[]{:S(2)}, u32[]{:S(2)}) collective-permute-start(bf16[9,48,768]{2,1,0:T(8,128)(2,1)S(1)} %collective-permute-done.17), channel_id=1, source_target_pairs={{0,4},{4,0},{8,12},{12,8},{16,20},{20,16},{24,28},{28,24},{1,5},{5... | collective-permute-start | bytes 1990664 | tf_op jit(solution)/shard_map/ppermute | solution.py:947
  157.1 35.2 %collective-permute-start.27 = (bf16[2,9,48,768]{3,2,1,0:T(8,128)(2,1)S(1)}, bf16[2,9,48,768]{3,2,1,0:T(8,128)(2,1)S(1)}, u32[]{:S(2)}, u32[]{:S(2)}) collective-permute-start(bf16[2,9,48,768]{3,2,1,0:T(8,128)(2,1)S(1)} %pad_maximum_fusion.2.refs_2_), channel_id=1, source_target_pairs={{0,1},{1,0},{2,3},{3,2},{4,5},{5,4},{6,7},{7,6},{8,9},{9,8},{10,11... | collective-permute-start | bytes 3981320 | tf_op jit(solution)/shard_map/ppermute | solution.py:947
  157.2 35.2 %collective-permute-start.26 = (bf16[9,48,768]{2,1,0:T(8,128)(2,1)S(1)}, bf16[9,48,768]{2,1,0:T(8,128)(2,1)S(1)}, u32[]{:S(2)}, u32[]{:S(2)}) collective-permute-start(bf16[9,48,768]{2,1,0:T(8,128)(2,1)S(1)} %collective-permute-done.20), channel_id=1, source_target_pairs={{0,4},{4,0},{8,12},{12,8},{16,20},{20,16},{24,28},{28,24},{1,5},{5... | collective-permute-start | bytes 1990664 | tf_op jit(solution)/shard_map/ppermute | solution.py:947
  167.0 16.1 %collective-permute-start.23 = (bf16[1536,128]{1,0:T(8,128)(2,1)S(1)}, bf16[1536,128]{1,0:T(8,128)(2,1)S(1)}, u32[]{:S(2)}, u32[]{:S(2)}) collective-permute-start(bf16[1536,128]{1,0:T(8,128)(2,1)S(1)} %mix.6), channel_id=1, source_target_pairs={{0,4},{4,0},{8,12},{12,8},{16,20},{20,16},{24,28},{28,24},{1,5},{5... | collective-permute-start | bytes 1179656 | tf_op jit(solution)/shard_map/ppermute | solution.py:947
  172.4 19.9 %collective-permute-start.25 = (bf16[1536,128]{1,0:T(8,128)(2,1)S(1)}, bf16[1536,128]{1,0:T(8,128)(2,1)S(1)}, u32[]{:S(2)}, u32[]{:S(2)}) collective-permute-start(bf16[1536,128]{1,0:T(8,128)(2,1)S(1)} %mix.4), channel_id=1, source_target_pairs={{0,12},{4,8},{8,4},{12,0},{16,28},{20,24},{24,20},{28,16},{1,13},{... | collective-permute-start | bytes 1179656 | tf_op jit(solution)/shard_map/ppermute | solution.py:947
  194.7 74.1 %collective-permute-start.29 = (bf16[768,768]{1,0:T(8,128)(2,1)}, bf16[768,768]{1,0:T(8,128)(2,1)}, u32[]{:S(2)}, u32[]{:S(2)}) collective-permute-start(bf16[768,768]{1,0:T(8,128)(2,1)} %assemble.1.weight_ref), channel_id=1, source_target_pairs={{0,4},{4,0},{8,12},{12,8},{16,20},{20,16},{24,28},{28,24},{1,5},{5... | collective-permute-start | bytes 3538952 | tf_op jit(solution)/shard_map/ppermute | solution.py:947
  195.6 73.2 %collective-permute-start.30 = (bf16[768,768]{1,0:T(8,128)(2,1)}, bf16[768,768]{1,0:T(8,128)(2,1)}, u32[]{:S(2)}, u32[]{:S(2)}) collective-permute-start(bf16[768,768]{1,0:T(8,128)(2,1)} %assemble.1.weight_ref), channel_id=1, source_target_pairs={{0,8},{4,12},{8,0},{12,4},{16,24},{20,28},{24,16},{28,20},{1,9},{5... | collective-permute-start | bytes 3538952 | tf_op jit(solution)/shard_map/ppermute | solution.py:947
  195.9 72.9 %collective-permute-start.31 = (bf16[768,768]{1,0:T(8,128)(2,1)}, bf16[768,768]{1,0:T(8,128)(2,1)}, u32[]{:S(2)}, u32[]{:S(2)}) collective-permute-start(bf16[768,768]{1,0:T(8,128)(2,1)} %assemble.1.weight_ref), channel_id=1, source_target_pairs={{0,12},{4,8},{8,4},{12,0},{16,28},{20,24},{24,20},{28,16},{1,13},{... | collective-permute-start | bytes 3538952 | tf_op jit(solution)/shard_map/ppermute | solution.py:947
  268.9 18.2 %collective-permute-start.33 = (bf16[1536,128]{1,0:T(8,128)(2,1)}, bf16[1536,128]{1,0:T(8,128)(2,1)S(1)}, u32[]{:S(2)}, u32[]{:S(2)}) collective-permute-start(bf16[1536,128]{1,0:T(8,128)(2,1)} %get-tuple-element.234), channel_id=1, source_target_pairs={{0,4},{4,0},{8,12},{12,8},{16,20},{20,16},{24,28},{28,24},{1,5},{5... | collective-permute-start | bytes 1179656 | tf_op jit(solution)/shard_map/ppermute | solution.py:947
  269.8 17.3 %collective-permute-start.34 = (bf16[1536,128]{1,0:T(8,128)(2,1)}, bf16[1536,128]{1,0:T(8,128)(2,1)S(1)}, u32[]{:S(2)}, u32[]{:S(2)}) collective-permute-start(bf16[1536,128]{1,0:T(8,128)(2,1)} %get-tuple-element.235), channel_id=1, source_target_pairs={{0,8},{4,12},{8,0},{12,4},{16,24},{20,28},{24,16},{28,20},{1,9},{5... | collective-permute-start | bytes 1179656 | tf_op jit(solution)/shard_map/ppermute | solution.py:947
  270.0 20.2 %collective-permute-start.35 = (bf16[1536,128]{1,0:T(8,128)(2,1)}, bf16[1536,128]{1,0:T(8,128)(2,1)S(1)}, u32[]{:S(2)}, u32[]{:S(2)}) collective-permute-start(bf16[1536,128]{1,0:T(8,128)(2,1)} %get-tuple-element.236), channel_id=1, source_target_pairs={{0,12},{4,8},{8,4},{12,0},{16,28},{20,24},{24,20},{28,16},{1,13},{... | collective-permute-start | bytes 1179656 | tf_op jit(solution)/shard_map/ppermute | solution.py:947
  290.2 37.1 %collective-permute-start.36 = (bf16[8,3,48,384]{3,2,1,0:T(8,128)(2,1)}, bf16[8,3,48,384]{3,2,1,0:T(8,128)(2,1)}, u32[]{:S(2)}, u32[]{:S(2)}) collective-permute-start(bf16[8,3,48,384]{3,2,1,0:T(8,128)(2,1)} %fusion.5), channel_id=1, source_target_pairs={{0,2},{1,3},{2,0},{3,1},{4,6},{5,7},{6,4},{7,5},{8,10},{9,11},{10,... | collective-permute-start | bytes 2654216 | tf_op jit(solution)/shard_map/ppermute | solution.py:947
  291.7 37.2 %collective-permute-start.37 = (bf16[8,3,48,384]{3,2,1,0:T(8,128)(2,1)}, bf16[8,3,48,384]{3,2,1,0:T(8,128)(2,1)}, u32[]{:S(2)}, u32[]{:S(2)}) collective-permute-start(bf16[8,3,48,384]{3,2,1,0:T(8,128)(2,1)} %fusion.6), channel_id=1, source_target_pairs={{0,4},{4,0},{8,12},{12,8},{16,20},{20,16},{24,28},{28,24},{1,5},{5... | collective-permute-start | bytes 2654216 | tf_op jit(solution)/shard_map/ppermute | solution.py:947
  292.6 39.4 %collective-permute-start.38 = (bf16[8,3,48,384]{3,2,1,0:T(8,128)(2,1)}, bf16[8,3,48,384]{3,2,1,0:T(8,128)(2,1)}, u32[]{:S(2)}, u32[]{:S(2)}) collective-permute-start(bf16[8,3,48,384]{3,2,1,0:T(8,128)(2,1)} %fusion.7), channel_id=1, source_target_pairs={{0,8},{4,12},{8,0},{12,4},{16,24},{20,28},{24,16},{28,20},{1,9},{5... | collective-permute-start | bytes 2654216 | tf_op jit(solution)/shard_map/ppermute | solution.py:947
  335.1 16.0 %collective-permute-start.39 = (bf16[4,3,48,384]{3,2,1,0:T(8,128)(2,1)S(1)}, bf16[4,3,48,384]{3,2,1,0:T(8,128)(2,1)S(1)}, u32[]{:S(2)}, u32[]{:S(2)}) collective-permute-start(bf16[4,3,48,384]{3,2,1,0:T(8,128)(2,1)S(1)} %slice.318), channel_id=1, source_target_pairs={{0,4},{4,0},{8,12},{12,8},{16,20},{20,16},{24,28},{28,24},{1,5},{5... | collective-permute-start | bytes 1327112 | tf_op jit(solution)/shard_map/ppermute | solution.py:947
  336.3 19.0 %collective-permute-start.40 = (bf16[4,3,48,384]{3,2,1,0:T(8,128)(2,1)S(1)}, bf16[4,3,48,384]{3,2,1,0:T(8,128)(2,1)S(1)}, u32[]{:S(2)}, u32[]{:S(2)}) collective-permute-start(bf16[4,3,48,384]{3,2,1,0:T(8,128)(2,1)S(1)} %slice.317), channel_id=1, source_target_pairs={{0,8},{4,12},{8,0},{12,4},{16,24},{20,28},{24,16},{28,20},{1,9},{5... | collective-permute-start | bytes 1327112 | tf_op jit(solution)/shard_map/ppermute | solution.py:947
  338.0 21.2 %collective-permute-start.41 = (bf16[4,3,48,384]{3,2,1,0:T(8,128)(2,1)S(1)}, bf16[4,3,48,384]{3,2,1,0:T(8,128)(2,1)S(1)}, u32[]{:S(2)}, u32[]{:S(2)}) collective-permute-start(bf16[4,3,48,384]{3,2,1,0:T(8,128)(2,1)S(1)} %slice.316), channel_id=1, source_target_pairs={{0,16},{4,20},{8,24},{12,28},{16,0},{20,4},{24,8},{28,12},{1,17},{... | collective-permute-start | bytes 1327112 | tf_op jit(solution)/shard_map/ppermute | solution.py:947
  360.1 26.8 %collective-permute-start.42 = (bf16[2,3,48,384]{3,2,1,0:T(8,128)(2,1)}, bf16[2,3,48,384]{3,2,1,0:T(8,128)(2,1)}, u32[]{:S(2)}, u32[]{:S(2)}) collective-permute-start(bf16[2,3,48,384]{3,2,1,0:T(8,128)(2,1)} %slice.321), channel_id=1, source_target_pairs={{0,8},{4,12},{8,0},{12,4},{16,24},{20,28},{24,16},{28,20},{1,9},{5... | collective-permute-start | bytes 663560 | tf_op jit(solution)/shard_map/ppermute | solution.py:947
  360.1 26.8 %collective-permute-start.43 = (bf16[2,3,48,384]{3,2,1,0:T(8,128)(2,1)}, bf16[2,3,48,384]{3,2,1,0:T(8,128)(2,1)}, u32[]{:S(2)}, u32[]{:S(2)}) collective-permute-start(bf16[2,3,48,384]{3,2,1,0:T(8,128)(2,1)} %slice.320), channel_id=1, source_target_pairs={{0,16},{4,20},{8,24},{12,28},{16,0},{20,4},{24,8},{28,12},{1,17},{... | collective-permute-start | bytes 663560 | tf_op jit(solution)/shard_map/ppermute | solution.py:947
  361.7 25.2 %collective-permute-start.44 = (bf16[2,3,48,384]{3,2,1,0:T(8,128)(2,1)}, bf16[2,3,48,384]{3,2,1,0:T(8,128)(2,1)}, u32[]{:S(2)}, u32[]{:S(2)}) collective-permute-start(bf16[2,3,48,384]{3,2,1,0:T(8,128)(2,1)} %slice.319), channel_id=1, source_target_pairs={{0,2},{1,3},{2,0},{3,1},{4,6},{5,7},{6,4},{7,5},{8,10},{9,11},{10,... | collective-permute-start | bytes 663560 | tf_op jit(solution)/shard_map/ppermute | solution.py:947
  373.1 44.0 %collective-permute-start.52 = (bf16[1024,768]{1,0:T(8,128)(2,1)}, bf16[1024,768]{1,0:T(8,128)(2,1)}, u32[]{:S(2)}, u32[]{:S(2)}) collective-permute-start(bf16[1024,768]{1,0:T(8,128)(2,1)} %gather_grads.5.refs_3_), channel_id=1, source_target_pairs={{0,12},{4,8},{8,4},{12,0},{16,28},{20,24},{24,20},{28,16},{1,13},{... | collective-permute-start | bytes 4718600 | tf_op jit(solution)/shard_map/ppermute | solution.py:947
  389.4 24.9 %collective-permute-start.49 = (bf16[1,3,48,384]{3,2,1,0:T(8,128)(2,1)S(1)}, bf16[1,3,48,384]{3,2,1,0:T(8,128)(2,1)S(1)}, u32[]{:S(2)}, u32[]{:S(2)}) collective-permute-start(bf16[1,3,48,384]{3,2,1,0:T(8,128)(2,1)S(1)} %slice.324), channel_id=1, source_target_pairs={{0,16},{4,20},{8,24},{12,28},{16,0},{20,4},{24,8},{28,12},{1,17},{... | collective-permute-start | bytes 331784 | tf_op jit(solution)/shard_map/ppermute | solution.py:947
  394.1 20.8 %collective-permute-start.50 = (bf16[1,3,48,384]{3,2,1,0:T(8,128)(2,1)S(1)}, bf16[1,3,48,384]{3,2,1,0:T(8,128)(2,1)S(1)}, u32[]{:S(2)}, u32[]{:S(2)}) collective-permute-start(bf16[1,3,48,384]{3,2,1,0:T(8,128)(2,1)S(1)} %slice.323), channel_id=1, source_target_pairs={{0,2},{1,3},{2,0},{3,1},{4,6},{5,7},{6,4},{7,5},{8,10},{9,11},{10,... | collective-permute-start | bytes 331784 | tf_op jit(solution)/shard_map/ppermute | solution.py:947
  395.7 17.3 %collective-permute-start.47 = (bf16[3,96,384]{2,1,0:T(8,128)(2,1)S(1)}, bf16[3,96,384]{2,1,0:T(8,128)(2,1)S(1)}, u32[]{:S(2)}, u32[]{:S(2)}) collective-permute-start(bf16[3,96,384]{2,1,0:T(8,128)(2,1)S(1)} %fusion.8), channel_id=1, source_target_pairs={{0,16},{4,20},{8,24},{12,28},{16,0},{20,4},{24,8},{28,12},{1,17},{... | collective-permute-start | bytes 663560 | tf_op jit(solution)/shard_map/ppermute | solution.py:947
  397.8 17.8 %collective-permute-start.51 = (bf16[1,3,48,384]{3,2,1,0:T(8,128)(2,1)S(1)}, bf16[1,3,48,384]{3,2,1,0:T(8,128)(2,1)S(1)}, u32[]{:S(2)}, u32[]{:S(2)}) collective-permute-start(bf16[1,3,48,384]{3,2,1,0:T(8,128)(2,1)S(1)} %slice.322), channel_id=1, source_target_pairs={{0,4},{4,0},{8,12},{12,8},{16,20},{20,16},{24,28},{28,24},{1,5},{5... | collective-permute-start | bytes 331784 | tf_op jit(solution)/shard_map/ppermute | solution.py:947
  419.3 44.5 %collective-permute-start.55 = (bf16[1024,768]{1,0:T(8,128)(2,1)}, bf16[1024,768]{1,0:T(8,128)(2,1)}, u32[]{:S(2)}, u32[]{:S(2)}) collective-permute-start(bf16[1024,768]{1,0:T(8,128)(2,1)} %gather_grads.7.refs_1_), channel_id=1, source_target_pairs={{0,4},{4,0},{8,12},{12,8},{16,20},{20,16},{24,28},{28,24},{1,5},{5... | collective-permute-start | bytes 4718600 | tf_op jit(solution)/shard_map/ppermute | solution.py:947
  420.5 43.2 %collective-permute-start.56 = (bf16[1024,768]{1,0:T(8,128)(2,1)}, bf16[1024,768]{1,0:T(8,128)(2,1)}, u32[]{:S(2)}, u32[]{:S(2)}) collective-permute-start(bf16[1024,768]{1,0:T(8,128)(2,1)} %gather_grads.4.refs_2_), channel_id=1, source_target_pairs={{0,8},{4,12},{8,0},{12,4},{16,24},{20,28},{24,16},{28,20},{1,9},{5... | collective-permute-start | bytes 4718600 | tf_op jit(solution)/shard_map/ppermute | solution.py:947
  450.6 20.7 %all-to-all-start.1 = ((bf16[8,3,96,96]{3,2,1,0:T(8,128)(2,1)}), bf16[8,3,96,96]{3,2,1,0:T(8,128)(2,1)}, u32[]{:S(2)}, u32[]{:S(2)}) async-start(bf16[8,3,96,96]{3,2,1,0:T(8,128)(2,1)} %copy-done.16), calls=%async_computation.1 | async-start | bytes 1179648 | tf_op jit(solution)/shard_map/all_to_all | solution.py:1206
  483.4 21.9 %all-to-all-start.2 = ((bf16[8,3,96,96]{3,2,1,0:T(8,128)(2,1)}), bf16[8,3,96,96]{3,2,1,0:T(8,128)(2,1)}, u32[]{:S(2)}, u32[]{:S(2)}) async-start(bf16[8,3,96,96]{3,2,1,0:T(8,128)(2,1)} %copy-done.32), calls=%async_computation.2 | async-start | bytes 1179648 | tf_op jit(solution)/shard_map/all_to_all | solution.py:1206
  488.4 16.9 %collective-permute-start.58 = (f32[12,768]{1,0:T(8,128)S(1)}, f32[12,768]{1,0:T(8,128)}, u32[]{:S(2)}, u32[]{:S(2)}) collective-permute-start(f32[12,768]{1,0:T(8,128)S(1)} %add.168), channel_id=1, source_target_pairs={{0,16},{4,20},{8,24},{12,28},{16,0},{20,4},{24,8},{28,12},{1,17},{... | collective-permute-start | bytes 110600 | tf_op jit(solution)/shard_map/ppermute | solution.py:947
  510.4 19.7 %all-to-all-start.3 = ((bf16[8,3,96,96]{3,2,1,0:T(8,128)(2,1)}), bf16[8,3,96,96]{3,2,1,0:T(8,128)(2,1)S(1)}, u32[]{:S(2)}, u32[]{:S(2)}) async-start(bf16[8,3,96,96]{3,2,1,0:T(8,128)(2,1)} %copy-done.17), calls=%async_computation.3 | async-start | bytes 1179648 | tf_op jit(solution)/shard_map/all_to_all | solution.py:1206
  (109 other events, 669.0 us)

commit v10 on v9

--- a/solution.py
+++ b/solution.py
@@ -1161,13 +1161,11 @@
     own_grads[3] = gather_grads(orders[3], sorted_back[3])
     own_grads[2] = gather_grads(orders[2], sorted_back[2])
     kept_now, sent_now = halves(joined(kept_now, got_now))
-    (sent_now, own_grads[2], own_grads[3], sorted_back) = together(
-        sent_now, own_grads[2], own_grads[3], sorted_back
-    )
+    own_grads[1] = gather_grads(orders[1], sorted_back[1])
+    (sent_now, own_grads[1:], sorted_back) = together(sent_now, own_grads[1:], sorted_back)
     got_now = exchanged(sent_now, 2)
     home_grads = [None, None, None, swap(own_grads[3], "tok", 3)]
-    for k in (1, 0):
-        own_grads[k] = gather_grads(orders[k], sorted_back[k])
+    own_grads[0] = gather_grads(orders[0], sorted_back[0])
     kept_qkv, sent_qkv, bias_qkv = qkv_back(jnp.stack([core, unit]).astype(jnp.int32), own_grads, unit_inputs)
     (got_now, kept_qkv, sent_qkv) = together(got_now, kept_qkv, sent_qkv)
     kept_now = joined(kept_now, got_now)

time: 540 us -> 535 us (level)
  waiting for transfers between devices: 94.4 us -> 88.7 us
  transfers between devices with their start and end apart: 64 -> 64, of which waited for: 22 -> 20; matrix products, arithmetic and copies ran while one was open for 15% -> 15% of each run, Pallas kernels for 39% -> 39%
where the time goes in v10:
time: 535 us; the launch traced here: 527 us
  Pallas kernels  225 us (42%)
  waiting for transfers between devices  88.7 us (17%)
  starting transfers between devices  85.5 us (16%)
  local copies, waits for them, and re-layouts  59.7 us (11%)
  other arithmetic  51.1 us (10%)
  matrix products  14.7 us (3%)
    pallas_call x1, Pallas kernels, layer(): pl.pallas_call(functools.partial(layer_body, n_shards), in_specs=[pl.Bloc...  69.8 us
    ppermute x57, waiting for transfers between devices, swap(): return lax.ppermute(value, axis, [(i, i ^ bit) for i in range(size)])  63.2 us
    ppermute x57, starting transfers between devices, swap(): return lax.ppermute(value, axis, [(i, i ^ bit) for i in range(size)])  62.3 us
    unnamed x191, local copies, waits for them, and re-layouts  42.1 us
    pallas_call x4, Pallas kernels, sort_rows(): pl.pallas_call(sort_body, grid=(HEADS_OWN,), in_specs=[pl.BlockSpec((8, c...  27.7 us
    pallas_call x4, Pallas kernels, gather_grads(): pl.pallas_call(gather_grads_body, grid=(HEADS_OWN,), in_specs=[pl.BlockSp...  20 us
    pallas_call x1, Pallas kernels, attend_back(): pl.pallas_call(attend_back_body, grid_spec=pltpu.PrefetchScalarGridSpec(n...  19.7 us
    pallas_call x4, Pallas kernels, mix(): pl.pallas_call(mix_body, grid=(HEADS_OWN,), in_specs=[pl.BlockSpec((8, co...  17.2 us
  transfers between devices with their start and end apart: 64, of which 20 were waited for; matrix products, arithmetic and copies ran while one was open for 15% of the time, Pallas kernels for 39%

profile of v10, /device:TPU:0, one launch (start us, length us, event | category | flops | bytes accessed | tf_op | source)
XLA Modules:
  0.0 527.2 jit_solution(17949662223677143301)
XLA Ops:
  0.6 3.0 collective-permute-start
  11.4 6.9 %places.1 = (s32[8,1024]{1,0:T(8,128)}, s32[8,1024]{1,0:T(8,128)}, s32[8,1024]{1,0:T(8,128)}, s32[8,1024]{1,0:T(8,128)}) custom-call(s32[2]{0:T(128)} %get-tuple-element.330.scalars_ref, s32[24,1024]{1,0:T(8,128)} %bitcast.127), custom_call_target="tpu_custom_call" | custom-call | tf_op jit(solution)/shard_map/places/pallas_call | solution.py:96
  18.3 14.9 %fusion = (bf16[3,768,768]{2,1,0:T(8,128)(2,1)}, bf16[3,768,768]{2,1,0:T(8,128)(2,1)}, bf16[3,768,768]{2,1,0:T(8,128)(2,1)}, bf16[3,768,768]{2,1,0:T(8,128)(2,1)S(1)}) fusion(f32[2,3,768,768]{3,2,1,0:T(8,128)} %param.18), kind=kLoop, calls=%fused_computation.2 | loop fusion | flops 10616832 | bytes 35389440 | tf_op jit(solution)/shard_map/convert_element_type | solution.py:1002
  63.2 13.8 %collective-permute-done.13 = bf16[4,48,768]{2,1,0:T(8,128)(2,1)S(1)} collective-permute-done((bf16[4,48,768]{2,1,0:T(8,128)(2,1)S(1)}, bf16[4,48,768]{2,1,0:T(8,128)(2,1)S(1)}, u32[]{:S(2)}, u32[]{:S(2)}) %collective-permute-start.13) | collective-permute-done | bytes 294944 | tf_op jit(solution)/shard_map/ppermute | solution.py:947
  80.0 5.1 collective-permute-start.15
  89.7 3.2 assemble.1.weight_ref
  95.0 6.5 %sort_rows.4.refs_0_ = bf16[6,1024,256]{2,1,0:T(8,128)(2,1)S(1)} custom-call(s32[8,1024]{1,0:T(8,128)S(1)} %copy-done.33, bf16[1024,768]{1,0:T(8,128)(2,1)S(1)} %bitcast.111, bf16[768,768]{1,0:T(8,128)(2,1)} %assemble.1.weight_ref, f32[1,768]{1,0:T(1,128)S(1)} %reshape.107.bias_ref), custom_call_target="tpu_custom_call" | custom-call | tf_op jit(solution)/shard_map/sort_rows/pallas_call | solution.py:221
  103.3 7.2 %sort_rows.5.refs_1_ = bf16[6,1024,256]{2,1,0:T(8,128)(2,1)S(1)} custom-call(s32[8,1024]{1,0:T(8,128)S(1)} %copy-done.37, bf16[1024,768]{1,0:T(8,128)(2,1)} %collective-permute-done.x_ref.refs_5_, bf16[768,768]{1,0:T(8,128)(2,1)} %assemble.1.weight_ref, f32[1,768]{1,0:T(1,128)S(1)} %reshape.107.bias_ref), custom_call_target="tpu_custom_call" | custom-call | tf_op jit(solution)/shard_map/sort_rows/pallas_call | solution.py:221
  114.9 7.1 %sort_rows.6.refs_2_ = bf16[6,1024,256]{2,1,0:T(8,128)(2,1)S(1)} custom-call(s32[8,1024]{1,0:T(8,128)S(1)} %copy-done.40, bf16[1024,768]{1,0:T(8,128)(2,1)} %collective-permute-done.1.x_ref.refs_6_, bf16[768,768]{1,0:T(8,128)(2,1)} %assemble.1.weight_ref, f32[1,768]{1,0:T(1,128)S(1)} %reshape.107.bias_ref), custom_call_target="tpu_custom_call" | custom-call | tf_op jit(solution)/shard_map/sort_rows/pallas_call | solution.py:221
  126.1 6.9 %sort_rows.7.refs_3_ = bf16[6,1024,256]{2,1,0:T(8,128)(2,1)S(1)} custom-call(s32[8,1024]{1,0:T(8,128)S(1)} %copy-done.43, bf16[1024,768]{1,0:T(8,128)(2,1)S(1)} %constant_dynamic-update-slice_fusion.5.x_ref.refs_7_, bf16[768,768]{1,0:T(8,128)(2,1)} %assemble.1.weight_ref, f32[1,768]{1,0:T(1,128)S(1)} %reshape.107.bias_ref), custom_call_target="tpu_custom_call" | custom-call | tf_op jit(solution)/shard_map/sort_rows/pallas_call | solution.py:221
  138.0 12.3 %attend.1 = (bf16[6,1024,128]{2,1,0:T(8,128)(2,1)S(1)}, bf16[6,1024,128]{2,1,0:T(8,128)(2,1)S(1)}, bf16[6,1024,128]{2,1,0:T(8,128)(2,1)S(1)}, bf16[6,1024,128]{2,1,0:T(8,128)(2,1)}) custom-call(s32[1]{0:T(128)} %bitcast.11.long_ref, bf16[6,1024,256]{2,1,0:T(8,128)(2,1)} %copy-done, bf16[6,1024,256]{2,1,0:T(8,128)(2,1)} %copy-done.1, ...), custom_call_target="tpu_custom_call" | custom-call | tf_op jit(solution)/shard_map/attend/pallas_call | solution.py:345
  150.2 5.6 %collective-permute-done.20 = bf16[9,48,768]{2,1,0:T(8,128)(2,1)S(1)} collective-permute-done((bf16[9,48,768]{2,1,0:T(8,128)(2,1)S(1)}, bf16[9,48,768]{2,1,0:T(8,128)(2,1)S(1)}, u32[]{:S(2)}, u32[]{:S(2)}) %collective-permute-start.20) | collective-permute-done | bytes 663584 | tf_op jit(solution)/shard_map/ppermute | solution.py:1090
  158.4 4.2 mix.4
  162.7 4.3 mix.6
  167.9 4.4 mix.7
  175.0 4.2 mix.5.refs_8_
  180.0 3.0 collective-permute-done.23.refs_9_
  184.4 7.9 %collective-permute-done.25.refs_11_ = bf16[1536,128]{1,0:T(8,128)(2,1)S(1)} collective-permute-done((bf16[1536,128]{1,0:T(8,128)(2,1)S(1)}, bf16[1536,128]{1,0:T(8,128)(2,1)S(1)}, u32[]{:S(2)}, u32[]{:S(2)}) %collective-permute-start.25) | collective-permute-done | bytes 393248 | tf_op jit(solution)/shard_map/ppermute | solution.py:947
  198.9 69.8 %layer.1 = (bf16[1024,768]{1,0:T(8,128)(2,1)}, f32[1024,768]{1,0:T(8,128)}, f32[16,768]{1,0:T(8,128)}, bf16[3,16,3,48,384]{4,3,2,1,0:T(8,128)(2,1)}, bf16[3,16,3...) custom-call(s32[22]{0:T(128)} %concatenate.28.table_ref, ...), custom_call_target="tpu_custom_call" | custom-call | tf_op jit(solution)/shard_map/layer/pallas_call | solution.py:713
  273.4 3.8 sort_grads.4.refs_4_
  277.9 4.6 convert_add_fusion
  287.1 3.1 collective-permute-done.35.rows_ref
  292.8 3.8 sort_grads.5.refs_5_
  297.8 4.2 sort_grads.6.refs_6_
  303.2 3.8 sort_grads.7.refs_7_
  308.2 19.7 %attend_back.1 = (bf16[6,1024,256]{2,1,0:T(8,128)(2,1)}, bf16[6,1024,256]{2,1,0:T(8,128)(2,1)}, bf16[6,1024,256]{2,1,0:T(8,128)(2,1)}, bf16[6,1024,256]{2,1,0:T(8,128)(2,1)}) custom-call(s32[1]{0:T(128)} %bitcast.11.long_ref, bf16[6,1024,256]{2,1,0:T(8,128)(2,1)} %copy-done, bf16[6,1024,256]{2,1,0:T(8,128)(2,1)} %copy-done.1, ...), custom_call_target="tpu_custom_call" | custom-call | tf_op jit(solution)/shard_map/attend_back/pallas_call | solution.py:389
  340.0 5.3 %gather_grads.4.refs_1_ = bf16[1024,768]{1,0:T(8,128)(2,1)} custom-call(s32[8,1024]{1,0:T(8,128)S(1)} %copy-done.38, bf16[6,1024,256]{2,1,0:T(8,128)(2,1)S(1)} %copy-done.15), custom_call_target="tpu_custom_call" | custom-call | tf_op jit(solution)/shard_map/gather_grads/pallas_call | solution.py:482
  345.3 5.1 gather_grads.5.refs_2_
  350.4 5.1 gather_grads.6.refs_3_
  362.9 4.6 gather_grads.7.refs_0_
  369.4 10.8 %qkv_back.1 = (bf16[2,3,96,384]{3,2,1,0:T(8,128)(2,1)}, bf16[2,3,96,384]{3,2,1,0:T(8,128)(2,1)}, f32[8,768]{1,0:T(8,128)}) custom-call(s32[2]{0:T(128)} %get-tuple-element.331.scalars_ref, bf16[1024,768]{1,0:T(8,128)(2,1)} %copy-done.6, bf16[1024,768]{1,0:T(8,128)(2,1)} %gather_grads.4.refs_1_, bf16[1024,768]{1,0:T(8,128)(2,1)} %gather_grads.5.refs_2_, ...), custom_call_target="tpu_custom_call" | custom-call | tf_op jit(solution)/shard_map/qkv_back/pallas_call | solution.py:778
  394.4 14.2 %collective-permute-done.47 = bf16[3,96,384]{2,1,0:T(8,128)(2,1)S(1)} collective-permute-done((bf16[3,96,384]{2,1,0:T(8,128)(2,1)S(1)}, bf16[3,96,384]{2,1,0:T(8,128)(2,1)S(1)}, u32[]{:S(2)}, u32[]{:S(2)}) %collective-permute-start.47) | collective-permute-done | bytes 221216 | tf_op jit(solution)/shard_map/ppermute | solution.py:947
  414.9 2.9 collective-permute-start.56
  427.3 4.1 all-to-all-start
  433.4 6.1 %all-to-all-done.got_ref = bf16[4,3,48,384]{3,2,1,0:T(8,128)(2,1)} async-done(((bf16[4,3,48,384]{3,2,1,0:T(8,128)(2,1)}), bf16[4,3,48,384]{3,2,1,0:T(8,128)(2,1)}, u32[]{:S(2)}, u32[]{:S(2)}) %all-to-all-start) | async-done | bytes 442400 | tf_op jit(solution)/shard_map/all_to_all | solution.py:1194
  440.5 4.4 rotate_in.1
  445.7 5.4 %all-to-all-start.1 = ((bf16[8,3,96,96]{3,2,1,0:T(8,128)(2,1)}), bf16[8,3,96,96]{3,2,1,0:T(8,128)(2,1)}, u32[]{:S(2)}, u32[]{:S(2)}) async-start(bf16[8,3,96,96]{3,2,1,0:T(8,128)(2,1)} %copy-done.16), calls=%async_computation.1 | async-start | bytes 1179648 | tf_op jit(solution)/shard_map/all_to_all | solution.py:1204
  454.0 3.3 fusion.19
  461.7 5.3 %all-to-all-done.1.got_ref = bf16[8,3,96,96]{3,2,1,0:T(8,128)(2,1)} async-done(((bf16[8,3,96,96]{3,2,1,0:T(8,128)(2,1)}), bf16[8,3,96,96]{3,2,1,0:T(8,128)(2,1)}, u32[]{:S(2)}, u32[]{:S(2)}) %all-to-all-start.1) | async-done | bytes 442400 | tf_op jit(solution)/shard_map/all_to_all | solution.py:1204
  469.3 8.9 %moments.1 = (f32[3,96,768]{2,1,0:T(8,128)}, f32[3,96,768]{2,1,0:T(8,128)}, bf16[8,3,96,96]{3,2,1,0:T(8,128)(2,1)S(1)}) custom-call(bf16[8,3,96,96]{3,2,1,0:T(8,128)(2,1)} %all-to-all-done.1.got_ref, bf16[3,768,768]{2,1,0:T(8,128)(2,1)} %get-tuple-element.283.high_ref, bf16[3,768,768]{2,1,0:T(8,128)(2,1)} %get-tuple-element.284.low_ref, ...), custom_call_target="tpu_custom_call" | custom-call | tf_op jit(solution)/shard_map/moments/pallas_call | solution.py:882
  479.0 4.2 all-to-all-start.2
  486.9 3.2 fusion.20
  490.1 4.9 add_add_fusion
  495.0 5.9 %collective-permute-done.58 = f32[12,768]{1,0:T(8,128)} collective-permute-done((f32[12,768]{1,0:T(8,128)S(1)}, f32[12,768]{1,0:T(8,128)}, u32[]{:S(2)}, u32[]{:S(2)}) %collective-permute-start.58) | collective-permute-done | bytes 36896 | tf_op jit(solution)/shard_map/ppermute | solution.py:947
  500.9 4.2 rotate_out.1
  506.0 3.6 all-to-all-start.3
  511.0 3.3 fusion.21
  517.1 8.4 %all-to-all-done.3.got_ref = bf16[8,3,96,96]{3,2,1,0:T(8,128)(2,1)S(1)} async-done(((bf16[8,3,96,96]{3,2,1,0:T(8,128)(2,1)}), bf16[8,3,96,96]{3,2,1,0:T(8,128)(2,1)S(1)}, u32[]{:S(2)}, u32[]{:S(2)}) %all-to-all-start.3) | async-done | bytes 442400 | tf_op jit(solution)/shard_map/all_to_all | solution.py:1204
  (382 shorter events, 167.9 us)
Async XLA Ops:
  0.6 37.7 %collective-permute-start = (bf16[1024,768]{1,0:T(8,128)(2,1)}, bf16[1024,768]{1,0:T(8,128)(2,1)}, u32[]{:S(2)}, u32[]{:S(2)}) collective-permute-start(bf16[1024,768]{1,0:T(8,128)(2,1)} %bitcast.107), channel_id=1, source_target_pairs={{0,4},{4,0},{8,12},{12,8},{16,20},{20,16},{24,28},{28,24},{1,5},{5... | collective-permute-start | bytes 4718600 | tf_op jit(solution)/shard_map/ppermute | solution.py:947
  3.7 36.2 %collective-permute-start.1 = (bf16[1024,768]{1,0:T(8,128)(2,1)}, bf16[1024,768]{1,0:T(8,128)(2,1)}, u32[]{:S(2)}, u32[]{:S(2)}) collective-permute-start(bf16[1024,768]{1,0:T(8,128)(2,1)} %bitcast.108), channel_id=1, source_target_pairs={{0,8},{4,12},{8,0},{12,4},{16,24},{20,28},{24,16},{28,20},{1,9},{5... | collective-permute-start | bytes 4718600 | tf_op jit(solution)/shard_map/ppermute | solution.py:947
  7.2 28.8 %collective-permute-start.2 = (bf16[3,96,768]{2,1,0:T(8,128)(2,1)}, bf16[3,96,768]{2,1,0:T(8,128)(2,1)}, u32[]{:S(2)}, u32[]{:S(2)}) collective-permute-start(bf16[3,96,768]{2,1,0:T(8,128)(2,1)} %convert_bitcast_fusion.refs_0_), channel_id=1, source_target_pairs={{0,1},{1,0},{2,3},{3,2},{4,5},{5,4},{6,7},{7,6},{8,9},{9,8},{10,11... | collective-permute-start | bytes 1327112 | tf_op jit(solution)/shard_map/ppermute | solution.py:947
  7.2 26.0 %collective-permute-start.3 = (bf16[3,96,768]{2,1,0:T(8,128)(2,1)}, bf16[3,96,768]{2,1,0:T(8,128)(2,1)}, u32[]{:S(2)}, u32[]{:S(2)}) collective-permute-start(bf16[3,96,768]{2,1,0:T(8,128)(2,1)} %convert_bitcast_fusion.refs_0_), channel_id=1, source_target_pairs={{0,2},{1,3},{2,0},{3,1},{4,6},{5,7},{6,4},{7,5},{8,10},{9,11},{10,... | collective-permute-start | bytes 1327112 | tf_op jit(solution)/shard_map/ppermute | solution.py:947
  41.9 16.0 %collective-permute-start.7 = (bf16[48,768]{1,0:T(8,128)(2,1)S(1)}, bf16[48,768]{1,0:T(8,128)(2,1)S(1)}, u32[]{:S(2)}, u32[]{:S(2)}) collective-permute-start(bf16[48,768]{1,0:T(8,128)(2,1)S(1)} %get-tuple-element.167), channel_id=1, source_target_pairs={{0,4},{4,0},{8,12},{12,8},{16,20},{20,16},{24,28},{28,24},{1,5},{5... | collective-permute-start | bytes 221192 | tf_op jit(solution)/shard_map/ppermute | solution.py:947
  42.4 15.6 %collective-permute-start.8 = (bf16[48,768]{1,0:T(8,128)(2,1)S(1)}, bf16[48,768]{1,0:T(8,128)(2,1)S(1)}, u32[]{:S(2)}, u32[]{:S(2)}) collective-permute-start(bf16[48,768]{1,0:T(8,128)(2,1)S(1)} %get-tuple-element.168), channel_id=1, source_target_pairs={{0,8},{4,12},{8,0},{12,4},{16,24},{20,28},{24,16},{28,20},{1,9},{5... | collective-permute-start | bytes 221192 | tf_op jit(solution)/shard_map/ppermute | solution.py:947
  44.1 13.9 %collective-permute-start.9 = (bf16[48,768]{1,0:T(8,128)(2,1)S(1)}, bf16[48,768]{1,0:T(8,128)(2,1)S(1)}, u32[]{:S(2)}, u32[]{:S(2)}) collective-permute-start(bf16[48,768]{1,0:T(8,128)(2,1)S(1)} %get-tuple-element.169), channel_id=1, source_target_pairs={{0,12},{4,8},{8,4},{12,0},{16,28},{20,24},{24,20},{28,16},{1,13},{... | collective-permute-start | bytes 221192 | tf_op jit(solution)/shard_map/ppermute | solution.py:947
  55.8 23.4 %collective-permute-start.5 = (bf16[512,768]{1,0:T(8,128)(2,1)}, bf16[512,768]{1,0:T(8,128)(2,1)}, u32[]{:S(2)}, u32[]{:S(2)}) collective-permute-start(bf16[512,768]{1,0:T(8,128)(2,1)} %slice.180), channel_id=1, source_target_pairs={{0,8},{4,12},{8,0},{12,4},{16,24},{20,28},{24,16},{28,20},{1,9},{5... | collective-permute-start | bytes 2359304 | tf_op jit(solution)/shard_map/ppermute | solution.py:947
  56.0 23.3 %collective-permute-start.6 = (bf16[512,768]{1,0:T(8,128)(2,1)}, bf16[512,768]{1,0:T(8,128)(2,1)}, u32[]{:S(2)}, u32[]{:S(2)}) collective-permute-start(bf16[512,768]{1,0:T(8,128)(2,1)} %slice.181), channel_id=1, source_target_pairs={{0,4},{4,0},{8,12},{12,8},{16,20},{20,16},{24,28},{28,24},{1,5},{5... | collective-permute-start | bytes 2359304 | tf_op jit(solution)/shard_map/ppermute | solution.py:947
  59.3 17.7 %collective-permute-start.13 = (bf16[4,48,768]{2,1,0:T(8,128)(2,1)S(1)}, bf16[4,48,768]{2,1,0:T(8,128)(2,1)S(1)}, u32[]{:S(2)}, u32[]{:S(2)}) collective-permute-start(bf16[4,48,768]{2,1,0:T(8,128)(2,1)S(1)} %pad_maximum_fusion.5), channel_id=1, source_target_pairs={{0,16},{4,20},{8,24},{12,28},{16,0},{20,4},{24,8},{28,12},{1,17},{... | collective-permute-start | bytes 884744 | tf_op jit(solution)/shard_map/ppermute | solution.py:947
  80.0 32.0 %collective-permute-start.15 = (bf16[9,48,768]{2,1,0:T(8,128)(2,1)}, bf16[9,48,768]{2,1,0:T(8,128)(2,1)}, u32[]{:S(2)}, u32[]{:S(2)}) collective-permute-start(bf16[9,48,768]{2,1,0:T(8,128)(2,1)} %copy-done.30), channel_id=1, source_target_pairs={{0,8},{4,12},{8,16},{12,20},{16,24},{20,28},{24,0},{28,4},{1,9},{5... | collective-permute-start | bytes 1990664 | tf_op jit(solution)/shard_map/ppermute | solution.py:1090
  85.1 27.0 %collective-permute-start.16 = (bf16[9,48,768]{2,1,0:T(8,128)(2,1)}, bf16[9,48,768]{2,1,0:T(8,128)(2,1)}, u32[]{:S(2)}, u32[]{:S(2)}) collective-permute-start(bf16[9,48,768]{2,1,0:T(8,128)(2,1)} %copy-done.30), channel_id=1, source_target_pairs={{0,4},{4,0},{8,12},{12,8},{16,20},{20,16},{24,28},{28,24},{1,5},{5... | collective-permute-start | bytes 1990664 | tf_op jit(solution)/shard_map/ppermute | solution.py:947
  113.3 21.3 %collective-permute-start.19 = (bf16[2,9,48,768]{3,2,1,0:T(8,128)(2,1)S(1)}, bf16[2,9,48,768]{3,2,1,0:T(8,128)(2,1)S(1)}, u32[]{:S(2)}, u32[]{:S(2)}) collective-permute-start(bf16[2,9,48,768]{3,2,1,0:T(8,128)(2,1)S(1)} %pad_maximum_fusion.refs_0_), channel_id=1, source_target_pairs={{0,1},{1,0},{2,3},{3,2},{4,5},{5,4},{6,7},{7,6},{8,9},{9,8},{10,11... | collective-permute-start | bytes 3981320 | tf_op jit(solution)/shard_map/ppermute | solution.py:947
  113.4 21.2 %collective-permute-start.17 = (bf16[9,48,768]{2,1,0:T(8,128)(2,1)}, bf16[9,48,768]{2,1,0:T(8,128)(2,1)S(1)}, u32[]{:S(2)}, u32[]{:S(2)}) collective-permute-start(bf16[9,48,768]{2,1,0:T(8,128)(2,1)} %collective-permute-done.15), channel_id=1, source_target_pairs={{0,8},{4,12},{8,16},{12,20},{16,24},{20,28},{24,0},{28,4},{1,9},{5... | collective-permute-start | bytes 1990664 | tf_op jit(solution)/shard_map/ppermute | solution.py:1090
  114.0 20.6 %collective-permute-start.18 = (bf16[9,48,768]{2,1,0:T(8,128)(2,1)}, bf16[9,48,768]{2,1,0:T(8,128)(2,1)S(1)}, u32[]{:S(2)}, u32[]{:S(2)}) collective-permute-start(bf16[9,48,768]{2,1,0:T(8,128)(2,1)} %collective-permute-done.15), channel_id=1, source_target_pairs={{0,4},{4,0},{8,12},{12,8},{16,20},{20,16},{24,28},{28,24},{1,5},{5... | collective-permute-start | bytes 1990664 | tf_op jit(solution)/shard_map/ppermute | solution.py:947
  136.3 19.5 %collective-permute-start.22 = (bf16[2,9,48,768]{3,2,1,0:T(8,128)(2,1)S(1)}, bf16[2,9,48,768]{3,2,1,0:T(8,128)(2,1)S(1)}, u32[]{:S(2)}, u32[]{:S(2)}) collective-permute-start(bf16[2,9,48,768]{3,2,1,0:T(8,128)(2,1)S(1)} %pad_maximum_fusion.1.refs_1_), channel_id=1, source_target_pairs={{0,1},{1,0},{2,3},{3,2},{4,5},{5,4},{6,7},{7,6},{8,9},{9,8},{10,11... | collective-permute-start | bytes 3981320 | tf_op jit(solution)/shard_map/ppermute | solution.py:947
  136.5 19.3 %collective-permute-start.20 = (bf16[9,48,768]{2,1,0:T(8,128)(2,1)S(1)}, bf16[9,48,768]{2,1,0:T(8,128)(2,1)S(1)}, u32[]{:S(2)}, u32[]{:S(2)}) collective-permute-start(bf16[9,48,768]{2,1,0:T(8,128)(2,1)S(1)} %collective-permute-done.17), channel_id=1, source_target_pairs={{0,8},{4,12},{8,16},{12,20},{16,24},{20,28},{24,0},{28,4},{1,9},{5... | collective-permute-start | bytes 1990664 | tf_op jit(solution)/shard_map/ppermute | solution.py:1090
  136.8 19.1 %collective-permute-start.21 = (bf16[9,48,768]{2,1,0:T(8,128)(2,1)S(1)}, bf16[9,48,768]{2,1,0:T(8,128)(2,1)S(1)}, u32[]{:S(2)}, u32[]{:S(2)}) collective-permute-start(bf16[9,48,768]{2,1,0:T(8,128)(2,1)S(1)} %collective-permute-done.17), channel_id=1, source_target_pairs={{0,4},{4,0},{8,12},{12,8},{16,20},{20,16},{24,28},{28,24},{1,5},{5... | collective-permute-start | bytes 1990664 | tf_op jit(solution)/shard_map/ppermute | solution.py:947
  157.1 35.2 %collective-permute-start.27 = (bf16[2,9,48,768]{3,2,1,0:T(8,128)(2,1)S(1)}, bf16[2,9,48,768]{3,2,1,0:T(8,128)(2,1)S(1)}, u32[]{:S(2)}, u32[]{:S(2)}) collective-permute-start(bf16[2,9,48,768]{3,2,1,0:T(8,128)(2,1)S(1)} %pad_maximum_fusion.2.refs_2_), channel_id=1, source_target_pairs={{0,1},{1,0},{2,3},{3,2},{4,5},{5,4},{6,7},{7,6},{8,9},{9,8},{10,11... | collective-permute-start | bytes 3981320 | tf_op jit(solution)/shard_map/ppermute | solution.py:947
  157.2 35.2 %collective-permute-start.26 = (bf16[9,48,768]{2,1,0:T(8,128)(2,1)S(1)}, bf16[9,48,768]{2,1,0:T(8,128)(2,1)S(1)}, u32[]{:S(2)}, u32[]{:S(2)}) collective-permute-start(bf16[9,48,768]{2,1,0:T(8,128)(2,1)S(1)} %collective-permute-done.20), channel_id=1, source_target_pairs={{0,4},{4,0},{8,12},{12,8},{16,20},{20,16},{24,28},{28,24},{1,5},{5... | collective-permute-start | bytes 1990664 | tf_op jit(solution)/shard_map/ppermute | solution.py:947
  167.0 16.1 %collective-permute-start.23 = (bf16[1536,128]{1,0:T(8,128)(2,1)S(1)}, bf16[1536,128]{1,0:T(8,128)(2,1)S(1)}, u32[]{:S(2)}, u32[]{:S(2)}) collective-permute-start(bf16[1536,128]{1,0:T(8,128)(2,1)S(1)} %mix.6), channel_id=1, source_target_pairs={{0,4},{4,0},{8,12},{12,8},{16,20},{20,16},{24,28},{28,24},{1,5},{5... | collective-permute-start | bytes 1179656 | tf_op jit(solution)/shard_map/ppermute | solution.py:947
  172.4 19.9 %collective-permute-start.25 = (bf16[1536,128]{1,0:T(8,128)(2,1)S(1)}, bf16[1536,128]{1,0:T(8,128)(2,1)S(1)}, u32[]{:S(2)}, u32[]{:S(2)}) collective-permute-start(bf16[1536,128]{1,0:T(8,128)(2,1)S(1)} %mix.4), channel_id=1, source_target_pairs={{0,12},{4,8},{8,4},{12,0},{16,28},{20,24},{24,20},{28,16},{1,13},{... | collective-permute-start | bytes 1179656 | tf_op jit(solution)/shard_map/ppermute | solution.py:947
  194.7 74.0 %collective-permute-start.29 = (bf16[768,768]{1,0:T(8,128)(2,1)}, bf16[768,768]{1,0:T(8,128)(2,1)}, u32[]{:S(2)}, u32[]{:S(2)}) collective-permute-start(bf16[768,768]{1,0:T(8,128)(2,1)} %assemble.1.weight_ref), channel_id=1, source_target_pairs={{0,4},{4,0},{8,12},{12,8},{16,20},{20,16},{24,28},{28,24},{1,5},{5... | collective-permute-start | bytes 3538952 | tf_op jit(solution)/shard_map/ppermute | solution.py:947
  195.6 73.1 %collective-permute-start.30 = (bf16[768,768]{1,0:T(8,128)(2,1)}, bf16[768,768]{1,0:T(8,128)(2,1)}, u32[]{:S(2)}, u32[]{:S(2)}) collective-permute-start(bf16[768,768]{1,0:T(8,128)(2,1)} %assemble.1.weight_ref), channel_id=1, source_target_pairs={{0,8},{4,12},{8,0},{12,4},{16,24},{20,28},{24,16},{28,20},{1,9},{5... | collective-permute-start | bytes 3538952 | tf_op jit(solution)/shard_map/ppermute | solution.py:947
  195.9 72.9 %collective-permute-start.31 = (bf16[768,768]{1,0:T(8,128)(2,1)}, bf16[768,768]{1,0:T(8,128)(2,1)}, u32[]{:S(2)}, u32[]{:S(2)}) collective-permute-start(bf16[768,768]{1,0:T(8,128)(2,1)} %assemble.1.weight_ref), channel_id=1, source_target_pairs={{0,12},{4,8},{8,4},{12,0},{16,28},{20,24},{24,20},{28,16},{1,13},{... | collective-permute-start | bytes 3538952 | tf_op jit(solution)/shard_map/ppermute | solution.py:947
  268.8 18.2 %collective-permute-start.33 = (bf16[1536,128]{1,0:T(8,128)(2,1)}, bf16[1536,128]{1,0:T(8,128)(2,1)S(1)}, u32[]{:S(2)}, u32[]{:S(2)}) collective-permute-start(bf16[1536,128]{1,0:T(8,128)(2,1)} %get-tuple-element.234), channel_id=1, source_target_pairs={{0,4},{4,0},{8,12},{12,8},{16,20},{20,16},{24,28},{28,24},{1,5},{5... | collective-permute-start | bytes 1179656 | tf_op jit(solution)/shard_map/ppermute | solution.py:947
  269.7 17.3 %collective-permute-start.34 = (bf16[1536,128]{1,0:T(8,128)(2,1)}, bf16[1536,128]{1,0:T(8,128)(2,1)S(1)}, u32[]{:S(2)}, u32[]{:S(2)}) collective-permute-start(bf16[1536,128]{1,0:T(8,128)(2,1)} %get-tuple-element.235), channel_id=1, source_target_pairs={{0,8},{4,12},{8,0},{12,4},{16,24},{20,28},{24,16},{28,20},{1,9},{5... | collective-permute-start | bytes 1179656 | tf_op jit(solution)/shard_map/ppermute | solution.py:947
  270.0 20.1 %collective-permute-start.35 = (bf16[1536,128]{1,0:T(8,128)(2,1)}, bf16[1536,128]{1,0:T(8,128)(2,1)S(1)}, u32[]{:S(2)}, u32[]{:S(2)}) collective-permute-start(bf16[1536,128]{1,0:T(8,128)(2,1)} %get-tuple-element.236), channel_id=1, source_target_pairs={{0,12},{4,8},{8,4},{12,0},{16,28},{20,24},{24,20},{28,16},{1,13},{... | collective-permute-start | bytes 1179656 | tf_op jit(solution)/shard_map/ppermute | solution.py:947
  290.2 37.8 %collective-permute-start.36 = (bf16[8,3,48,384]{3,2,1,0:T(8,128)(2,1)}, bf16[8,3,48,384]{3,2,1,0:T(8,128)(2,1)}, u32[]{:S(2)}, u32[]{:S(2)}) collective-permute-start(bf16[8,3,48,384]{3,2,1,0:T(8,128)(2,1)} %fusion.5), channel_id=1, source_target_pairs={{0,2},{1,3},{2,0},{3,1},{4,6},{5,7},{6,4},{7,5},{8,10},{9,11},{10,... | collective-permute-start | bytes 2654216 | tf_op jit(solution)/shard_map/ppermute | solution.py:947
  291.7 37.8 %collective-permute-start.37 = (bf16[8,3,48,384]{3,2,1,0:T(8,128)(2,1)}, bf16[8,3,48,384]{3,2,1,0:T(8,128)(2,1)}, u32[]{:S(2)}, u32[]{:S(2)}) collective-permute-start(bf16[8,3,48,384]{3,2,1,0:T(8,128)(2,1)} %fusion.6), channel_id=1, source_target_pairs={{0,4},{4,0},{8,12},{12,8},{16,20},{20,16},{24,28},{28,24},{1,5},{5... | collective-permute-start | bytes 2654216 | tf_op jit(solution)/shard_map/ppermute | solution.py:947
  292.5 40.0 %collective-permute-start.38 = (bf16[8,3,48,384]{3,2,1,0:T(8,128)(2,1)}, bf16[8,3,48,384]{3,2,1,0:T(8,128)(2,1)}, u32[]{:S(2)}, u32[]{:S(2)}) collective-permute-start(bf16[8,3,48,384]{3,2,1,0:T(8,128)(2,1)} %fusion.7), channel_id=1, source_target_pairs={{0,8},{4,12},{8,0},{12,4},{16,24},{20,28},{24,16},{28,20},{1,9},{5... | collective-permute-start | bytes 2654216 | tf_op jit(solution)/shard_map/ppermute | solution.py:947
  335.7 19.8 %collective-permute-start.39 = (bf16[4,3,48,384]{3,2,1,0:T(8,128)(2,1)S(1)}, bf16[4,3,48,384]{3,2,1,0:T(8,128)(2,1)S(1)}, u32[]{:S(2)}, u32[]{:S(2)}) collective-permute-start(bf16[4,3,48,384]{3,2,1,0:T(8,128)(2,1)S(1)} %slice.318), channel_id=1, source_target_pairs={{0,4},{4,0},{8,12},{12,8},{16,20},{20,16},{24,28},{28,24},{1,5},{5... | collective-permute-start | bytes 1327112 | tf_op jit(solution)/shard_map/ppermute | solution.py:947
  336.9 19.4 %collective-permute-start.40 = (bf16[4,3,48,384]{3,2,1,0:T(8,128)(2,1)S(1)}, bf16[4,3,48,384]{3,2,1,0:T(8,128)(2,1)S(1)}, u32[]{:S(2)}, u32[]{:S(2)}) collective-permute-start(bf16[4,3,48,384]{3,2,1,0:T(8,128)(2,1)S(1)} %slice.317), channel_id=1, source_target_pairs={{0,8},{4,12},{8,0},{12,4},{16,24},{20,28},{24,16},{28,20},{1,9},{5... | collective-permute-start | bytes 1327112 | tf_op jit(solution)/shard_map/ppermute | solution.py:947
  338.7 19.8 %collective-permute-start.41 = (bf16[4,3,48,384]{3,2,1,0:T(8,128)(2,1)S(1)}, bf16[4,3,48,384]{3,2,1,0:T(8,128)(2,1)S(1)}, u32[]{:S(2)}, u32[]{:S(2)}) collective-permute-start(bf16[4,3,48,384]{3,2,1,0:T(8,128)(2,1)S(1)} %slice.316), channel_id=1, source_target_pairs={{0,16},{4,20},{8,24},{12,28},{16,0},{20,4},{24,8},{28,12},{1,17},{... | collective-permute-start | bytes 1327112 | tf_op jit(solution)/shard_map/ppermute | solution.py:947
  359.3 23.1 %collective-permute-start.42 = (bf16[2,3,48,384]{3,2,1,0:T(8,128)(2,1)}, bf16[2,3,48,384]{3,2,1,0:T(8,128)(2,1)}, u32[]{:S(2)}, u32[]{:S(2)}) collective-permute-start(bf16[2,3,48,384]{3,2,1,0:T(8,128)(2,1)} %slice.321), channel_id=1, source_target_pairs={{0,8},{4,12},{8,0},{12,4},{16,24},{20,28},{24,16},{28,20},{1,9},{5... | collective-permute-start | bytes 663560 | tf_op jit(solution)/shard_map/ppermute | solution.py:947
  359.7 22.7 %collective-permute-start.43 = (bf16[2,3,48,384]{3,2,1,0:T(8,128)(2,1)}, bf16[2,3,48,384]{3,2,1,0:T(8,128)(2,1)}, u32[]{:S(2)}, u32[]{:S(2)}) collective-permute-start(bf16[2,3,48,384]{3,2,1,0:T(8,128)(2,1)} %slice.320), channel_id=1, source_target_pairs={{0,16},{4,20},{8,24},{12,28},{16,0},{20,4},{24,8},{28,12},{1,17},{... | collective-permute-start | bytes 663560 | tf_op jit(solution)/shard_map/ppermute | solution.py:947
  362.3 20.0 %collective-permute-start.44 = (bf16[2,3,48,384]{3,2,1,0:T(8,128)(2,1)}, bf16[2,3,48,384]{3,2,1,0:T(8,128)(2,1)}, u32[]{:S(2)}, u32[]{:S(2)}) collective-permute-start(bf16[2,3,48,384]{3,2,1,0:T(8,128)(2,1)} %slice.319), channel_id=1, source_target_pairs={{0,2},{1,3},{2,0},{3,1},{4,6},{5,7},{6,4},{7,5},{8,10},{9,11},{10,... | collective-permute-start | bytes 663560 | tf_op jit(solution)/shard_map/ppermute | solution.py:947
  368.6 44.1 %collective-permute-start.52 = (bf16[1024,768]{1,0:T(8,128)(2,1)}, bf16[1024,768]{1,0:T(8,128)(2,1)}, u32[]{:S(2)}, u32[]{:S(2)}) collective-permute-start(bf16[1024,768]{1,0:T(8,128)(2,1)} %gather_grads.6.refs_3_), channel_id=1, source_target_pairs={{0,12},{4,8},{8,4},{12,0},{16,28},{20,24},{24,20},{28,16},{1,13},{... | collective-permute-start | bytes 4718600 | tf_op jit(solution)/shard_map/ppermute | solution.py:947
  384.8 24.7 %collective-permute-start.49 = (bf16[1,3,48,384]{3,2,1,0:T(8,128)(2,1)S(1)}, bf16[1,3,48,384]{3,2,1,0:T(8,128)(2,1)S(1)}, u32[]{:S(2)}, u32[]{:S(2)}) collective-permute-start(bf16[1,3,48,384]{3,2,1,0:T(8,128)(2,1)S(1)} %slice.324), channel_id=1, source_target_pairs={{0,16},{4,20},{8,24},{12,28},{16,0},{20,4},{24,8},{28,12},{1,17},{... | collective-permute-start | bytes 331784 | tf_op jit(solution)/shard_map/ppermute | solution.py:947
  388.2 22.0 %collective-permute-start.50 = (bf16[1,3,48,384]{3,2,1,0:T(8,128)(2,1)S(1)}, bf16[1,3,48,384]{3,2,1,0:T(8,128)(2,1)S(1)}, u32[]{:S(2)}, u32[]{:S(2)}) collective-permute-start(bf16[1,3,48,384]{3,2,1,0:T(8,128)(2,1)S(1)} %slice.323), channel_id=1, source_target_pairs={{0,2},{1,3},{2,0},{3,1},{4,6},{5,7},{6,4},{7,5},{8,10},{9,11},{10,... | collective-permute-start | bytes 331784 | tf_op jit(solution)/shard_map/ppermute | solution.py:947
  389.8 18.8 %collective-permute-start.47 = (bf16[3,96,384]{2,1,0:T(8,128)(2,1)S(1)}, bf16[3,96,384]{2,1,0:T(8,128)(2,1)S(1)}, u32[]{:S(2)}, u32[]{:S(2)}) collective-permute-start(bf16[3,96,384]{2,1,0:T(8,128)(2,1)S(1)} %fusion.8), channel_id=1, source_target_pairs={{0,16},{4,20},{8,24},{12,28},{16,0},{20,4},{24,8},{28,12},{1,17},{... | collective-permute-start | bytes 663560 | tf_op jit(solution)/shard_map/ppermute | solution.py:947
  393.1 17.7 %collective-permute-start.51 = (bf16[1,3,48,384]{3,2,1,0:T(8,128)(2,1)S(1)}, bf16[1,3,48,384]{3,2,1,0:T(8,128)(2,1)S(1)}, u32[]{:S(2)}, u32[]{:S(2)}) collective-permute-start(bf16[1,3,48,384]{3,2,1,0:T(8,128)(2,1)S(1)} %slice.322), channel_id=1, source_target_pairs={{0,4},{4,0},{8,12},{12,8},{16,20},{20,16},{24,28},{28,24},{1,5},{5... | collective-permute-start | bytes 331784 | tf_op jit(solution)/shard_map/ppermute | solution.py:947
  414.0 45.4 %collective-permute-start.55 = (bf16[1024,768]{1,0:T(8,128)(2,1)}, bf16[1024,768]{1,0:T(8,128)(2,1)}, u32[]{:S(2)}, u32[]{:S(2)}) collective-permute-start(bf16[1024,768]{1,0:T(8,128)(2,1)} %gather_grads.4.refs_1_), channel_id=1, source_target_pairs={{0,4},{4,0},{8,12},{12,8},{16,20},{20,16},{24,28},{28,24},{1,5},{5... | collective-permute-start | bytes 4718600 | tf_op jit(solution)/shard_map/ppermute | solution.py:947
  414.9 44.6 %collective-permute-start.56 = (bf16[1024,768]{1,0:T(8,128)(2,1)}, bf16[1024,768]{1,0:T(8,128)(2,1)}, u32[]{:S(2)}, u32[]{:S(2)}) collective-permute-start(bf16[1024,768]{1,0:T(8,128)(2,1)} %gather_grads.5.refs_2_), channel_id=1, source_target_pairs={{0,8},{4,12},{8,0},{12,4},{16,24},{20,28},{24,16},{28,20},{1,9},{5... | collective-permute-start | bytes 4718600 | tf_op jit(solution)/shard_map/ppermute | solution.py:947
  445.7 21.3 %all-to-all-start.1 = ((bf16[8,3,96,96]{3,2,1,0:T(8,128)(2,1)}), bf16[8,3,96,96]{3,2,1,0:T(8,128)(2,1)}, u32[]{:S(2)}, u32[]{:S(2)}) async-start(bf16[8,3,96,96]{3,2,1,0:T(8,128)(2,1)} %copy-done.16), calls=%async_computation.1 | async-start | bytes 1179648 | tf_op jit(solution)/shard_map/all_to_all | solution.py:1204
  479.0 21.9 %all-to-all-start.2 = ((bf16[8,3,96,96]{3,2,1,0:T(8,128)(2,1)}), bf16[8,3,96,96]{3,2,1,0:T(8,128)(2,1)}, u32[]{:S(2)}, u32[]{:S(2)}) async-start(bf16[8,3,96,96]{3,2,1,0:T(8,128)(2,1)} %copy-done.32), calls=%async_computation.2 | async-start | bytes 1179648 | tf_op jit(solution)/shard_map/all_to_all | solution.py:1204
  484.1 16.9 %collective-permute-start.58 = (f32[12,768]{1,0:T(8,128)S(1)}, f32[12,768]{1,0:T(8,128)}, u32[]{:S(2)}, u32[]{:S(2)}) collective-permute-start(f32[12,768]{1,0:T(8,128)S(1)} %add.168), channel_id=1, source_target_pairs={{0,16},{4,20},{8,24},{12,28},{16,0},{20,4},{24,8},{28,12},{1,17},{... | collective-permute-start | bytes 110600 | tf_op jit(solution)/shard_map/ppermute | solution.py:947
  506.0 19.6 %all-to-all-start.3 = ((bf16[8,3,96,96]{3,2,1,0:T(8,128)(2,1)}), bf16[8,3,96,96]{3,2,1,0:T(8,128)(2,1)S(1)}, u32[]{:S(2)}, u32[]{:S(2)}) async-start(bf16[8,3,96,96]{3,2,1,0:T(8,128)(2,1)} %copy-done.17), calls=%async_computation.3 | async-start | bytes 1179648 | tf_op jit(solution)/shard_map/all_to_all | solution.py:1204
  (109 other events, 652.3 us)
